TPU v7x, 32 devices: a whole 2x2x4 slice. The times are simulated.
32 devices in a mesh: gx: 4 (over z), gy: 4 (over y, core), ma: 2 (over x).
Axes of the slice: x: 2, y: 2, z: 4, core: 2. Of those that a mesh axis runs over, the one named last changes fastest.
Arguments:
- mode_fields: bfloat16 [3, 128, 64, 512], P(None, 'ma', 'gx', 'gy'), may hold values from -6 to 6
- cell_volumes: float32 [64, 512], P('gx', 'gy'), may hold values from 0.25 to 4
Outputs:
- convection: float32 [128, 128, 128], P(('gx', 'gy'), 'ma')
All inputs are finite; a program needn't handle non-finite values.
Results may differ from a plain program's by a relative error of at most 0.0051.
Values may be sent and summed in bfloat16 or wider, within the bound.
No kernel may reach another device: no remote copies, remote signals or barrier semaphores. Data moves between devices by JAX's collectives and lax.ppermute only.
A program may use at most 128 MiB of HBM per device.

v0:
```python
import math

import jax
import jax.numpy as jnp
from jax import lax
from jax.sharding import PartitionSpec as P


def padded_2(block, sides, width):
    for axis, dim in sides:
        count = lax.axis_size(axis)
        forward = [(i, i + 1) for i in range(count - 1)]
        backward = [(target, source) for source, target in forward]
        low = lax.ppermute(
            lax.slice_in_dim(block, block.shape[dim] - width, None, axis=dim), axis, forward
        )
        high = lax.ppermute(lax.slice_in_dim(block, 0, width, axis=dim), axis, backward)
        block = jnp.concatenate([low, block, high], axis=dim)
    return block


def rows_tensor(values, own_modes, slopes, weights):
    mode_count = values.shape[1]
    pair_width = own_modes.shape[1]
    row_count = values.shape[2]
    cell_count = values.shape[3]
    weighted = (weights[None, None] * values.astype(jnp.float32)).astype(jnp.bfloat16)
    flattened = jnp.transpose(weighted, (1, 0, 2, 3)).reshape(
        mode_count, 3 * row_count * cell_count
    )
    slope_float = jnp.transpose(
        slopes.reshape(2, 3, mode_count, row_count, cell_count), (0, 2, 1, 3, 4)
    ).astype(jnp.float32)
    block_size = min(8, pair_width)
    results = []
    for offset in range(0, pair_width, block_size):
        selected = own_modes[:, offset : offset + block_size].astype(jnp.float32)
        pairing = (
            selected[0][:, None, None, :, :] * slope_float[0][None]
            + selected[1][:, None, None, :, :] * slope_float[1][None]
        ).astype(jnp.bfloat16)
        products = lax.dot_general(
            flattened,
            pairing.reshape(block_size * mode_count, 3 * row_count * cell_count),
            (((1,), (1,)), ((), ())),
            preferred_element_type=jnp.float32,
        )
        results.append(products.reshape(mode_count, block_size, mode_count))
    return jnp.concatenate(results, 1)


def shards(mode_fields, cell_volumes):
    padded = padded_2(mode_fields, (("gx", 2), ("gy", 3)), 1)
    widened = padded.astype(jnp.float32)
    along_first = (widened[:, :, 2:, 1:-1] - widened[:, :, :-2, 1:-1]) * 0.5
    along_second = (widened[:, :, 1:-1, 2:] - widened[:, :, 1:-1, :-2]) * 0.5
    slopes = jnp.concatenate([along_first, along_second], 0).astype(jnp.bfloat16)
    stacked = jnp.concatenate([mode_fields, slopes], 0)
    total_cells = (
        cell_volumes.shape[0] * lax.axis_size("gx") * cell_volumes.shape[1] * lax.axis_size("gy")
    )
    weights = cell_volumes * (1.0 / math.sqrt(total_cells))
    regrouped = lax.all_to_all(stacked, "ma", split_axis=2, concat_axis=1, tiled=True)
    half_rows = regrouped.shape[2]
    row_start = lax.axis_index("ma") * half_rows
    own_weights = lax.dynamic_slice_in_dim(weights, row_start, half_rows, 0)
    mode_count = regrouped.shape[1]
    owners = lax.axis_size("ma")
    group_count = lax.axis_size("gx") * lax.axis_size("gy")
    share_size = mode_count // owners
    rows_each = mode_count // group_count
    halves_list = []
    for owner_index in range(owners):
        local_tensor = rows_tensor(
            regrouped[0:3],
            regrouped[0:2, owner_index * share_size : (owner_index + 1) * share_size],
            regrouped[3:9],
            own_weights,
        )
        halves_list.append(local_tensor.reshape(group_count, rows_each, share_size, mode_count))
    arranged = jnp.stack(halves_list, 1).reshape(
        group_count * owners * rows_each, share_size, mode_count
    )
    return lax.psum_scatter(arranged, ("gx", "gy", "ma"), scatter_dimension=0, tiled=True)


def solution(mesh):
    in_specs = (P(None, "ma", "gx", "gy"), P("gx", "gy"))
    out_specs = P(("gx", "gy"), "ma", None)
    return jax.shard_map(shards, mesh=mesh, in_specs=in_specs, out_specs=out_specs, check_vma=False)
```

profile of v0, /device:TPU:0, one launch (start us, length us, event | category | flops | bytes accessed | tf_op | source)
XLA Modules:
  0.0 313.5 jit_solution(15274118224512031289)
XLA Ops:
  6.5 2.3 copy.99
  9.2 4.9 %collective-permute-start = (bf16[3,64,1,128]{1,2,3,0:T(2,128)(2,1)S(1)}, bf16[3,64,1,128]{1,2,3,0:T(2,128)(2,1)S(1)}, u32[]{:S(2)}, u32[]{:S(2)}) collective-permute-start(bf16[3,64,1,128]{1,2,3,0:T(2,128)(2,1)S(1)} %get-tuple-element.27), channel_id=1, source_target_pairs={{0,8},{8,16},{16,24},{1,9},{9,17},{17,25},{2,10},{10,18},{18,26},{... | collective-permute-start | bytes 147464 | tf_op jit(solution)/shard_map/ppermute | solution.py:14
  15.4 2.8 collective-permute-done
  18.3 4.1 %collective-permute-done.1 = bf16[3,64,1,128]{1,2,3,0:T(2,128)(2,1)S(1)} collective-permute-done((bf16[3,64,1,128]{1,2,3,0:T(2,128)(2,1)S(1)}, bf16[3,64,1,128]{1,2,3,0:T(2,128)(2,1)S(1)}, u32[]{:S(2)}, u32[]{:S(2)}) %collective-permute-start.1) | collective-permute-done | bytes 49184 | tf_op jit(solution)/shard_map/ppermute | solution.py:17
  25.0 3.5 %collective-permute-done.3 = bf16[3,64,18,1]{1,2,3,0:T(8,128)(2,1)S(1)} collective-permute-done((bf16[3,64,18,1]{1,2,3,0:T(8,128)(2,1)S(1)}, bf16[3,64,18,1]{1,2,3,0:T(8,128)(2,1)S(1)}, u32[]{:S(2)}, u32[]{:S(2)}) %collective-permute-start.3) | collective-permute-done | bytes 6944 | tf_op jit(solution)/shard_map/ppermute | solution.py:17
  28.6 2.3 maximum_convert_fusion
  31.9 2.7 pad_maximum_fusion.1
  34.5 6.9 %copy.100 = bf16[9,64,16,128]{3,1,0,2:T(8,128)(2,1)} copy(bf16[9,64,16,128]{1,2,3,0:T(8,128)(2,1)} %pad_maximum_fusion.1) | data formatting | bytes 4718592 | tf_op jit(solution)/shard_map/concatenate | solution.py:58
  41.5 3.8 %all-to-all-start = ((bf16[9,64,16,128]{3,1,0,2:T(8,128)(2,1)}), bf16[9,64,16,128]{3,1,0,2:T(8,128)(2,1)S(1)}, u32[]{:S(2)}, u32[]{:S(2)}) async-start(bf16[9,64,16,128]{3,1,0,2:T(8,128)(2,1)} %copy.100), calls=%async_computation | async-start | bytes 4718592 | tf_op jit(solution)/shard_map/all_to_all | solution.py:63
  45.5 27.2 %all-to-all-done = bf16[9,64,16,128]{3,1,0,2:T(8,128)(2,1)S(1)} async-done(((bf16[9,64,16,128]{3,1,0,2:T(8,128)(2,1)}), bf16[9,64,16,128]{3,1,0,2:T(8,128)(2,1)S(1)}, u32[]{:S(2)}, u32[]{:S(2)}) %all-to-all-start) | async-done | bytes 2359328 | tf_op jit(solution)/shard_map/all_to_all | solution.py:63
  78.4 2.2 fusion.35
  80.6 2.2 fusion.51
  82.8 2.2 fusion.33
  85.0 2.4 fusion.31
  87.5 2.2 fusion.29
  89.7 2.2 fusion.27
  91.9 2.2 fusion.25
  94.1 2.2 fusion.23
  96.3 2.2 fusion.21
  98.5 2.2 fusion.49
  100.7 2.6 fusion.47
  103.4 2.2 fusion.45
  115.5 8.3 %copy.123 = f32[16,2,8,64,128]{4,3,2,1,0:T(8,128)} copy(f32[16,2,8,64,128]{4,2,0,3,1:T(8,128)S(1)} %pad_maximum_fusion) | data formatting | bytes 16777216 | tf_op jit(solution)/shard_map/stack | solution.py:81
  123.8 182.7 %reduce-scatter.2.cloned.1.call-done = f32[8,64,128]{2,1,0:T(8,128)} async-done(((f32[256,64,128]{2,1,0:T(8,128)}), f32[8,64,128]{2,1,0:T(8,128)}) %reduce-scatter.2.cloned.1.call-update) | async-done | bytes 262160 | tf_op jit(solution)/shard_map/reduce_scatter | solution.py:84
  (36 shorter events, 20.9 us)
Async XLA Ops:
  9.2 9.1 %collective-permute-start = (bf16[3,64,1,128]{1,2,3,0:T(2,128)(2,1)S(1)}, bf16[3,64,1,128]{1,2,3,0:T(2,128)(2,1)S(1)}, u32[]{:S(2)}, u32[]{:S(2)}) collective-permute-start(bf16[3,64,1,128]{1,2,3,0:T(2,128)(2,1)S(1)} %get-tuple-element.27), channel_id=1, source_target_pairs={{0,8},{8,16},{16,24},{1,9},{9,17},{17,25},{2,10},{10,18},{18,26},{... | collective-permute-start | bytes 147464 | tf_op jit(solution)/shard_map/ppermute | solution.py:14
  14.1 8.3 %collective-permute-start.1 = (bf16[3,64,1,128]{1,2,3,0:T(2,128)(2,1)S(1)}, bf16[3,64,1,128]{1,2,3,0:T(2,128)(2,1)S(1)}, u32[]{:S(2)}, u32[]{:S(2)}) collective-permute-start(bf16[3,64,1,128]{1,2,3,0:T(2,128)(2,1)S(1)} %get-tuple-element.28), channel_id=1, source_target_pairs={{8,0},{16,8},{24,16},{9,1},{17,9},{25,17},{10,2},{18,10},{26,18},{... | collective-permute-start | bytes 147464 | tf_op jit(solution)/shard_map/ppermute | solution.py:17
  22.4 2.6 collective-permute-start.2
  23.7 4.8 %collective-permute-start.3 = (bf16[3,64,18,1]{1,2,3,0:T(8,128)(2,1)S(1)}, bf16[3,64,18,1]{1,2,3,0:T(8,128)(2,1)S(1)}, u32[]{:S(2)}, u32[]{:S(2)}) collective-permute-start(bf16[3,64,18,1]{1,2,3,0:T(8,128)(2,1)S(1)} %get-tuple-element.26), channel_id=1, source_target_pairs={{2,0},{4,2},{6,4},{3,1},{5,3},{7,5},{10,8},{12,10},{14,12},{11,9},... | collective-permute-start | bytes 20744 | tf_op jit(solution)/shard_map/ppermute | solution.py:17
  34.5 11.0 %copy-start = (f32[16,128]{1,0:T(8,128)S(1)}, f32[16,128]{1,0:T(8,128)}, u32[]{:S(2)}) copy-start(f32[16,128]{1,0:T(8,128)} %param.3) | copy-start | bytes 24580
  41.5 31.3 %all-to-all-start = ((bf16[9,64,16,128]{3,1,0,2:T(8,128)(2,1)}), bf16[9,64,16,128]{3,1,0,2:T(8,128)(2,1)S(1)}, u32[]{:S(2)}, u32[]{:S(2)}) async-start(bf16[9,64,16,128]{3,1,0,2:T(8,128)(2,1)} %copy.100), calls=%async_computation | async-start | bytes 4718592 | tf_op jit(solution)/shard_map/all_to_all | solution.py:63
  45.3 261.2 %reduce-scatter.2.cloned.1.call-start = ((), (), s32[]{:S(2)}) async-start(), calls=%async_computation.2 | async-start | bytes 8650752 | tf_op jit(solution)/shard_map/reduce_scatter | solution.py:84
Sparse Core Ops, SparseCore 0:
  123.9 182.5 reduce-scatter.1
where the time goes:
time: 318 us; the launch traced here: 314 us
  waiting for transfers between devices  220 us (69%)
  matrix products  35.9 us (11%)
  local copies, waits for them, and re-layouts  22.7 us (7%)
  between operations  14 us (4%)
  starting transfers between devices  12.8 us (4%)
  other arithmetic  7.72 us (2%)
    reduce_scatter x1, waiting for transfers between devices, shards(): lax.psum_scatter(arranged, ('gx', 'gy', 'ma'), scatter_dimension=0, tiled...  183 us
    dot_general x16, matrix products, rows_tensor(): lax.dot_general(flattened, pairing.reshape(block_size * mode_count, 3 * r...  35.9 us
    all_to_all x1, waiting for transfers between devices, shards(): lax.all_to_all(stacked, 'ma', split_axis=2, concat_axis=1, tiled=True)  27.2 us
    another operation x1, local copies, waits for them, and re-layouts, shards(): jnp.stack(halves_list, 1)  8.26 us
    ppermute x2, waiting for transfers between devices, padded_2(): lax.ppermute(lax.slice_in_dim(block, 0, width, axis=dim), axis, backward)  7.65 us
    concatenate x1, local copies, waits for them, and re-layouts, shards(): stacked = jnp.concatenate([mode_fields, slopes], 0)  6.93 us
  transfers between devices with their start and end apart: 6, of which 5 were waited for; matrix products, arithmetic and copies ran while one was open for 0% of the time, Pallas kernels for 0%

commit v1 on v0

v1 whole, which is shorter than its diff:
```python
import functools
import math

import jax
import jax.numpy as jnp
from jax import lax
from jax.experimental import pallas as pl
from jax.experimental.pallas import tpu as pltpu
from jax.sharding import PartitionSpec as P

BF16 = jnp.bfloat16
F32 = jnp.float32


def bits_of(count):
    return count.bit_length() - 1


def send_order(mesh_sizes):
    order = []
    for axis in ("gy", "gx"):
        order += [(axis, bit) for bit in range(bits_of(mesh_sizes[axis]))]
    return order


def source_bits(mesh_sizes, rows_each):
    row_bits = bits_of(rows_each)
    base = {"gy": row_bits, "gx": row_bits + bits_of(mesh_sizes["gy"])}
    found = list(range(row_bits))
    for axis, bit in reversed(send_order(mesh_sizes)):
        found.append(base[axis] + bit)
    return found


def tensor_kernel(own_ref, other_ref, slope_ref, weight_ref, out_ref, left, right, *, bits, block, rows_each):
    row_count, _, share, cells = own_ref.shape
    step = pl.program_id(0)
    gy_count = lax.axis_size("gy")
    top = bits_of(2 * share) - 1

    @pl.when(step == 0)
    def _():
        for x in range(row_count):
            weight = weight_ref[pl.ds(x, 1), :]
            for half, ref in enumerate((own_ref, other_ref)):
                for a in range(3):
                    value = (weight * ref[x, a].astype(F32)).astype(BF16)
                    left[x, a, half * share : (half + 1) * share, :] = value.astype(F32)
            for b in range(2):
                both = jnp.concatenate([own_ref[x, b], other_ref[x, b]], 0)
                right[(2 * x + b) * cells : (2 * x + b + 1) * cells, :] = both.T

    here = (lax.axis_index("gx") * gy_count + lax.axis_index("gy")) * rows_each
    here = here ^ (lax.axis_index("ma") << top)
    start = here
    position = step * block
    for place, bit in enumerate(bits):
        start = start ^ (((position >> place) & 1) << bit)
    columns = []
    for x in range(row_count):
        slopes = [slope_ref[x, n] for n in range(6)]
        sums = [[], []]
        for row in range(block):
            offset = 0
            for place, bit in enumerate(bits):
                offset |= ((row >> place) & 1) << bit
            test = [
                jnp.concatenate(
                    [left[x, a, pl.ds(start ^ offset, 16, stride=0), :].astype(BF16)] * (share // 16), 0
                )
                for a in range(3)
            ]
            for b in range(2):
                sums[b].append(
                    test[0] * slopes[3 * b] + test[1] * slopes[3 * b + 1] + test[2] * slopes[3 * b + 2]
                )
        columns += [jnp.concatenate(sums[0], 0), jnp.concatenate(sums[1], 0)]
    sums = jnp.concatenate(columns, 1)
    out_ref[...] = jnp.dot(sums, right[...], preferred_element_type=F32).reshape(out_ref.shape)


def partial_tensor(own, other, slopes, weights, mesh_sizes, rows_each):
    row_count, _, share, cells = own.shape
    block = 8
    body = functools.partial(
        tensor_kernel, bits=source_bits(mesh_sizes, rows_each), block=block, rows_each=rows_each
    )
    whole = lambda array: pl.BlockSpec(array.shape, lambda g: (0,) * array.ndim, pipeline_mode=pl.Buffered(1))
    modes = 2 * share
    return pl.pallas_call(
        body,
        grid=(modes // block,),
        out_shape=jax.ShapeDtypeStruct((modes, share, modes), F32),
        in_specs=[whole(own), whole(other), whole(slopes), whole(weights)],
        out_specs=pl.BlockSpec((block, share, modes), lambda g: (g, 0, 0)),
        scratch_shapes=[
            pltpu.VMEM((row_count, 3, modes, cells), F32),
            pltpu.VMEM((row_count * 2 * cells, modes), BF16),
        ],
        compiler_params=pltpu.CompilerParams(vmem_limit_bytes=58 << 20),
        cost_estimate=pl.CostEstimate(
            flops=4 * modes * share * modes * row_count * cells, bytes_accessed=8 << 20, transcendentals=0
        ),
    )(own, other, slopes, weights)


def neighbours(axis):
    count = lax.axis_size(axis)
    forward = [(i, i + 1) for i in range(count - 1)]
    return forward, [(target, source) for source, target in forward]


def shards(mode_fields, cell_volumes, mesh_sizes):
    total_cells = (
        cell_volumes.shape[0] * mesh_sizes["gx"] * cell_volumes.shape[1] * mesh_sizes["gy"]
    )
    weights = cell_volumes * (1.0 / math.sqrt(total_cells))
    own = jnp.transpose(mode_fields, (2, 0, 1, 3))
    swap = [(0, 1), (1, 0)]
    share = own.shape[2]
    rows_each = 2 * share // (mesh_sizes["gx"] * mesh_sizes["gy"])

    forward, backward = neighbours("gx")
    above = lax.ppermute(own[-1:], "gx", forward)
    below = lax.ppermute(own[:1], "gx", backward)
    forward, backward = neighbours("gy")
    before = lax.ppermute(own[:, :, :, -1], "gy", forward)
    after = lax.ppermute(own[:, :, :, 0], "gy", backward)
    other = lax.ppermute(own, "ma", swap)

    tall = jnp.concatenate([above, own, below], 0).astype(F32)
    along_first = (tall[2:] - tall[:-2]) * 0.5
    wide = jnp.concatenate([before[..., None], own, after[..., None]], 3).astype(F32)
    along_second = (wide[..., 2:] - wide[..., :-2]) * 0.5
    slopes = jnp.concatenate([along_first, along_second], 1).astype(BF16)

    partial = partial_tensor(own, other, slopes, weights, mesh_sizes, rows_each)
    for axis, bit in send_order(mesh_sizes):
        pairs = [(i, i ^ (1 << bit)) for i in range(mesh_sizes[axis])]
        half = partial.shape[0] // 2
        arrived = lax.ppermute(partial[half:].astype(BF16), axis, pairs)
        partial = partial[:half] + arrived.astype(F32)
    partial = jnp.transpose(partial, (0, 2, 1))
    arrived = lax.ppermute(partial[:, share:], "ma", swap)
    kept = partial[:, :share]
    first = lax.axis_index("ma") == 0
    return jnp.concatenate([jnp.where(first, kept, arrived), jnp.where(first, arrived, kept)], 2)


def solution(mesh):
    in_specs = (P(None, "ma", "gx", "gy"), P("gx", "gy"))
    out_specs = P(("gx", "gy"), "ma", None)
    body = functools.partial(shards, mesh_sizes=dict(mesh.shape))
    return jax.shard_map(body, mesh=mesh, in_specs=in_specs, out_specs=out_specs, check_vma=False)
```

time: 318 us -> 91.2 us (0.29); the launches traced: 314 us -> 90.9 us
  waiting for transfers between devices: 220 us -> 34.9 us
  matrix products: 35.9 us -> 0 us
  Pallas kernels: 0 us -> 24.1 us
  local copies, waits for them, and re-layouts: 22.7 us -> 7.26 us
  between operations: 14 us -> 0.23 us
  starting transfers between devices: 12.8 us -> 18.5 us
    reduce_scatter x1 -> x0, waiting for transfers between devices: 183 us -> none  [shards(): lax.psum_scatter(arranged, ('gx', 'gy', 'ma'), scatter_dimension=0, tiled...]
    dot_general x16 -> x0, matrix products: 35.9 us -> none  [rows_tensor(): lax.dot_general(flattened, pairing.reshape(block_size * mode_count, 3 * r...]
    all_to_all x1 -> x0, waiting for transfers between devices: 27.2 us -> none  [shards(): lax.all_to_all(stacked, 'ma', split_axis=2, concat_axis=1, tiled=True)]
    ppermute x4 -> x10, waiting for transfers between devices: 10.5 us -> 34.9 us  [the longest x4 25.7 us: shards(): arrived = lax.ppermute(partial[half:].astype(BF16), axis, pairs)]
    pallas_call x0 -> x1, Pallas kernels: none -> 24.1 us  [partial_tensor(): pl.pallas_call(body, grid=(modes // block,), out_shape=jax.ShapeDtypeStru...]
    ppermute x4 -> x10, starting transfers between devices: 8.81 us -> 18.5 us  [the longest x4 6.45 us: shards(): arrived = lax.ppermute(partial[half:].astype(BF16), axis, pairs)]
    another operation x1 -> x0, local copies, waits for them, and re-layouts: 8.26 us -> none  [shards(): jnp.stack(halves_list, 1)]
    concatenate x1, local copies, waits for them, and re-layouts: 6.93 us -> 0.89 us  [shards(): jnp.concatenate([jnp.where(first, kept, arrived), jnp.where(first, arrive...]
  transfers between devices with their start and end apart: 6 -> 10, of which waited for: 5 -> 7; matrix products, arithmetic and copies ran while one was open for 0% -> 6% of each run, Pallas kernels for 0% -> 0%
where the time goes in v1:
time: 91.2 us; the launch traced here: 90.9 us
  waiting for transfers between devices  34.9 us (38%)
  Pallas kernels  24.1 us (26%)
  starting transfers between devices  18.5 us (20%)
  local copies, waits for them, and re-layouts  7.26 us (8%)
  other arithmetic  5.92 us (6%)
    ppermute x4, waiting for transfers between devices, shards(): arrived = lax.ppermute(partial[half:].astype(BF16), axis, pairs)  25.7 us
    pallas_call x1, Pallas kernels, partial_tensor(): pl.pallas_call(body, grid=(modes // block,), out_shape=jax.ShapeDtypeStru...  24.1 us
    ppermute x4, starting transfers between devices, shards(): arrived = lax.ppermute(partial[half:].astype(BF16), axis, pairs)  6.45 us
    ppermute x1, waiting for transfers between devices, shards(): arrived = lax.ppermute(partial[:, share:], 'ma', swap)  4.93 us
    ppermute x1, starting transfers between devices, shards(): above = lax.ppermute(own[-1:], 'gx', forward)  3.48 us
    ppermute x1, starting transfers between devices, shards(): other = lax.ppermute(own, 'ma', swap)  3 us
    ppermute x1, waiting for transfers between devices, shards(): other = lax.ppermute(own, 'ma', swap)  2.48 us
    unnamed x7, local copies, waits for them, and re-layouts  2.24 us
  transfers between devices with their start and end apart: 10, of which 7 were waited for; matrix products, arithmetic and copies ran while one was open for 6% of the time, Pallas kernels for 0%

profile of v1, /device:TPU:0, one launch (start us, length us, event | category | flops | bytes accessed | tf_op | source)
XLA Modules:
  0.0 90.9 jit_solution(6292521619000648629)
XLA Ops:
  0.0 1.3 %copy.20 = bf16[3,64,16,128]{3,1,0,2:T(8,128)(2,1)S(1)} copy(bf16[3,64,16,128]{3,2,1,0:T(8,128)(2,1)} %param.2) | data formatting | bytes 1572864 | tf_op args[0]
  1.4 3.0 %collective-permute-start = (bf16[16,3,64,128]{3,2,1,0:T(8,128)(2,1)S(1)}, bf16[16,3,64,128]{3,2,1,0:T(8,128)(2,1)S(1)}, u32[]{:S(2)}, u32[]{:S(2)}) collective-permute-start(bf16[16,3,64,128]{3,2,1,0:T(8,128)(2,1)S(1)} %bitcast.9), channel_id=1, source_target_pairs={{0,1},{1,0},{2,3},{3,2},{4,5},{5,4},{6,7},{7,6},{8,9},{9,8},{10,11... | collective-permute-start | bytes 2359304 | tf_op jit(solution)/shard_map/ppermute | solution.py:129
  5.1 1.4 %collective-permute-start.3 = (bf16[16,3,64]{2,0,1:T(8,128)(2,1)S(1)}, bf16[16,3,64]{2,0,1:T(8,128)(2,1)S(1)}, u32[]{:S(2)}, u32[]{:S(2)}) collective-permute-start(bf16[16,3,64]{2,0,1:T(8,128)(2,1)S(1)} %bitcast.15), channel_id=1, source_target_pairs={{0,2},{2,4},{4,6},{1,3},{3,5},{5,7},{8,10},{10,12},{12,14},{9,11},... | collective-permute-start | bytes 18440 | tf_op jit(solution)/shard_map/ppermute | solution.py:127
  6.9 1.3 %collective-permute-start.4 = (bf16[16,3,64]{2,0,1:T(8,128)(2,1)S(1)}, bf16[16,3,64]{2,0,1:T(8,128)(2,1)S(1)}, u32[]{:S(2)}, u32[]{:S(2)}) collective-permute-start(bf16[16,3,64]{2,0,1:T(8,128)(2,1)S(1)} %bitcast.17), channel_id=1, source_target_pairs={{2,0},{4,2},{6,4},{3,1},{5,3},{7,5},{10,8},{12,10},{14,12},{11,9},... | collective-permute-start | bytes 18440 | tf_op jit(solution)/shard_map/ppermute | solution.py:128
  8.2 3.5 %collective-permute-start.1 = (bf16[1,3,64,128]{3,2,1,0:T(8,128)(2,1)S(1)}, bf16[1,3,64,128]{3,2,1,0:T(8,128)(2,1)S(1)}, u32[]{:S(2)}, u32[]{:S(2)}) collective-permute-start(bf16[1,3,64,128]{3,2,1,0:T(8,128)(2,1)S(1)} %get-tuple-element.5), channel_id=1, source_target_pairs={{0,8},{8,16},{16,24},{1,9},{9,17},{17,25},{2,10},{10,18},{18,26},{... | collective-permute-start | bytes 147464 | tf_op jit(solution)/shard_map/ppermute | solution.py:124
  11.7 1.3 %collective-permute-start.2 = (bf16[1,3,64,128]{3,2,1,0:T(8,128)(2,1)S(1)}, bf16[1,3,64,128]{3,2,1,0:T(8,128)(2,1)S(1)}, u32[]{:S(2)}, u32[]{:S(2)}) collective-permute-start(bf16[1,3,64,128]{3,2,1,0:T(8,128)(2,1)S(1)} %get-tuple-element.6), channel_id=1, source_target_pairs={{8,0},{16,8},{24,16},{9,1},{17,9},{25,17},{10,2},{18,10},{26,18},{... | collective-permute-start | bytes 147464 | tf_op jit(solution)/shard_map/ppermute | solution.py:125
  14.6 0.9 maximum_convert_fusion
  16.0 1.7 %collective-permute-done.2 = bf16[1,3,64,128]{3,2,1,0:T(8,128)(2,1)S(1)} collective-permute-done((bf16[1,3,64,128]{3,2,1,0:T(8,128)(2,1)S(1)}, bf16[1,3,64,128]{3,2,1,0:T(8,128)(2,1)S(1)}, u32[]{:S(2)}, u32[]{:S(2)}) %collective-permute-start.2) | collective-permute-done | bytes 49184 | tf_op jit(solution)/shard_map/ppermute | solution.py:125
  18.1 1.3 %pad_maximum_fusion.slope_ref = bf16[16,6,64,128]{3,2,1,0:T(8,128)(2,1)} fusion(bf16[16,3,64,128]{3,2,1,0:T(8,128)(2,1)S(1)} %fusion.1, bf16[16,3,64,128]{3,2,1,0:T(8,128)(2,1)S(1)} %fusion.3), kind=kLoop, calls=%fused_computation.9 | loop fusion | flops 786432 | bytes 3145728 | tf_op jit(solution)/shard_map/concatenate | solution.py:135
  19.4 2.5 %collective-permute-done.other_ref = bf16[16,3,64,128]{3,2,1,0:T(8,128)(2,1)S(1)} collective-permute-done((bf16[16,3,64,128]{3,2,1,0:T(8,128)(2,1)S(1)}, bf16[16,3,64,128]{3,2,1,0:T(8,128)(2,1)S(1)}, u32[]{:S(2)}, u32[]{:S(2)}) %collective-permute-start) | collective-permute-done | bytes 786464 | tf_op jit(solution)/shard_map/ppermute | solution.py:129
  21.9 0.9 copy-done.2
  22.8 24.1 %shard_map.28 = f32[128,64,128]{2,1,0:T(8,128)} custom-call(bf16[16,3,64,128]{3,2,1,0:T(8,128)(2,1)} %bitcast.14, bf16[16,3,64,128]{3,2,1,0:T(8,128)(2,1)} %copy-done.2, bf16[16,6,64,128]{3,2,1,0:T(8,128)(2,1)} %pad_maximum_fusion.slope_ref, f32[16,128]{1,0:T(8,128)} %broadcast_multiply_fusion.weight_ref), custom_call_target="tpu_custom_call" | custom-call | flops 8589934592 | bytes 8388608 | tf_op jit(solution)/shard_map/pallas_call | solution.py:90
  46.9 1.8 %slice.118 = bf16[64,64,128]{2,1,0:T(8,128)(2,1)S(1)} slice(f32[128,64,128]{2,1,0:T(8,128)} %shard_map.28), slice={[64:128], [0:64], [0:128]} | slice | bytes 2097152 | tf_op jit(solution)/shard_map/slice | solution.py:141
  48.8 2.6 %collective-permute-done.5 = bf16[64,64,128]{2,1,0:T(8,128)(2,1)S(1)} collective-permute-done((bf16[64,64,128]{2,1,0:T(8,128)(2,1)S(1)}, bf16[64,64,128]{2,1,0:T(8,128)(2,1)S(1)}, u32[]{:S(2)}, u32[]{:S(2)}) %collective-permute-start.5) | collective-permute-done | bytes 1048608 | tf_op jit(solution)/shard_map/ppermute | solution.py:141
  51.5 1.9 %slice_add_fusion = f32[64,64,128]{2,1,0:T(8,128)S(1)} fusion(f32[128,64,128]{2,1,0:T(8,128)} %shard_map.28, bf16[64,64,128]{2,1,0:T(8,128)(2,1)S(1)} %collective-permute-done.5), kind=kLoop, calls=%fused_computation.1 | loop fusion | flops 1048576 | bytes 5242880 | tf_op jit(solution)/shard_map/add | solution.py:142
  53.5 1.9 %collective-permute-start.6 = (bf16[32,64,128]{2,1,0:T(8,128)(2,1)S(1)}, bf16[32,64,128]{2,1,0:T(8,128)(2,1)S(1)}, u32[]{:S(2)}, u32[]{:S(2)}) collective-permute-start(bf16[32,64,128]{2,1,0:T(8,128)(2,1)S(1)} %slice.119), channel_id=1, source_target_pairs={{0,4},{2,6},{4,0},{6,2},{1,5},{3,7},{5,1},{7,3},{8,12},{10,14},{12... | collective-permute-start | bytes 1572872 | tf_op jit(solution)/shard_map/ppermute | solution.py:141
  55.4 12.2 %collective-permute-done.6 = bf16[32,64,128]{2,1,0:T(8,128)(2,1)S(1)} collective-permute-done((bf16[32,64,128]{2,1,0:T(8,128)(2,1)S(1)}, bf16[32,64,128]{2,1,0:T(8,128)(2,1)S(1)}, u32[]{:S(2)}, u32[]{:S(2)}) %collective-permute-start.6) | collective-permute-done | bytes 524320 | tf_op jit(solution)/shard_map/ppermute | solution.py:141
  67.8 1.8 %collective-permute-start.7 = (bf16[16,64,128]{2,1,0:T(8,128)(2,1)S(1)}, bf16[16,64,128]{2,1,0:T(8,128)(2,1)S(1)}, u32[]{:S(2)}, u32[]{:S(2)}) collective-permute-start(bf16[16,64,128]{2,1,0:T(8,128)(2,1)S(1)} %slice.120), channel_id=1, source_target_pairs={{0,8},{8,0},{16,24},{24,16},{1,9},{9,1},{17,25},{25,17},{2,10},{10... | collective-permute-start | bytes 786440 | tf_op jit(solution)/shard_map/ppermute | solution.py:141
  69.6 5.9 %collective-permute-done.7 = bf16[16,64,128]{2,1,0:T(8,128)(2,1)S(1)} collective-permute-done((bf16[16,64,128]{2,1,0:T(8,128)(2,1)S(1)}, bf16[16,64,128]{2,1,0:T(8,128)(2,1)S(1)}, u32[]{:S(2)}, u32[]{:S(2)}) %collective-permute-start.7) | collective-permute-done | bytes 262176 | tf_op jit(solution)/shard_map/ppermute | solution.py:141
  75.6 2.7 %collective-permute-start.8 = (bf16[8,64,128]{2,1,0:T(8,128)(2,1)S(1)}, bf16[8,64,128]{2,1,0:T(8,128)(2,1)S(1)}, u32[]{:S(2)}, u32[]{:S(2)}) collective-permute-start(bf16[8,64,128]{2,1,0:T(8,128)(2,1)S(1)} %slice.121), channel_id=1, source_target_pairs={{0,16},{8,24},{16,0},{24,8},{1,17},{9,25},{17,1},{25,9},{2,18},{10... | collective-permute-start | bytes 393224 | tf_op jit(solution)/shard_map/ppermute | solution.py:141
  78.3 5.0 %collective-permute-done.8 = bf16[8,64,128]{2,1,0:T(8,128)(2,1)S(1)} collective-permute-done((bf16[8,64,128]{2,1,0:T(8,128)(2,1)S(1)}, bf16[8,64,128]{2,1,0:T(8,128)(2,1)S(1)}, u32[]{:S(2)}, u32[]{:S(2)}) %collective-permute-start.8) | collective-permute-done | bytes 131104 | tf_op jit(solution)/shard_map/ppermute | solution.py:141
  83.4 1.5 %collective-permute-start.9 = (f32[8,64,64]{1,2,0:T(8,128)S(1)}, f32[8,64,64]{1,2,0:T(8,128)S(1)}, u32[]{:S(2)}, u32[]{:S(2)}) collective-permute-start(f32[8,64,64]{1,2,0:T(8,128)S(1)} %slice.93), channel_id=1, source_target_pairs={{0,1},{1,0},{2,3},{3,2},{4,5},{5,4},{6,7},{7,6},{8,9},{9,8},{10,11... | collective-permute-start | bytes 393224 | tf_op jit(solution)/shard_map/ppermute | solution.py:144
  84.9 4.9 %collective-permute-done.9 = f32[8,64,64]{1,2,0:T(8,128)S(1)} collective-permute-done((f32[8,64,64]{1,2,0:T(8,128)S(1)}, f32[8,64,64]{1,2,0:T(8,128)S(1)}, u32[]{:S(2)}, u32[]{:S(2)}) %collective-permute-start.9) | collective-permute-done | bytes 131104 | tf_op jit(solution)/shard_map/ppermute | solution.py:144
  90.0 0.9 copy.18
  (28 shorter events, 4.2 us)
Async XLA Ops:
  1.3 16.4 %copy-start = (bf16[3,64,16,128]{3,1,0,2:T(8,128)(2,1)}, bf16[3,64,16,128]{3,1,0,2:T(8,128)(2,1)S(1)}, u32[]{:S(2)}) copy-start(bf16[3,64,16,128]{3,1,0,2:T(8,128)(2,1)S(1)} %copy.20) | copy-start | bytes 2359300
  1.3 11.7 %copy-start.1 = (f32[16,128]{1,0:T(8,128)S(1)}, f32[16,128]{1,0:T(8,128)}, u32[]{:S(2)}) copy-start(f32[16,128]{1,0:T(8,128)} %param.3) | copy-start | bytes 24580
  1.4 20.5 %collective-permute-start = (bf16[16,3,64,128]{3,2,1,0:T(8,128)(2,1)S(1)}, bf16[16,3,64,128]{3,2,1,0:T(8,128)(2,1)S(1)}, u32[]{:S(2)}, u32[]{:S(2)}) collective-permute-start(bf16[16,3,64,128]{3,2,1,0:T(8,128)(2,1)S(1)} %bitcast.9), channel_id=1, source_target_pairs={{0,1},{1,0},{2,3},{3,2},{4,5},{5,4},{6,7},{7,6},{8,9},{9,8},{10,11... | collective-permute-start | bytes 2359304 | tf_op jit(solution)/shard_map/ppermute | solution.py:129
  5.1 8.5 %collective-permute-start.3 = (bf16[16,3,64]{2,0,1:T(8,128)(2,1)S(1)}, bf16[16,3,64]{2,0,1:T(8,128)(2,1)S(1)}, u32[]{:S(2)}, u32[]{:S(2)}) collective-permute-start(bf16[16,3,64]{2,0,1:T(8,128)(2,1)S(1)} %bitcast.15), channel_id=1, source_target_pairs={{0,2},{2,4},{4,6},{1,3},{3,5},{5,7},{8,10},{10,12},{12,14},{9,11},... | collective-permute-start | bytes 18440 | tf_op jit(solution)/shard_map/ppermute | solution.py:127
  6.9 7.2 %collective-permute-start.4 = (bf16[16,3,64]{2,0,1:T(8,128)(2,1)S(1)}, bf16[16,3,64]{2,0,1:T(8,128)(2,1)S(1)}, u32[]{:S(2)}, u32[]{:S(2)}) collective-permute-start(bf16[16,3,64]{2,0,1:T(8,128)(2,1)S(1)} %bitcast.17), channel_id=1, source_target_pairs={{2,0},{4,2},{6,4},{3,1},{5,3},{7,5},{10,8},{12,10},{14,12},{11,9},... | collective-permute-start | bytes 18440 | tf_op jit(solution)/shard_map/ppermute | solution.py:128
  8.2 7.8 %collective-permute-start.1 = (bf16[1,3,64,128]{3,2,1,0:T(8,128)(2,1)S(1)}, bf16[1,3,64,128]{3,2,1,0:T(8,128)(2,1)S(1)}, u32[]{:S(2)}, u32[]{:S(2)}) collective-permute-start(bf16[1,3,64,128]{3,2,1,0:T(8,128)(2,1)S(1)} %get-tuple-element.5), channel_id=1, source_target_pairs={{0,8},{8,16},{16,24},{1,9},{9,17},{17,25},{2,10},{10,18},{18,26},{... | collective-permute-start | bytes 147464 | tf_op jit(solution)/shard_map/ppermute | solution.py:124
  11.7 6.0 %collective-permute-start.2 = (bf16[1,3,64,128]{3,2,1,0:T(8,128)(2,1)S(1)}, bf16[1,3,64,128]{3,2,1,0:T(8,128)(2,1)S(1)}, u32[]{:S(2)}, u32[]{:S(2)}) collective-permute-start(bf16[1,3,64,128]{3,2,1,0:T(8,128)(2,1)S(1)} %get-tuple-element.6), channel_id=1, source_target_pairs={{8,0},{16,8},{24,16},{9,1},{17,9},{25,17},{10,2},{18,10},{26,18},{... | collective-permute-start | bytes 147464 | tf_op jit(solution)/shard_map/ppermute | solution.py:125
  21.9 0.9 copy-start.2
  48.7 2.7 %collective-permute-start.5 = (bf16[64,64,128]{2,1,0:T(8,128)(2,1)S(1)}, bf16[64,64,128]{2,1,0:T(8,128)(2,1)S(1)}, u32[]{:S(2)}, u32[]{:S(2)}) collective-permute-start(bf16[64,64,128]{2,1,0:T(8,128)(2,1)S(1)} %slice.118), channel_id=1, source_target_pairs={{0,2},{2,0},{4,6},{6,4},{1,3},{3,1},{5,7},{7,5},{8,10},{10,8},{12,... | collective-permute-start | bytes 3145736 | tf_op jit(solution)/shard_map/ppermute | solution.py:141
  53.5 14.1 %collective-permute-start.6 = (bf16[32,64,128]{2,1,0:T(8,128)(2,1)S(1)}, bf16[32,64,128]{2,1,0:T(8,128)(2,1)S(1)}, u32[]{:S(2)}, u32[]{:S(2)}) collective-permute-start(bf16[32,64,128]{2,1,0:T(8,128)(2,1)S(1)} %slice.119), channel_id=1, source_target_pairs={{0,4},{2,6},{4,0},{6,2},{1,5},{3,7},{5,1},{7,3},{8,12},{10,14},{12... | collective-permute-start | bytes 1572872 | tf_op jit(solution)/shard_map/ppermute | solution.py:141
  67.8 7.7 %collective-permute-start.7 = (bf16[16,64,128]{2,1,0:T(8,128)(2,1)S(1)}, bf16[16,64,128]{2,1,0:T(8,128)(2,1)S(1)}, u32[]{:S(2)}, u32[]{:S(2)}) collective-permute-start(bf16[16,64,128]{2,1,0:T(8,128)(2,1)S(1)} %slice.120), channel_id=1, source_target_pairs={{0,8},{8,0},{16,24},{24,16},{1,9},{9,1},{17,25},{25,17},{2,10},{10... | collective-permute-start | bytes 786440 | tf_op jit(solution)/shard_map/ppermute | solution.py:141
  75.6 7.7 %collective-permute-start.8 = (bf16[8,64,128]{2,1,0:T(8,128)(2,1)S(1)}, bf16[8,64,128]{2,1,0:T(8,128)(2,1)S(1)}, u32[]{:S(2)}, u32[]{:S(2)}) collective-permute-start(bf16[8,64,128]{2,1,0:T(8,128)(2,1)S(1)} %slice.121), channel_id=1, source_target_pairs={{0,16},{8,24},{16,0},{24,8},{1,17},{9,25},{17,1},{25,9},{2,18},{10... | collective-permute-start | bytes 393224 | tf_op jit(solution)/shard_map/ppermute | solution.py:141
  83.4 6.4 %collective-permute-start.9 = (f32[8,64,64]{1,2,0:T(8,128)S(1)}, f32[8,64,64]{1,2,0:T(8,128)S(1)}, u32[]{:S(2)}, u32[]{:S(2)}) collective-permute-start(f32[8,64,64]{1,2,0:T(8,128)S(1)} %slice.93), channel_id=1, source_target_pairs={{0,1},{1,0},{2,3},{3,2},{4,5},{5,4},{6,7},{7,6},{8,9},{9,8},{10,11... | collective-permute-start | bytes 393224 | tf_op jit(solution)/shard_map/ppermute | solution.py:144

commit v2 on v1

v2 whole, which is shorter than its diff:
```python
import functools
import math

import jax
import jax.numpy as jnp
from jax import lax
from jax.experimental import pallas as pl
from jax.experimental.pallas import tpu as pltpu
from jax.sharding import PartitionSpec as P

BF16 = jnp.bfloat16
F32 = jnp.float32


def bits_of(count):
    return count.bit_length() - 1


def send_order(mesh_sizes):
    order = []
    for axis in ("gy", "gx"):
        order += [(axis, bit) for bit in range(bits_of(mesh_sizes[axis]))]
    return order


def source_bits(mesh_sizes, rows_each, chunks):
    row_bits = bits_of(rows_each)
    base = {"gy": row_bits, "gx": row_bits + bits_of(mesh_sizes["gy"])}
    inner = row_bits - bits_of(chunks)
    found = list(range(inner))
    for axis, bit in reversed(send_order(mesh_sizes)):
        found.append(base[axis] + bit)
    return found + list(range(inner, row_bits))


def tensor_kernel(*refs, bits, block, rows_each, first_step, split):
    own_ref, other_ref, slope_ref, weight_ref = refs[:4]
    refs = refs[4:]
    before_ref = None
    if first_step is not None:
        before_ref, refs = refs[0], refs[1:]
    if split:
        keep_ref, send_ref, left, right = refs
    else:
        keep_ref, left, right = refs
    row_count, _, share, cells = own_ref.shape
    step = pl.program_id(0)
    top = bits_of(2 * share) - 1

    @pl.when(step == 0)
    def _():
        for x in range(row_count):
            weight = weight_ref[pl.ds(x, 1), :]
            for half, ref in enumerate((own_ref, other_ref)):
                for a in range(3):
                    value = (weight * ref[x, a].astype(F32)).astype(BF16)
                    left[x, a, half * share : (half + 1) * share, :] = value.astype(F32)
                for b in range(2):
                    right[
                        half * share : (half + 1) * share, (2 * x + b) * cells : (2 * x + b + 1) * cells
                    ] = ref[x, b]

    here = (lax.axis_index("gx") * lax.axis_size("gy") + lax.axis_index("gy")) * rows_each
    start = here ^ (lax.axis_index("ma") << top)
    if split:
        steps = pl.num_programs(0)
        position = (first_step + lax.rem(step + steps // 2, steps)) * block
    else:
        position = step * block
    for place, bit in enumerate(bits):
        start = start ^ (((position >> place) & 1) << bit)
    columns = []
    for x in range(row_count):
        slopes = [slope_ref[x, n] for n in range(6)]
        sums = [[], []]
        for row in range(block):
            offset = 0
            for place, bit in enumerate(bits):
                offset |= ((row >> place) & 1) << bit
            test = [
                jnp.concatenate(
                    [left[x, a, pl.ds(start ^ offset, 16, stride=0), :].astype(BF16)] * (share // 16), 0
                )
                for a in range(3)
            ]
            for b in range(2):
                sums[b].append(
                    test[0] * slopes[3 * b] + test[1] * slopes[3 * b + 1] + test[2] * slopes[3 * b + 2]
                )
        columns += [jnp.concatenate(sums[0], 0), jnp.concatenate(sums[1], 0)]
    sums = jnp.concatenate(columns, 1)
    product = lax.dot_general(sums, right[...], (((1,), (1,)), ((), ())), preferred_element_type=F32)
    product = product.reshape(block, share, 2 * share)
    if before_ref is not None:
        product = product + before_ref[...]
    if not split:
        keep_ref[...] = product
    else:
        half = pl.num_programs(0) // 2

        @pl.when(step < half)
        def _():
            send_ref[...] = product.astype(BF16)

        @pl.when(step >= half)
        def _():
            keep_ref[...] = product


def partial_tensor(own, other, slopes, weights, mesh_sizes, rows_each, chunks, chunk=None, before=None):
    row_count, _, share, cells = own.shape
    modes = 2 * share
    block = 16
    split = chunk is not None
    count = modes // chunks if split else modes
    steps = count // block
    half = steps // 2
    first_step = chunk * steps if split else None
    body = functools.partial(
        tensor_kernel,
        bits=source_bits(mesh_sizes, rows_each, chunks),
        block=block,
        rows_each=rows_each,
        first_step=first_step,
        split=split,
    )
    whole = lambda array: pl.BlockSpec(array.shape, lambda g: (0,) * array.ndim, pipeline_mode=pl.Buffered(1))
    shape = (block, share, modes)
    place = lambda g: (g + half) % steps
    operands = [own, other, slopes, weights]
    in_specs = [whole(array) for array in operands]
    if split:
        operands.append(before)
        in_specs.append(pl.BlockSpec(shape, lambda g: (first_step + place(g), 0, 0)))
        out_shape = (
            jax.ShapeDtypeStruct((count // 2, share, modes), F32),
            jax.ShapeDtypeStruct((count // 2, share, modes), BF16),
        )
        out_specs = (
            pl.BlockSpec(shape, lambda g: (jnp.maximum(g - half, 0), 0, 0)),
            pl.BlockSpec(shape, lambda g: (jnp.minimum(g, half - 1), 0, 0)),
        )
    else:
        out_shape = jax.ShapeDtypeStruct((count, share, modes), F32)
        out_specs = pl.BlockSpec(shape, lambda g: (g, 0, 0))
    return pl.pallas_call(
        body,
        grid=(steps,),
        out_shape=out_shape,
        in_specs=in_specs,
        out_specs=out_specs,
        scratch_shapes=[
            pltpu.VMEM((row_count, 3, modes, cells), F32),
            pltpu.VMEM((modes, row_count * 2 * cells), BF16),
        ],
        compiler_params=pltpu.CompilerParams(vmem_limit_bytes=40 << 20),
        cost_estimate=pl.CostEstimate(
            flops=8 * count * share * modes * row_count * cells, bytes_accessed=8 << 20, transcendentals=0
        ),
    )(*operands)


def neighbours(axis):
    count = lax.axis_size(axis)
    forward = [(i, i + 1) for i in range(count - 1)]
    return forward, [(target, source) for source, target in forward]


def halve(kept, sent, mesh_sizes):
    for axis, bit in send_order(mesh_sizes):
        pairs = [(i, i ^ (1 << bit)) for i in range(mesh_sizes[axis])]
        arrived = lax.ppermute(sent, axis, pairs)
        half = kept.shape[0] // 2
        if (axis, bit) != send_order(mesh_sizes)[-1]:
            sent = (kept[half:] + arrived[half:].astype(F32)).astype(BF16)
            kept = kept[:half] + arrived[:half].astype(F32)
        else:
            kept = kept + arrived.astype(F32)
    return kept


def shards(mode_fields, cell_volumes, mesh_sizes):
    total_cells = (
        cell_volumes.shape[0] * mesh_sizes["gx"] * cell_volumes.shape[1] * mesh_sizes["gy"]
    )
    weights = cell_volumes * (1.0 / math.sqrt(total_cells))
    own = jnp.transpose(mode_fields, (2, 0, 1, 3))
    swap = [(0, 1), (1, 0)]
    row_count, _, share, _ = own.shape
    rows_each = 2 * share // (mesh_sizes["gx"] * mesh_sizes["gy"])
    chunks = 2 if rows_each > 1 else 1
    quarter = row_count // 4

    def inner_rows(array):
        return array[quarter : 3 * quarter]

    def outer_rows(array):
        return jnp.concatenate([array[:quarter], array[3 * quarter :]], 0)

    own_inner, own_outer = inner_rows(own), outer_rows(own)
    other_inner = lax.ppermute(own_inner, "ma", swap)
    forward, backward = neighbours("gy")
    before = lax.ppermute(own[:, :, :, -1], "gy", forward)
    after = lax.ppermute(own[:, :, :, 0], "gy", backward)
    forward, backward = neighbours("gx")
    above = lax.ppermute(own[-1:], "gx", forward)
    below = lax.ppermute(own[:1], "gx", backward)
    own_outer_held, other_inner = lax.optimization_barrier((own_outer, other_inner))
    other_outer = lax.ppermute(own_outer_held, "ma", swap)

    def along_second(rows):
        wide = jnp.concatenate([rows(before)[..., None], rows(own), rows(after)[..., None]], 3).astype(F32)
        return (wide[..., 2:] - wide[..., :-2]) * 0.5

    tall = own[quarter - 1 : 3 * quarter + 1].astype(F32)
    slopes_inner = jnp.concatenate([(tall[2:] - tall[:-2]) * 0.5, along_second(inner_rows)], 1).astype(BF16)
    upper = jnp.concatenate([above, own[: quarter + 1]], 0).astype(F32)
    lower = jnp.concatenate([own[3 * quarter - 1 :], below], 0).astype(F32)
    tall = jnp.concatenate([upper[2:] - upper[:-2], lower[2:] - lower[:-2]], 0) * 0.5
    slopes_outer = jnp.concatenate([tall, along_second(outer_rows)], 1).astype(BF16)

    inner = partial_tensor(
        own_inner, other_inner, slopes_inner, inner_rows(weights), mesh_sizes, rows_each, chunks
    )
    results = []
    first = lax.axis_index("ma") == 0
    for chunk in range(chunks):
        kept, sent = partial_tensor(
            own_outer, other_outer, slopes_outer, outer_rows(weights), mesh_sizes, rows_each, chunks, chunk, inner
        )
        summed = halve(kept, sent, mesh_sizes)
        summed = jnp.transpose(summed, (0, 2, 1))
        arrived = lax.ppermute(summed[:, share:], "ma", swap)
        kept = summed[:, :share]
        results.append(jnp.concatenate([jnp.where(first, kept, arrived), jnp.where(first, arrived, kept)], 2))
    return jnp.concatenate(results, 0)


def solution(mesh):
    in_specs = (P(None, "ma", "gx", "gy"), P("gx", "gy"))
    out_specs = P(("gx", "gy"), "ma", None)
    body = functools.partial(shards, mesh_sizes=dict(mesh.shape))
    return jax.shard_map(body, mesh=mesh, in_specs=in_specs, out_specs=out_specs, check_vma=False)
```

time: 91.2 us -> 82.6 us (0.906)
  waiting for transfers between devices: 34.9 us -> 21.7 us
  starting transfers between devices: 18.5 us -> 26.6 us
  Pallas kernels: 24.1 us -> 22.1 us
  other arithmetic: 5.92 us -> 4.23 us
    ppermute x6 -> x12, waiting for transfers between devices: 33.2 us -> 21.7 us  [the longest x8 15.3 us: halve(): arrived = lax.ppermute(sent, axis, pairs)]
    ppermute x6 -> x12, starting transfers between devices: 11 us -> 16.1 us  [the longest x8 11 us: halve(): arrived = lax.ppermute(sent, axis, pairs)]
    add x3 -> x0, other arithmetic: 2.15 us -> none  [shards(): partial = partial[:half] + arrived.astype(F32)]
    convert_element_type x2 -> x11, other arithmetic: 1.03 us -> 3.13 us  [the longest x2 0.94 us: along_second(): jnp.concatenate([rows(before)[..., None], rows(own), rows(after)[..., Non...]
    ppermute x1, starting transfers between devices: 3.48 us -> 5.56 us  [shards(): above = lax.ppermute(own[-1:], 'gx', forward)]
    pallas_call x1 -> x3, Pallas kernels: 24.1 us -> 22.1 us  [partial_tensor(): pl.pallas_call(body, grid=(steps,), out_shape=out_shape, in_specs=in_spec...]
    ppermute x1, waiting for transfers between devices: 1.69 us -> 0.01 us  [shards(): below = lax.ppermute(own[:1], 'gx', backward)]
    concatenate x2 -> x5, other arithmetic: 1.36 us -> 0.23 us  [the longest x1 0.07 us: shards(): jnp.concatenate([(tall[2:] - tall[:-2]) * 0.5, along_second(inner_rows)], 1)]
  transfers between devices with their start and end apart: 10 -> 16, of which waited for: 7 -> 7; matrix products, arithmetic and copies ran while one was open for 6% -> 9% of each run, Pallas kernels for 0% -> 20%
where the time goes in v2:
time: 82.6 us; the launch traced here: 82.2 us
  starting transfers between devices  26.6 us (32%)
  Pallas kernels  22.1 us (27%)
  waiting for transfers between devices  21.7 us (26%)
  local copies, waits for them, and re-layouts  7.16 us (9%)
  other arithmetic  4.23 us (5%)
    pallas_call x3, Pallas kernels, partial_tensor(): pl.pallas_call(body, grid=(steps,), out_shape=out_shape, in_specs=in_spec...  22.1 us
    ppermute x8, waiting for transfers between devices, halve(): arrived = lax.ppermute(sent, axis, pairs)  15.3 us
    ppermute x8, starting transfers between devices, halve(): arrived = lax.ppermute(sent, axis, pairs)  11 us
    ppermute x1, starting transfers between devices, shards(): above = lax.ppermute(own[-1:], 'gx', forward)  5.56 us
    ppermute x2, waiting for transfers between devices, shards(): arrived = lax.ppermute(summed[:, share:], 'ma', swap)  4.61 us
    ppermute x1, starting transfers between devices, shards(): other_outer = lax.ppermute(own_outer_held, 'ma', swap)  2.43 us
    ppermute x1, starting transfers between devices, shards(): before = lax.ppermute(own[:, :, :, -1], 'gy', forward)  2.35 us
    unnamed x7, local copies, waits for them, and re-layouts  2.18 us
  transfers between devices with their start and end apart: 16, of which 7 were waited for; matrix products, arithmetic and copies ran while one was open for 9% of the time, Pallas kernels for 20%

profile of v2, /device:TPU:0, one launch (start us, length us, event | category | flops | bytes accessed | tf_op | source)
XLA Modules:
  0.0 82.2 jit_solution(17557799475973854695)
XLA Ops:
  0.0 1.3 %copy.36 = bf16[3,64,16,128]{3,1,0,2:T(8,128)(2,1)S(1)} copy(bf16[3,64,16,128]{3,2,1,0:T(8,128)(2,1)} %param.2) | data formatting | bytes 1572864 | tf_op args[0]
  2.1 2.3 %collective-permute-start.4 = (bf16[16,3,64]{2,0,1:T(8,128)(2,1)S(1)}, bf16[16,3,64]{2,0,1:T(8,128)(2,1)S(1)}, u32[]{:S(2)}, u32[]{:S(2)}) collective-permute-start(bf16[16,3,64]{2,0,1:T(8,128)(2,1)S(1)} %bitcast.24), channel_id=1, source_target_pairs={{0,2},{2,4},{4,6},{1,3},{3,5},{5,7},{8,10},{10,12},{12,14},{9,11},... | collective-permute-start | bytes 18440 | tf_op jit(solution)/shard_map/ppermute | solution.py:203
  4.8 1.3 %collective-permute-start.5 = (bf16[16,3,64]{2,0,1:T(8,128)(2,1)S(1)}, bf16[16,3,64]{2,0,1:T(8,128)(2,1)S(1)}, u32[]{:S(2)}, u32[]{:S(2)}) collective-permute-start(bf16[16,3,64]{2,0,1:T(8,128)(2,1)S(1)} %bitcast.23), channel_id=1, source_target_pairs={{2,0},{4,2},{6,4},{3,1},{5,3},{7,5},{10,8},{12,10},{14,12},{11,9},... | collective-permute-start | bytes 18440 | tf_op jit(solution)/shard_map/ppermute | solution.py:204
  6.8 1.3 %collective-permute-start.3 = (bf16[1,3,64,128]{3,2,1,0:T(8,128)(2,1)}, bf16[1,3,64,128]{3,2,1,0:T(8,128)(2,1)}, u32[]{:S(2)}, u32[]{:S(2)}) collective-permute-start(bf16[1,3,64,128]{3,2,1,0:T(8,128)(2,1)} %get-tuple-element.26), channel_id=1, source_target_pairs={{8,0},{16,8},{24,16},{9,1},{17,9},{25,17},{10,2},{18,10},{26,18},{... | collective-permute-start | bytes 147464 | tf_op jit(solution)/shard_map/ppermute | solution.py:207
  8.0 5.6 %collective-permute-start.2 = (bf16[1,3,64,128]{3,2,1,0:T(8,128)(2,1)}, bf16[1,3,64,128]{3,2,1,0:T(8,128)(2,1)}, u32[]{:S(2)}, u32[]{:S(2)}) collective-permute-start(bf16[1,3,64,128]{3,2,1,0:T(8,128)(2,1)} %get-tuple-element.25), channel_id=1, source_target_pairs={{0,8},{8,16},{16,24},{1,9},{9,17},{17,25},{2,10},{10,18},{18,26},{... | collective-permute-start | bytes 147464 | tf_op jit(solution)/shard_map/ppermute | solution.py:206
  13.6 2.0 %collective-permute-start = (bf16[8,3,64,128]{3,2,1,0:T(8,128)(2,1)S(1)}, bf16[8,3,64,128]{3,2,1,0:T(8,128)(2,1)S(1)}, u32[]{:S(2)}, u32[]{:S(2)}) collective-permute-start(bf16[8,3,64,128]{3,2,1,0:T(8,128)(2,1)S(1)} %slice.235.refs_0_), channel_id=1, source_target_pairs={{0,1},{1,0},{2,3},{3,2},{4,5},{5,4},{6,7},{7,6},{8,9},{9,8},{10,11... | collective-permute-start | bytes 1179656 | tf_op jit(solution)/shard_map/ppermute | solution.py:201
  22.5 1.8 %collective-permute-done.refs_1_ = bf16[8,3,64,128]{3,2,1,0:T(8,128)(2,1)S(1)} collective-permute-done((bf16[8,3,64,128]{3,2,1,0:T(8,128)(2,1)S(1)}, bf16[8,3,64,128]{3,2,1,0:T(8,128)(2,1)S(1)}, u32[]{:S(2)}, u32[]{:S(2)}) %collective-permute-start) | collective-permute-done | bytes 393248 | tf_op jit(solution)/shard_map/ppermute | solution.py:201
  24.3 2.4 %collective-permute-start.1 = (bf16[8,3,64,128]{3,2,1,0:T(8,128)(2,1)S(1)}, bf16[8,3,64,128]{3,2,1,0:T(8,128)(2,1)S(1)}, u32[]{:S(2)}, u32[]{:S(2)}) collective-permute-start(bf16[8,3,64,128]{3,2,1,0:T(8,128)(2,1)S(1)} %pad_maximum_fusion.2.refs_0_), channel_id=1, source_target_pairs={{0,1},{1,0},{2,3},{3,2},{4,5},{5,4},{6,7},{7,6},{8,9},{9,8},{10,11... | collective-permute-start | bytes 1179656 | tf_op jit(solution)/shard_map/ppermute | solution.py:209
  26.7 10.6 %shard_map.28.refs_4_ = f32[128,64,128]{2,1,0:T(8,128)S(1)} custom-call(bf16[8,3,64,128]{3,2,1,0:T(8,128)(2,1)S(1)} %slice.235.refs_0_, bf16[8,3,64,128]{3,2,1,0:T(8,128)(2,1)S(1)} %collective-permute-done.refs_1_, bf16[8,6,64,128]{3,2,1,0:T(8,128)(2,1)S(1)} %pad_maximum_fusion.1.refs_2_, f32[8,128]{1,0:T(8,128)S(1)} %slice.261.refs_3_), custom_call_target="tpu_custom_call" | custom-call | flops 8589934592 | bytes 8388608 | tf_op jit(solution)/shard_map/pallas_call | solution.py:146
  37.3 5.8 %shard_map.29 = (f32[32,64,128]{2,1,0:T(8,128)S(1)}, bf16[32,64,128]{2,1,0:T(8,128)(2,1)S(1)}) custom-call(bf16[8,3,64,128]{3,2,1,0:T(8,128)(2,1)S(1)} %pad_maximum_fusion.2.refs_0_, bf16[8,3,64,128]{3,2,1,0:T(8,128)(2,1)S(1)} %collective-permute-done.1.refs_1_, bf16[8,6,64,128]{3,2,1,0:T(8,128)(2,1)S(1)} %pad_maximum_fusion.refs_2_, ...), custom_call_target="tpu_custom_call" | custom-call | flops 4294967296 | bytes 8388608 | tf_op jit(solution)/shard_map/pallas_call | solution.py:146
  43.6 5.8 %shard_map.30 = (f32[32,64,128]{2,1,0:T(8,128)S(1)}, bf16[32,64,128]{2,1,0:T(8,128)(2,1)S(1)}) custom-call(bf16[8,3,64,128]{3,2,1,0:T(8,128)(2,1)S(1)} %pad_maximum_fusion.2.refs_0_, bf16[8,3,64,128]{3,2,1,0:T(8,128)(2,1)S(1)} %collective-permute-done.1.refs_1_, bf16[8,6,64,128]{3,2,1,0:T(8,128)(2,1)S(1)} %pad_maximum_fusion.refs_2_, ...), custom_call_target="tpu_custom_call" | custom-call | flops 4294967296 | bytes 8388608 | tf_op jit(solution)/shard_map/pallas_call | solution.py:146
  49.7 2.3 %collective-permute-start.7 = (bf16[16,64,128]{2,1,0:T(8,128)(2,1)S(1)}, bf16[16,64,128]{2,1,0:T(8,128)(2,1)S(1)}, u32[]{:S(2)}, u32[]{:S(2)}) collective-permute-start(bf16[16,64,128]{2,1,0:T(8,128)(2,1)S(1)} %get-tuple-element.17), channel_id=1, source_target_pairs={{0,4},{2,6},{4,0},{6,2},{1,5},{3,7},{5,1},{7,3},{8,12},{10,14},{12... | collective-permute-start | bytes 786440 | tf_op jit(solution)/shard_map/ppermute | solution.py:172
  52.1 1.4 %collective-permute-start.12 = (bf16[16,64,128]{2,1,0:T(8,128)(2,1)S(1)}, bf16[16,64,128]{2,1,0:T(8,128)(2,1)S(1)}, u32[]{:S(2)}, u32[]{:S(2)}) collective-permute-start(bf16[16,64,128]{2,1,0:T(8,128)(2,1)S(1)} %get-tuple-element.19), channel_id=1, source_target_pairs={{0,4},{2,6},{4,0},{6,2},{1,5},{3,7},{5,1},{7,3},{8,12},{10,14},{12... | collective-permute-start | bytes 786440 | tf_op jit(solution)/shard_map/ppermute | solution.py:172
  53.5 5.6 %collective-permute-done.7 = bf16[16,64,128]{2,1,0:T(8,128)(2,1)S(1)} collective-permute-done((bf16[16,64,128]{2,1,0:T(8,128)(2,1)S(1)}, bf16[16,64,128]{2,1,0:T(8,128)(2,1)S(1)}, u32[]{:S(2)}, u32[]{:S(2)}) %collective-permute-start.7) | collective-permute-done | bytes 262176 | tf_op jit(solution)/shard_map/ppermute | solution.py:172
  59.2 1.1 %collective-permute-start.8 = (bf16[8,64,128]{2,1,0:T(8,128)(2,1)S(1)}, bf16[8,64,128]{2,1,0:T(8,128)(2,1)S(1)}, u32[]{:S(2)}, u32[]{:S(2)}) collective-permute-start(bf16[8,64,128]{2,1,0:T(8,128)(2,1)S(1)} %get-tuple-element.21), channel_id=1, source_target_pairs={{0,8},{8,0},{16,24},{24,16},{1,9},{9,1},{17,25},{25,17},{2,10},{10... | collective-permute-start | bytes 393224 | tf_op jit(solution)/shard_map/ppermute | solution.py:172
  60.2 3.9 %collective-permute-done.12 = bf16[16,64,128]{2,1,0:T(8,128)(2,1)S(1)} collective-permute-done((bf16[16,64,128]{2,1,0:T(8,128)(2,1)S(1)}, bf16[16,64,128]{2,1,0:T(8,128)(2,1)S(1)}, u32[]{:S(2)}, u32[]{:S(2)}) %collective-permute-start.12) | collective-permute-done | bytes 262176 | tf_op jit(solution)/shard_map/ppermute | solution.py:172
  64.2 1.0 %collective-permute-start.13 = (bf16[8,64,128]{2,1,0:T(8,128)(2,1)S(1)}, bf16[8,64,128]{2,1,0:T(8,128)(2,1)S(1)}, u32[]{:S(2)}, u32[]{:S(2)}) collective-permute-start(bf16[8,64,128]{2,1,0:T(8,128)(2,1)S(1)} %get-tuple-element.23), channel_id=1, source_target_pairs={{0,8},{8,0},{16,24},{24,16},{1,9},{9,1},{17,25},{25,17},{2,10},{10... | collective-permute-start | bytes 393224 | tf_op jit(solution)/shard_map/ppermute | solution.py:172
  65.3 1.7 %collective-permute-start.9 = (bf16[4,64,128]{2,1,0:T(8,128)(2,1)S(1)}, bf16[4,64,128]{2,1,0:T(8,128)(2,1)S(1)}, u32[]{:S(2)}, u32[]{:S(2)}) collective-permute-start(bf16[4,64,128]{2,1,0:T(8,128)(2,1)S(1)} %fusion.12), channel_id=1, source_target_pairs={{0,16},{8,24},{16,0},{24,8},{1,17},{9,25},{17,1},{25,9},{2,18},{10... | collective-permute-start | bytes 196616 | tf_op jit(solution)/shard_map/ppermute | solution.py:172
  67.0 3.1 %collective-permute-done.13 = bf16[8,64,128]{2,1,0:T(8,128)(2,1)S(1)} collective-permute-done((bf16[8,64,128]{2,1,0:T(8,128)(2,1)S(1)}, bf16[8,64,128]{2,1,0:T(8,128)(2,1)S(1)}, u32[]{:S(2)}, u32[]{:S(2)}) %collective-permute-start.13) | collective-permute-done | bytes 131104 | tf_op jit(solution)/shard_map/ppermute | solution.py:172
  70.1 2.8 %collective-permute-start.14 = (bf16[4,64,128]{2,1,0:T(8,128)(2,1)S(1)}, bf16[4,64,128]{2,1,0:T(8,128)(2,1)S(1)}, u32[]{:S(2)}, u32[]{:S(2)}) collective-permute-start(bf16[4,64,128]{2,1,0:T(8,128)(2,1)S(1)} %fusion.9), channel_id=1, source_target_pairs={{0,16},{8,24},{16,0},{24,8},{1,17},{9,25},{17,1},{25,9},{2,18},{10... | collective-permute-start | bytes 196616 | tf_op jit(solution)/shard_map/ppermute | solution.py:172
  73.3 2.7 %collective-permute-done.14 = bf16[4,64,128]{2,1,0:T(8,128)(2,1)S(1)} collective-permute-done((bf16[4,64,128]{2,1,0:T(8,128)(2,1)S(1)}, bf16[4,64,128]{2,1,0:T(8,128)(2,1)S(1)}, u32[]{:S(2)}, u32[]{:S(2)}) %collective-permute-start.14) | collective-permute-done | bytes 65568 | tf_op jit(solution)/shard_map/ppermute | solution.py:172
  76.6 1.5 %collective-permute-done.10 = f32[4,64,64]{1,2,0:T(8,128)S(1)} collective-permute-done((f32[4,64,64]{1,2,0:T(8,128)S(1)}, f32[4,64,64]{1,2,0:T(8,128)S(1)}, u32[]{:S(2)}, u32[]{:S(2)}) %collective-permute-start.10) | collective-permute-done | bytes 65568 | tf_op jit(solution)/shard_map/ppermute | solution.py:233
  78.1 3.1 %collective-permute-done.15 = f32[4,64,64]{1,2,0:T(8,128)S(1)} collective-permute-done((f32[4,64,64]{1,2,0:T(8,128)S(1)}, f32[4,64,64]{1,2,0:T(8,128)S(1)}, u32[]{:S(2)}, u32[]{:S(2)}) %collective-permute-start.15) | collective-permute-done | bytes 65568 | tf_op jit(solution)/shard_map/ppermute | solution.py:233
  81.3 0.9 %copy.34 = f32[8,64,128]{2,1,0:T(8,128)} copy(f32[8,64,128]{1,2,0:T(8,128)S(1)} %maximum_maximum_fusion) | data formatting | bytes 524288 | tf_op jit(solution)/shard_map/concatenate | solution.py:236
  (66 shorter events, 10.5 us)
Async XLA Ops:
  2.1 15.1 %collective-permute-start.4 = (bf16[16,3,64]{2,0,1:T(8,128)(2,1)S(1)}, bf16[16,3,64]{2,0,1:T(8,128)(2,1)S(1)}, u32[]{:S(2)}, u32[]{:S(2)}) collective-permute-start(bf16[16,3,64]{2,0,1:T(8,128)(2,1)S(1)} %bitcast.24), channel_id=1, source_target_pairs={{0,2},{2,4},{4,6},{1,3},{3,5},{5,7},{8,10},{10,12},{12,14},{9,11},... | collective-permute-start | bytes 18440 | tf_op jit(solution)/shard_map/ppermute | solution.py:203
  4.8 12.8 %collective-permute-start.5 = (bf16[16,3,64]{2,0,1:T(8,128)(2,1)S(1)}, bf16[16,3,64]{2,0,1:T(8,128)(2,1)S(1)}, u32[]{:S(2)}, u32[]{:S(2)}) collective-permute-start(bf16[16,3,64]{2,0,1:T(8,128)(2,1)S(1)} %bitcast.23), channel_id=1, source_target_pairs={{2,0},{4,2},{6,4},{3,1},{5,3},{7,5},{10,8},{12,10},{14,12},{11,9},... | collective-permute-start | bytes 18440 | tf_op jit(solution)/shard_map/ppermute | solution.py:204
  6.8 13.2 %collective-permute-start.3 = (bf16[1,3,64,128]{3,2,1,0:T(8,128)(2,1)}, bf16[1,3,64,128]{3,2,1,0:T(8,128)(2,1)}, u32[]{:S(2)}, u32[]{:S(2)}) collective-permute-start(bf16[1,3,64,128]{3,2,1,0:T(8,128)(2,1)} %get-tuple-element.26), channel_id=1, source_target_pairs={{8,0},{16,8},{24,16},{9,1},{17,9},{25,17},{10,2},{18,10},{26,18},{... | collective-permute-start | bytes 147464 | tf_op jit(solution)/shard_map/ppermute | solution.py:207
  8.0 13.2 %collective-permute-start.2 = (bf16[1,3,64,128]{3,2,1,0:T(8,128)(2,1)}, bf16[1,3,64,128]{3,2,1,0:T(8,128)(2,1)}, u32[]{:S(2)}, u32[]{:S(2)}) collective-permute-start(bf16[1,3,64,128]{3,2,1,0:T(8,128)(2,1)} %get-tuple-element.25), channel_id=1, source_target_pairs={{0,8},{8,16},{16,24},{1,9},{9,17},{17,25},{2,10},{10,18},{18,26},{... | collective-permute-start | bytes 147464 | tf_op jit(solution)/shard_map/ppermute | solution.py:206
  13.6 10.7 %collective-permute-start = (bf16[8,3,64,128]{3,2,1,0:T(8,128)(2,1)S(1)}, bf16[8,3,64,128]{3,2,1,0:T(8,128)(2,1)S(1)}, u32[]{:S(2)}, u32[]{:S(2)}) collective-permute-start(bf16[8,3,64,128]{3,2,1,0:T(8,128)(2,1)S(1)} %slice.235.refs_0_), channel_id=1, source_target_pairs={{0,1},{1,0},{2,3},{3,2},{4,5},{5,4},{6,7},{7,6},{8,9},{9,8},{10,11... | collective-permute-start | bytes 1179656 | tf_op jit(solution)/shard_map/ppermute | solution.py:201
  16.5 0.7 copy-start.2
  19.4 0.9 %copy-start.1 = (bf16[5,3,64,128]{3,2,1,0:T(8,128)(2,1)S(1)}, bf16[5,3,64,128]{3,2,1,0:T(8,128)(2,1)}, u32[]{:S(2)}) copy-start(bf16[5,3,64,128]{3,2,1,0:T(8,128)(2,1)} %get-tuple-element.28) | copy-start | bytes 737284
  19.9 1.4 %copy-start = (bf16[5,3,64,128]{3,2,1,0:T(8,128)(2,1)S(1)}, bf16[5,3,64,128]{3,2,1,0:T(8,128)(2,1)}, u32[]{:S(2)}) copy-start(bf16[5,3,64,128]{3,2,1,0:T(8,128)(2,1)} %get-tuple-element.27) | copy-start | bytes 737284
  24.3 13.0 %collective-permute-start.1 = (bf16[8,3,64,128]{3,2,1,0:T(8,128)(2,1)S(1)}, bf16[8,3,64,128]{3,2,1,0:T(8,128)(2,1)S(1)}, u32[]{:S(2)}, u32[]{:S(2)}) collective-permute-start(bf16[8,3,64,128]{3,2,1,0:T(8,128)(2,1)S(1)} %pad_maximum_fusion.2.refs_0_), channel_id=1, source_target_pairs={{0,1},{1,0},{2,3},{3,2},{4,5},{5,4},{6,7},{7,6},{8,9},{9,8},{10,11... | collective-permute-start | bytes 1179656 | tf_op jit(solution)/shard_map/ppermute | solution.py:209
  43.1 6.4 %collective-permute-start.6 = (bf16[32,64,128]{2,1,0:T(8,128)(2,1)S(1)}, bf16[32,64,128]{2,1,0:T(8,128)(2,1)S(1)}, u32[]{:S(2)}, u32[]{:S(2)}) collective-permute-start(bf16[32,64,128]{2,1,0:T(8,128)(2,1)S(1)} %get-tuple-element.14), channel_id=1, source_target_pairs={{0,2},{2,0},{4,6},{6,4},{1,3},{3,1},{5,7},{7,5},{8,10},{10,8},{12,... | collective-permute-start | bytes 1572872 | tf_op jit(solution)/shard_map/ppermute | solution.py:172
  49.4 2.6 %collective-permute-start.11 = (bf16[32,64,128]{2,1,0:T(8,128)(2,1)S(1)}, bf16[32,64,128]{2,1,0:T(8,128)(2,1)S(1)}, u32[]{:S(2)}, u32[]{:S(2)}) collective-permute-start(bf16[32,64,128]{2,1,0:T(8,128)(2,1)S(1)} %get-tuple-element.16), channel_id=1, source_target_pairs={{0,2},{2,0},{4,6},{6,4},{1,3},{3,1},{5,7},{7,5},{8,10},{10,8},{12,... | collective-permute-start | bytes 1572872 | tf_op jit(solution)/shard_map/ppermute | solution.py:172
  49.7 9.4 %collective-permute-start.7 = (bf16[16,64,128]{2,1,0:T(8,128)(2,1)S(1)}, bf16[16,64,128]{2,1,0:T(8,128)(2,1)S(1)}, u32[]{:S(2)}, u32[]{:S(2)}) collective-permute-start(bf16[16,64,128]{2,1,0:T(8,128)(2,1)S(1)} %get-tuple-element.17), channel_id=1, source_target_pairs={{0,4},{2,6},{4,0},{6,2},{1,5},{3,7},{5,1},{7,3},{8,12},{10,14},{12... | collective-permute-start | bytes 786440 | tf_op jit(solution)/shard_map/ppermute | solution.py:172
  52.1 12.0 %collective-permute-start.12 = (bf16[16,64,128]{2,1,0:T(8,128)(2,1)S(1)}, bf16[16,64,128]{2,1,0:T(8,128)(2,1)S(1)}, u32[]{:S(2)}, u32[]{:S(2)}) collective-permute-start(bf16[16,64,128]{2,1,0:T(8,128)(2,1)S(1)} %get-tuple-element.19), channel_id=1, source_target_pairs={{0,4},{2,6},{4,0},{6,2},{1,5},{3,7},{5,1},{7,3},{8,12},{10,14},{12... | collective-permute-start | bytes 786440 | tf_op jit(solution)/shard_map/ppermute | solution.py:172
  59.2 6.1 %collective-permute-start.8 = (bf16[8,64,128]{2,1,0:T(8,128)(2,1)S(1)}, bf16[8,64,128]{2,1,0:T(8,128)(2,1)S(1)}, u32[]{:S(2)}, u32[]{:S(2)}) collective-permute-start(bf16[8,64,128]{2,1,0:T(8,128)(2,1)S(1)} %get-tuple-element.21), channel_id=1, source_target_pairs={{0,8},{8,0},{16,24},{24,16},{1,9},{9,1},{17,25},{25,17},{2,10},{10... | collective-permute-start | bytes 393224 | tf_op jit(solution)/shard_map/ppermute | solution.py:172
  64.2 5.9 %collective-permute-start.13 = (bf16[8,64,128]{2,1,0:T(8,128)(2,1)S(1)}, bf16[8,64,128]{2,1,0:T(8,128)(2,1)S(1)}, u32[]{:S(2)}, u32[]{:S(2)}) collective-permute-start(bf16[8,64,128]{2,1,0:T(8,128)(2,1)S(1)} %get-tuple-element.23), channel_id=1, source_target_pairs={{0,8},{8,0},{16,24},{24,16},{1,9},{9,1},{17,25},{25,17},{2,10},{10... | collective-permute-start | bytes 393224 | tf_op jit(solution)/shard_map/ppermute | solution.py:172
  65.3 7.7 %collective-permute-start.9 = (bf16[4,64,128]{2,1,0:T(8,128)(2,1)S(1)}, bf16[4,64,128]{2,1,0:T(8,128)(2,1)S(1)}, u32[]{:S(2)}, u32[]{:S(2)}) collective-permute-start(bf16[4,64,128]{2,1,0:T(8,128)(2,1)S(1)} %fusion.12), channel_id=1, source_target_pairs={{0,16},{8,24},{16,0},{24,8},{1,17},{9,25},{17,1},{25,9},{2,18},{10... | collective-permute-start | bytes 196616 | tf_op jit(solution)/shard_map/ppermute | solution.py:172
  70.1 5.9 %collective-permute-start.14 = (bf16[4,64,128]{2,1,0:T(8,128)(2,1)S(1)}, bf16[4,64,128]{2,1,0:T(8,128)(2,1)S(1)}, u32[]{:S(2)}, u32[]{:S(2)}) collective-permute-start(bf16[4,64,128]{2,1,0:T(8,128)(2,1)S(1)} %fusion.9), channel_id=1, source_target_pairs={{0,16},{8,24},{16,0},{24,8},{1,17},{9,25},{17,1},{25,9},{2,18},{10... | collective-permute-start | bytes 196616 | tf_op jit(solution)/shard_map/ppermute | solution.py:172
  73.1 5.0 %collective-permute-start.10 = (f32[4,64,64]{1,2,0:T(8,128)S(1)}, f32[4,64,64]{1,2,0:T(8,128)S(1)}, u32[]{:S(2)}, u32[]{:S(2)}) collective-permute-start(f32[4,64,64]{1,2,0:T(8,128)S(1)} %slice.273), channel_id=1, source_target_pairs={{0,1},{1,0},{2,3},{3,2},{4,5},{5,4},{6,7},{7,6},{8,9},{9,8},{10,11... | collective-permute-start | bytes 196616 | tf_op jit(solution)/shard_map/ppermute | solution.py:233
  76.2 5.0 %collective-permute-start.15 = (f32[4,64,64]{1,2,0:T(8,128)S(1)}, f32[4,64,64]{1,2,0:T(8,128)S(1)}, u32[]{:S(2)}, u32[]{:S(2)}) collective-permute-start(f32[4,64,64]{1,2,0:T(8,128)S(1)} %slice.285), channel_id=1, source_target_pairs={{0,1},{1,0},{2,3},{3,2},{4,5},{5,4},{6,7},{7,6},{8,9},{9,8},{10,11... | collective-permute-start | bytes 196616 | tf_op jit(solution)/shard_map/ppermute | solution.py:233

commit v3 on v1

v3 whole, which is shorter than its diff:
```python
import functools
import math

import jax
import jax.numpy as jnp
from jax import lax
from jax.experimental import pallas as pl
from jax.experimental.pallas import tpu as pltpu
from jax.sharding import PartitionSpec as P

BF16 = jnp.bfloat16
F32 = jnp.float32


def bits_of(count):
    return count.bit_length() - 1


def send_order(sizes):
    order = []
    for axis in ("gy", "gx"):
        order += [(axis, bit) for bit in range(bits_of(sizes[axis]))]
    return order


def source_bits(sizes, rows_each, chunks):
    row_bits = bits_of(rows_each)
    base = {"gy": row_bits, "gx": row_bits + bits_of(sizes["gy"])}
    inner = row_bits - bits_of(chunks)
    found = list(range(inner))
    for axis, bit in reversed(send_order(sizes)):
        found.append(base[axis] + bit)
    return found + list(range(inner, row_bits))


def slopes_kernel(own_ref, before_ref, after_ref, *refs, rows):
    out_ref = refs[-1]
    last = own_ref.shape[0] - 1
    before = before_ref[...].astype(F32).T
    after = after_ref[...].astype(F32).T
    cells = own_ref.shape[3]
    lane = lax.broadcasted_iota(jnp.int32, own_ref.shape[2:], 1)
    for place, x in enumerate(rows):
        for a in range(3):
            down = (refs[0][0, a] if x == 0 else own_ref[x - 1, a]).astype(F32)
            up = (refs[1][0, a] if x == last else own_ref[x + 1, a]).astype(F32)
            out_ref[place, a] = ((up - down) * 0.5).astype(BF16)
            value = own_ref[x, a].astype(F32)
            column = 3 * x + a
            down = jnp.where(lane == 0, before[:, column : column + 1], pltpu.roll(value, 1, 1))
            up = jnp.where(lane == cells - 1, after[:, column : column + 1], pltpu.roll(value, cells - 1, 1))
            out_ref[place, 3 + a] = ((up - down) * 0.5).astype(BF16)


def slopes_of(own, before, after, rows, token, edges):
    row_count, _, share, cells = own.shape
    return pl.pallas_call(
        functools.partial(slopes_kernel, rows=rows),
        out_shape=jax.ShapeDtypeStruct((len(rows), 6, share, cells), BF16),
        in_specs=[pl.BlockSpec(memory_space=pltpu.VMEM)] * (4 + len(edges)),
        out_specs=pl.BlockSpec(memory_space=pltpu.VMEM),
        compiler_params=pltpu.CompilerParams(vmem_limit_bytes=16 << 20),
        cost_estimate=pl.CostEstimate(flops=1, bytes_accessed=1024, transcendentals=0),
    )(own, before.reshape(3 * row_count, share), after.reshape(3 * row_count, share), *edges, token)


def chunks_of(rows_each):
    return 2 if rows_each > 1 else 1


def tensor_kernel(*refs, bits, block, rows_each, first_step):
    own_ref, other_ref, slope_ref, weight_ref = refs[:4]
    before_ref = refs[4] if len(refs) == 8 else None
    out_ref, left, right = refs[-3:]
    row_count, _, share, cells = own_ref.shape
    step = pl.program_id(0)
    top = bits_of(2 * share) - 1

    @pl.when(step == 0)
    def _():
        for x in range(row_count):
            weight = weight_ref[pl.ds(x, 1), :]
            for half, ref in enumerate((own_ref, other_ref)):
                for a in range(3):
                    value = (weight * ref[x, a].astype(F32)).astype(BF16)
                    left[x, a, half * share : (half + 1) * share, :] = value.astype(F32)
                for b in range(2):
                    right[
                        half * share : (half + 1) * share, (2 * x + b) * cells : (2 * x + b + 1) * cells
                    ] = ref[x, b]

    here = (lax.axis_index("gx") * lax.axis_size("gy") + lax.axis_index("gy")) * rows_each
    start = here ^ (lax.axis_index("ma") << top)
    position = (first_step + step) * block
    for place, bit in enumerate(bits):
        start = start ^ (((position >> place) & 1) << bit)
    columns = []
    for x in range(row_count):
        slopes = [slope_ref[x, n] for n in range(6)]
        sums = [[], []]
        for row in range(block):
            offset = 0
            for place, bit in enumerate(bits):
                offset |= ((row >> place) & 1) << bit
            test = [
                jnp.concatenate(
                    [left[x, a, pl.ds(start ^ offset, 16, stride=0), :].astype(BF16)] * (share // 16), 0
                )
                for a in range(3)
            ]
            for b in range(2):
                sums[b].append(
                    test[0] * slopes[3 * b] + test[1] * slopes[3 * b + 1] + test[2] * slopes[3 * b + 2]
                )
        columns += [jnp.concatenate(sums[0], 0), jnp.concatenate(sums[1], 0)]
    sums = jnp.concatenate(columns, 1)
    product = lax.dot_general(sums, right[...], (((1,), (1,)), ((), ())), preferred_element_type=F32)
    product = product.reshape(block, share, 2 * share)
    if before_ref is not None:
        product = product + before_ref[...]
    out_ref[...] = product.astype(out_ref.dtype)


def partial_tensor(own, other, slopes, weights, sizes, positions, before=None, dtype=F32):
    row_count, _, share, cells = own.shape
    modes = 2 * share
    low, high = positions
    block = min(16, high - low)
    first_step = low // block
    rows_each = modes // (sizes["gx"] * sizes["gy"])
    body = functools.partial(
        tensor_kernel,
        bits=source_bits(sizes, rows_each, chunks_of(rows_each)),
        block=block,
        rows_each=rows_each,
        first_step=first_step,
    )
    whole = lambda array: pl.BlockSpec(array.shape, lambda g: (0,) * array.ndim, pipeline_mode=pl.Buffered(1))
    shape = (block, share, modes)
    operands = [own, other, slopes, weights]
    in_specs = [whole(array) for array in operands]
    if before is not None:
        operands.append(before)
        in_specs.append(pl.BlockSpec(shape, lambda g: (first_step + g, 0, 0)))
    return pl.pallas_call(
        body,
        grid=((high - low) // block,),
        out_shape=jax.ShapeDtypeStruct((high - low, share, modes), dtype),
        in_specs=in_specs,
        out_specs=pl.BlockSpec(shape, lambda g: (g, 0, 0)),
        scratch_shapes=[
            pltpu.VMEM((row_count, 3, modes, cells), F32),
            pltpu.VMEM((modes, row_count * 2 * cells), BF16),
        ],
        compiler_params=pltpu.CompilerParams(vmem_limit_bytes=20 << 20),
        cost_estimate=pl.CostEstimate(
            flops=8 * (high - low) * share * modes * row_count * cells, bytes_accessed=4 << 20, transcendentals=0
        ),
    )(*operands)


def neighbours(axis):
    count = lax.axis_size(axis)
    forward = [(i, i + 1) for i in range(count - 1)]
    return forward, [(target, source) for source, target in forward]


def flip(array, flips, sizes):
    axes = tuple(sorted({axis for axis, _ in flips}, key=("gx", "gy", "ma").index))
    strides = {}
    count = 1
    for axis in reversed(axes):
        strides[axis] = count
        count *= sizes[axis]
    change = 0
    for axis, bit in flips:
        change |= strides[axis] << bit
    return lax.ppermute(array, axes, [(i, i ^ change) for i in range(count)])


def subsets(stage):
    for code in range(1, 1 << len(stage)):
        yield code, [stage[n] for n in range(len(stage)) if (code >> (len(stage) - 1 - n)) & 1]


def stages_of(sizes, last):
    order = send_order(sizes)
    stages = [[order[0]]]
    rest = order[1:]
    if last:
        stages.append(rest[:2])
        rest = rest[2:]
    stages += [[entry] for entry in rest]
    return stages


def pieces_sum(kept, arrived, low, high):
    total = kept[low:high].astype(F32)
    for array in arrived:
        total = total + array[low:high].astype(F32)
    return total


def halve_stages(kept, arrived, stages, sizes):
    for stage in stages[:-1]:
        parts = 1 << len(stage)
        length = kept.shape[0] // parts
        received = []
        for code, flips in reversed(list(subsets(stage))):
            sent = pieces_sum(kept, arrived, code * length, (code + 1) * length).astype(BF16)
            received.append(flip(sent, flips, sizes))
        kept, arrived = pieces_sum(kept, arrived, 0, length), received
    return kept, arrived


def finish(kept, arrived, stage, sizes, share):
    total = pieces_sum(kept, arrived, 0, kept.shape[0])
    count = total.shape[0]
    pair = 2 if count % 4 == 0 else 1
    total = jnp.transpose(total.reshape(count // pair, pair * share, 2 * share), (0, 2, 1))
    length = count // pair // 2
    pieces = {}
    stage = stage + [("ma", 0)]
    for code, flips in reversed(list(subsets(stage))):
        above, swapped = code >> 1, code & 1
        sent = total[above * length : (above + 1) * length, swapped * share : (swapped + 1) * share]
        pieces[code] = flip(sent.astype(BF16), flips, sizes).astype(F32)
    mine = total[:length, :share] + pieces[2]
    theirs = pieces[1] + pieces[3]
    first = lax.axis_index("ma") == 0
    rows = []
    for part in range(pair):
        lanes = slice(part * share, (part + 1) * share)
        one, two = mine[:, :, lanes], theirs[:, :, lanes]
        rows.append(jnp.concatenate([jnp.where(first, one, two), jnp.where(first, two, one)], 2))
    return jnp.stack(rows, 1).reshape(count // 2, share, 2 * share)


def shards(mode_fields, cell_volumes, sizes):
    total_cells = cell_volumes.shape[0] * sizes["gx"] * cell_volumes.shape[1] * sizes["gy"]
    weights = cell_volumes * (1.0 / math.sqrt(total_cells))
    barrier = lax.optimization_barrier
    own = jnp.transpose(mode_fields, (2, 0, 1, 3))
    row_count, _, share, _ = own.shape
    modes = 2 * share
    quarter = row_count // 4

    def inner_rows(array):
        return array[quarter : 3 * quarter]

    def outer_rows(array):
        return jnp.concatenate([array[:quarter], array[3 * quarter :]], 0)

    own_inner, own_outer = inner_rows(own), outer_rows(own)
    other_inner = flip(own_inner, [("ma", 0)], sizes)
    forward, backward = neighbours("gy")
    before = lax.ppermute(own[:, :, :, -1], "gy", forward)
    after = lax.ppermute(own[:, :, :, 0], "gy", backward)
    forward, backward = neighbours("gx")
    held, before, after = barrier((own, before, after))
    above = lax.ppermute(held[-1:], "gx", forward)
    below = lax.ppermute(held[:1], "gx", backward)
    token = other_inner[:1, 0, :8] + other_inner[1:2, 0, :8]
    own_outer_held, above, below = barrier((own_outer, above, below))
    other_outer = flip(own_outer_held, [("ma", 0)], sizes)
    all_rows = tuple(range(row_count))
    slopes_inner = slopes_of(own, before, after, all_rows[quarter : 3 * quarter], token, [])
    slopes_outer = slopes_of(
        own, before, after, all_rows[:quarter] + all_rows[3 * quarter :], token, [above, below]
    )

    inner = partial_tensor(own_inner, other_inner, slopes_inner, inner_rows(weights), sizes, (0, modes))
    outer_weights = outer_rows(weights)
    chunks = chunks_of(modes // (sizes["gx"] * sizes["gy"]))
    length = modes // chunks
    results = []
    for chunk in range(chunks):
        low, middle, high = chunk * length, chunk * length + length // 2, (chunk + 1) * length
        outer = functools.partial(partial_tensor, own_outer, other_outer, slopes_outer, sizes=sizes, before=inner)
        stages = stages_of(sizes, chunk == chunks - 1)
        sent = outer(weights=outer_weights, positions=(middle, high), dtype=BF16)
        outer_weights, sent = barrier((outer_weights, sent))
        arrived = [flip(sent, stages[0], sizes)]
        kept = outer(weights=outer_weights, positions=(low, middle))
        if chunk < chunks - 1:
            outer_weights, kept, arrived = barrier((outer_weights, kept, arrived))
        results.append((kept, arrived, stages))
    finished = []
    for kept, arrived, stages in results:
        kept, arrived = halve_stages(kept, arrived, stages[1:], sizes)
        finished.append(finish(kept, arrived, stages[-1], sizes, share))
    return jnp.concatenate(finished, 0)


def solution(mesh):
    in_specs = (P(None, "ma", "gx", "gy"), P("gx", "gy"))
    out_specs = P(("gx", "gy"), "ma", None)
    body = functools.partial(shards, sizes=dict(mesh.shape))
    return jax.shard_map(body, mesh=mesh, in_specs=in_specs, out_specs=out_specs, check_vma=False)
```

time: 91.2 us -> 78 us (0.86)
  waiting for transfers between devices: 34.9 us -> 18 us
  starting transfers between devices: 18.5 us -> 29.3 us
  other arithmetic: 5.92 us -> 1.45 us
  local copies, waits for them, and re-layouts: 7.26 us -> 5.21 us
    ppermute x8 -> x17, waiting for transfers between devices: 34.8 us -> 16.6 us  [the longest x15 12 us: flip(): return lax.ppermute(array, axes, [(i, i ^ change) for i in range(count)])]
    ppermute x8 -> x17, starting transfers between devices: 15.7 us -> 25.7 us  [the longest x15 20.9 us: flip(): return lax.ppermute(array, axes, [(i, i ^ change) for i in range(count)])]
    add x3 -> x7, other arithmetic: 2.15 us -> 0.2 us  [the longest x2 0.14 us: pieces_sum(): total = total + array[low:high].astype(F32)]
    slice x6 -> x7, local copies, waits for them, and re-layouts: 2.05 us -> 0.27 us  [the longest x2 0.2 us: finish(): total[above * length:(above + 1) * length, swapped * share:(swapped + 1)...]
    ppermute x1, waiting for transfers between devices: 0.01 us -> 1.37 us  [shards(): after = lax.ppermute(own[:, :, :, 0], 'gy', backward)]
    unnamed x7, local copies, waits for them, and re-layouts: 2.24 us -> 3.54 us
    broadcast_in_dim x2 -> x0, local copies, waits for them, and re-layouts: 0.97 us -> none  [the longest x1 0.49 us: shards(): after[..., None]]
    pallas_call x1 -> x7, Pallas kernels: 24.1 us -> 23.5 us  [the longest x5 22.1 us: partial_tensor(): pl.pallas_call(body, grid=((high - low) // block,), out_shape=jax.ShapeDt...]
  transfers between devices with their start and end apart: 10 -> 19, of which waited for: 7 -> 9; matrix products, arithmetic and copies ran while one was open for 6% -> 1% of each run, Pallas kernels for 0% -> 26%
where the time goes in v3:
time: 78 us; the launch traced here: 77.8 us
  starting transfers between devices  29.3 us (38%)
  Pallas kernels  23.5 us (30%)
  waiting for transfers between devices  18 us (23%)
  local copies, waits for them, and re-layouts  5.21 us (7%)
  other arithmetic  1.45 us (2%)
    pallas_call x5, Pallas kernels, partial_tensor(): pl.pallas_call(body, grid=((high - low) // block,), out_shape=jax.ShapeDt...  22.1 us
    ppermute x15, starting transfers between devices, flip(): return lax.ppermute(array, axes, [(i, i ^ change) for i in range(count)])  20.9 us
    ppermute x15, waiting for transfers between devices, flip(): return lax.ppermute(array, axes, [(i, i ^ change) for i in range(count)])  12 us
    ppermute x1, waiting for transfers between devices, shards(): below = lax.ppermute(held[:1], 'gx', backward)  4.25 us
    unnamed x7, local copies, waits for them, and re-layouts  3.54 us
    ppermute x1, starting transfers between devices, shards(): above = lax.ppermute(held[-1:], 'gx', forward)  3.48 us
    ppermute x1, starting transfers between devices, shards(): before = lax.ppermute(own[:, :, :, -1], 'gy', forward)  2.35 us
  transfers between devices with their start and end apart: 19, of which 9 were waited for; matrix products, arithmetic and copies ran while one was open for 1% of the time, Pallas kernels for 26%

profile of v3, /device:TPU:0, one launch (start us, length us, event | category | flops | bytes accessed | tf_op | source)
XLA Modules:
  0.0 77.8 jit_solution(7400525616173985973)
XLA Ops:
  0.0 1.3 %copy.14 = bf16[3,64,16,128]{3,1,0,2:T(8,128)(2,1)S(1)} copy(bf16[3,64,16,128]{3,2,1,0:T(8,128)(2,1)} %param.2) | data formatting | bytes 1572864 | tf_op args[0]
  2.1 2.3 %collective-permute-start = (bf16[16,3,64]{2,0,1:T(8,128)(2,1)S(1)}, bf16[16,3,64]{2,0,1:T(8,128)(2,1)S(1)}, u32[]{:S(2)}, u32[]{:S(2)}) collective-permute-start(bf16[16,3,64]{2,0,1:T(8,128)(2,1)S(1)} %bitcast.35), channel_id=1, source_target_pairs={{0,2},{2,4},{4,6},{1,3},{3,5},{5,7},{8,10},{10,12},{12,14},{9,11},... | collective-permute-start | bytes 18440 | tf_op jit(solution)/shard_map/ppermute | solution.py:257
  4.8 1.3 %collective-permute-start.1 = (bf16[16,3,64]{2,0,1:T(8,128)(2,1)S(1)}, bf16[16,3,64]{2,0,1:T(8,128)(2,1)S(1)}, u32[]{:S(2)}, u32[]{:S(2)}) collective-permute-start(bf16[16,3,64]{2,0,1:T(8,128)(2,1)S(1)} %bitcast.36), channel_id=1, source_target_pairs={{2,0},{4,2},{6,4},{3,1},{5,3},{7,5},{10,8},{12,10},{14,12},{11,9},... | collective-permute-start | bytes 18440 | tf_op jit(solution)/shard_map/ppermute | solution.py:258
  6.2 2.4 %collective-permute-start.5 = (bf16[8,3,64,128]{3,2,1,0:T(8,128)(2,1)S(1)}, bf16[8,3,64,128]{3,2,1,0:T(8,128)(2,1)S(1)}, u32[]{:S(2)}, u32[]{:S(2)}) collective-permute-start(bf16[8,3,64,128]{3,2,1,0:T(8,128)(2,1)S(1)} %slice.188.refs_0_), channel_id=1, source_target_pairs={{0,1},{1,0},{2,3},{3,2},{4,5},{5,4},{6,7},{7,6},{8,9},{9,8},{10,11... | collective-permute-start | bytes 1179656 | tf_op jit(solution)/shard_map/ppermute | solution.py:178
  8.7 1.4 %collective-permute-done.1 = bf16[16,3,64]{2,0,1:T(8,128)(2,1)S(1)} collective-permute-done((bf16[16,3,64]{2,0,1:T(8,128)(2,1)S(1)}, bf16[16,3,64]{2,0,1:T(8,128)(2,1)S(1)}, u32[]{:S(2)}, u32[]{:S(2)}) %collective-permute-start.1) | collective-permute-done | bytes 6176 | tf_op jit(solution)/shard_map/ppermute | solution.py:258
  10.0 3.5 %collective-permute-start.2 = (bf16[1,3,64,128]{3,2,1,0:T(8,128)(2,1)S(1)}, bf16[1,3,64,128]{3,2,1,0:T(8,128)(2,1)S(1)}, u32[]{:S(2)}, u32[]{:S(2)}) collective-permute-start(bf16[1,3,64,128]{3,2,1,0:T(8,128)(2,1)S(1)} %get-tuple-element.37), channel_id=1, source_target_pairs={{0,8},{8,16},{16,24},{1,9},{9,17},{17,25},{2,10},{10,18},{18,26},{... | collective-permute-start | bytes 147464 | tf_op jit(solution)/shard_map/ppermute | solution.py:261
  13.5 1.3 %collective-permute-start.3 = (bf16[1,3,64,128]{3,2,1,0:T(8,128)(2,1)S(1)}, bf16[1,3,64,128]{3,2,1,0:T(8,128)(2,1)S(1)}, u32[]{:S(2)}, u32[]{:S(2)}) collective-permute-start(bf16[1,3,64,128]{3,2,1,0:T(8,128)(2,1)S(1)} %get-tuple-element.36), channel_id=1, source_target_pairs={{8,0},{16,8},{24,16},{9,1},{17,9},{25,17},{10,2},{18,10},{26,18},{... | collective-permute-start | bytes 147464 | tf_op jit(solution)/shard_map/ppermute | solution.py:262
  15.3 4.3 %collective-permute-done.3.refs_1_ = bf16[1,3,64,128]{3,2,1,0:T(8,128)(2,1)S(1)} collective-permute-done((bf16[1,3,64,128]{3,2,1,0:T(8,128)(2,1)S(1)}, bf16[1,3,64,128]{3,2,1,0:T(8,128)(2,1)S(1)}, u32[]{:S(2)}, u32[]{:S(2)}) %collective-permute-start.3) | collective-permute-done | bytes 49184 | tf_op jit(solution)/shard_map/ppermute | solution.py:262
  19.5 1.6 %collective-permute-start.4 = (bf16[8,3,64,128]{3,2,1,0:T(8,128)(2,1)S(1)}, bf16[8,3,64,128]{3,2,1,0:T(8,128)(2,1)S(1)}, u32[]{:S(2)}, u32[]{:S(2)}) collective-permute-start(bf16[8,3,64,128]{3,2,1,0:T(8,128)(2,1)S(1)} %pad_maximum_fusion.refs_0_), channel_id=1, source_target_pairs={{0,1},{1,0},{2,3},{3,2},{4,5},{5,4},{6,7},{7,6},{8,9},{9,8},{10,11... | collective-permute-start | bytes 1179656 | tf_op jit(solution)/shard_map/ppermute | solution.py:178
  21.8 10.6 %shard_map.30.refs_4_ = f32[128,64,128]{2,1,0:T(8,128)S(1)} custom-call(bf16[8,3,64,128]{3,2,1,0:T(8,128)(2,1)S(1)} %slice.188.refs_0_, bf16[8,3,64,128]{3,2,1,0:T(8,128)(2,1)S(1)} %collective-permute-done.5.refs_1_, bf16[8,6,64,128]{3,2,1,0:T(8,128)(2,1)S(1)} %shard_map.29.refs_2_, f32[8,128]{1,0:T(8,128)S(1)} %slice.191.refs_3_), custom_call_target="tpu_custom_call" | custom-call | flops 8589934592 | bytes 4194304 | tf_op jit(solution)/shard_map/pallas_call | solution.py:145
  33.1 2.9 %shard_map.31 = bf16[32,64,128]{2,1,0:T(8,128)(2,1)S(1)} custom-call(bf16[8,3,64,128]{3,2,1,0:T(8,128)(2,1)S(1)} %pad_maximum_fusion.refs_0_, bf16[8,3,64,128]{3,2,1,0:T(8,128)(2,1)S(1)} %collective-permute-done.4.refs_1_, bf16[8,6,64,128]{3,2,1,0:T(8,128)(2,1)S(1)} %shard_map.28.refs_2_, f32[8,128]{1,0:T(8,128)S(1)} %pad_maximum_fusion.4.refs_3_, ...), custom_call_target="tpu_custom_call" | custom-call | flops 2147483648 | bytes 4194304 | tf_op jit(solution)/shard_map/pallas_call | solution.py:145
  37.1 2.9 %shard_map.32 = f32[32,64,128]{2,1,0:T(8,128)S(1)} custom-call(bf16[8,3,64,128]{3,2,1,0:T(8,128)(2,1)S(1)} %pad_maximum_fusion.refs_0_, bf16[8,3,64,128]{3,2,1,0:T(8,128)(2,1)S(1)} %collective-permute-done.4.refs_1_, bf16[8,6,64,128]{3,2,1,0:T(8,128)(2,1)S(1)} %shard_map.28.refs_2_, f32[8,128]{1,0:T(8,128)S(1)} %pad_maximum_fusion.4.refs_3_, ...), custom_call_target="tpu_custom_call" | custom-call | flops 2147483648 | bytes 4194304 | tf_op jit(solution)/shard_map/pallas_call | solution.py:145
  40.1 1.5 %collective-permute-start.7 = (bf16[16,64,128]{2,1,0:T(8,128)(2,1)S(1)}, bf16[16,64,128]{2,1,0:T(8,128)(2,1)S(1)}, u32[]{:S(2)}, u32[]{:S(2)}) collective-permute-start(bf16[16,64,128]{2,1,0:T(8,128)(2,1)S(1)} %get-tuple-element.31), channel_id=1, source_target_pairs={{0,4},{2,6},{4,0},{6,2},{1,5},{3,7},{5,1},{7,3},{8,12},{10,14},{12... | collective-permute-start | bytes 786440 | tf_op jit(solution)/shard_map/ppermute | solution.py:178
  41.6 2.2 %copy-done.1 = f32[128,64,128]{2,1,0:T(8,128)S(1)} copy-done((f32[128,64,128]{2,1,0:T(8,128)S(1)}, f32[128,64,128]{2,1,0:T(8,128)}, u32[]{:S(2)}) %copy-start.1) | copy-done | bytes 4194328
  43.8 2.9 %shard_map.33 = bf16[32,64,128]{2,1,0:T(8,128)(2,1)S(1)} custom-call(bf16[8,3,64,128]{3,2,1,0:T(8,128)(2,1)S(1)} %pad_maximum_fusion.refs_0_, bf16[8,3,64,128]{3,2,1,0:T(8,128)(2,1)S(1)} %collective-permute-done.4.refs_1_, bf16[8,6,64,128]{3,2,1,0:T(8,128)(2,1)S(1)} %shard_map.28.refs_2_, f32[8,128]{1,0:T(8,128)S(1)} %pad_maximum_fusion.4.refs_3_, ...), custom_call_target="tpu_custom_call" | custom-call | flops 2147483648 | bytes 4194304 | tf_op jit(solution)/shard_map/pallas_call | solution.py:145
  46.9 1.6 %collective-permute-done.7 = bf16[16,64,128]{2,1,0:T(8,128)(2,1)S(1)} collective-permute-done((bf16[16,64,128]{2,1,0:T(8,128)(2,1)S(1)}, bf16[16,64,128]{2,1,0:T(8,128)(2,1)S(1)}, u32[]{:S(2)}, u32[]{:S(2)}) %collective-permute-start.7) | collective-permute-done | bytes 262176 | tf_op jit(solution)/shard_map/ppermute | solution.py:178
  48.6 1.6 %collective-permute-start.8 = (bf16[8,64,128]{2,1,0:T(8,128)(2,1)S(1)}, bf16[8,64,128]{2,1,0:T(8,128)(2,1)S(1)}, u32[]{:S(2)}, u32[]{:S(2)}) collective-permute-start(bf16[8,64,128]{2,1,0:T(8,128)(2,1)S(1)} %fusion.6), channel_id=1, source_target_pairs={{0,8},{8,0},{16,24},{24,16},{1,9},{9,1},{17,25},{25,17},{2,10},{10... | collective-permute-start | bytes 393224 | tf_op jit(solution)/shard_map/ppermute | solution.py:178
  50.2 2.8 %shard_map.34 = f32[32,64,128]{2,1,0:T(8,128)S(1)} custom-call(bf16[8,3,64,128]{3,2,1,0:T(8,128)(2,1)S(1)} %pad_maximum_fusion.refs_0_, bf16[8,3,64,128]{3,2,1,0:T(8,128)(2,1)S(1)} %collective-permute-done.4.refs_1_, bf16[8,6,64,128]{3,2,1,0:T(8,128)(2,1)S(1)} %shard_map.28.refs_2_, f32[8,128]{1,0:T(8,128)S(1)} %pad_maximum_fusion.4.refs_3_, ...), custom_call_target="tpu_custom_call" | custom-call | flops 2147483648 | bytes 4194304 | tf_op jit(solution)/shard_map/pallas_call | solution.py:145
  53.8 2.7 %collective-permute-start.9 = (bf16[2,64,128]{1,2,0:T(8,128)(2,1)S(1)}, bf16[2,64,128]{1,2,0:T(8,128)(2,1)S(1)}, u32[]{:S(2)}, u32[]{:S(2)}) collective-permute-start(bf16[2,64,128]{1,2,0:T(8,128)(2,1)S(1)} %get-tuple-element.50), channel_id=1, source_target_pairs={{0,16},{8,24},{16,0},{24,8},{1,17},{9,25},{17,1},{25,9},{2,18},{10... | collective-permute-start | bytes 98312 | tf_op jit(solution)/shard_map/ppermute | solution.py:178
  58.4 3.0 %collective-permute-start.13 = (bf16[8,64,128]{2,1,0:T(8,128)(2,1)S(1)}, bf16[8,64,128]{2,1,0:T(8,128)(2,1)S(1)}, u32[]{:S(2)}, u32[]{:S(2)}) collective-permute-start(bf16[8,64,128]{2,1,0:T(8,128)(2,1)S(1)} %get-tuple-element.33), channel_id=1, source_target_pairs={{0,12},{2,14},{4,8},{6,10},{8,4},{10,6},{12,0},{14,2},{16,28},{18,... | collective-permute-start | bytes 393224 | tf_op jit(solution)/shard_map/ppermute | solution.py:178
  62.0 4.5 %collective-permute-done.13 = bf16[8,64,128]{2,1,0:T(8,128)(2,1)S(1)} collective-permute-done((bf16[8,64,128]{2,1,0:T(8,128)(2,1)S(1)}, bf16[8,64,128]{2,1,0:T(8,128)(2,1)S(1)}, u32[]{:S(2)}, u32[]{:S(2)}) %collective-permute-start.13) | collective-permute-done | bytes 131104 | tf_op jit(solution)/shard_map/ppermute | solution.py:178
  67.2 2.4 %collective-permute-start.16 = (bf16[2,64,128]{1,2,0:T(8,128)(2,1)S(1)}, bf16[2,64,128]{1,2,0:T(8,128)(2,1)S(1)}, u32[]{:S(2)}, u32[]{:S(2)}) collective-permute-start(bf16[2,64,128]{1,2,0:T(8,128)(2,1)S(1)} %get-tuple-element.53), channel_id=1, source_target_pairs={{0,16},{8,24},{16,0},{24,8},{1,17},{9,25},{17,1},{25,9},{2,18},{10... | collective-permute-start | bytes 98312 | tf_op jit(solution)/shard_map/ppermute | solution.py:178
  71.8 2.7 %collective-permute-done.16 = bf16[2,64,128]{1,2,0:T(8,128)(2,1)S(1)} collective-permute-done((bf16[2,64,128]{1,2,0:T(8,128)(2,1)S(1)}, bf16[2,64,128]{1,2,0:T(8,128)(2,1)S(1)}, u32[]{:S(2)}, u32[]{:S(2)}) %collective-permute-start.16) | collective-permute-done | bytes 32800 | tf_op jit(solution)/shard_map/ppermute | solution.py:178
  74.5 2.1 %collective-permute-done.18 = bf16[2,64,128]{1,2,0:T(8,128)(2,1)S(1)} collective-permute-done((bf16[2,64,128]{1,2,0:T(8,128)(2,1)S(1)}, bf16[2,64,128]{1,2,0:T(8,128)(2,1)S(1)}, u32[]{:S(2)}, u32[]{:S(2)}) %collective-permute-start.18) | collective-permute-done | bytes 32800 | tf_op jit(solution)/shard_map/ppermute | solution.py:178
  (67 shorter events, 11.9 us)
Async XLA Ops:
  0.0 8.6 %copy-start.2 = (f32[16,128]{1,0:T(8,128)S(1)}, f32[16,128]{1,0:T(8,128)}, u32[]{:S(2)}) copy-start(f32[16,128]{1,0:T(8,128)} %param.3) | copy-start | bytes 24580
  2.1 6.5 %collective-permute-start = (bf16[16,3,64]{2,0,1:T(8,128)(2,1)S(1)}, bf16[16,3,64]{2,0,1:T(8,128)(2,1)S(1)}, u32[]{:S(2)}, u32[]{:S(2)}) collective-permute-start(bf16[16,3,64]{2,0,1:T(8,128)(2,1)S(1)} %bitcast.35), channel_id=1, source_target_pairs={{0,2},{2,4},{4,6},{1,3},{3,5},{5,7},{8,10},{10,12},{12,14},{9,11},... | collective-permute-start | bytes 18440 | tf_op jit(solution)/shard_map/ppermute | solution.py:257
  4.8 5.2 %collective-permute-start.1 = (bf16[16,3,64]{2,0,1:T(8,128)(2,1)S(1)}, bf16[16,3,64]{2,0,1:T(8,128)(2,1)S(1)}, u32[]{:S(2)}, u32[]{:S(2)}) collective-permute-start(bf16[16,3,64]{2,0,1:T(8,128)(2,1)S(1)} %bitcast.36), channel_id=1, source_target_pairs={{2,0},{4,2},{6,4},{3,1},{5,3},{7,5},{10,8},{12,10},{14,12},{11,9},... | collective-permute-start | bytes 18440 | tf_op jit(solution)/shard_map/ppermute | solution.py:258
  6.2 13.4 %collective-permute-start.5 = (bf16[8,3,64,128]{3,2,1,0:T(8,128)(2,1)S(1)}, bf16[8,3,64,128]{3,2,1,0:T(8,128)(2,1)S(1)}, u32[]{:S(2)}, u32[]{:S(2)}) collective-permute-start(bf16[8,3,64,128]{3,2,1,0:T(8,128)(2,1)S(1)} %slice.188.refs_0_), channel_id=1, source_target_pairs={{0,1},{1,0},{2,3},{3,2},{4,5},{5,4},{6,7},{7,6},{8,9},{9,8},{10,11... | collective-permute-start | bytes 1179656 | tf_op jit(solution)/shard_map/ppermute | solution.py:178
  10.0 5.2 %collective-permute-start.2 = (bf16[1,3,64,128]{3,2,1,0:T(8,128)(2,1)S(1)}, bf16[1,3,64,128]{3,2,1,0:T(8,128)(2,1)S(1)}, u32[]{:S(2)}, u32[]{:S(2)}) collective-permute-start(bf16[1,3,64,128]{3,2,1,0:T(8,128)(2,1)S(1)} %get-tuple-element.37), channel_id=1, source_target_pairs={{0,8},{8,16},{16,24},{1,9},{9,17},{17,25},{2,10},{10,18},{18,26},{... | collective-permute-start | bytes 147464 | tf_op jit(solution)/shard_map/ppermute | solution.py:261
  13.5 6.0 %collective-permute-start.3 = (bf16[1,3,64,128]{3,2,1,0:T(8,128)(2,1)S(1)}, bf16[1,3,64,128]{3,2,1,0:T(8,128)(2,1)S(1)}, u32[]{:S(2)}, u32[]{:S(2)}) collective-permute-start(bf16[1,3,64,128]{3,2,1,0:T(8,128)(2,1)S(1)} %get-tuple-element.36), channel_id=1, source_target_pairs={{8,0},{16,8},{24,16},{9,1},{17,9},{25,17},{10,2},{18,10},{26,18},{... | collective-permute-start | bytes 147464 | tf_op jit(solution)/shard_map/ppermute | solution.py:262
  19.5 13.6 %collective-permute-start.4 = (bf16[8,3,64,128]{3,2,1,0:T(8,128)(2,1)S(1)}, bf16[8,3,64,128]{3,2,1,0:T(8,128)(2,1)S(1)}, u32[]{:S(2)}, u32[]{:S(2)}) collective-permute-start(bf16[8,3,64,128]{3,2,1,0:T(8,128)(2,1)S(1)} %pad_maximum_fusion.refs_0_), channel_id=1, source_target_pairs={{0,1},{1,0},{2,3},{3,2},{4,5},{5,4},{6,7},{7,6},{8,9},{9,8},{10,11... | collective-permute-start | bytes 1179656 | tf_op jit(solution)/shard_map/ppermute | solution.py:178
  32.4 4.7 %copy-start = (f32[128,64,128]{2,1,0:T(8,128)}, f32[128,64,128]{2,1,0:T(8,128)S(1)}, u32[]{:S(2)}) copy-start(f32[128,64,128]{2,1,0:T(8,128)S(1)} %shard_map.30.refs_4_) | copy-start | bytes 12582916
  36.1 3.9 %collective-permute-start.6 = (bf16[32,64,128]{2,1,0:T(8,128)(2,1)S(1)}, bf16[32,64,128]{2,1,0:T(8,128)(2,1)S(1)}, u32[]{:S(2)}, u32[]{:S(2)}) collective-permute-start(bf16[32,64,128]{2,1,0:T(8,128)(2,1)S(1)} %shard_map.31), channel_id=1, source_target_pairs={{0,2},{2,0},{4,6},{6,4},{1,3},{3,1},{5,7},{7,5},{8,10},{10,8},{12,... | collective-permute-start | bytes 1572872 | tf_op jit(solution)/shard_map/ppermute | solution.py:178
  40.1 8.4 %collective-permute-start.7 = (bf16[16,64,128]{2,1,0:T(8,128)(2,1)S(1)}, bf16[16,64,128]{2,1,0:T(8,128)(2,1)S(1)}, u32[]{:S(2)}, u32[]{:S(2)}) collective-permute-start(bf16[16,64,128]{2,1,0:T(8,128)(2,1)S(1)} %get-tuple-element.31), channel_id=1, source_target_pairs={{0,4},{2,6},{4,0},{6,2},{1,5},{3,7},{5,1},{7,3},{8,12},{10,14},{12... | collective-permute-start | bytes 786440 | tf_op jit(solution)/shard_map/ppermute | solution.py:178
  41.6 2.2 %copy-start.1 = (f32[128,64,128]{2,1,0:T(8,128)S(1)}, f32[128,64,128]{2,1,0:T(8,128)}, u32[]{:S(2)}) copy-start(f32[128,64,128]{2,1,0:T(8,128)} %copy-done) | copy-start | bytes 12582916
  46.6 11.6 %collective-permute-start.12 = (bf16[32,64,128]{2,1,0:T(8,128)(2,1)S(1)}, bf16[32,64,128]{2,1,0:T(8,128)(2,1)S(1)}, u32[]{:S(2)}, u32[]{:S(2)}) collective-permute-start(bf16[32,64,128]{2,1,0:T(8,128)(2,1)S(1)} %shard_map.33), channel_id=1, source_target_pairs={{0,2},{2,0},{4,6},{6,4},{1,3},{3,1},{5,7},{7,5},{8,10},{10,8},{12,... | collective-permute-start | bytes 1572872 | tf_op jit(solution)/shard_map/ppermute | solution.py:178
  48.6 5.0 %collective-permute-start.8 = (bf16[8,64,128]{2,1,0:T(8,128)(2,1)S(1)}, bf16[8,64,128]{2,1,0:T(8,128)(2,1)S(1)}, u32[]{:S(2)}, u32[]{:S(2)}) collective-permute-start(bf16[8,64,128]{2,1,0:T(8,128)(2,1)S(1)} %fusion.6), channel_id=1, source_target_pairs={{0,8},{8,0},{16,24},{24,16},{1,9},{9,1},{17,25},{25,17},{2,10},{10... | collective-permute-start | bytes 393224 | tf_op jit(solution)/shard_map/ppermute | solution.py:178
  53.8 7.7 %collective-permute-start.9 = (bf16[2,64,128]{1,2,0:T(8,128)(2,1)S(1)}, bf16[2,64,128]{1,2,0:T(8,128)(2,1)S(1)}, u32[]{:S(2)}, u32[]{:S(2)}) collective-permute-start(bf16[2,64,128]{1,2,0:T(8,128)(2,1)S(1)} %get-tuple-element.50), channel_id=1, source_target_pairs={{0,16},{8,24},{16,0},{24,8},{1,17},{9,25},{17,1},{25,9},{2,18},{10... | collective-permute-start | bytes 98312 | tf_op jit(solution)/shard_map/ppermute | solution.py:178
  56.5 13.1 %collective-permute-start.10 = (bf16[2,64,128]{1,2,0:T(8,128)(2,1)S(1)}, bf16[2,64,128]{1,2,0:T(8,128)(2,1)S(1)}, u32[]{:S(2)}, u32[]{:S(2)}) collective-permute-start(bf16[2,64,128]{1,2,0:T(8,128)(2,1)S(1)} %get-tuple-element.52), channel_id=1, source_target_pairs={{0,1},{1,0},{2,3},{3,2},{4,5},{5,4},{6,7},{7,6},{8,9},{9,8},{10,11... | collective-permute-start | bytes 98312 | tf_op jit(solution)/shard_map/ppermute | solution.py:178
  57.5 12.1 %collective-permute-start.11 = (bf16[2,64,128]{1,2,0:T(8,128)(2,1)S(1)}, bf16[2,64,128]{1,2,0:T(8,128)(2,1)S(1)}, u32[]{:S(2)}, u32[]{:S(2)}) collective-permute-start(bf16[2,64,128]{1,2,0:T(8,128)(2,1)S(1)} %get-tuple-element.51), channel_id=1, source_target_pairs={{0,17},{1,16},{8,25},{9,24},{16,1},{17,0},{24,9},{25,8},{2,19},{3,... | collective-permute-start | bytes 98312 | tf_op jit(solution)/shard_map/ppermute | solution.py:178
  58.4 8.1 %collective-permute-start.13 = (bf16[8,64,128]{2,1,0:T(8,128)(2,1)S(1)}, bf16[8,64,128]{2,1,0:T(8,128)(2,1)S(1)}, u32[]{:S(2)}, u32[]{:S(2)}) collective-permute-start(bf16[8,64,128]{2,1,0:T(8,128)(2,1)S(1)} %get-tuple-element.33), channel_id=1, source_target_pairs={{0,12},{2,14},{4,8},{6,10},{8,4},{10,6},{12,0},{14,2},{16,28},{18,... | collective-permute-start | bytes 393224 | tf_op jit(solution)/shard_map/ppermute | solution.py:178
  61.4 5.6 %collective-permute-start.14 = (bf16[8,64,128]{2,1,0:T(8,128)(2,1)S(1)}, bf16[8,64,128]{2,1,0:T(8,128)(2,1)S(1)}, u32[]{:S(2)}, u32[]{:S(2)}) collective-permute-start(bf16[8,64,128]{2,1,0:T(8,128)(2,1)S(1)} %get-tuple-element.35), channel_id=1, source_target_pairs={{0,4},{2,6},{4,0},{6,2},{1,5},{3,7},{5,1},{7,3},{8,12},{10,14},{12... | collective-permute-start | bytes 393224 | tf_op jit(solution)/shard_map/ppermute | solution.py:178
  61.5 5.5 %collective-permute-start.15 = (bf16[8,64,128]{2,1,0:T(8,128)(2,1)S(1)}, bf16[8,64,128]{2,1,0:T(8,128)(2,1)S(1)}, u32[]{:S(2)}, u32[]{:S(2)}) collective-permute-start(bf16[8,64,128]{2,1,0:T(8,128)(2,1)S(1)} %get-tuple-element.34), channel_id=1, source_target_pairs={{0,8},{8,0},{16,24},{24,16},{1,9},{9,1},{17,25},{25,17},{2,10},{10... | collective-permute-start | bytes 393224 | tf_op jit(solution)/shard_map/ppermute | solution.py:178
  67.2 7.2 %collective-permute-start.16 = (bf16[2,64,128]{1,2,0:T(8,128)(2,1)S(1)}, bf16[2,64,128]{1,2,0:T(8,128)(2,1)S(1)}, u32[]{:S(2)}, u32[]{:S(2)}) collective-permute-start(bf16[2,64,128]{1,2,0:T(8,128)(2,1)S(1)} %get-tuple-element.53), channel_id=1, source_target_pairs={{0,16},{8,24},{16,0},{24,8},{1,17},{9,25},{17,1},{25,9},{2,18},{10... | collective-permute-start | bytes 98312 | tf_op jit(solution)/shard_map/ppermute | solution.py:178
  69.6 4.9 %collective-permute-start.17 = (bf16[2,64,128]{1,2,0:T(8,128)(2,1)S(1)}, bf16[2,64,128]{1,2,0:T(8,128)(2,1)S(1)}, u32[]{:S(2)}, u32[]{:S(2)}) collective-permute-start(bf16[2,64,128]{1,2,0:T(8,128)(2,1)S(1)} %get-tuple-element.55), channel_id=1, source_target_pairs={{0,1},{1,0},{2,3},{3,2},{4,5},{5,4},{6,7},{7,6},{8,9},{9,8},{10,11... | collective-permute-start | bytes 98312 | tf_op jit(solution)/shard_map/ppermute | solution.py:178
  70.6 6.1 %collective-permute-start.18 = (bf16[2,64,128]{1,2,0:T(8,128)(2,1)S(1)}, bf16[2,64,128]{1,2,0:T(8,128)(2,1)S(1)}, u32[]{:S(2)}, u32[]{:S(2)}) collective-permute-start(bf16[2,64,128]{1,2,0:T(8,128)(2,1)S(1)} %get-tuple-element.54), channel_id=1, source_target_pairs={{0,17},{1,16},{8,25},{9,24},{16,1},{17,0},{24,9},{25,8},{2,19},{3,... | collective-permute-start | bytes 98312 | tf_op jit(solution)/shard_map/ppermute | solution.py:178

commit v4 on v3

--- a/solution.py
+++ b/solution.py
@@ -145,7 +145,8 @@
     return pl.pallas_call(
         body,
         grid=((high - low) // block,),
-        out_shape=jax.ShapeDtypeStruct((high - low, share, modes), dtype),
+        out_shape=jax.ShapeDtypeStruct((high - low, share, modes), dtype) if before is not None
+        else pltpu.VMEM((high - low, share, modes), dtype),
         in_specs=in_specs,
         out_specs=pl.BlockSpec(shape, lambda g: (g, 0, 0)),
         scratch_shapes=[
@@ -183,57 +184,87 @@
         yield code, [stage[n] for n in range(len(stage)) if (code >> (len(stage) - 1 - n)) & 1]
 
 
-def stages_of(sizes, last):
+def stages_of(sizes):
     order = send_order(sizes)
-    stages = [[order[0]]]
-    rest = order[1:]
-    if last:
-        stages.append(rest[:2])
-        rest = rest[2:]
-    stages += [[entry] for entry in rest]
-    return stages
-
-
-def pieces_sum(kept, arrived, low, high):
-    total = kept[low:high].astype(F32)
-    for array in arrived:
+    return [[order[0]], order[1:3]] + [[entry] for entry in order[3:]]
+
+
+def term_sum(terms, low, high):
+    total = terms[0][low:high].astype(F32)
+    for array in terms[1:]:
         total = total + array[low:high].astype(F32)
     return total
 
 
-def halve_stages(kept, arrived, stages, sizes):
-    for stage in stages[:-1]:
-        parts = 1 << len(stage)
-        length = kept.shape[0] // parts
-        received = []
-        for code, flips in reversed(list(subsets(stage))):
-            sent = pieces_sum(kept, arrived, code * length, (code + 1) * length).astype(BF16)
-            received.append(flip(sent, flips, sizes))
-        kept, arrived = pieces_sum(kept, arrived, 0, length), received
-    return kept, arrived
-
-
-def finish(kept, arrived, stage, sizes, share):
-    total = pieces_sum(kept, arrived, 0, kept.shape[0])
-    count = total.shape[0]
+def sends(terms, count, stage):
+    length = count >> len(stage)
+    return [
+        term_sum(terms, code * length, (code + 1) * length).astype(BF16)
+        for code, _ in reversed(list(subsets(stage)))
+    ]
+
+
+def exchange(terms, stage, sent, sizes):
+    received = [flip(array, flips, sizes) for array, (_, flips) in zip(sent, reversed(list(subsets(stage))))]
+    return terms + received
+
+
+def combine_kernel(*refs, chunks, terms, pair):
+    outs = refs[chunks * terms :]
+    count, share, modes = refs[0].shape
+    each = count // 2 // pair
+    for above in range(2):
+        for chunk in range(chunks):
+            for place in range(each):
+                rows = pl.ds(above * (count // 2) + place * pair, pair)
+                total = refs[chunk * terms][rows].astype(F32)
+                for ref in refs[chunk * terms + 1 : (chunk + 1) * terms]:
+                    total = total + ref[rows].astype(F32)
+                total = total.reshape(pair * share, modes).T
+                for swapped in range(2):
+                    out = outs[2 * above + swapped]
+                    out[chunk * each + place] = total[swapped * share : (swapped + 1) * share].astype(out.dtype)
+
+
+def assemble_kernel(own_ref, swapped_ref, above_ref, both_ref, out_ref, *, pair):
+    count, share, width = own_ref.shape
+    first = lax.axis_index("ma") == 0
+    for place in range(count):
+        mine = own_ref[place] + above_ref[place].astype(F32)
+        theirs = swapped_ref[place].astype(F32) + both_ref[place].astype(F32)
+        low = jnp.where(first, mine, theirs)
+        high = jnp.where(first, theirs, mine)
+        for part in range(pair):
+            lanes = slice(part * (width // pair), (part + 1) * (width // pair))
+            out_ref[place * pair + part] = jnp.concatenate([low[:, lanes], high[:, lanes]], 1)
+
+
+def finish(chunk_terms, count, stage, sizes):
+    chunks, terms = len(chunk_terms), len(chunk_terms[0])
+    _, share, modes = chunk_terms[0][0].shape
     pair = 2 if count % 4 == 0 else 1
-    total = jnp.transpose(total.reshape(count // pair, pair * share, 2 * share), (0, 2, 1))
-    length = count // pair // 2
-    pieces = {}
+    places = chunks * count // 2 // pair
+    shape = (places, share, pair * share)
+    whole = lambda shape: pl.BlockSpec(shape, lambda g: (0,) * len(shape))
+    parts = pl.pallas_call(
+        functools.partial(combine_kernel, chunks=chunks, terms=terms, pair=pair),
+        grid=(1,),
+        out_shape=[jax.ShapeDtypeStruct(shape, dtype) for dtype in (F32, BF16, BF16, BF16)],
+        in_specs=[whole((count, share, modes))] * (chunks * terms),
+        out_specs=[whole(shape)] * 4,
+        compiler_params=pltpu.CompilerParams(vmem_limit_bytes=16 << 20),
+        cost_estimate=pl.CostEstimate(flops=1, bytes_accessed=1024, transcendentals=0),
+    )(*[array for terms in chunk_terms for array in terms])
     stage = stage + [("ma", 0)]
-    for code, flips in reversed(list(subsets(stage))):
-        above, swapped = code >> 1, code & 1
-        sent = total[above * length : (above + 1) * length, swapped * share : (swapped + 1) * share]
-        pieces[code] = flip(sent.astype(BF16), flips, sizes).astype(F32)
-    mine = total[:length, :share] + pieces[2]
-    theirs = pieces[1] + pieces[3]
-    first = lax.axis_index("ma") == 0
-    rows = []
-    for part in range(pair):
-        lanes = slice(part * share, (part + 1) * share)
-        one, two = mine[:, :, lanes], theirs[:, :, lanes]
-        rows.append(jnp.concatenate([jnp.where(first, one, two), jnp.where(first, two, one)], 2))
-    return jnp.stack(rows, 1).reshape(count // 2, share, 2 * share)
+    arrived = {code: flip(parts[code], flips, sizes) for code, flips in reversed(list(subsets(stage)))}
+    return pl.pallas_call(
+        functools.partial(assemble_kernel, pair=pair),
+        out_shape=jax.ShapeDtypeStruct((places * pair, share, modes), F32),
+        in_specs=[pl.BlockSpec(memory_space=pltpu.VMEM)] * 4,
+        out_specs=pl.BlockSpec(memory_space=pltpu.VMEM),
+        compiler_params=pltpu.CompilerParams(vmem_limit_bytes=16 << 20),
+        cost_estimate=pl.CostEstimate(flops=1, bytes_accessed=1024, transcendentals=0),
+    )(parts[0], arrived[1], arrived[2], arrived[3])
 
 
 def shards(mode_fields, cell_volumes, sizes):
@@ -253,14 +284,15 @@
 
     own_inner, own_outer = inner_rows(own), outer_rows(own)
     other_inner = flip(own_inner, [("ma", 0)], sizes)
+    token = flip(own[quarter, 0, :16], [("ma", 0)], sizes)
+    held, token = barrier((own, token))
     forward, backward = neighbours("gy")
-    before = lax.ppermute(own[:, :, :, -1], "gy", forward)
-    after = lax.ppermute(own[:, :, :, 0], "gy", backward)
+    before = lax.ppermute(held[:, :, :, -1], "gy", forward)
+    after = lax.ppermute(held[:, :, :, 0], "gy", backward)
     forward, backward = neighbours("gx")
     held, before, after = barrier((own, before, after))
     above = lax.ppermute(held[-1:], "gx", forward)
     below = lax.ppermute(held[:1], "gx", backward)
-    token = other_inner[:1, 0, :8] + other_inner[1:2, 0, :8]
     own_outer_held, above, below = barrier((own_outer, above, below))
     other_outer = flip(own_outer_held, [("ma", 0)], sizes)
     all_rows = tuple(range(row_count))
@@ -273,23 +305,24 @@
     outer_weights = outer_rows(weights)
     chunks = chunks_of(modes // (sizes["gx"] * sizes["gy"]))
     length = modes // chunks
+    stages = stages_of(sizes)
     results = []
     for chunk in range(chunks):
         low, middle, high = chunk * length, chunk * length + length // 2, (chunk + 1) * length
         outer = functools.partial(partial_tensor, own_outer, other_outer, slopes_outer, sizes=sizes, before=inner)
-        stages = stages_of(sizes, chunk == chunks - 1)
         sent = outer(weights=outer_weights, positions=(middle, high), dtype=BF16)
         outer_weights, sent = barrier((outer_weights, sent))
-        arrived = [flip(sent, stages[0], sizes)]
-        kept = outer(weights=outer_weights, positions=(low, middle))
+        arrived = flip(sent, stages[0], sizes)
+        terms = [outer(weights=outer_weights, positions=(low, middle)), arrived]
+        sent = sends(terms, length // 2, stages[1])
         if chunk < chunks - 1:
-            outer_weights, kept, arrived = barrier((outer_weights, kept, arrived))
-        results.append((kept, arrived, stages))
-    finished = []
-    for kept, arrived, stages in results:
-        kept, arrived = halve_stages(kept, arrived, stages[1:], sizes)
-        finished.append(finish(kept, arrived, stages[-1], sizes, share))
-    return jnp.concatenate(finished, 0)
+            outer_weights, sent = barrier((outer_weights, sent))
+        results.append(exchange(terms, stages[1], sent, sizes))
+    count = (length // 2) >> len(stages[1])
+    for stage in stages[2:-1]:
+        results = [exchange(terms, stage, sends(terms, count, stage), sizes) for terms in results]
+        count = count >> len(stage)
+    return finish(results, count, stages[-1], sizes)
 
 
 def solution(mesh):

time: 78 us -> 72.7 us (0.932)
  starting transfers between devices: 29.3 us -> 26.5 us
  waiting for transfers between devices: 18 us -> 15.8 us
  local copies, waits for them, and re-layouts: 5.21 us -> 3.75 us
  Pallas kernels: 23.5 us -> 24.5 us
    ppermute x1, waiting for transfers between devices: 4.25 us -> 0.01 us  [shards(): below = lax.ppermute(held[:1], 'gx', backward)]
    ppermute x2, waiting for transfers between devices: 1.37 us -> 4.21 us  [the longest x1 4.21 us: shards(): after = lax.ppermute(held[:, :, :, 0], 'gy', backward)]
    ppermute x15 -> x14, starting transfers between devices: 20.9 us -> 18.1 us  [flip(): return lax.ppermute(array, axes, [(i, i ^ change) for i in range(count)])]
    unnamed x7 -> x1, local copies, waits for them, and re-layouts: 3.54 us -> 1.34 us
    ppermute x1, starting transfers between devices: 3.48 us -> 4.55 us  [shards(): above = lax.ppermute(held[-1:], 'gx', forward)]
    pallas_call x0 -> x2, Pallas kernels: none -> 1.06 us  [the longest x1 0.84 us: finish(): pl.pallas_call(functools.partial(assemble_kernel, pair=pair), out_shape=j...]
    ppermute x2, starting transfers between devices: 3.63 us -> 2.57 us  [the longest x1 1.29 us: shards(): after = lax.ppermute(held[:, :, :, 0], 'gy', backward)]
    ppermute x15 -> x14, waiting for transfers between devices: 12 us -> 11.3 us  [flip(): return lax.ppermute(array, axes, [(i, i ^ change) for i in range(count)])]
  transfers between devices with their start and end apart: 19 -> 18, of which waited for: 9 -> 8; matrix products, arithmetic and copies ran while one was open for 1% -> 5% of each run, Pallas kernels for 26% -> 24%
where the time goes in v4:
time: 72.7 us; the launch traced here: 72.4 us
  starting transfers between devices  26.5 us (36%)
  Pallas kernels  24.5 us (34%)
  waiting for transfers between devices  15.8 us (22%)
  local copies, waits for them, and re-layouts  3.75 us (5%)
  other arithmetic  1.61 us (2%)
    pallas_call x5, Pallas kernels, partial_tensor(): pl.pallas_call(body, grid=((high - low) // block,), out_shape=jax.ShapeDt...  22.1 us
    ppermute x14, starting transfers between devices, flip(): return lax.ppermute(array, axes, [(i, i ^ change) for i in range(count)])  18.1 us
    ppermute x14, waiting for transfers between devices, flip(): return lax.ppermute(array, axes, [(i, i ^ change) for i in range(count)])  11.3 us
    ppermute x1, starting transfers between devices, shards(): above = lax.ppermute(held[-1:], 'gx', forward)  4.55 us
    ppermute x1, waiting for transfers between devices, shards(): after = lax.ppermute(held[:, :, :, 0], 'gy', backward)  4.21 us
  transfers between devices with their start and end apart: 18, of which 8 were waited for; matrix products, arithmetic and copies ran while one was open for 5% of the time, Pallas kernels for 24%

profile of v4, /device:TPU:0, one launch (start us, length us, event | category | flops | bytes accessed | tf_op | source)
XLA Modules:
  0.0 72.4 jit_solution(6911157879385912129)
XLA Ops:
  0.0 1.3 %copy.10 = bf16[3,64,16,128]{3,1,0,2:T(8,128)(2,1)S(1)} copy(bf16[3,64,16,128]{3,2,1,0:T(8,128)(2,1)} %param.2) | data formatting | bytes 1572864 | tf_op args[0]
  1.3 3.0 %collective-permute-start = (bf16[16,128]{1,0:T(8,128)(2,1)S(1)}, bf16[16,128]{1,0:T(8,128)(2,1)S(1)}, u32[]{:S(2)}, u32[]{:S(2)}) collective-permute-start(bf16[16,128]{1,0:T(8,128)(2,1)S(1)} %slice_bitcast_fusion), channel_id=1, source_target_pairs={{0,1},{1,0},{2,3},{3,2},{4,5},{5,4},{6,7},{7,6},{8,9},{9,8},{10,11... | collective-permute-start | bytes 12296 | tf_op jit(solution)/shard_map/ppermute | solution.py:179
  7.7 1.3 %collective-permute-start.1 = (bf16[16,3,64]{2,0,1:T(8,128)(2,1)S(1)}, bf16[16,3,64]{2,0,1:T(8,128)(2,1)S(1)}, u32[]{:S(2)}, u32[]{:S(2)}) collective-permute-start(bf16[16,3,64]{2,0,1:T(8,128)(2,1)S(1)} %bitcast.15), channel_id=1, source_target_pairs={{0,2},{2,4},{4,6},{1,3},{3,5},{5,7},{8,10},{10,12},{12,14},{9,11},... | collective-permute-start | bytes 18440 | tf_op jit(solution)/shard_map/ppermute | solution.py:290
  9.0 1.3 %collective-permute-start.2 = (bf16[16,3,64]{2,0,1:T(8,128)(2,1)}, bf16[16,3,64]{2,0,1:T(8,128)(2,1)S(1)}, u32[]{:S(2)}, u32[]{:S(2)}) collective-permute-start(bf16[16,3,64]{2,0,1:T(8,128)(2,1)} %bitcast.14), channel_id=1, source_target_pairs={{2,0},{4,2},{6,4},{3,1},{5,3},{7,5},{10,8},{12,10},{14,12},{11,9},... | collective-permute-start | bytes 18440 | tf_op jit(solution)/shard_map/ppermute | solution.py:291
  10.3 4.2 %collective-permute-done.2 = bf16[16,3,64]{2,0,1:T(8,128)(2,1)S(1)} collective-permute-done((bf16[16,3,64]{2,0,1:T(8,128)(2,1)}, bf16[16,3,64]{2,0,1:T(8,128)(2,1)S(1)}, u32[]{:S(2)}, u32[]{:S(2)}) %collective-permute-start.2) | collective-permute-done | bytes 6176 | tf_op jit(solution)/shard_map/ppermute | solution.py:291
  14.5 1.3 %collective-permute-start.4 = (bf16[1,3,64,128]{3,2,1,0:T(8,128)(2,1)S(1)}, bf16[1,3,64,128]{3,2,1,0:T(8,128)(2,1)S(1)}, u32[]{:S(2)}, u32[]{:S(2)}) collective-permute-start(bf16[1,3,64,128]{3,2,1,0:T(8,128)(2,1)S(1)} %get-tuple-element.51), channel_id=1, source_target_pairs={{8,0},{16,8},{24,16},{9,1},{17,9},{25,17},{10,2},{18,10},{26,18},{... | collective-permute-start | bytes 147464 | tf_op jit(solution)/shard_map/ppermute | solution.py:295
  15.8 4.5 %collective-permute-start.3 = (bf16[1,3,64,128]{3,2,1,0:T(8,128)(2,1)S(1)}, bf16[1,3,64,128]{3,2,1,0:T(8,128)(2,1)S(1)}, u32[]{:S(2)}, u32[]{:S(2)}) collective-permute-start(bf16[1,3,64,128]{3,2,1,0:T(8,128)(2,1)S(1)} %get-tuple-element.52), channel_id=1, source_target_pairs={{0,8},{8,16},{16,24},{1,9},{9,17},{17,25},{2,10},{10,18},{18,26},{... | collective-permute-start | bytes 147464 | tf_op jit(solution)/shard_map/ppermute | solution.py:294
  22.1 1.5 %collective-permute-start.5 = (bf16[8,3,64,128]{3,2,1,0:T(8,128)(2,1)S(1)}, bf16[8,3,64,128]{3,2,1,0:T(8,128)(2,1)S(1)}, u32[]{:S(2)}, u32[]{:S(2)}) collective-permute-start(bf16[8,3,64,128]{3,2,1,0:T(8,128)(2,1)S(1)} %pad_maximum_fusion.refs_0_), channel_id=1, source_target_pairs={{0,1},{1,0},{2,3},{3,2},{4,5},{5,4},{6,7},{7,6},{8,9},{9,8},{10,11... | collective-permute-start | bytes 1179656 | tf_op jit(solution)/shard_map/ppermute | solution.py:179
  24.3 10.6 %shard_map.30.refs_4_ = f32[128,64,128]{2,1,0:T(8,128)S(1)} custom-call(bf16[8,3,64,128]{3,2,1,0:T(8,128)(2,1)S(1)} %slice.97.refs_0_, bf16[8,3,64,128]{3,2,1,0:T(8,128)(2,1)S(1)} %collective-permute-done.6.refs_1_, bf16[8,6,64,128]{3,2,1,0:T(8,128)(2,1)S(1)} %shard_map.29.refs_2_, f32[8,128]{1,0:T(8,128)S(1)} %slice.98.refs_3_), custom_call_target="tpu_custom_call" | custom-call | flops 8589934592 | bytes 4194304 | tf_op jit(solution)/shard_map/pallas_call | solution.py:145
  34.9 2.9 %shard_map.31 = bf16[32,64,128]{2,1,0:T(8,128)(2,1)S(1)} custom-call(bf16[8,3,64,128]{3,2,1,0:T(8,128)(2,1)S(1)} %pad_maximum_fusion.refs_0_, bf16[8,3,64,128]{3,2,1,0:T(8,128)(2,1)S(1)} %collective-permute-done.5.refs_1_, bf16[8,6,64,128]{3,2,1,0:T(8,128)(2,1)S(1)} %shard_map.28.refs_2_, f32[8,128]{1,0:T(8,128)S(1)} %pad_maximum_fusion.1.refs_3_, ...), custom_call_target="tpu_custom_call" | custom-call | flops 2147483648 | bytes 4194304 | tf_op jit(solution)/shard_map/pallas_call | solution.py:145
  37.9 1.4 %collective-permute-start.7 = (bf16[32,64,128]{2,1,0:T(8,128)(2,1)S(1)}, bf16[32,64,128]{2,1,0:T(8,128)(2,1)S(1)}, u32[]{:S(2)}, u32[]{:S(2)}) collective-permute-start(bf16[32,64,128]{2,1,0:T(8,128)(2,1)S(1)} %shard_map.31), channel_id=1, source_target_pairs={{0,2},{2,0},{4,6},{6,4},{1,3},{3,1},{5,7},{7,5},{8,10},{10,8},{12,... | collective-permute-start | bytes 1572872 | tf_op jit(solution)/shard_map/ppermute | solution.py:179
  39.3 2.8 %shard_map.32.refs_0_ = f32[32,64,128]{2,1,0:T(8,128)S(1)} custom-call(bf16[8,3,64,128]{3,2,1,0:T(8,128)(2,1)S(1)} %pad_maximum_fusion.refs_0_, bf16[8,3,64,128]{3,2,1,0:T(8,128)(2,1)S(1)} %collective-permute-done.5.refs_1_, bf16[8,6,64,128]{3,2,1,0:T(8,128)(2,1)S(1)} %shard_map.28.refs_2_, f32[8,128]{1,0:T(8,128)S(1)} %pad_maximum_fusion.1.refs_3_, ...), custom_call_target="tpu_custom_call" | custom-call | flops 2147483648 | bytes 4194304 | tf_op jit(solution)/shard_map/pallas_call | solution.py:145
  42.3 2.9 %shard_map.33 = bf16[32,64,128]{2,1,0:T(8,128)(2,1)S(1)} custom-call(bf16[8,3,64,128]{3,2,1,0:T(8,128)(2,1)S(1)} %pad_maximum_fusion.refs_0_, bf16[8,3,64,128]{3,2,1,0:T(8,128)(2,1)S(1)} %collective-permute-done.5.refs_1_, bf16[8,6,64,128]{3,2,1,0:T(8,128)(2,1)S(1)} %shard_map.28.refs_2_, f32[8,128]{1,0:T(8,128)S(1)} %pad_maximum_fusion.1.refs_3_, ...), custom_call_target="tpu_custom_call" | custom-call | flops 2147483648 | bytes 4194304 | tf_op jit(solution)/shard_map/pallas_call | solution.py:145
  45.3 3.2 %collective-permute-start.8 = (bf16[8,64,128]{2,1,0:T(8,128)(2,1)S(1)}, bf16[8,64,128]{2,1,0:T(8,128)(2,1)S(1)}, u32[]{:S(2)}, u32[]{:S(2)}) collective-permute-start(bf16[8,64,128]{2,1,0:T(8,128)(2,1)S(1)} %get-tuple-element.35), channel_id=1, source_target_pairs={{0,12},{2,14},{4,8},{6,10},{8,4},{10,6},{12,0},{14,2},{16,28},{18,... | collective-permute-start | bytes 393224 | tf_op jit(solution)/shard_map/ppermute | solution.py:179
  49.0 2.8 %shard_map.34.refs_5_ = f32[32,64,128]{2,1,0:T(8,128)S(1)} custom-call(bf16[8,3,64,128]{3,2,1,0:T(8,128)(2,1)S(1)} %pad_maximum_fusion.refs_0_, bf16[8,3,64,128]{3,2,1,0:T(8,128)(2,1)S(1)} %collective-permute-done.5.refs_1_, bf16[8,6,64,128]{3,2,1,0:T(8,128)(2,1)S(1)} %shard_map.28.refs_2_, f32[8,128]{1,0:T(8,128)S(1)} %pad_maximum_fusion.1.refs_3_, ...), custom_call_target="tpu_custom_call" | custom-call | flops 2147483648 | bytes 4194304 | tf_op jit(solution)/shard_map/pallas_call | solution.py:145
  52.0 1.5 %collective-permute-start.14 = (bf16[8,64,128]{2,1,0:T(8,128)(2,1)S(1)}, bf16[8,64,128]{2,1,0:T(8,128)(2,1)S(1)}, u32[]{:S(2)}, u32[]{:S(2)}) collective-permute-start(bf16[8,64,128]{2,1,0:T(8,128)(2,1)S(1)} %get-tuple-element.45), channel_id=1, source_target_pairs={{0,8},{8,0},{16,24},{24,16},{1,9},{9,1},{17,25},{25,17},{2,10},{10... | collective-permute-start | bytes 393224 | tf_op jit(solution)/shard_map/ppermute | solution.py:179
  53.5 2.0 %collective-permute-start.13 = (bf16[8,64,128]{2,1,0:T(8,128)(2,1)S(1)}, bf16[8,64,128]{2,1,0:T(8,128)(2,1)S(1)}, u32[]{:S(2)}, u32[]{:S(2)}) collective-permute-start(bf16[8,64,128]{2,1,0:T(8,128)(2,1)S(1)} %get-tuple-element.46), channel_id=1, source_target_pairs={{0,4},{2,6},{4,0},{6,2},{1,5},{3,7},{5,1},{7,3},{8,12},{10,14},{12... | collective-permute-start | bytes 393224 | tf_op jit(solution)/shard_map/ppermute | solution.py:179
  55.8 2.2 %collective-permute-done.14.refs_9_ = bf16[8,64,128]{2,1,0:T(8,128)(2,1)S(1)} collective-permute-done((bf16[8,64,128]{2,1,0:T(8,128)(2,1)S(1)}, bf16[8,64,128]{2,1,0:T(8,128)(2,1)S(1)}, u32[]{:S(2)}, u32[]{:S(2)}) %collective-permute-start.14) | collective-permute-done | bytes 131104 | tf_op jit(solution)/shard_map/ppermute | solution.py:179
  58.0 2.3 %collective-permute-done.13.refs_8_ = bf16[8,64,128]{2,1,0:T(8,128)(2,1)S(1)} collective-permute-done((bf16[8,64,128]{2,1,0:T(8,128)(2,1)S(1)}, bf16[8,64,128]{2,1,0:T(8,128)(2,1)S(1)}, u32[]{:S(2)}, u32[]{:S(2)}) %collective-permute-start.13) | collective-permute-done | bytes 131104 | tf_op jit(solution)/shard_map/ppermute | solution.py:179
  60.3 1.1 %collective-permute-done.12.refs_7_ = bf16[8,64,128]{2,1,0:T(8,128)(2,1)S(1)} collective-permute-done((bf16[8,64,128]{2,1,0:T(8,128)(2,1)S(1)}, bf16[8,64,128]{2,1,0:T(8,128)(2,1)S(1)}, u32[]{:S(2)}, u32[]{:S(2)}) %collective-permute-start.12) | collective-permute-done | bytes 131104 | tf_op jit(solution)/shard_map/ppermute | solution.py:179
  62.3 2.5 %collective-permute-start.16 = (bf16[4,64,128]{2,1,0:T(8,128)(2,1)S(1)}, bf16[4,64,128]{2,1,0:T(8,128)(2,1)S(1)}, u32[]{:S(2)}, u32[]{:S(2)}) collective-permute-start(bf16[4,64,128]{2,1,0:T(8,128)(2,1)S(1)} %get-tuple-element.43), channel_id=1, source_target_pairs={{0,16},{8,24},{16,0},{24,8},{1,17},{9,25},{17,1},{25,9},{2,18},{10... | collective-permute-start | bytes 196616 | tf_op jit(solution)/shard_map/ppermute | solution.py:179
  64.8 1.3 %collective-permute-start.17 = (bf16[4,64,128]{2,1,0:T(8,128)(2,1)S(1)}, bf16[4,64,128]{2,1,0:T(8,128)(2,1)S(1)}, u32[]{:S(2)}, u32[]{:S(2)}) collective-permute-start(bf16[4,64,128]{2,1,0:T(8,128)(2,1)S(1)} %get-tuple-element.44), channel_id=1, source_target_pairs={{0,17},{1,16},{8,25},{9,24},{16,1},{17,0},{24,9},{25,8},{2,19},{3,... | collective-permute-start | bytes 196616 | tf_op jit(solution)/shard_map/ppermute | solution.py:179
  66.1 3.3 %collective-permute-done.16.above_ref = bf16[4,64,128]{2,1,0:T(8,128)(2,1)S(1)} collective-permute-done((bf16[4,64,128]{2,1,0:T(8,128)(2,1)S(1)}, bf16[4,64,128]{2,1,0:T(8,128)(2,1)S(1)}, u32[]{:S(2)}, u32[]{:S(2)}) %collective-permute-start.16) | collective-permute-done | bytes 65568 | tf_op jit(solution)/shard_map/ppermute | solution.py:179
  69.4 2.2 %collective-permute-done.17.both_ref = bf16[4,64,128]{2,1,0:T(8,128)(2,1)S(1)} collective-permute-done((bf16[4,64,128]{2,1,0:T(8,128)(2,1)S(1)}, bf16[4,64,128]{2,1,0:T(8,128)(2,1)S(1)}, u32[]{:S(2)}, u32[]{:S(2)}) %collective-permute-start.17) | collective-permute-done | bytes 65568 | tf_op jit(solution)/shard_map/ppermute | solution.py:179
  (40 shorter events, 8.5 us)
Async XLA Ops:
  1.3 4.6 %collective-permute-start = (bf16[16,128]{1,0:T(8,128)(2,1)S(1)}, bf16[16,128]{1,0:T(8,128)(2,1)S(1)}, u32[]{:S(2)}, u32[]{:S(2)}) collective-permute-start(bf16[16,128]{1,0:T(8,128)(2,1)S(1)} %slice_bitcast_fusion), channel_id=1, source_target_pairs={{0,1},{1,0},{2,3},{3,2},{4,5},{5,4},{6,7},{7,6},{8,9},{9,8},{10,11... | collective-permute-start | bytes 12296 | tf_op jit(solution)/shard_map/ppermute | solution.py:179
  4.4 20.0 %collective-permute-start.6 = (bf16[8,3,64,128]{3,2,1,0:T(8,128)(2,1)S(1)}, bf16[8,3,64,128]{3,2,1,0:T(8,128)(2,1)S(1)}, u32[]{:S(2)}, u32[]{:S(2)}) collective-permute-start(bf16[8,3,64,128]{3,2,1,0:T(8,128)(2,1)S(1)} %slice.97.refs_0_), channel_id=1, source_target_pairs={{0,1},{1,0},{2,3},{3,2},{4,5},{5,4},{6,7},{7,6},{8,9},{9,8},{10,11... | collective-permute-start | bytes 1179656 | tf_op jit(solution)/shard_map/ppermute | solution.py:179
  7.7 2.6 %collective-permute-start.1 = (bf16[16,3,64]{2,0,1:T(8,128)(2,1)S(1)}, bf16[16,3,64]{2,0,1:T(8,128)(2,1)S(1)}, u32[]{:S(2)}, u32[]{:S(2)}) collective-permute-start(bf16[16,3,64]{2,0,1:T(8,128)(2,1)S(1)} %bitcast.15), channel_id=1, source_target_pairs={{0,2},{2,4},{4,6},{1,3},{3,5},{5,7},{8,10},{10,12},{12,14},{9,11},... | collective-permute-start | bytes 18440 | tf_op jit(solution)/shard_map/ppermute | solution.py:290
  9.0 5.6 %collective-permute-start.2 = (bf16[16,3,64]{2,0,1:T(8,128)(2,1)}, bf16[16,3,64]{2,0,1:T(8,128)(2,1)S(1)}, u32[]{:S(2)}, u32[]{:S(2)}) collective-permute-start(bf16[16,3,64]{2,0,1:T(8,128)(2,1)} %bitcast.14), channel_id=1, source_target_pairs={{2,0},{4,2},{6,4},{3,1},{5,3},{7,5},{10,8},{12,10},{14,12},{11,9},... | collective-permute-start | bytes 18440 | tf_op jit(solution)/shard_map/ppermute | solution.py:291
  14.5 7.3 %collective-permute-start.4 = (bf16[1,3,64,128]{3,2,1,0:T(8,128)(2,1)S(1)}, bf16[1,3,64,128]{3,2,1,0:T(8,128)(2,1)S(1)}, u32[]{:S(2)}, u32[]{:S(2)}) collective-permute-start(bf16[1,3,64,128]{3,2,1,0:T(8,128)(2,1)S(1)} %get-tuple-element.51), channel_id=1, source_target_pairs={{8,0},{16,8},{24,16},{9,1},{17,9},{25,17},{10,2},{18,10},{26,18},{... | collective-permute-start | bytes 147464 | tf_op jit(solution)/shard_map/ppermute | solution.py:295
  15.8 6.3 %collective-permute-start.3 = (bf16[1,3,64,128]{3,2,1,0:T(8,128)(2,1)S(1)}, bf16[1,3,64,128]{3,2,1,0:T(8,128)(2,1)S(1)}, u32[]{:S(2)}, u32[]{:S(2)}) collective-permute-start(bf16[1,3,64,128]{3,2,1,0:T(8,128)(2,1)S(1)} %get-tuple-element.52), channel_id=1, source_target_pairs={{0,8},{8,16},{16,24},{1,9},{9,17},{17,25},{2,10},{10,18},{18,26},{... | collective-permute-start | bytes 147464 | tf_op jit(solution)/shard_map/ppermute | solution.py:294
  22.1 12.8 %collective-permute-start.5 = (bf16[8,3,64,128]{3,2,1,0:T(8,128)(2,1)S(1)}, bf16[8,3,64,128]{3,2,1,0:T(8,128)(2,1)S(1)}, u32[]{:S(2)}, u32[]{:S(2)}) collective-permute-start(bf16[8,3,64,128]{3,2,1,0:T(8,128)(2,1)S(1)} %pad_maximum_fusion.refs_0_), channel_id=1, source_target_pairs={{0,1},{1,0},{2,3},{3,2},{4,5},{5,4},{6,7},{7,6},{8,9},{9,8},{10,11... | collective-permute-start | bytes 1179656 | tf_op jit(solution)/shard_map/ppermute | solution.py:179
  37.9 4.3 %collective-permute-start.7 = (bf16[32,64,128]{2,1,0:T(8,128)(2,1)S(1)}, bf16[32,64,128]{2,1,0:T(8,128)(2,1)S(1)}, u32[]{:S(2)}, u32[]{:S(2)}) collective-permute-start(bf16[32,64,128]{2,1,0:T(8,128)(2,1)S(1)} %shard_map.31), channel_id=1, source_target_pairs={{0,2},{2,0},{4,6},{6,4},{1,3},{3,1},{5,7},{7,5},{8,10},{10,8},{12,... | collective-permute-start | bytes 1572872 | tf_op jit(solution)/shard_map/ppermute | solution.py:179
  45.2 6.7 %collective-permute-start.11 = (bf16[32,64,128]{2,1,0:T(8,128)(2,1)S(1)}, bf16[32,64,128]{2,1,0:T(8,128)(2,1)S(1)}, u32[]{:S(2)}, u32[]{:S(2)}) collective-permute-start(bf16[32,64,128]{2,1,0:T(8,128)(2,1)S(1)} %shard_map.33), channel_id=1, source_target_pairs={{0,2},{2,0},{4,6},{6,4},{1,3},{3,1},{5,7},{7,5},{8,10},{10,8},{12,... | collective-permute-start | bytes 1572872 | tf_op jit(solution)/shard_map/ppermute | solution.py:179
  45.3 10.3 %collective-permute-start.8 = (bf16[8,64,128]{2,1,0:T(8,128)(2,1)S(1)}, bf16[8,64,128]{2,1,0:T(8,128)(2,1)S(1)}, u32[]{:S(2)}, u32[]{:S(2)}) collective-permute-start(bf16[8,64,128]{2,1,0:T(8,128)(2,1)S(1)} %get-tuple-element.35), channel_id=1, source_target_pairs={{0,12},{2,14},{4,8},{6,10},{8,4},{10,6},{12,0},{14,2},{16,28},{18,... | collective-permute-start | bytes 393224 | tf_op jit(solution)/shard_map/ppermute | solution.py:179
  48.5 7.3 %collective-permute-start.9 = (bf16[8,64,128]{2,1,0:T(8,128)(2,1)S(1)}, bf16[8,64,128]{2,1,0:T(8,128)(2,1)S(1)}, u32[]{:S(2)}, u32[]{:S(2)}) collective-permute-start(bf16[8,64,128]{2,1,0:T(8,128)(2,1)S(1)} %get-tuple-element.36), channel_id=1, source_target_pairs={{0,4},{2,6},{4,0},{6,2},{1,5},{3,7},{5,1},{7,3},{8,12},{10,14},{12... | collective-permute-start | bytes 393224 | tf_op jit(solution)/shard_map/ppermute | solution.py:179
  48.5 7.3 %collective-permute-start.10 = (bf16[8,64,128]{2,1,0:T(8,128)(2,1)S(1)}, bf16[8,64,128]{2,1,0:T(8,128)(2,1)S(1)}, u32[]{:S(2)}, u32[]{:S(2)}) collective-permute-start(bf16[8,64,128]{2,1,0:T(8,128)(2,1)S(1)} %get-tuple-element.37), channel_id=1, source_target_pairs={{0,8},{8,0},{16,24},{24,16},{1,9},{9,1},{17,25},{25,17},{2,10},{10... | collective-permute-start | bytes 393224 | tf_op jit(solution)/shard_map/ppermute | solution.py:179
  52.0 6.0 %collective-permute-start.14 = (bf16[8,64,128]{2,1,0:T(8,128)(2,1)S(1)}, bf16[8,64,128]{2,1,0:T(8,128)(2,1)S(1)}, u32[]{:S(2)}, u32[]{:S(2)}) collective-permute-start(bf16[8,64,128]{2,1,0:T(8,128)(2,1)S(1)} %get-tuple-element.45), channel_id=1, source_target_pairs={{0,8},{8,0},{16,24},{24,16},{1,9},{9,1},{17,25},{25,17},{2,10},{10... | collective-permute-start | bytes 393224 | tf_op jit(solution)/shard_map/ppermute | solution.py:179
  53.5 6.8 %collective-permute-start.13 = (bf16[8,64,128]{2,1,0:T(8,128)(2,1)S(1)}, bf16[8,64,128]{2,1,0:T(8,128)(2,1)S(1)}, u32[]{:S(2)}, u32[]{:S(2)}) collective-permute-start(bf16[8,64,128]{2,1,0:T(8,128)(2,1)S(1)} %get-tuple-element.46), channel_id=1, source_target_pairs={{0,4},{2,6},{4,0},{6,2},{1,5},{3,7},{5,1},{7,3},{8,12},{10,14},{12... | collective-permute-start | bytes 393224 | tf_op jit(solution)/shard_map/ppermute | solution.py:179
  55.6 5.9 %collective-permute-start.12 = (bf16[8,64,128]{2,1,0:T(8,128)(2,1)S(1)}, bf16[8,64,128]{2,1,0:T(8,128)(2,1)S(1)}, u32[]{:S(2)}, u32[]{:S(2)}) collective-permute-start(bf16[8,64,128]{2,1,0:T(8,128)(2,1)S(1)} %get-tuple-element.47), channel_id=1, source_target_pairs={{0,12},{2,14},{4,8},{6,10},{8,4},{10,6},{12,0},{14,2},{16,28},{18,... | collective-permute-start | bytes 393224 | tf_op jit(solution)/shard_map/ppermute | solution.py:179
  61.6 4.5 %collective-permute-start.15 = (bf16[4,64,128]{2,1,0:T(8,128)(2,1)S(1)}, bf16[4,64,128]{2,1,0:T(8,128)(2,1)S(1)}, u32[]{:S(2)}, u32[]{:S(2)}) collective-permute-start(bf16[4,64,128]{2,1,0:T(8,128)(2,1)S(1)} %get-tuple-element.42), channel_id=1, source_target_pairs={{0,1},{1,0},{2,3},{3,2},{4,5},{5,4},{6,7},{7,6},{8,9},{9,8},{10,11... | collective-permute-start | bytes 196616 | tf_op jit(solution)/shard_map/ppermute | solution.py:179
  62.3 7.1 %collective-permute-start.16 = (bf16[4,64,128]{2,1,0:T(8,128)(2,1)S(1)}, bf16[4,64,128]{2,1,0:T(8,128)(2,1)S(1)}, u32[]{:S(2)}, u32[]{:S(2)}) collective-permute-start(bf16[4,64,128]{2,1,0:T(8,128)(2,1)S(1)} %get-tuple-element.43), channel_id=1, source_target_pairs={{0,16},{8,24},{16,0},{24,8},{1,17},{9,25},{17,1},{25,9},{2,18},{10... | collective-permute-start | bytes 196616 | tf_op jit(solution)/shard_map/ppermute | solution.py:179
  64.8 6.8 %collective-permute-start.17 = (bf16[4,64,128]{2,1,0:T(8,128)(2,1)S(1)}, bf16[4,64,128]{2,1,0:T(8,128)(2,1)S(1)}, u32[]{:S(2)}, u32[]{:S(2)}) collective-permute-start(bf16[4,64,128]{2,1,0:T(8,128)(2,1)S(1)} %get-tuple-element.44), channel_id=1, source_target_pairs={{0,17},{1,16},{8,25},{9,24},{16,1},{17,0},{24,9},{25,8},{2,19},{3,... | collective-permute-start | bytes 196616 | tf_op jit(solution)/shard_map/ppermute | solution.py:179

commit v5 on v4

--- a/solution.py
+++ b/solution.py
@@ -23,14 +23,13 @@
     return order
 
 
-def source_bits(sizes, rows_each, chunks):
+def source_bits(sizes, rows_each):
     row_bits = bits_of(rows_each)
     base = {"gy": row_bits, "gx": row_bits + bits_of(sizes["gy"])}
-    inner = row_bits - bits_of(chunks)
-    found = list(range(inner))
+    found = list(range(row_bits))
     for axis, bit in reversed(send_order(sizes)):
         found.append(base[axis] + bit)
-    return found + list(range(inner, row_bits))
+    return found
 
 
 def slopes_kernel(own_ref, before_ref, after_ref, *refs, rows):
@@ -64,12 +63,8 @@
     )(own, before.reshape(3 * row_count, share), after.reshape(3 * row_count, share), *edges, token)
 
 
-def chunks_of(rows_each):
-    return 2 if rows_each > 1 else 1
-
-
-def tensor_kernel(*refs, bits, block, rows_each, first_step):
-    own_ref, other_ref, slope_ref, weight_ref = refs[:4]
+def tensor_kernel(*refs, bits, block, rows_each, first_step, rows, scale):
+    own_ref, other_ref, slope_ref, volume_ref = refs[:4]
     before_ref = refs[4] if len(refs) == 8 else None
     out_ref, left, right = refs[-3:]
     row_count, _, share, cells = own_ref.shape
@@ -79,7 +74,7 @@
     @pl.when(step == 0)
     def _():
         for x in range(row_count):
-            weight = weight_ref[pl.ds(x, 1), :]
+            weight = volume_ref[pl.ds(rows[x], 1), :] * scale
             for half, ref in enumerate((own_ref, other_ref)):
                 for a in range(3):
                     value = (weight * ref[x, a].astype(F32)).astype(BF16)
@@ -121,23 +116,26 @@
     out_ref[...] = product.astype(out_ref.dtype)
 
 
-def partial_tensor(own, other, slopes, weights, sizes, positions, before=None, dtype=F32):
+def partial_tensor(own, other, slopes, volumes, rows, sizes, positions, before=None, dtype=F32):
     row_count, _, share, cells = own.shape
     modes = 2 * share
     low, high = positions
     block = min(16, high - low)
     first_step = low // block
-    rows_each = modes // (sizes["gx"] * sizes["gy"])
+    devices = sizes["gx"] * sizes["gy"]
+    rows_each = modes // devices
     body = functools.partial(
         tensor_kernel,
-        bits=source_bits(sizes, rows_each, chunks_of(rows_each)),
+        bits=source_bits(sizes, rows_each),
         block=block,
         rows_each=rows_each,
         first_step=first_step,
+        rows=rows,
+        scale=1.0 / math.sqrt(volumes.shape[0] * volumes.shape[1] * devices),
     )
     whole = lambda array: pl.BlockSpec(array.shape, lambda g: (0,) * array.ndim, pipeline_mode=pl.Buffered(1))
     shape = (block, share, modes)
-    operands = [own, other, slopes, weights]
+    operands = [own, other, slopes, volumes]
     in_specs = [whole(array) for array in operands]
     if before is not None:
         operands.append(before)
@@ -199,31 +197,28 @@
 def sends(terms, count, stage):
     length = count >> len(stage)
     return [
-        term_sum(terms, code * length, (code + 1) * length).astype(BF16)
-        for code, _ in reversed(list(subsets(stage)))
+        term_sum(terms, code * length, (code + 1) * length).astype(BF16) for code, _ in subsets(stage)
     ]
 
 
-def exchange(terms, stage, sent, sizes):
-    received = [flip(array, flips, sizes) for array, (_, flips) in zip(sent, reversed(list(subsets(stage))))]
-    return terms + received
-
-
-def combine_kernel(*refs, chunks, terms, pair):
-    outs = refs[chunks * terms :]
+def exchange(stage, sent, sizes):
+    return [flip(array, flips, sizes) for array, (_, flips) in zip(sent, subsets(stage))]
+
+
+def combine_kernel(*refs, terms, pair):
+    outs = refs[terms:]
     count, share, modes = refs[0].shape
     each = count // 2 // pair
     for above in range(2):
-        for chunk in range(chunks):
-            for place in range(each):
-                rows = pl.ds(above * (count // 2) + place * pair, pair)
-                total = refs[chunk * terms][rows].astype(F32)
-                for ref in refs[chunk * terms + 1 : (chunk + 1) * terms]:
-                    total = total + ref[rows].astype(F32)
-                total = total.reshape(pair * share, modes).T
-                for swapped in range(2):
-                    out = outs[2 * above + swapped]
-                    out[chunk * each + place] = total[swapped * share : (swapped + 1) * share].astype(out.dtype)
+        for place in range(each):
+            rows = pl.ds(above * (count // 2) + place * pair, pair)
+            total = refs[0][rows].astype(F32)
+            for ref in refs[1:terms]:
+                total = total + ref[rows].astype(F32)
+            total = total.reshape(pair * share, modes).T
+            for swapped in range(2):
+                out = outs[2 * above + swapped]
+                out[place] = total[swapped * share : (swapped + 1) * share].astype(out.dtype)
 
 
 def assemble_kernel(own_ref, swapped_ref, above_ref, both_ref, out_ref, *, pair):
@@ -239,22 +234,42 @@
             out_ref[place * pair + part] = jnp.concatenate([low[:, lanes], high[:, lanes]], 1)
 
 
-def finish(chunk_terms, count, stage, sizes):
-    chunks, terms = len(chunk_terms), len(chunk_terms[0])
-    _, share, modes = chunk_terms[0][0].shape
+def sum_kernel(*refs):
+    total = refs[0][...].astype(F32)
+    for ref in refs[1:-1]:
+        total = total + ref[...].astype(F32)
+    refs[-1][...] = total
+
+
+def summed(terms, count, cost):
+    shape = (count, *terms[0].shape[1:])
+    whole = pl.BlockSpec(shape, lambda g: (0,) * len(shape))
+    return pl.pallas_call(
+        sum_kernel,
+        grid=(1,),
+        out_shape=jax.ShapeDtypeStruct(shape, F32),
+        in_specs=[whole] * len(terms),
+        out_specs=whole,
+        compiler_params=pltpu.CompilerParams(vmem_limit_bytes=16 << 20),
+        cost_estimate=pl.CostEstimate(flops=cost, bytes_accessed=1024, transcendentals=0),
+    )(*terms)
+
+
+def finish(terms, count, stage, sizes):
+    _, share, modes = terms[0].shape
     pair = 2 if count % 4 == 0 else 1
-    places = chunks * count // 2 // pair
+    places = count // 2 // pair
     shape = (places, share, pair * share)
     whole = lambda shape: pl.BlockSpec(shape, lambda g: (0,) * len(shape))
     parts = pl.pallas_call(
-        functools.partial(combine_kernel, chunks=chunks, terms=terms, pair=pair),
+        functools.partial(combine_kernel, terms=len(terms), pair=pair),
         grid=(1,),
         out_shape=[jax.ShapeDtypeStruct(shape, dtype) for dtype in (F32, BF16, BF16, BF16)],
-        in_specs=[whole((count, share, modes))] * (chunks * terms),
+        in_specs=[whole((count, share, modes))] * len(terms),
         out_specs=[whole(shape)] * 4,
         compiler_params=pltpu.CompilerParams(vmem_limit_bytes=16 << 20),
         cost_estimate=pl.CostEstimate(flops=1, bytes_accessed=1024, transcendentals=0),
-    )(*[array for terms in chunk_terms for array in terms])
+    )(*terms)
     stage = stage + [("ma", 0)]
     arrived = {code: flip(parts[code], flips, sizes) for code, flips in reversed(list(subsets(stage)))}
     return pl.pallas_call(
@@ -268,61 +283,58 @@
 
 
 def shards(mode_fields, cell_volumes, sizes):
-    total_cells = cell_volumes.shape[0] * sizes["gx"] * cell_volumes.shape[1] * sizes["gy"]
-    weights = cell_volumes * (1.0 / math.sqrt(total_cells))
     barrier = lax.optimization_barrier
     own = jnp.transpose(mode_fields, (2, 0, 1, 3))
     row_count, _, share, _ = own.shape
     modes = 2 * share
     quarter = row_count // 4
-
-    def inner_rows(array):
-        return array[quarter : 3 * quarter]
-
-    def outer_rows(array):
-        return jnp.concatenate([array[:quarter], array[3 * quarter :]], 0)
-
-    own_inner, own_outer = inner_rows(own), outer_rows(own)
+    all_rows = tuple(range(row_count))
+    inner_rows = all_rows[quarter : 3 * quarter]
+    outer_rows = all_rows[:quarter] + all_rows[3 * quarter :]
+    own_inner = own[quarter : 3 * quarter]
+    own_outer = jnp.concatenate([own[:quarter], own[3 * quarter :]], 0)
+
     other_inner = flip(own_inner, [("ma", 0)], sizes)
     token = flip(own[quarter, 0, :16], [("ma", 0)], sizes)
-    held, token = barrier((own, token))
+    edges = own[:, :, :, -1], own[:, :, :, 0], own[-1:], own[:1]
+    edges, token = barrier((edges, token))
     forward, backward = neighbours("gy")
-    before = lax.ppermute(held[:, :, :, -1], "gy", forward)
-    after = lax.ppermute(held[:, :, :, 0], "gy", backward)
+    before = lax.ppermute(edges[0], "gy", forward)
+    after = lax.ppermute(edges[1], "gy", backward)
     forward, backward = neighbours("gx")
-    held, before, after = barrier((own, before, after))
-    above = lax.ppermute(held[-1:], "gx", forward)
-    below = lax.ppermute(held[:1], "gx", backward)
-    own_outer_held, above, below = barrier((own_outer, above, below))
+    above = lax.ppermute(edges[2], "gx", forward)
+    below = lax.ppermute(edges[3], "gx", backward)
+    own_outer_held, before, after = barrier((own_outer, before, after))
     other_outer = flip(own_outer_held, [("ma", 0)], sizes)
-    all_rows = tuple(range(row_count))
-    slopes_inner = slopes_of(own, before, after, all_rows[quarter : 3 * quarter], token, [])
-    slopes_outer = slopes_of(
-        own, before, after, all_rows[:quarter] + all_rows[3 * quarter :], token, [above, below]
+    slopes_inner = slopes_of(own, before, after, inner_rows, token, [])
+    slopes_outer = slopes_of(own, before, after, outer_rows, token, [above, below])
+
+    inner = partial_tensor(own_inner, other_inner, slopes_inner, cell_volumes, inner_rows, sizes, (0, modes))
+    outer = functools.partial(
+        partial_tensor, own_outer, other_outer, slopes_outer, rows=outer_rows, sizes=sizes, before=inner
     )
-
-    inner = partial_tensor(own_inner, other_inner, slopes_inner, inner_rows(weights), sizes, (0, modes))
-    outer_weights = outer_rows(weights)
-    chunks = chunks_of(modes // (sizes["gx"] * sizes["gy"]))
-    length = modes // chunks
     stages = stages_of(sizes)
-    results = []
-    for chunk in range(chunks):
-        low, middle, high = chunk * length, chunk * length + length // 2, (chunk + 1) * length
-        outer = functools.partial(partial_tensor, own_outer, other_outer, slopes_outer, sizes=sizes, before=inner)
-        sent = outer(weights=outer_weights, positions=(middle, high), dtype=BF16)
-        outer_weights, sent = barrier((outer_weights, sent))
-        arrived = flip(sent, stages[0], sizes)
-        terms = [outer(weights=outer_weights, positions=(low, middle)), arrived]
-        sent = sends(terms, length // 2, stages[1])
-        if chunk < chunks - 1:
-            outer_weights, sent = barrier((outer_weights, sent))
-        results.append(exchange(terms, stages[1], sent, sizes))
-    count = (length // 2) >> len(stages[1])
+    half, quarter = modes // 2, modes // 4
+    cell_count = mode_fields.shape[2] * mode_fields.shape[3]
+    sent = outer(cell_volumes, positions=(half, modes), dtype=BF16)
+    cell_volumes, sent = barrier((cell_volumes, sent))
+    arrived = flip(sent, stages[0], sizes)
+    upper = outer(cell_volumes, positions=(quarter, half))
+    eighth = quarter // 2
+    sent = [
+        (upper[at : at + eighth] + arrived[quarter + at : quarter + at + eighth].astype(F32)).astype(BF16)
+        for at in (0, eighth)
+    ]
+    cell_volumes, sent = barrier((cell_volumes, sent))
+    lower = outer(cell_volumes, positions=(0, quarter))
+    sent = [(lower[eighth:] + arrived[eighth:quarter].astype(F32)).astype(BF16)] + sent
+    received = exchange(stages[1], sent, sizes)
+    count = eighth
+    terms = [summed([lower, arrived] + received[1:], count, 2 * quarter * modes * share * cell_count), received[0]]
     for stage in stages[2:-1]:
-        results = [exchange(terms, stage, sends(terms, count, stage), sizes) for terms in results]
+        terms = terms + exchange(stage, sends(terms, count, stage), sizes)
         count = count >> len(stage)
-    return finish(results, count, stages[-1], sizes)
+    return finish(terms, count, stages[-1], sizes)
 
 
 def solution(mesh):

time: 72.7 us -> 70.5 us (0.970)
  starting transfers between devices: 26.5 us -> 23.3 us
  waiting for transfers between devices: 15.8 us -> 18 us
  other arithmetic: 1.61 us -> 0.25 us
    ppermute x14 -> x10, waiting for transfers between devices: 11.3 us -> 15.5 us  [flip(): return lax.ppermute(array, axes, [(i, i ^ change) for i in range(count)])]
    ppermute x14 -> x10, starting transfers between devices: 18.1 us -> 15.4 us  [flip(): return lax.ppermute(array, axes, [(i, i ^ change) for i in range(count)])]
    ppermute x4, waiting for transfers between devices: 4.48 us -> 2.48 us  [the longest x1 2.48 us: shards(): below = lax.ppermute(edges[3], 'gx', backward)]
    pallas_call x5 -> x4, Pallas kernels: 22.1 us -> 22.2 us  [partial_tensor(): pl.pallas_call(body, grid=((high - low) // block,), out_shape=jax.ShapeDt...]
    slice x8 -> x6, local copies, waits for them, and re-layouts: 2.35 us -> 2.42 us  [the longest x4 2.36 us: shards(): edges = (own[:, :, :, -1], own[:, :, :, 0], own[-1:], own[:1])]
  transfers between devices with their start and end apart: 18 -> 14, of which waited for: 8 -> 5; matrix products, arithmetic and copies ran while one was open for 5% -> 4% of each run, Pallas kernels for 24% -> 26%
where the time goes in v5:
time: 70.5 us; the launch traced here: 70.3 us
  Pallas kernels  24.8 us (35%)
  starting transfers between devices  23.3 us (33%)
  waiting for transfers between devices  18 us (26%)
  local copies, waits for them, and re-layouts  3.83 us (5%)
    pallas_call x4, Pallas kernels, partial_tensor(): pl.pallas_call(body, grid=((high - low) // block,), out_shape=jax.ShapeDt...  22.2 us
    ppermute x10, waiting for transfers between devices, flip(): return lax.ppermute(array, axes, [(i, i ^ change) for i in range(count)])  15.5 us
    ppermute x10, starting transfers between devices, flip(): return lax.ppermute(array, axes, [(i, i ^ change) for i in range(count)])  15.4 us
    ppermute x1, starting transfers between devices, shards(): above = lax.ppermute(edges[2], 'gx', forward)  3.83 us
    ppermute x1, waiting for transfers between devices, shards(): below = lax.ppermute(edges[3], 'gx', backward)  2.48 us
    slice x4, local copies, waits for them, and re-layouts, shards(): edges = (own[:, :, :, -1], own[:, :, :, 0], own[-1:], own[:1])  2.36 us
    ppermute x1, starting transfers between devices, shards(): before = lax.ppermute(edges[0], 'gy', forward)  1.45 us
  transfers between devices with their start and end apart: 14, of which 5 were waited for; matrix products, arithmetic and copies ran while one was open for 4% of the time, Pallas kernels for 26%

profile of v5, /device:TPU:0, one launch (start us, length us, event | category | flops | bytes accessed | tf_op | source)
XLA Modules:
  0.0 70.3 jit_solution(2583315234280123131)
XLA Ops:
  0.0 1.3 %copy.10 = bf16[3,64,16,128]{3,1,0,2:T(8,128)(2,1)S(1)} copy(bf16[3,64,16,128]{3,2,1,0:T(8,128)(2,1)} %param.2) | data formatting | bytes 1572864 | tf_op args[0]
  1.3 3.0 %collective-permute-start = (bf16[16,128]{1,0:T(8,128)(2,1)S(1)}, bf16[16,128]{1,0:T(8,128)(2,1)S(1)}, u32[]{:S(2)}, u32[]{:S(2)}) collective-permute-start(bf16[16,128]{1,0:T(8,128)(2,1)S(1)} %slice_bitcast_fusion), channel_id=1, source_target_pairs={{0,1},{1,0},{2,3},{3,2},{4,5},{5,4},{6,7},{7,6},{8,9},{9,8},{10,11... | collective-permute-start | bytes 12296 | tf_op jit(solution)/shard_map/ppermute | solution.py:177
  5.5 1.0 %copy.5 = bf16[16,3,64,1]{2,0,3,1:T(8,128)(2,1)} copy(bf16[16,3,64,1]{3,2,1,0:T(8,128)(2,1)S(1)} %get-tuple-element.44) | data formatting | bytes 12288 | tf_op jit(solution)/shard_map/slice | solution.py:299
  6.9 1.4 %collective-permute-start.1 = (bf16[16,3,64]{2,0,1:T(8,128)(2,1)}, bf16[16,3,64]{2,0,1:T(8,128)(2,1)S(1)}, u32[]{:S(2)}, u32[]{:S(2)}) collective-permute-start(bf16[16,3,64]{2,0,1:T(8,128)(2,1)} %bitcast.15), channel_id=1, source_target_pairs={{0,2},{2,4},{4,6},{1,3},{3,5},{5,7},{8,10},{10,12},{12,14},{9,11},... | collective-permute-start | bytes 18440 | tf_op jit(solution)/shard_map/ppermute | solution.py:302
  8.4 1.3 %collective-permute-start.2 = (bf16[16,3,64]{2,0,1:T(8,128)(2,1)S(1)}, bf16[16,3,64]{2,0,1:T(8,128)(2,1)S(1)}, u32[]{:S(2)}, u32[]{:S(2)}) collective-permute-start(bf16[16,3,64]{2,0,1:T(8,128)(2,1)S(1)} %bitcast.14), channel_id=1, source_target_pairs={{2,0},{4,2},{6,4},{3,1},{5,3},{7,5},{10,8},{12,10},{14,12},{11,9},... | collective-permute-start | bytes 18440 | tf_op jit(solution)/shard_map/ppermute | solution.py:303
  9.7 3.8 %collective-permute-start.4 = (bf16[1,3,64,128]{3,2,1,0:T(8,128)(2,1)}, bf16[1,3,64,128]{3,2,1,0:T(8,128)(2,1)S(1)}, u32[]{:S(2)}, u32[]{:S(2)}) collective-permute-start(bf16[1,3,64,128]{3,2,1,0:T(8,128)(2,1)} %get-tuple-element.27), channel_id=1, source_target_pairs={{0,8},{8,16},{16,24},{1,9},{9,17},{17,25},{2,10},{10,18},{18,26},{... | collective-permute-start | bytes 147464 | tf_op jit(solution)/shard_map/ppermute | solution.py:305
  13.5 1.3 %collective-permute-start.5 = (bf16[1,3,64,128]{3,2,1,0:T(8,128)(2,1)}, bf16[1,3,64,128]{3,2,1,0:T(8,128)(2,1)S(1)}, u32[]{:S(2)}, u32[]{:S(2)}) collective-permute-start(bf16[1,3,64,128]{3,2,1,0:T(8,128)(2,1)} %get-tuple-element.28), channel_id=1, source_target_pairs={{8,0},{16,8},{24,16},{9,1},{17,9},{25,17},{10,2},{18,10},{26,18},{... | collective-permute-start | bytes 147464 | tf_op jit(solution)/shard_map/ppermute | solution.py:306
  14.9 1.6 %collective-permute-start.3 = (bf16[8,3,64,128]{3,2,1,0:T(8,128)(2,1)S(1)}, bf16[8,3,64,128]{3,2,1,0:T(8,128)(2,1)S(1)}, u32[]{:S(2)}, u32[]{:S(2)}) collective-permute-start(bf16[8,3,64,128]{3,2,1,0:T(8,128)(2,1)S(1)} %pad_maximum_fusion.refs_0_), channel_id=1, source_target_pairs={{0,1},{1,0},{2,3},{3,2},{4,5},{5,4},{6,7},{7,6},{8,9},{9,8},{10,11... | collective-permute-start | bytes 1179656 | tf_op jit(solution)/shard_map/ppermute | solution.py:177
  17.2 2.5 %collective-permute-done.5.refs_1_ = bf16[1,3,64,128]{3,2,1,0:T(8,128)(2,1)S(1)} collective-permute-done((bf16[1,3,64,128]{3,2,1,0:T(8,128)(2,1)}, bf16[1,3,64,128]{3,2,1,0:T(8,128)(2,1)S(1)}, u32[]{:S(2)}, u32[]{:S(2)}) %collective-permute-start.5) | collective-permute-done | bytes 49184 | tf_op jit(solution)/shard_map/ppermute | solution.py:306
  19.7 0.7 shard_map.28.refs_2_
  20.4 10.7 %shard_map.30.refs_4_ = f32[128,64,128]{2,1,0:T(8,128)S(1)} custom-call(bf16[8,3,64,128]{3,2,1,0:T(8,128)(2,1)S(1)} %slice.63.refs_0_, bf16[8,3,64,128]{3,2,1,0:T(8,128)(2,1)S(1)} %collective-permute-done.6.refs_1_, bf16[8,6,64,128]{3,2,1,0:T(8,128)(2,1)S(1)} %shard_map.29.refs_2_, f32[16,128]{1,0:T(8,128)S(1)} %copy-done), custom_call_target="tpu_custom_call" | custom-call | flops 8589934592 | bytes 4194304 | tf_op jit(solution)/shard_map/pallas_call | solution.py:143
  31.1 5.7 %shard_map.31 = bf16[64,64,128]{2,1,0:T(8,128)(2,1)S(1)} custom-call(bf16[8,3,64,128]{3,2,1,0:T(8,128)(2,1)S(1)} %pad_maximum_fusion.refs_0_, bf16[8,3,64,128]{3,2,1,0:T(8,128)(2,1)S(1)} %collective-permute-done.3.refs_1_, bf16[8,6,64,128]{3,2,1,0:T(8,128)(2,1)S(1)} %shard_map.28.refs_2_, f32[16,128]{1,0:T(8,128)S(1)} %copy-done, ...), custom_call_target="tpu_custom_call" | custom-call | flops 4294967296 | bytes 4194304 | tf_op jit(solution)/shard_map/pallas_call | solution.py:143
  36.8 1.7 %collective-permute-start.7 = (bf16[64,64,128]{2,1,0:T(8,128)(2,1)S(1)}, bf16[64,64,128]{2,1,0:T(8,128)(2,1)S(1)}, u32[]{:S(2)}, u32[]{:S(2)}) collective-permute-start(bf16[64,64,128]{2,1,0:T(8,128)(2,1)S(1)} %shard_map.31), channel_id=1, source_target_pairs={{0,2},{2,0},{4,6},{6,4},{1,3},{3,1},{5,7},{7,5},{8,10},{10,8},{12,... | collective-permute-start | bytes 3145736 | tf_op jit(solution)/shard_map/ppermute | solution.py:177
  38.6 2.9 %shard_map.32 = f32[32,64,128]{2,1,0:T(8,128)S(1)} custom-call(bf16[8,3,64,128]{3,2,1,0:T(8,128)(2,1)S(1)} %pad_maximum_fusion.refs_0_, bf16[8,3,64,128]{3,2,1,0:T(8,128)(2,1)S(1)} %collective-permute-done.3.refs_1_, bf16[8,6,64,128]{3,2,1,0:T(8,128)(2,1)S(1)} %shard_map.28.refs_2_, f32[16,128]{1,0:T(8,128)S(1)} %copy-done, ...), custom_call_target="tpu_custom_call" | custom-call | flops 2147483648 | bytes 4194304 | tf_op jit(solution)/shard_map/pallas_call | solution.py:143
  41.6 2.9 %collective-permute-start.8 = (bf16[16,64,128]{2,1,0:T(8,128)(2,1)S(1)}, bf16[16,64,128]{2,1,0:T(8,128)(2,1)S(1)}, u32[]{:S(2)}, u32[]{:S(2)}) collective-permute-start(bf16[16,64,128]{2,1,0:T(8,128)(2,1)S(1)} %get-tuple-element.33), channel_id=1, source_target_pairs={{0,4},{2,6},{4,0},{6,2},{1,5},{3,7},{5,1},{7,3},{8,12},{10,14},{12... | collective-permute-start | bytes 786440 | tf_op jit(solution)/shard_map/ppermute | solution.py:177
  44.6 1.1 %collective-permute-start.9 = (bf16[16,64,128]{2,1,0:T(8,128)(2,1)S(1)}, bf16[16,64,128]{2,1,0:T(8,128)(2,1)S(1)}, u32[]{:S(2)}, u32[]{:S(2)}) collective-permute-start(bf16[16,64,128]{2,1,0:T(8,128)(2,1)S(1)} %get-tuple-element.34), channel_id=1, source_target_pairs={{0,12},{2,14},{4,8},{6,10},{8,4},{10,6},{12,0},{14,2},{16,28},{18,... | collective-permute-start | bytes 786440 | tf_op jit(solution)/shard_map/ppermute | solution.py:177
  45.7 2.9 %shard_map.33.refs_0_ = f32[32,64,128]{2,1,0:T(8,128)S(1)} custom-call(bf16[8,3,64,128]{3,2,1,0:T(8,128)(2,1)S(1)} %pad_maximum_fusion.refs_0_, bf16[8,3,64,128]{3,2,1,0:T(8,128)(2,1)S(1)} %collective-permute-done.3.refs_1_, bf16[8,6,64,128]{3,2,1,0:T(8,128)(2,1)S(1)} %shard_map.28.refs_2_, f32[16,128]{1,0:T(8,128)S(1)} %copy-done, ...), custom_call_target="tpu_custom_call" | custom-call | flops 2147483648 | bytes 4194304 | tf_op jit(solution)/shard_map/pallas_call | solution.py:143
  49.3 7.9 %collective-permute-done.8.refs_2_ = bf16[16,64,128]{2,1,0:T(8,128)(2,1)S(1)} collective-permute-done((bf16[16,64,128]{2,1,0:T(8,128)(2,1)S(1)}, bf16[16,64,128]{2,1,0:T(8,128)(2,1)S(1)}, u32[]{:S(2)}, u32[]{:S(2)}) %collective-permute-start.8) | collective-permute-done | bytes 262176 | tf_op jit(solution)/shard_map/ppermute | solution.py:177
  57.2 1.2 %collective-permute-done.10.refs_1_ = bf16[16,64,128]{2,1,0:T(8,128)(2,1)S(1)} collective-permute-done((bf16[16,64,128]{2,1,0:T(8,128)(2,1)S(1)}, bf16[16,64,128]{2,1,0:T(8,128)(2,1)S(1)}, u32[]{:S(2)}, u32[]{:S(2)}) %collective-permute-start.10) | collective-permute-done | bytes 262176 | tf_op jit(solution)/shard_map/ppermute | solution.py:177
  58.7 1.5 %collective-permute-start.11 = (bf16[4,64,128]{2,1,0:T(8,128)(2,1)S(1)}, bf16[4,64,128]{2,1,0:T(8,128)(2,1)S(1)}, u32[]{:S(2)}, u32[]{:S(2)}) collective-permute-start(bf16[4,64,128]{2,1,0:T(8,128)(2,1)S(1)} %get-tuple-element.36), channel_id=1, source_target_pairs={{0,1},{1,0},{2,3},{3,2},{4,5},{5,4},{6,7},{7,6},{8,9},{9,8},{10,11... | collective-permute-start | bytes 196616 | tf_op jit(solution)/shard_map/ppermute | solution.py:177
  60.2 2.6 %collective-permute-start.12 = (bf16[4,64,128]{2,1,0:T(8,128)(2,1)S(1)}, bf16[4,64,128]{2,1,0:T(8,128)(2,1)S(1)}, u32[]{:S(2)}, u32[]{:S(2)}) collective-permute-start(bf16[4,64,128]{2,1,0:T(8,128)(2,1)S(1)} %get-tuple-element.37), channel_id=1, source_target_pairs={{0,16},{8,24},{16,0},{24,8},{1,17},{9,25},{17,1},{25,9},{2,18},{10... | collective-permute-start | bytes 196616 | tf_op jit(solution)/shard_map/ppermute | solution.py:177
  63.1 3.9 %collective-permute-done.12.above_ref = bf16[4,64,128]{2,1,0:T(8,128)(2,1)S(1)} collective-permute-done((bf16[4,64,128]{2,1,0:T(8,128)(2,1)S(1)}, bf16[4,64,128]{2,1,0:T(8,128)(2,1)S(1)}, u32[]{:S(2)}, u32[]{:S(2)}) %collective-permute-start.12) | collective-permute-done | bytes 65568 | tf_op jit(solution)/shard_map/ppermute | solution.py:177
  67.0 2.5 %collective-permute-done.13.both_ref = bf16[4,64,128]{2,1,0:T(8,128)(2,1)S(1)} collective-permute-done((bf16[4,64,128]{2,1,0:T(8,128)(2,1)S(1)}, bf16[4,64,128]{2,1,0:T(8,128)(2,1)S(1)}, u32[]{:S(2)}, u32[]{:S(2)}) %collective-permute-start.13) | collective-permute-done | bytes 65568 | tf_op jit(solution)/shard_map/ppermute | solution.py:177
  69.5 0.8 %shard_map.36 = f32[8,64,128]{2,1,0:T(8,128)} custom-call(f32[4,64,128]{2,1,0:T(8,128)S(1)} %get-tuple-element.35.own_ref, bf16[4,64,128]{2,1,0:T(8,128)(2,1)S(1)} %collective-permute-done.11.swapped_ref, bf16[4,64,128]{2,1,0:T(8,128)(2,1)S(1)} %collective-permute-done.12.above_ref, bf16[4,64,128]{2,1,0:T(8,128)(2,1)S(1)} %collective-permute-done.13.both_ref), custom_call_target="tpu_custom_call" | custom-call | flops 1 | bytes 1024 | tf_op jit(solution)/shard_map/pallas_call | solution.py:275
  (30 shorter events, 3.7 us)
Async XLA Ops:
  1.3 5.5 %collective-permute-start = (bf16[16,128]{1,0:T(8,128)(2,1)S(1)}, bf16[16,128]{1,0:T(8,128)(2,1)S(1)}, u32[]{:S(2)}, u32[]{:S(2)}) collective-permute-start(bf16[16,128]{1,0:T(8,128)(2,1)S(1)} %slice_bitcast_fusion), channel_id=1, source_target_pairs={{0,1},{1,0},{2,3},{3,2},{4,5},{5,4},{6,7},{7,6},{8,9},{9,8},{10,11... | collective-permute-start | bytes 12296 | tf_op jit(solution)/shard_map/ppermute | solution.py:177
  4.4 16.0 %copy-start = (f32[16,128]{1,0:T(8,128)S(1)}, f32[16,128]{1,0:T(8,128)}, u32[]{:S(2)}) copy-start(f32[16,128]{1,0:T(8,128)} %refs_3_.5) | copy-start | bytes 24580
  4.4 16.0 %collective-permute-start.6 = (bf16[8,3,64,128]{3,2,1,0:T(8,128)(2,1)S(1)}, bf16[8,3,64,128]{3,2,1,0:T(8,128)(2,1)S(1)}, u32[]{:S(2)}, u32[]{:S(2)}) collective-permute-start(bf16[8,3,64,128]{3,2,1,0:T(8,128)(2,1)S(1)} %slice.63.refs_0_), channel_id=1, source_target_pairs={{0,1},{1,0},{2,3},{3,2},{4,5},{5,4},{6,7},{7,6},{8,9},{9,8},{10,11... | collective-permute-start | bytes 1179656 | tf_op jit(solution)/shard_map/ppermute | solution.py:177
  6.9 7.9 %collective-permute-start.1 = (bf16[16,3,64]{2,0,1:T(8,128)(2,1)}, bf16[16,3,64]{2,0,1:T(8,128)(2,1)S(1)}, u32[]{:S(2)}, u32[]{:S(2)}) collective-permute-start(bf16[16,3,64]{2,0,1:T(8,128)(2,1)} %bitcast.15), channel_id=1, source_target_pairs={{0,2},{2,4},{4,6},{1,3},{3,5},{5,7},{8,10},{10,12},{12,14},{9,11},... | collective-permute-start | bytes 18440 | tf_op jit(solution)/shard_map/ppermute | solution.py:302
  8.4 6.5 %collective-permute-start.2 = (bf16[16,3,64]{2,0,1:T(8,128)(2,1)S(1)}, bf16[16,3,64]{2,0,1:T(8,128)(2,1)S(1)}, u32[]{:S(2)}, u32[]{:S(2)}) collective-permute-start(bf16[16,3,64]{2,0,1:T(8,128)(2,1)S(1)} %bitcast.14), channel_id=1, source_target_pairs={{2,0},{4,2},{6,4},{3,1},{5,3},{7,5},{10,8},{12,10},{14,12},{11,9},... | collective-permute-start | bytes 18440 | tf_op jit(solution)/shard_map/ppermute | solution.py:303
  9.7 7.5 %collective-permute-start.4 = (bf16[1,3,64,128]{3,2,1,0:T(8,128)(2,1)}, bf16[1,3,64,128]{3,2,1,0:T(8,128)(2,1)S(1)}, u32[]{:S(2)}, u32[]{:S(2)}) collective-permute-start(bf16[1,3,64,128]{3,2,1,0:T(8,128)(2,1)} %get-tuple-element.27), channel_id=1, source_target_pairs={{0,8},{8,16},{16,24},{1,9},{9,17},{17,25},{2,10},{10,18},{18,26},{... | collective-permute-start | bytes 147464 | tf_op jit(solution)/shard_map/ppermute | solution.py:305
  13.5 6.2 %collective-permute-start.5 = (bf16[1,3,64,128]{3,2,1,0:T(8,128)(2,1)}, bf16[1,3,64,128]{3,2,1,0:T(8,128)(2,1)S(1)}, u32[]{:S(2)}, u32[]{:S(2)}) collective-permute-start(bf16[1,3,64,128]{3,2,1,0:T(8,128)(2,1)} %get-tuple-element.28), channel_id=1, source_target_pairs={{8,0},{16,8},{24,16},{9,1},{17,9},{25,17},{10,2},{18,10},{26,18},{... | collective-permute-start | bytes 147464 | tf_op jit(solution)/shard_map/ppermute | solution.py:306
  14.9 16.2 %collective-permute-start.3 = (bf16[8,3,64,128]{3,2,1,0:T(8,128)(2,1)S(1)}, bf16[8,3,64,128]{3,2,1,0:T(8,128)(2,1)S(1)}, u32[]{:S(2)}, u32[]{:S(2)}) collective-permute-start(bf16[8,3,64,128]{3,2,1,0:T(8,128)(2,1)S(1)} %pad_maximum_fusion.refs_0_), channel_id=1, source_target_pairs={{0,1},{1,0},{2,3},{3,2},{4,5},{5,4},{6,7},{7,6},{8,9},{9,8},{10,11... | collective-permute-start | bytes 1179656 | tf_op jit(solution)/shard_map/ppermute | solution.py:177
  36.8 4.6 %collective-permute-start.7 = (bf16[64,64,128]{2,1,0:T(8,128)(2,1)S(1)}, bf16[64,64,128]{2,1,0:T(8,128)(2,1)S(1)}, u32[]{:S(2)}, u32[]{:S(2)}) collective-permute-start(bf16[64,64,128]{2,1,0:T(8,128)(2,1)S(1)} %shard_map.31), channel_id=1, source_target_pairs={{0,2},{2,0},{4,6},{6,4},{1,3},{3,1},{5,7},{7,5},{8,10},{10,8},{12,... | collective-permute-start | bytes 3145736 | tf_op jit(solution)/shard_map/ppermute | solution.py:177
  41.6 15.5 %collective-permute-start.8 = (bf16[16,64,128]{2,1,0:T(8,128)(2,1)S(1)}, bf16[16,64,128]{2,1,0:T(8,128)(2,1)S(1)}, u32[]{:S(2)}, u32[]{:S(2)}) collective-permute-start(bf16[16,64,128]{2,1,0:T(8,128)(2,1)S(1)} %get-tuple-element.33), channel_id=1, source_target_pairs={{0,4},{2,6},{4,0},{6,2},{1,5},{3,7},{5,1},{7,3},{8,12},{10,14},{12... | collective-permute-start | bytes 786440 | tf_op jit(solution)/shard_map/ppermute | solution.py:177
  44.6 12.5 %collective-permute-start.9 = (bf16[16,64,128]{2,1,0:T(8,128)(2,1)S(1)}, bf16[16,64,128]{2,1,0:T(8,128)(2,1)S(1)}, u32[]{:S(2)}, u32[]{:S(2)}) collective-permute-start(bf16[16,64,128]{2,1,0:T(8,128)(2,1)S(1)} %get-tuple-element.34), channel_id=1, source_target_pairs={{0,12},{2,14},{4,8},{6,10},{8,4},{10,6},{12,0},{14,2},{16,28},{18,... | collective-permute-start | bytes 786440 | tf_op jit(solution)/shard_map/ppermute | solution.py:177
  48.7 9.8 %collective-permute-start.10 = (bf16[16,64,128]{2,1,0:T(8,128)(2,1)S(1)}, bf16[16,64,128]{2,1,0:T(8,128)(2,1)S(1)}, u32[]{:S(2)}, u32[]{:S(2)}) collective-permute-start(bf16[16,64,128]{2,1,0:T(8,128)(2,1)S(1)} %fusion), channel_id=1, source_target_pairs={{0,8},{8,0},{16,24},{24,16},{1,9},{9,1},{17,25},{25,17},{2,10},{10... | collective-permute-start | bytes 786440 | tf_op jit(solution)/shard_map/ppermute | solution.py:177
  58.7 4.5 %collective-permute-start.11 = (bf16[4,64,128]{2,1,0:T(8,128)(2,1)S(1)}, bf16[4,64,128]{2,1,0:T(8,128)(2,1)S(1)}, u32[]{:S(2)}, u32[]{:S(2)}) collective-permute-start(bf16[4,64,128]{2,1,0:T(8,128)(2,1)S(1)} %get-tuple-element.36), channel_id=1, source_target_pairs={{0,1},{1,0},{2,3},{3,2},{4,5},{5,4},{6,7},{7,6},{8,9},{9,8},{10,11... | collective-permute-start | bytes 196616 | tf_op jit(solution)/shard_map/ppermute | solution.py:177
  60.2 6.8 %collective-permute-start.12 = (bf16[4,64,128]{2,1,0:T(8,128)(2,1)S(1)}, bf16[4,64,128]{2,1,0:T(8,128)(2,1)S(1)}, u32[]{:S(2)}, u32[]{:S(2)}) collective-permute-start(bf16[4,64,128]{2,1,0:T(8,128)(2,1)S(1)} %get-tuple-element.37), channel_id=1, source_target_pairs={{0,16},{8,24},{16,0},{24,8},{1,17},{9,25},{17,1},{25,9},{2,18},{10... | collective-permute-start | bytes 196616 | tf_op jit(solution)/shard_map/ppermute | solution.py:177
  62.8 6.7 %collective-permute-start.13 = (bf16[4,64,128]{2,1,0:T(8,128)(2,1)S(1)}, bf16[4,64,128]{2,1,0:T(8,128)(2,1)S(1)}, u32[]{:S(2)}, u32[]{:S(2)}) collective-permute-start(bf16[4,64,128]{2,1,0:T(8,128)(2,1)S(1)} %get-tuple-element.38), channel_id=1, source_target_pairs={{0,17},{1,16},{8,25},{9,24},{16,1},{17,0},{24,9},{25,8},{2,19},{3,... | collective-permute-start | bytes 196616 | tf_op jit(solution)/shard_map/ppermute | solution.py:177

commit v6 on v5

--- a/solution.py
+++ b/solution.py
@@ -10,6 +10,7 @@
 
 BF16 = jnp.bfloat16
 F32 = jnp.float32
+BLOCKS = 8
 
 
 def bits_of(count):
@@ -32,41 +33,49 @@
     return found
 
 
-def slopes_kernel(own_ref, before_ref, after_ref, *refs, rows):
+def slopes_kernel(own_ref, *refs, rows, parts):
     out_ref = refs[-1]
     last = own_ref.shape[0] - 1
-    before = before_ref[...].astype(F32).T
-    after = after_ref[...].astype(F32).T
     cells = own_ref.shape[3]
-    lane = lax.broadcasted_iota(jnp.int32, own_ref.shape[2:], 1)
+    if 1 in parts:
+        before = refs[0][...].astype(F32).T
+        after = refs[1][...].astype(F32).T
+        lane = lax.broadcasted_iota(jnp.int32, own_ref.shape[2:], 1)
     for place, x in enumerate(rows):
         for a in range(3):
-            down = (refs[0][0, a] if x == 0 else own_ref[x - 1, a]).astype(F32)
-            up = (refs[1][0, a] if x == last else own_ref[x + 1, a]).astype(F32)
-            out_ref[place, a] = ((up - down) * 0.5).astype(BF16)
-            value = own_ref[x, a].astype(F32)
-            column = 3 * x + a
-            down = jnp.where(lane == 0, before[:, column : column + 1], pltpu.roll(value, 1, 1))
-            up = jnp.where(lane == cells - 1, after[:, column : column + 1], pltpu.roll(value, cells - 1, 1))
-            out_ref[place, 3 + a] = ((up - down) * 0.5).astype(BF16)
-
-
-def slopes_of(own, before, after, rows, token, edges):
-    row_count, _, share, cells = own.shape
+            if 0 in parts:
+                down = (refs[2][0, a] if x == 0 else own_ref[x - 1, a]).astype(F32)
+                up = (refs[3][0, a] if x == last else own_ref[x + 1, a]).astype(F32)
+                out_ref[place, a] = ((up - down) * 0.5).astype(BF16)
+            if 1 in parts:
+                value = own_ref[x, a].astype(F32)
+                column = 3 * x + a
+                down = jnp.where(lane == 0, before[:, column : column + 1], pltpu.roll(value, 1, 1))
+                up = jnp.where(lane == cells - 1, after[:, column : column + 1], pltpu.roll(value, cells - 1, 1))
+                out_ref[place, 3 * parts.index(1) + a] = ((up - down) * 0.5).astype(BF16)
+
+
+def slopes_of(own, rows, parts, *others):
+    _, _, share, cells = own.shape
     return pl.pallas_call(
-        functools.partial(slopes_kernel, rows=rows),
-        out_shape=jax.ShapeDtypeStruct((len(rows), 6, share, cells), BF16),
-        in_specs=[pl.BlockSpec(memory_space=pltpu.VMEM)] * (4 + len(edges)),
+        functools.partial(slopes_kernel, rows=rows, parts=parts),
+        out_shape=jax.ShapeDtypeStruct((len(rows), 3 * len(parts), share, cells), BF16),
+        in_specs=[pl.BlockSpec(memory_space=pltpu.VMEM)] * (1 + len(others)),
         out_specs=pl.BlockSpec(memory_space=pltpu.VMEM),
         compiler_params=pltpu.CompilerParams(vmem_limit_bytes=16 << 20),
         cost_estimate=pl.CostEstimate(flops=1, bytes_accessed=1024, transcendentals=0),
-    )(own, before.reshape(3 * row_count, share), after.reshape(3 * row_count, share), *edges, token)
-
-
-def tensor_kernel(*refs, bits, block, rows_each, first_step, rows, scale):
+    )(own, *others)
+
+
+def sum_of(left, right):
+    return left[0] * right[0] + left[1] * right[1] + left[2] * right[2]
+
+
+def tensor_kernel(*refs, bits, block, rows_each, first_block, stride, rows, scale, parts, outputs):
     own_ref, other_ref, slope_ref, volume_ref = refs[:4]
-    before_ref = refs[4] if len(refs) == 8 else None
-    out_ref, left, right = refs[-3:]
+    left, right = refs[-2:]
+    out_refs = refs[-2 - outputs : -2]
+    before_ref = refs[4] if len(refs) == 7 + outputs else None
     row_count, _, share, cells = own_ref.shape
     step = pl.program_id(0)
     top = bits_of(2 * share) - 1
@@ -79,20 +88,19 @@
                 for a in range(3):
                     value = (weight * ref[x, a].astype(F32)).astype(BF16)
                     left[x, a, half * share : (half + 1) * share, :] = value.astype(F32)
-                for b in range(2):
-                    right[
-                        half * share : (half + 1) * share, (2 * x + b) * cells : (2 * x + b + 1) * cells
-                    ] = ref[x, b]
+                for place, b in enumerate(parts):
+                    lanes = len(parts) * x + place
+                    right[half * share : (half + 1) * share, lanes * cells : (lanes + 1) * cells] = ref[x, b]
 
     here = (lax.axis_index("gx") * lax.axis_size("gy") + lax.axis_index("gy")) * rows_each
     start = here ^ (lax.axis_index("ma") << top)
-    position = (first_step + step) * block
+    position = (first_block + stride * step) * block
     for place, bit in enumerate(bits):
         start = start ^ (((position >> place) & 1) << bit)
     columns = []
     for x in range(row_count):
-        slopes = [slope_ref[x, n] for n in range(6)]
-        sums = [[], []]
+        slopes = [slope_ref[x, n] for n in range(3 * len(parts))]
+        sums = [[] for _ in parts]
         for row in range(block):
             offset = 0
             for place, bit in enumerate(bits):
@@ -103,25 +111,30 @@
                 )
                 for a in range(3)
             ]
-            for b in range(2):
-                sums[b].append(
-                    test[0] * slopes[3 * b] + test[1] * slopes[3 * b + 1] + test[2] * slopes[3 * b + 2]
-                )
-        columns += [jnp.concatenate(sums[0], 0), jnp.concatenate(sums[1], 0)]
+            for place, found in enumerate(sums):
+                found.append(sum_of(test, slopes[3 * place : 3 * place + 3]))
+        columns += [jnp.concatenate(found, 0) for found in sums]
     sums = jnp.concatenate(columns, 1)
     product = lax.dot_general(sums, right[...], (((1,), (1,)), ((), ())), preferred_element_type=F32)
     product = product.reshape(block, share, 2 * share)
     if before_ref is not None:
         product = product + before_ref[...]
-    out_ref[...] = product.astype(out_ref.dtype)
-
-
-def partial_tensor(own, other, slopes, volumes, rows, sizes, positions, before=None, dtype=F32):
+    if outputs == 1:
+        out_refs[0][...] = product.astype(out_refs[0].dtype)
+    else:
+        for place, out_ref in enumerate(out_refs):
+
+            @pl.when(step == place)
+            def _(out_ref=out_ref):
+                out_ref[...] = product.astype(out_ref.dtype)
+
+
+def partial_tensor(own, other, slopes, volumes, rows, sizes, blocks, before=None, dtypes=(F32,), parts=(0, 1)):
     row_count, _, share, cells = own.shape
     modes = 2 * share
-    low, high = positions
-    block = min(16, high - low)
-    first_step = low // block
+    block = modes // BLOCKS
+    stride = blocks[1] - blocks[0] if len(blocks) > 1 else 1
+    outputs = len(dtypes)
     devices = sizes["gx"] * sizes["gy"]
     rows_each = modes // devices
     body = functools.partial(
@@ -129,8 +142,11 @@
         bits=source_bits(sizes, rows_each),
         block=block,
         rows_each=rows_each,
-        first_step=first_step,
+        first_block=blocks[0],
+        stride=stride,
+        outputs=outputs,
         rows=rows,
+        parts=parts,
         scale=1.0 / math.sqrt(volumes.shape[0] * volumes.shape[1] * devices),
     )
     whole = lambda array: pl.BlockSpec(array.shape, lambda g: (0,) * array.ndim, pipeline_mode=pl.Buffered(1))
@@ -139,21 +155,28 @@
     in_specs = [whole(array) for array in operands]
     if before is not None:
         operands.append(before)
-        in_specs.append(pl.BlockSpec(shape, lambda g: (first_step + g, 0, 0)))
+        in_specs.append(pl.BlockSpec(shape, lambda g: (blocks[0] + stride * g, 0, 0)))
+    if outputs > 1:
+        out_shape = [jax.ShapeDtypeStruct(shape, dtype) for dtype in dtypes]
+        out_specs = [pl.BlockSpec(shape, lambda g: (0, 0, 0))] * outputs
+    else:
+        out_shape = (pltpu.VMEM if len(blocks) == BLOCKS else jax.ShapeDtypeStruct)(
+            (len(blocks) * block, share, modes), dtypes[0]
+        )
+        out_specs = pl.BlockSpec(shape, lambda g: (g, 0, 0))
     return pl.pallas_call(
         body,
-        grid=((high - low) // block,),
-        out_shape=jax.ShapeDtypeStruct((high - low, share, modes), dtype) if before is not None
-        else pltpu.VMEM((high - low, share, modes), dtype),
+        grid=(len(blocks),),
+        out_shape=out_shape,
         in_specs=in_specs,
-        out_specs=pl.BlockSpec(shape, lambda g: (g, 0, 0)),
+        out_specs=out_specs,
         scratch_shapes=[
             pltpu.VMEM((row_count, 3, modes, cells), F32),
-            pltpu.VMEM((modes, row_count * 2 * cells), BF16),
+            pltpu.VMEM((modes, row_count * len(parts) * cells), BF16),
         ],
         compiler_params=pltpu.CompilerParams(vmem_limit_bytes=20 << 20),
         cost_estimate=pl.CostEstimate(
-            flops=8 * (high - low) * share * modes * row_count * cells, bytes_accessed=4 << 20, transcendentals=0
+            flops=4 * len(parts) * len(blocks) * block * share * modes * row_count * cells, bytes_accessed=4 << 20, transcendentals=0
         ),
     )(*operands)
 
@@ -197,12 +220,13 @@
 def sends(terms, count, stage):
     length = count >> len(stage)
     return [
-        term_sum(terms, code * length, (code + 1) * length).astype(BF16) for code, _ in subsets(stage)
+        term_sum(terms, code * length, (code + 1) * length).astype(BF16)
+        for code, _ in list(subsets(stage))[::-1]
     ]
 
 
 def exchange(stage, sent, sizes):
-    return [flip(array, flips, sizes) for array, (_, flips) in zip(sent, subsets(stage))]
+    return [flip(array, flips, sizes) for array, (_, flips) in zip(sent, list(subsets(stage))[::-1])]
 
 
 def combine_kernel(*refs, terms, pair):
@@ -296,41 +320,42 @@
 
     other_inner = flip(own_inner, [("ma", 0)], sizes)
     token = flip(own[quarter, 0, :16], [("ma", 0)], sizes)
-    edges = own[:, :, :, -1], own[:, :, :, 0], own[-1:], own[:1]
-    edges, token = barrier((edges, token))
+    edges, token = barrier(((own[:, :, :, -1], own[:, :, :, 0]), token))
     forward, backward = neighbours("gy")
     before = lax.ppermute(edges[0], "gy", forward)
     after = lax.ppermute(edges[1], "gy", backward)
-    forward, backward = neighbours("gx")
-    above = lax.ppermute(edges[2], "gx", forward)
-    below = lax.ppermute(edges[3], "gx", backward)
     own_outer_held, before, after = barrier((own_outer, before, after))
     other_outer = flip(own_outer_held, [("ma", 0)], sizes)
-    slopes_inner = slopes_of(own, before, after, inner_rows, token, [])
-    slopes_outer = slopes_of(own, before, after, outer_rows, token, [above, below])
-
-    inner = partial_tensor(own_inner, other_inner, slopes_inner, cell_volumes, inner_rows, sizes, (0, modes))
+
+    inner = functools.partial(
+        partial_tensor, own_inner, other_inner, volumes=cell_volumes, rows=inner_rows, sizes=sizes, blocks=range(BLOCKS)
+    )
+    so_far = inner(slopes_of(own, inner_rows, (0,)), parts=(0,))
+    edges, so_far = barrier(((own[-1:], own[:1]), so_far))
+    forward, backward = neighbours("gx")
+    above = lax.ppermute(edges[0], "gx", forward)
+    below = lax.ppermute(edges[1], "gx", backward)
+    before = before.reshape(3 * row_count, share)
+    after = after.reshape(3 * row_count, share)
+    so_far = inner(slopes_of(own, inner_rows, (1,), before, after, token), parts=(1,), before=so_far)
+
+    slopes_outer = slopes_of(own, outer_rows, (0, 1), before, after, above, below)
     outer = functools.partial(
-        partial_tensor, own_outer, other_outer, slopes_outer, rows=outer_rows, sizes=sizes, before=inner
+        partial_tensor, own_outer, other_outer, slopes_outer, rows=outer_rows, sizes=sizes, before=so_far
     )
     stages = stages_of(sizes)
-    half, quarter = modes // 2, modes // 4
+    count = modes // BLOCKS
     cell_count = mode_fields.shape[2] * mode_fields.shape[3]
-    sent = outer(cell_volumes, positions=(half, modes), dtype=BF16)
+    sent = outer(cell_volumes, blocks=(5, 6, 7), dtypes=(BF16,))
     cell_volumes, sent = barrier((cell_volumes, sent))
     arrived = flip(sent, stages[0], sizes)
-    upper = outer(cell_volumes, positions=(quarter, half))
-    eighth = quarter // 2
-    sent = [
-        (upper[at : at + eighth] + arrived[quarter + at : quarter + at + eighth].astype(F32)).astype(BF16)
-        for at in (0, eighth)
-    ]
+    kept = outer(cell_volumes, blocks=(1, 2, 3))
+    sent = [term_sum([kept, arrived], at * count, (at + 1) * count).astype(BF16) for at in range(3)]
     cell_volumes, sent = barrier((cell_volumes, sent))
-    lower = outer(cell_volumes, positions=(0, quarter))
-    sent = [(lower[eighth:] + arrived[eighth:quarter].astype(F32)).astype(BF16)] + sent
-    received = exchange(stages[1], sent, sizes)
-    count = eighth
-    terms = [summed([lower, arrived] + received[1:], count, 2 * quarter * modes * share * cell_count), received[0]]
+    received = exchange(stages[1], sent[::-1], sizes)
+    sent, kept = outer(cell_volumes, blocks=(4, 0), dtypes=(BF16, F32))
+    arrived = flip(sent, stages[0], sizes)
+    terms = [summed(received, count, 16 * count * modes * share * cell_count), kept, arrived]
     for stage in stages[2:-1]:
         terms = terms + exchange(stage, sends(terms, count, stage), sizes)
         count = count >> len(stage)

time: 70.5 us -> 73.4 us (1.041)
  Pallas kernels: 24.8 us -> 26.9 us
  other arithmetic: 0.25 us -> 1.29 us
  starting transfers between devices: 23.3 us -> 22.5 us
  local copies, waits for them, and re-layouts: 3.83 us -> 4.57 us
    ppermute x1, waiting for transfers between devices: 0.01 us -> 2.68 us  [shards(): after = lax.ppermute(edges[1], 'gy', backward)]
    ppermute x2, waiting for transfers between devices: 2.48 us -> 0.01 us  [the longest x1 0.01 us: shards(): above = lax.ppermute(edges[0], 'gx', forward)]
    pallas_call x6 -> x8, Pallas kernels: 23.6 us -> 25.8 us  [the longest x5 24.3 us: partial_tensor(): pl.pallas_call(body, grid=(len(blocks),), out_shape=out_shape, in_specs=i...]
    concatenate x1, other arithmetic: 0.04 us -> 1.06 us  [shards(): own_outer = jnp.concatenate([own[:quarter], own[3 * quarter:]], 0)]
    ppermute x10 -> x11, waiting for transfers between devices: 15.5 us -> 14.9 us  [flip(): return lax.ppermute(array, axes, [(i, i ^ change) for i in range(count)])]
    ppermute x10 -> x11, starting transfers between devices: 15.4 us -> 15 us  [flip(): return lax.ppermute(array, axes, [(i, i ^ change) for i in range(count)])]
  transfers between devices with their start and end apart: 14 -> 15, of which waited for: 5 -> 6; matrix products, arithmetic and copies ran while one was open for 4% -> 6% of each run, Pallas kernels for 26% -> 29%
where the time goes in v6:
time: 73.4 us; the launch traced here: 73.1 us
  Pallas kernels  26.9 us (37%)
  starting transfers between devices  22.5 us (31%)
  waiting for transfers between devices  17.6 us (24%)
  local copies, waits for them, and re-layouts  4.57 us (6%)
  other arithmetic  1.29 us (2%)
    pallas_call x5, Pallas kernels, partial_tensor(): pl.pallas_call(body, grid=(len(blocks),), out_shape=out_shape, in_specs=i...  24.3 us
    ppermute x11, starting transfers between devices, flip(): return lax.ppermute(array, axes, [(i, i ^ change) for i in range(count)])  15 us
    ppermute x11, waiting for transfers between devices, flip(): return lax.ppermute(array, axes, [(i, i ^ change) for i in range(count)])  14.9 us
    ppermute x1, starting transfers between devices, shards(): above = lax.ppermute(edges[0], 'gx', forward)  3.48 us
    ppermute x1, waiting for transfers between devices, shards(): after = lax.ppermute(edges[1], 'gy', backward)  2.68 us
    slice x3, local copies, waits for them, and re-layouts, shards(): edges, token = barrier(((own[:, :, :, -1], own[:, :, :, 0]), token))  1.72 us
  transfers between devices with their start and end apart: 15, of which 6 were waited for; matrix products, arithmetic and copies ran while one was open for 6% of the time, Pallas kernels for 29%

profile of v6, /device:TPU:0, one launch (start us, length us, event | category | flops | bytes accessed | tf_op | source)
XLA Modules:
  0.0 73.1 jit_solution(16210286231770422781)
XLA Ops:
  0.0 1.3 %copy.10 = bf16[3,64,16,128]{3,1,0,2:T(8,128)(2,1)S(1)} copy(bf16[3,64,16,128]{3,2,1,0:T(8,128)(2,1)} %param.2) | data formatting | bytes 1572864 | tf_op args[0]
  1.3 3.0 %collective-permute-start = (bf16[16,128]{1,0:T(8,128)(2,1)S(1)}, bf16[16,128]{1,0:T(8,128)(2,1)S(1)}, u32[]{:S(2)}, u32[]{:S(2)}) collective-permute-start(bf16[16,128]{1,0:T(8,128)(2,1)S(1)} %slice_bitcast_fusion), channel_id=1, source_target_pairs={{0,1},{1,0},{2,3},{3,2},{4,5},{5,4},{6,7},{7,6},{8,9},{9,8},{10,11... | collective-permute-start | bytes 12296 | tf_op jit(solution)/shard_map/ppermute | solution.py:200
  7.6 1.4 %collective-permute-start.1 = (bf16[16,3,64]{2,0,1:T(8,128)(2,1)}, bf16[16,3,64]{2,0,1:T(8,128)(2,1)S(1)}, u32[]{:S(2)}, u32[]{:S(2)}) collective-permute-start(bf16[16,3,64]{2,0,1:T(8,128)(2,1)} %bitcast.1), channel_id=1, source_target_pairs={{0,2},{2,4},{4,6},{1,3},{3,5},{5,7},{8,10},{10,12},{12,14},{9,11},... | collective-permute-start | bytes 18440 | tf_op jit(solution)/shard_map/ppermute | solution.py:325
  9.1 1.3 %collective-permute-start.2 = (bf16[16,3,64]{2,0,1:T(8,128)(2,1)S(1)}, bf16[16,3,64]{2,0,1:T(8,128)(2,1)S(1)}, u32[]{:S(2)}, u32[]{:S(2)}) collective-permute-start(bf16[16,3,64]{2,0,1:T(8,128)(2,1)S(1)} %bitcast.15), channel_id=1, source_target_pairs={{2,0},{4,2},{6,4},{3,1},{5,3},{7,5},{10,8},{12,10},{14,12},{11,9},... | collective-permute-start | bytes 18440 | tf_op jit(solution)/shard_map/ppermute | solution.py:326
  10.4 1.1 %pad_maximum_fusion.refs_0_ = bf16[8,3,64,128]{3,2,1,0:T(8,128)(2,1)S(1)} fusion(bf16[4,3,64,128]{3,2,1,0:T(8,128)(2,1)} %get-tuple-element.55, bf16[4,3,64,128]{3,2,1,0:T(8,128)(2,1)} %get-tuple-element.54), kind=kLoop, calls=%fused_computation.7 | loop fusion | flops 196608 | bytes 786432 | tf_op jit(solution)/shard_map/concatenate | solution.py:319
  11.6 2.7 %collective-permute-done.2 = bf16[16,3,64]{2,0,1:T(8,128)(2,1)S(1)} collective-permute-done((bf16[16,3,64]{2,0,1:T(8,128)(2,1)S(1)}, bf16[16,3,64]{2,0,1:T(8,128)(2,1)S(1)}, u32[]{:S(2)}, u32[]{:S(2)}) %collective-permute-start.2) | collective-permute-done | bytes 6176 | tf_op jit(solution)/shard_map/ppermute | solution.py:326
  14.3 1.6 %collective-permute-start.3 = (bf16[8,3,64,128]{3,2,1,0:T(8,128)(2,1)S(1)}, bf16[8,3,64,128]{3,2,1,0:T(8,128)(2,1)S(1)}, u32[]{:S(2)}, u32[]{:S(2)}) collective-permute-start(bf16[8,3,64,128]{3,2,1,0:T(8,128)(2,1)S(1)} %pad_maximum_fusion.refs_0_), channel_id=1, source_target_pairs={{0,1},{1,0},{2,3},{3,2},{4,5},{5,4},{6,7},{7,6},{8,9},{9,8},{10,11... | collective-permute-start | bytes 1179656 | tf_op jit(solution)/shard_map/ppermute | solution.py:200
  16.6 6.2 %shard_map.29.refs_4_ = f32[128,64,128]{2,1,0:T(8,128)S(1)} custom-call(bf16[8,3,64,128]{3,2,1,0:T(8,128)(2,1)S(1)} %slice.63.refs_0_, bf16[8,3,64,128]{3,2,1,0:T(8,128)(2,1)S(1)} %collective-permute-done.4.refs_1_, bf16[8,3,64,128]{3,2,1,0:T(8,128)(2,1)S(1)} %shard_map.28.refs_2_, f32[16,128]{1,0:T(8,128)S(1)} %copy-done), custom_call_target="tpu_custom_call" | custom-call | flops 4294967296 | bytes 4194304 | tf_op jit(solution)/shard_map/pallas_call | solution.py:167
  22.8 3.5 %collective-permute-start.5 = (bf16[1,3,64,128]{3,2,1,0:T(8,128)(2,1)S(1)}, bf16[1,3,64,128]{3,2,1,0:T(8,128)(2,1)S(1)}, u32[]{:S(2)}, u32[]{:S(2)}) collective-permute-start(bf16[1,3,64,128]{3,2,1,0:T(8,128)(2,1)S(1)} %copy-done.2), channel_id=1, source_target_pairs={{0,8},{8,16},{16,24},{1,9},{9,17},{17,25},{2,10},{10,18},{18,26},{... | collective-permute-start | bytes 147464 | tf_op jit(solution)/shard_map/ppermute | solution.py:336
  26.3 1.3 %collective-permute-start.6 = (bf16[1,3,64,128]{3,2,1,0:T(8,128)(2,1)S(1)}, bf16[1,3,64,128]{3,2,1,0:T(8,128)(2,1)S(1)}, u32[]{:S(2)}, u32[]{:S(2)}) collective-permute-start(bf16[1,3,64,128]{3,2,1,0:T(8,128)(2,1)S(1)} %copy-done.1), channel_id=1, source_target_pairs={{8,0},{16,8},{24,16},{9,1},{17,9},{25,17},{10,2},{18,10},{26,18},{... | collective-permute-start | bytes 147464 | tf_op jit(solution)/shard_map/ppermute | solution.py:337
  27.6 6.6 %shard_map.32.refs_4_ = f32[128,64,128]{2,1,0:T(8,128)S(1)} custom-call(bf16[8,3,64,128]{3,2,1,0:T(8,128)(2,1)S(1)} %slice.63.refs_0_, bf16[8,3,64,128]{3,2,1,0:T(8,128)(2,1)S(1)} %collective-permute-done.4.refs_1_, bf16[8,3,64,128]{3,2,1,0:T(8,128)(2,1)S(1)} %shard_map.31.refs_2_, f32[16,128]{1,0:T(8,128)S(1)} %copy-done, f32[128,64,128]{2,1,0:T(8,128)S(1)} %shard_map.29.refs_4_), custom_call_target="tpu_custom_call" | custom-call | flops 4294967296 | bytes 4194304 | tf_op jit(solution)/shard_map/pallas_call | solution.py:167
  34.9 4.3 %shard_map.33 = bf16[48,64,128]{2,1,0:T(8,128)(2,1)S(1)} custom-call(bf16[8,3,64,128]{3,2,1,0:T(8,128)(2,1)S(1)} %pad_maximum_fusion.refs_0_, bf16[8,3,64,128]{3,2,1,0:T(8,128)(2,1)S(1)} %collective-permute-done.3.refs_1_, bf16[8,6,64,128]{3,2,1,0:T(8,128)(2,1)S(1)} %shard_map.30.refs_2_, f32[16,128]{1,0:T(8,128)S(1)} %copy-done, ...), custom_call_target="tpu_custom_call" | custom-call | flops 3221225472 | bytes 4194304 | tf_op jit(solution)/shard_map/pallas_call | solution.py:167
  39.3 1.8 %collective-permute-start.7 = (bf16[48,64,128]{2,1,0:T(8,128)(2,1)S(1)}, bf16[48,64,128]{2,1,0:T(8,128)(2,1)S(1)}, u32[]{:S(2)}, u32[]{:S(2)}) collective-permute-start(bf16[48,64,128]{2,1,0:T(8,128)(2,1)S(1)} %shard_map.33), channel_id=1, source_target_pairs={{0,2},{2,0},{4,6},{6,4},{1,3},{3,1},{5,7},{7,5},{8,10},{10,8},{12,... | collective-permute-start | bytes 2359304 | tf_op jit(solution)/shard_map/ppermute | solution.py:200
  41.1 4.2 %shard_map.34 = f32[48,64,128]{2,1,0:T(8,128)S(1)} custom-call(bf16[8,3,64,128]{3,2,1,0:T(8,128)(2,1)S(1)} %pad_maximum_fusion.refs_0_, bf16[8,3,64,128]{3,2,1,0:T(8,128)(2,1)S(1)} %collective-permute-done.3.refs_1_, bf16[8,6,64,128]{3,2,1,0:T(8,128)(2,1)S(1)} %shard_map.30.refs_2_, f32[16,128]{1,0:T(8,128)S(1)} %copy-done, ...), custom_call_target="tpu_custom_call" | custom-call | flops 3221225472 | bytes 4194304 | tf_op jit(solution)/shard_map/pallas_call | solution.py:167
  45.6 2.4 %collective-permute-start.10 = (bf16[16,64,128]{2,1,0:T(8,128)(2,1)S(1)}, bf16[16,64,128]{2,1,0:T(8,128)(2,1)S(1)}, u32[]{:S(2)}, u32[]{:S(2)}) collective-permute-start(bf16[16,64,128]{2,1,0:T(8,128)(2,1)S(1)} %get-tuple-element.39), channel_id=1, source_target_pairs={{0,8},{8,0},{16,24},{24,16},{1,9},{9,1},{17,25},{25,17},{2,10},{10... | collective-permute-start | bytes 786440 | tf_op jit(solution)/shard_map/ppermute | solution.py:200
  48.4 1.2 %collective-permute-start.9 = (bf16[16,64,128]{2,1,0:T(8,128)(2,1)S(1)}, bf16[16,64,128]{2,1,0:T(8,128)(2,1)S(1)}, u32[]{:S(2)}, u32[]{:S(2)}) collective-permute-start(bf16[16,64,128]{2,1,0:T(8,128)(2,1)S(1)} %get-tuple-element.38), channel_id=1, source_target_pairs={{0,4},{2,6},{4,0},{6,2},{1,5},{3,7},{5,1},{7,3},{8,12},{10,14},{12... | collective-permute-start | bytes 786440 | tf_op jit(solution)/shard_map/ppermute | solution.py:200
  49.6 3.0 %shard_map.36 = (bf16[16,64,128]{2,1,0:T(8,128)(2,1)S(1)}, f32[16,64,128]{2,1,0:T(8,128)S(1)}) custom-call(bf16[8,3,64,128]{3,2,1,0:T(8,128)(2,1)S(1)} %pad_maximum_fusion.refs_0_, bf16[8,3,64,128]{3,2,1,0:T(8,128)(2,1)S(1)} %collective-permute-done.3.refs_1_, bf16[8,6,64,128]{3,2,1,0:T(8,128)(2,1)S(1)} %shard_map.30.refs_2_, f32[16,128]{1,0:T(8,128)S(1)} %copy-done, ...), custom_call_target="tpu_custom_call" | custom-call | flops 2147483648 | bytes 4194304 | tf_op jit(solution)/shard_map/pallas_call | solution.py:167
  52.6 2.5 %collective-permute-done.10.refs_2_ = bf16[16,64,128]{2,1,0:T(8,128)(2,1)S(1)} collective-permute-done((bf16[16,64,128]{2,1,0:T(8,128)(2,1)S(1)}, bf16[16,64,128]{2,1,0:T(8,128)(2,1)S(1)}, u32[]{:S(2)}, u32[]{:S(2)}) %collective-permute-start.10) | collective-permute-done | bytes 262176 | tf_op jit(solution)/shard_map/ppermute | solution.py:200
  55.1 5.9 %collective-permute-done.8.refs_0_ = bf16[16,64,128]{2,1,0:T(8,128)(2,1)S(1)} collective-permute-done((bf16[16,64,128]{2,1,0:T(8,128)(2,1)S(1)}, bf16[16,64,128]{2,1,0:T(8,128)(2,1)S(1)}, u32[]{:S(2)}, u32[]{:S(2)}) %collective-permute-start.8) | collective-permute-done | bytes 262176 | tf_op jit(solution)/shard_map/ppermute | solution.py:200
  61.0 1.4 %collective-permute-done.9.refs_1_ = bf16[16,64,128]{2,1,0:T(8,128)(2,1)S(1)} collective-permute-done((bf16[16,64,128]{2,1,0:T(8,128)(2,1)S(1)}, bf16[16,64,128]{2,1,0:T(8,128)(2,1)S(1)}, u32[]{:S(2)}, u32[]{:S(2)}) %collective-permute-start.9) | collective-permute-done | bytes 262176 | tf_op jit(solution)/shard_map/ppermute | solution.py:200
  63.4 2.7 %collective-permute-start.13 = (bf16[4,64,128]{2,1,0:T(8,128)(2,1)S(1)}, bf16[4,64,128]{2,1,0:T(8,128)(2,1)S(1)}, u32[]{:S(2)}, u32[]{:S(2)}) collective-permute-start(bf16[4,64,128]{2,1,0:T(8,128)(2,1)S(1)} %get-tuple-element.45), channel_id=1, source_target_pairs={{0,16},{8,24},{16,0},{24,8},{1,17},{9,25},{17,1},{25,9},{2,18},{10... | collective-permute-start | bytes 196616 | tf_op jit(solution)/shard_map/ppermute | solution.py:200
  66.1 1.2 %collective-permute-start.14 = (bf16[4,64,128]{2,1,0:T(8,128)(2,1)S(1)}, bf16[4,64,128]{2,1,0:T(8,128)(2,1)S(1)}, u32[]{:S(2)}, u32[]{:S(2)}) collective-permute-start(bf16[4,64,128]{2,1,0:T(8,128)(2,1)S(1)} %get-tuple-element.46), channel_id=1, source_target_pairs={{0,17},{1,16},{8,25},{9,24},{16,1},{17,0},{24,9},{25,8},{2,19},{3,... | collective-permute-start | bytes 196616 | tf_op jit(solution)/shard_map/ppermute | solution.py:200
  67.2 1.3 %collective-permute-done.13.above_ref = bf16[4,64,128]{2,1,0:T(8,128)(2,1)S(1)} collective-permute-done((bf16[4,64,128]{2,1,0:T(8,128)(2,1)S(1)}, bf16[4,64,128]{2,1,0:T(8,128)(2,1)S(1)}, u32[]{:S(2)}, u32[]{:S(2)}) %collective-permute-start.13) | collective-permute-done | bytes 65568 | tf_op jit(solution)/shard_map/ppermute | solution.py:200
  68.6 3.7 %collective-permute-done.14.both_ref = bf16[4,64,128]{2,1,0:T(8,128)(2,1)S(1)} collective-permute-done((bf16[4,64,128]{2,1,0:T(8,128)(2,1)S(1)}, bf16[4,64,128]{2,1,0:T(8,128)(2,1)S(1)}, u32[]{:S(2)}, u32[]{:S(2)}) %collective-permute-start.14) | collective-permute-done | bytes 65568 | tf_op jit(solution)/shard_map/ppermute | solution.py:200
  (37 shorter events, 7.2 us)
Async XLA Ops:
  1.3 6.3 %collective-permute-start = (bf16[16,128]{1,0:T(8,128)(2,1)S(1)}, bf16[16,128]{1,0:T(8,128)(2,1)S(1)}, u32[]{:S(2)}, u32[]{:S(2)}) collective-permute-start(bf16[16,128]{1,0:T(8,128)(2,1)S(1)} %slice_bitcast_fusion), channel_id=1, source_target_pairs={{0,1},{1,0},{2,3},{3,2},{4,5},{5,4},{6,7},{7,6},{8,9},{9,8},{10,11... | collective-permute-start | bytes 12296 | tf_op jit(solution)/shard_map/ppermute | solution.py:200
  4.4 12.2 %copy-start = (f32[16,128]{1,0:T(8,128)S(1)}, f32[16,128]{1,0:T(8,128)}, u32[]{:S(2)}) copy-start(f32[16,128]{1,0:T(8,128)} %refs_3_.7) | copy-start | bytes 24580
  4.4 12.1 %collective-permute-start.4 = (bf16[8,3,64,128]{3,2,1,0:T(8,128)(2,1)S(1)}, bf16[8,3,64,128]{3,2,1,0:T(8,128)(2,1)S(1)}, u32[]{:S(2)}, u32[]{:S(2)}) collective-permute-start(bf16[8,3,64,128]{3,2,1,0:T(8,128)(2,1)S(1)} %slice.63.refs_0_), channel_id=1, source_target_pairs={{0,1},{1,0},{2,3},{3,2},{4,5},{5,4},{6,7},{7,6},{8,9},{9,8},{10,11... | collective-permute-start | bytes 1179656 | tf_op jit(solution)/shard_map/ppermute | solution.py:200
  7.6 3.9 %collective-permute-start.1 = (bf16[16,3,64]{2,0,1:T(8,128)(2,1)}, bf16[16,3,64]{2,0,1:T(8,128)(2,1)S(1)}, u32[]{:S(2)}, u32[]{:S(2)}) collective-permute-start(bf16[16,3,64]{2,0,1:T(8,128)(2,1)} %bitcast.1), channel_id=1, source_target_pairs={{0,2},{2,4},{4,6},{1,3},{3,5},{5,7},{8,10},{10,12},{12,14},{9,11},... | collective-permute-start | bytes 18440 | tf_op jit(solution)/shard_map/ppermute | solution.py:325
  9.1 5.2 %collective-permute-start.2 = (bf16[16,3,64]{2,0,1:T(8,128)(2,1)S(1)}, bf16[16,3,64]{2,0,1:T(8,128)(2,1)S(1)}, u32[]{:S(2)}, u32[]{:S(2)}) collective-permute-start(bf16[16,3,64]{2,0,1:T(8,128)(2,1)S(1)} %bitcast.15), channel_id=1, source_target_pairs={{2,0},{4,2},{6,4},{3,1},{5,3},{7,5},{10,8},{12,10},{14,12},{11,9},... | collective-permute-start | bytes 18440 | tf_op jit(solution)/shard_map/ppermute | solution.py:326
  14.3 20.6 %collective-permute-start.3 = (bf16[8,3,64,128]{3,2,1,0:T(8,128)(2,1)S(1)}, bf16[8,3,64,128]{3,2,1,0:T(8,128)(2,1)S(1)}, u32[]{:S(2)}, u32[]{:S(2)}) collective-permute-start(bf16[8,3,64,128]{3,2,1,0:T(8,128)(2,1)S(1)} %pad_maximum_fusion.refs_0_), channel_id=1, source_target_pairs={{0,1},{1,0},{2,3},{3,2},{4,5},{5,4},{6,7},{7,6},{8,9},{9,8},{10,11... | collective-permute-start | bytes 1179656 | tf_op jit(solution)/shard_map/ppermute | solution.py:200
  16.5 6.2 %copy-start.2 = (bf16[1,3,64,128]{3,2,1,0:T(8,128)(2,1)S(1)}, bf16[1,3,64,128]{3,2,1,0:T(8,128)(2,1)}, u32[]{:S(2)}) copy-start(bf16[1,3,64,128]{3,2,1,0:T(8,128)(2,1)} %get-tuple-element.31) | copy-start | bytes 147460
  16.5 9.7 %copy-start.1 = (bf16[1,3,64,128]{3,2,1,0:T(8,128)(2,1)S(1)}, bf16[1,3,64,128]{3,2,1,0:T(8,128)(2,1)}, u32[]{:S(2)}) copy-start(bf16[1,3,64,128]{3,2,1,0:T(8,128)(2,1)} %get-tuple-element.32) | copy-start | bytes 147460
  22.8 11.4 %collective-permute-start.5 = (bf16[1,3,64,128]{3,2,1,0:T(8,128)(2,1)S(1)}, bf16[1,3,64,128]{3,2,1,0:T(8,128)(2,1)S(1)}, u32[]{:S(2)}, u32[]{:S(2)}) collective-permute-start(bf16[1,3,64,128]{3,2,1,0:T(8,128)(2,1)S(1)} %copy-done.2), channel_id=1, source_target_pairs={{0,8},{8,16},{16,24},{1,9},{9,17},{17,25},{2,10},{10,18},{18,26},{... | collective-permute-start | bytes 147464 | tf_op jit(solution)/shard_map/ppermute | solution.py:336
  26.3 7.9 %collective-permute-start.6 = (bf16[1,3,64,128]{3,2,1,0:T(8,128)(2,1)S(1)}, bf16[1,3,64,128]{3,2,1,0:T(8,128)(2,1)S(1)}, u32[]{:S(2)}, u32[]{:S(2)}) collective-permute-start(bf16[1,3,64,128]{3,2,1,0:T(8,128)(2,1)S(1)} %copy-done.1), channel_id=1, source_target_pairs={{8,0},{16,8},{24,16},{9,1},{17,9},{25,17},{10,2},{18,10},{26,18},{... | collective-permute-start | bytes 147464 | tf_op jit(solution)/shard_map/ppermute | solution.py:337
  39.3 6.1 %collective-permute-start.7 = (bf16[48,64,128]{2,1,0:T(8,128)(2,1)S(1)}, bf16[48,64,128]{2,1,0:T(8,128)(2,1)S(1)}, u32[]{:S(2)}, u32[]{:S(2)}) collective-permute-start(bf16[48,64,128]{2,1,0:T(8,128)(2,1)S(1)} %shard_map.33), channel_id=1, source_target_pairs={{0,2},{2,0},{4,6},{6,4},{1,3},{3,1},{5,7},{7,5},{8,10},{10,8},{12,... | collective-permute-start | bytes 2359304 | tf_op jit(solution)/shard_map/ppermute | solution.py:200
  45.6 9.5 %collective-permute-start.10 = (bf16[16,64,128]{2,1,0:T(8,128)(2,1)S(1)}, bf16[16,64,128]{2,1,0:T(8,128)(2,1)S(1)}, u32[]{:S(2)}, u32[]{:S(2)}) collective-permute-start(bf16[16,64,128]{2,1,0:T(8,128)(2,1)S(1)} %get-tuple-element.39), channel_id=1, source_target_pairs={{0,8},{8,0},{16,24},{24,16},{1,9},{9,1},{17,25},{25,17},{2,10},{10... | collective-permute-start | bytes 786440 | tf_op jit(solution)/shard_map/ppermute | solution.py:200
  48.0 13.0 %collective-permute-start.8 = (bf16[16,64,128]{2,1,0:T(8,128)(2,1)S(1)}, bf16[16,64,128]{2,1,0:T(8,128)(2,1)S(1)}, u32[]{:S(2)}, u32[]{:S(2)}) collective-permute-start(bf16[16,64,128]{2,1,0:T(8,128)(2,1)S(1)} %get-tuple-element.37), channel_id=1, source_target_pairs={{0,12},{2,14},{4,8},{6,10},{8,4},{10,6},{12,0},{14,2},{16,28},{18,... | collective-permute-start | bytes 786440 | tf_op jit(solution)/shard_map/ppermute | solution.py:200
  48.4 14.1 %collective-permute-start.9 = (bf16[16,64,128]{2,1,0:T(8,128)(2,1)S(1)}, bf16[16,64,128]{2,1,0:T(8,128)(2,1)S(1)}, u32[]{:S(2)}, u32[]{:S(2)}) collective-permute-start(bf16[16,64,128]{2,1,0:T(8,128)(2,1)S(1)} %get-tuple-element.38), channel_id=1, source_target_pairs={{0,4},{2,6},{4,0},{6,2},{1,5},{3,7},{5,1},{7,3},{8,12},{10,14},{12... | collective-permute-start | bytes 786440 | tf_op jit(solution)/shard_map/ppermute | solution.py:200
  52.5 10.0 %collective-permute-start.11 = (bf16[16,64,128]{2,1,0:T(8,128)(2,1)S(1)}, bf16[16,64,128]{2,1,0:T(8,128)(2,1)S(1)}, u32[]{:S(2)}, u32[]{:S(2)}) collective-permute-start(bf16[16,64,128]{2,1,0:T(8,128)(2,1)S(1)} %get-tuple-element.42), channel_id=1, source_target_pairs={{0,2},{2,0},{4,6},{6,4},{1,3},{3,1},{5,7},{7,5},{8,10},{10,8},{12,... | collective-permute-start | bytes 786440 | tf_op jit(solution)/shard_map/ppermute | solution.py:200
  62.8 4.5 %collective-permute-start.12 = (bf16[4,64,128]{2,1,0:T(8,128)(2,1)S(1)}, bf16[4,64,128]{2,1,0:T(8,128)(2,1)S(1)}, u32[]{:S(2)}, u32[]{:S(2)}) collective-permute-start(bf16[4,64,128]{2,1,0:T(8,128)(2,1)S(1)} %get-tuple-element.44), channel_id=1, source_target_pairs={{0,1},{1,0},{2,3},{3,2},{4,5},{5,4},{6,7},{7,6},{8,9},{9,8},{10,11... | collective-permute-start | bytes 196616 | tf_op jit(solution)/shard_map/ppermute | solution.py:200
  63.4 5.2 %collective-permute-start.13 = (bf16[4,64,128]{2,1,0:T(8,128)(2,1)S(1)}, bf16[4,64,128]{2,1,0:T(8,128)(2,1)S(1)}, u32[]{:S(2)}, u32[]{:S(2)}) collective-permute-start(bf16[4,64,128]{2,1,0:T(8,128)(2,1)S(1)} %get-tuple-element.45), channel_id=1, source_target_pairs={{0,16},{8,24},{16,0},{24,8},{1,17},{9,25},{17,1},{25,9},{2,18},{10... | collective-permute-start | bytes 196616 | tf_op jit(solution)/shard_map/ppermute | solution.py:200
  66.1 6.2 %collective-permute-start.14 = (bf16[4,64,128]{2,1,0:T(8,128)(2,1)S(1)}, bf16[4,64,128]{2,1,0:T(8,128)(2,1)S(1)}, u32[]{:S(2)}, u32[]{:S(2)}) collective-permute-start(bf16[4,64,128]{2,1,0:T(8,128)(2,1)S(1)} %get-tuple-element.46), channel_id=1, source_target_pairs={{0,17},{1,16},{8,25},{9,24},{16,1},{17,0},{24,9},{25,8},{2,19},{3,... | collective-permute-start | bytes 196616 | tf_op jit(solution)/shard_map/ppermute | solution.py:200

commit v7 on v6

--- a/solution.py
+++ b/solution.py
@@ -33,38 +33,44 @@
     return found
 
 
-def slopes_kernel(own_ref, *refs, rows, parts):
+def slopes_kernel(own_ref, columns_ref, *refs, rows):
     out_ref = refs[-1]
     last = own_ref.shape[0] - 1
-    cells = own_ref.shape[3]
-    if 1 in parts:
-        before = refs[0][...].astype(F32).T
-        after = refs[1][...].astype(F32).T
-        lane = lax.broadcasted_iota(jnp.int32, own_ref.shape[2:], 1)
+    share, cells = own_ref.shape[2:]
+
+    def edge(ref, axis, step):
+        at = lax.axis_index(axis) + step
+        inside = jnp.logical_and(at >= 0, at < lax.axis_size(axis))
+        at = jnp.clip(at, 0, lax.axis_size(axis) - 1)
+        values = ref[at, 0 if step < 0 else 1].astype(F32)
+        return jnp.where(inside, values, jnp.zeros_like(values))
+
+    before, after = edge(columns_ref, "gy", -1).T, edge(columns_ref, "gy", 1).T
+    above = edge(refs[0], "gx", -1) if 0 in rows else None
+    below = edge(refs[0], "gx", 1) if last in rows else None
+    lane = lax.broadcasted_iota(jnp.int32, (share, cells), 1)
     for place, x in enumerate(rows):
         for a in range(3):
-            if 0 in parts:
-                down = (refs[2][0, a] if x == 0 else own_ref[x - 1, a]).astype(F32)
-                up = (refs[3][0, a] if x == last else own_ref[x + 1, a]).astype(F32)
-                out_ref[place, a] = ((up - down) * 0.5).astype(BF16)
-            if 1 in parts:
-                value = own_ref[x, a].astype(F32)
-                column = 3 * x + a
-                down = jnp.where(lane == 0, before[:, column : column + 1], pltpu.roll(value, 1, 1))
-                up = jnp.where(lane == cells - 1, after[:, column : column + 1], pltpu.roll(value, cells - 1, 1))
-                out_ref[place, 3 * parts.index(1) + a] = ((up - down) * 0.5).astype(BF16)
-
-
-def slopes_of(own, rows, parts, *others):
+            down = above[a] if x == 0 else own_ref[x - 1, a].astype(F32)
+            up = below[a] if x == last else own_ref[x + 1, a].astype(F32)
+            out_ref[place, a] = ((up - down) * 0.5).astype(BF16)
+            value = own_ref[x, a].astype(F32)
+            column = 3 * x + a
+            down = jnp.where(lane == 0, before[:, column : column + 1], pltpu.roll(value, 1, 1))
+            up = jnp.where(lane == cells - 1, after[:, column : column + 1], pltpu.roll(value, cells - 1, 1))
+            out_ref[place, 3 + a] = ((up - down) * 0.5).astype(BF16)
+
+
+def slopes_of(own, rows, *edges):
     _, _, share, cells = own.shape
     return pl.pallas_call(
-        functools.partial(slopes_kernel, rows=rows, parts=parts),
-        out_shape=jax.ShapeDtypeStruct((len(rows), 3 * len(parts), share, cells), BF16),
-        in_specs=[pl.BlockSpec(memory_space=pltpu.VMEM)] * (1 + len(others)),
+        functools.partial(slopes_kernel, rows=rows),
+        out_shape=jax.ShapeDtypeStruct((len(rows), 6, share, cells), BF16),
+        in_specs=[pl.BlockSpec(memory_space=pltpu.VMEM)] * (1 + len(edges)),
         out_specs=pl.BlockSpec(memory_space=pltpu.VMEM),
         compiler_params=pltpu.CompilerParams(vmem_limit_bytes=16 << 20),
         cost_estimate=pl.CostEstimate(flops=1, bytes_accessed=1024, transcendentals=0),
-    )(own, *others)
+    )(own, *edges)
 
 
 def sum_of(left, right):
@@ -319,43 +325,41 @@
     own_outer = jnp.concatenate([own[:quarter], own[3 * quarter :]], 0)
 
     other_inner = flip(own_inner, [("ma", 0)], sizes)
-    token = flip(own[quarter, 0, :16], [("ma", 0)], sizes)
-    edges, token = barrier(((own[:, :, :, -1], own[:, :, :, 0]), token))
-    forward, backward = neighbours("gy")
-    before = lax.ppermute(edges[0], "gy", forward)
-    after = lax.ppermute(edges[1], "gy", backward)
-    own_outer_held, before, after = barrier((own_outer, before, after))
+    columns = jnp.stack([own[:, :, :, -1], own[:, :, :, 0]]).reshape(2, 3 * row_count, share)
+    columns = lax.all_gather(columns, "gy")
+    edge_rows = lax.all_gather(jnp.stack([own[-1], own[0]]), "gx")
+    own_outer_held, columns = barrier((own_outer, columns))
     other_outer = flip(own_outer_held, [("ma", 0)], sizes)
 
-    inner = functools.partial(
-        partial_tensor, own_inner, other_inner, volumes=cell_volumes, rows=inner_rows, sizes=sizes, blocks=range(BLOCKS)
+    so_far = partial_tensor(
+        own_inner,
+        other_inner,
+        slopes_of(own, inner_rows, columns),
+        cell_volumes,
+        inner_rows,
+        sizes,
+        range(BLOCKS),
     )
-    so_far = inner(slopes_of(own, inner_rows, (0,)), parts=(0,))
-    edges, so_far = barrier(((own[-1:], own[:1]), so_far))
-    forward, backward = neighbours("gx")
-    above = lax.ppermute(edges[0], "gx", forward)
-    below = lax.ppermute(edges[1], "gx", backward)
-    before = before.reshape(3 * row_count, share)
-    after = after.reshape(3 * row_count, share)
-    so_far = inner(slopes_of(own, inner_rows, (1,), before, after, token), parts=(1,), before=so_far)
-
-    slopes_outer = slopes_of(own, outer_rows, (0, 1), before, after, above, below)
+    edge_rows, so_far = barrier((edge_rows, so_far))
+    slopes_outer = slopes_of(own, outer_rows, columns, edge_rows)
     outer = functools.partial(
         partial_tensor, own_outer, other_outer, slopes_outer, rows=outer_rows, sizes=sizes, before=so_far
     )
     stages = stages_of(sizes)
     count = modes // BLOCKS
     cell_count = mode_fields.shape[2] * mode_fields.shape[3]
-    sent = outer(cell_volumes, blocks=(5, 6, 7), dtypes=(BF16,))
+    sent = outer(cell_volumes, blocks=(4, 5, 6, 7), dtypes=(BF16,))
     cell_volumes, sent = barrier((cell_volumes, sent))
     arrived = flip(sent, stages[0], sizes)
-    kept = outer(cell_volumes, blocks=(1, 2, 3))
-    sent = [term_sum([kept, arrived], at * count, (at + 1) * count).astype(BF16) for at in range(3)]
+    upper = outer(cell_volumes, blocks=(2, 3))
+    upper_terms = [upper, arrived[2 * count :]]
+    sent = [term_sum(upper_terms, at * count, (at + 1) * count).astype(BF16) for at in range(2)]
     cell_volumes, sent = barrier((cell_volumes, sent))
+    lower = outer(cell_volumes, blocks=(0, 1))
+    sent = [term_sum([lower, arrived], count, 2 * count).astype(BF16)] + sent
     received = exchange(stages[1], sent[::-1], sizes)
-    sent, kept = outer(cell_volumes, blocks=(4, 0), dtypes=(BF16, F32))
-    arrived = flip(sent, stages[0], sizes)
-    terms = [summed(received, count, 16 * count * modes * share * cell_count), kept, arrived]
+    cost = 16 * count * modes * share * cell_count
+    terms = [summed([lower, arrived] + received[:2], count, cost), received[2]]
     for stage in stages[2:-1]:
         terms = terms + exchange(stage, sends(terms, count, stage), sizes)
         count = count >> len(stage)

time: 73.4 us -> 74.7 us (1.018)
  blocking collectives: 0 us -> 20.7 us
  starting transfers between devices: 22.5 us -> 11.5 us
  waiting for transfers between devices: 17.6 us -> 14.7 us
  Pallas kernels: 26.9 us -> 24.6 us
  local copies, waits for them, and re-layouts: 4.57 us -> 2.64 us
  other arithmetic: 1.29 us -> 0.27 us
    all_gather x0 -> x2, blocking collectives: none -> 20.7 us  [the longest x1 15.4 us: shards(): edge_rows = lax.all_gather(jnp.stack([own[-1], own[0]]), 'gx')]
    ppermute x4 -> x0, starting transfers between devices: 7.52 us -> none  [the longest x1 3.48 us: shards(): above = lax.ppermute(edges[0], 'gx', forward)]
    ppermute x11 -> x9, starting transfers between devices: 15 us -> 11.5 us  [flip(): return lax.ppermute(array, axes, [(i, i ^ change) for i in range(count)])]
    ppermute x4 -> x0, waiting for transfers between devices: 2.69 us -> none  [the longest x1 2.68 us: shards(): after = lax.ppermute(edges[1], 'gy', backward)]
    pallas_call x5 -> x4, Pallas kernels: 24.3 us -> 22 us  [partial_tensor(): pl.pallas_call(body, grid=(len(blocks),), out_shape=out_shape, in_specs=i...]
    slice x4 -> x2, local copies, waits for them, and re-layouts: 2.37 us -> 1.19 us  [the longest x1 1.18 us: shards(): own[:, :, :, -1]]
    concatenate x1, other arithmetic: 1.06 us -> 0.04 us  [shards(): own_outer = jnp.concatenate([own[:quarter], own[3 * quarter:]], 0)]
    ppermute x11 -> x9, waiting for transfers between devices: 14.9 us -> 14.7 us  [flip(): return lax.ppermute(array, axes, [(i, i ^ change) for i in range(count)])]
  transfers between devices with their start and end apart: 15 -> 9, of which waited for: 6 -> 4; matrix products, arithmetic and copies ran while one was open for 6% -> 2% of each run, Pallas kernels for 29% -> 24%
where the time goes in v7:
time: 74.7 us; the launch traced here: 74.6 us
  Pallas kernels  24.6 us (33%)
  blocking collectives  20.7 us (28%)
  waiting for transfers between devices  14.7 us (20%)
  starting transfers between devices  11.5 us (15%)
  local copies, waits for them, and re-layouts  2.64 us (4%)
    pallas_call x4, Pallas kernels, partial_tensor(): pl.pallas_call(body, grid=(len(blocks),), out_shape=out_shape, in_specs=i...  22 us
    all_gather x1, blocking collectives, shards(): edge_rows = lax.all_gather(jnp.stack([own[-1], own[0]]), 'gx')  15.4 us
    ppermute x9, waiting for transfers between devices, flip(): return lax.ppermute(array, axes, [(i, i ^ change) for i in range(count)])  14.7 us
    ppermute x9, starting transfers between devices, flip(): return lax.ppermute(array, axes, [(i, i ^ change) for i in range(count)])  11.5 us
    all_gather x1, blocking collectives, shards(): columns = lax.all_gather(columns, 'gy')  5.34 us
  transfers between devices with their start and end apart: 9, of which 4 were waited for; matrix products, arithmetic and copies ran while one was open for 2% of the time, Pallas kernels for 24%

profile of v7, /device:TPU:0, one launch (start us, length us, event | category | flops | bytes accessed | tf_op | source)
XLA Modules:
  0.0 74.6 jit_solution(17277428053154555367)
XLA Ops:
  0.0 1.3 %copy.7 = bf16[3,64,16,128]{3,1,0,2:T(8,128)(2,1)S(1)} copy(bf16[3,64,16,128]{3,2,1,0:T(8,128)(2,1)} %param.2) | data formatting | bytes 1572864 | tf_op args[0]
  1.4 3.0 %collective-permute-start.1 = (bf16[8,3,64,128]{3,2,1,0:T(8,128)(2,1)S(1)}, bf16[8,3,64,128]{3,2,1,0:T(8,128)(2,1)S(1)}, u32[]{:S(2)}, u32[]{:S(2)}) collective-permute-start(bf16[8,3,64,128]{3,2,1,0:T(8,128)(2,1)S(1)} %slice.61.refs_0_), channel_id=1, source_target_pairs={{0,1},{1,0},{2,3},{3,2},{4,5},{5,4},{6,7},{7,6},{8,9},{9,8},{10,11... | collective-permute-start | bytes 1179656 | tf_op jit(solution)/shard_map/ppermute | solution.py:206
  4.4 1.2 %slice_reduce_fusion.1 = (bf16[16,3,64]{2,1,0:T(4,128)(2,1)S(1)}, bf16[16,3,64]{2,1,0:T(4,128)(2,1)S(1)}) fusion(bf16[16,3,64,128]{3,2,1,0:T(8,128)(2,1)S(1)} %bitcast.6), kind=kLoop, calls=%fused_computation.1 | loop fusion | bytes 24576 | tf_op jit(solution)/shard_map/slice | solution.py:328
  5.7 5.3 %all_gather.9.columns_ref = bf16[4,2,48,64]{3,2,1,0:T(8,128)(2,1)S(1)} all-gather(bf16[1,2,48,64]{3,2,1,0:T(8,128)(2,1)S(1)} %pad_maximum_fusion.2), channel_id=1, replica_groups=mesh['gx'=4,'gy'=4,'ma'=2] {'gy'}, dimensions={0}, use_global_device_ids=true | all-gather | bytes 61440 | tf_op jit(solution)/shard_map/all_gather | solution.py:329
  11.0 0.1 collective-permute-start
  11.2 0.7 shard_map.28.refs_2_
  12.0 15.4 %all-gather = bf16[8,3,64,128]{3,2,1,0:T(8,128)(2,1)S(1)} all-gather(bf16[2,3,64,128]{3,2,1,0:T(8,128)(2,1)S(1)} %pad_maximum_fusion.1), channel_id=2, replica_groups=mesh['gx'=4,'gy'=4,'ma'=2] {'gx'}, dimensions={0}, use_global_device_ids=true | all-gather | bytes 491520 | tf_op jit(solution)/shard_map/all_gather | solution.py:330
  27.3 10.6 %shard_map.29.refs_4_ = f32[128,64,128]{2,1,0:T(8,128)S(1)} custom-call(bf16[8,3,64,128]{3,2,1,0:T(8,128)(2,1)S(1)} %slice.61.refs_0_, bf16[8,3,64,128]{3,2,1,0:T(8,128)(2,1)S(1)} %collective-permute-done.1.refs_1_, bf16[8,6,64,128]{3,2,1,0:T(8,128)(2,1)S(1)} %shard_map.28.refs_2_, f32[16,128]{1,0:T(8,128)S(1)} %copy-done), custom_call_target="tpu_custom_call" | custom-call | flops 8589934592 | bytes 4194304 | tf_op jit(solution)/shard_map/pallas_call | solution.py:173
  37.9 0.7 shard_map.30.refs_2_
  38.6 5.7 %shard_map.31 = bf16[64,64,128]{2,1,0:T(8,128)(2,1)S(1)} custom-call(bf16[8,3,64,128]{3,2,1,0:T(8,128)(2,1)S(1)} %pad_maximum_fusion.refs_0_, bf16[8,3,64,128]{3,2,1,0:T(8,128)(2,1)S(1)} %collective-permute-done.refs_1_, bf16[8,6,64,128]{3,2,1,0:T(8,128)(2,1)S(1)} %shard_map.30.refs_2_, f32[16,128]{1,0:T(8,128)S(1)} %copy-done, ...), custom_call_target="tpu_custom_call" | custom-call | flops 4294967296 | bytes 4194304 | tf_op jit(solution)/shard_map/pallas_call | solution.py:173
  44.4 2.9 %shard_map.32 = f32[32,64,128]{2,1,0:T(8,128)S(1)} custom-call(bf16[8,3,64,128]{3,2,1,0:T(8,128)(2,1)S(1)} %pad_maximum_fusion.refs_0_, bf16[8,3,64,128]{3,2,1,0:T(8,128)(2,1)S(1)} %collective-permute-done.refs_1_, bf16[8,6,64,128]{3,2,1,0:T(8,128)(2,1)S(1)} %shard_map.30.refs_2_, f32[16,128]{1,0:T(8,128)S(1)} %copy-done, f32[128,64,128]{2,1,0:T(8,128)S(1)} %shard_map.29.refs_4_), custom_call_target="tpu_custom_call" | custom-call | flops 2147483648 | bytes 4194304 | tf_op jit(solution)/shard_map/pallas_call | solution.py:173
  47.5 3.1 %collective-permute-start.3 = (bf16[16,64,128]{2,1,0:T(8,128)(2,1)S(1)}, bf16[16,64,128]{2,1,0:T(8,128)(2,1)S(1)}, u32[]{:S(2)}, u32[]{:S(2)}) collective-permute-start(bf16[16,64,128]{2,1,0:T(8,128)(2,1)S(1)} %get-tuple-element.25), channel_id=1, source_target_pairs={{0,12},{2,14},{4,8},{6,10},{8,4},{10,6},{12,0},{14,2},{16,28},{18,... | collective-permute-start | bytes 786440 | tf_op jit(solution)/shard_map/ppermute | solution.py:206
  50.6 0.6 collective-permute-start.4
  51.2 2.9 %shard_map.33.refs_0_ = f32[32,64,128]{2,1,0:T(8,128)S(1)} custom-call(bf16[8,3,64,128]{3,2,1,0:T(8,128)(2,1)S(1)} %pad_maximum_fusion.refs_0_, bf16[8,3,64,128]{3,2,1,0:T(8,128)(2,1)S(1)} %collective-permute-done.refs_1_, bf16[8,6,64,128]{3,2,1,0:T(8,128)(2,1)S(1)} %shard_map.30.refs_2_, f32[16,128]{1,0:T(8,128)S(1)} %copy-done, ...), custom_call_target="tpu_custom_call" | custom-call | flops 2147483648 | bytes 4194304 | tf_op jit(solution)/shard_map/pallas_call | solution.py:173
  54.1 0.1 collective-permute-start.5
  54.3 3.5 %collective-permute-done.3.refs_2_ = bf16[16,64,128]{2,1,0:T(8,128)(2,1)S(1)} collective-permute-done((bf16[16,64,128]{2,1,0:T(8,128)(2,1)S(1)}, bf16[16,64,128]{2,1,0:T(8,128)(2,1)S(1)}, u32[]{:S(2)}, u32[]{:S(2)}) %collective-permute-start.3) | collective-permute-done | bytes 262176 | tf_op jit(solution)/shard_map/ppermute | solution.py:206
  57.7 5.5 %collective-permute-done.4.refs_3_ = bf16[16,64,128]{2,1,0:T(8,128)(2,1)S(1)} collective-permute-done((bf16[16,64,128]{2,1,0:T(8,128)(2,1)S(1)}, bf16[16,64,128]{2,1,0:T(8,128)(2,1)S(1)}, u32[]{:S(2)}, u32[]{:S(2)}) %collective-permute-start.4) | collective-permute-done | bytes 262176 | tf_op jit(solution)/shard_map/ppermute | solution.py:206
  63.4 0.2 shard_map.35
  63.6 1.6 %collective-permute-start.6 = (bf16[4,64,128]{2,1,0:T(8,128)(2,1)S(1)}, bf16[4,64,128]{2,1,0:T(8,128)(2,1)S(1)}, u32[]{:S(2)}, u32[]{:S(2)}) collective-permute-start(bf16[4,64,128]{2,1,0:T(8,128)(2,1)S(1)} %get-tuple-element.28), channel_id=1, source_target_pairs={{0,1},{1,0},{2,3},{3,2},{4,5},{5,4},{6,7},{7,6},{8,9},{9,8},{10,11... | collective-permute-start | bytes 196616 | tf_op jit(solution)/shard_map/ppermute | solution.py:206
  65.1 2.5 %collective-permute-start.7 = (bf16[4,64,128]{2,1,0:T(8,128)(2,1)S(1)}, bf16[4,64,128]{2,1,0:T(8,128)(2,1)S(1)}, u32[]{:S(2)}, u32[]{:S(2)}) collective-permute-start(bf16[4,64,128]{2,1,0:T(8,128)(2,1)S(1)} %get-tuple-element.29), channel_id=1, source_target_pairs={{0,16},{8,24},{16,0},{24,8},{1,17},{9,25},{17,1},{25,9},{2,18},{10... | collective-permute-start | bytes 196616 | tf_op jit(solution)/shard_map/ppermute | solution.py:206
  67.6 0.4 collective-permute-start.8
  68.0 2.6 %collective-permute-done.7.above_ref = bf16[4,64,128]{2,1,0:T(8,128)(2,1)S(1)} collective-permute-done((bf16[4,64,128]{2,1,0:T(8,128)(2,1)S(1)}, bf16[4,64,128]{2,1,0:T(8,128)(2,1)S(1)}, u32[]{:S(2)}, u32[]{:S(2)}) %collective-permute-start.7) | collective-permute-done | bytes 65568 | tf_op jit(solution)/shard_map/ppermute | solution.py:206
  70.6 3.1 %collective-permute-done.8.both_ref = bf16[4,64,128]{2,1,0:T(8,128)(2,1)S(1)} collective-permute-done((bf16[4,64,128]{2,1,0:T(8,128)(2,1)S(1)}, bf16[4,64,128]{2,1,0:T(8,128)(2,1)S(1)}, u32[]{:S(2)}, u32[]{:S(2)}) %collective-permute-start.8) | collective-permute-done | bytes 65568 | tf_op jit(solution)/shard_map/ppermute | solution.py:206
  73.7 0.8 %shard_map.36 = f32[8,64,128]{2,1,0:T(8,128)} custom-call(f32[4,64,128]{2,1,0:T(8,128)S(1)} %get-tuple-element.27.own_ref, bf16[4,64,128]{2,1,0:T(8,128)(2,1)S(1)} %collective-permute-done.6.swapped_ref, bf16[4,64,128]{2,1,0:T(8,128)(2,1)S(1)} %collective-permute-done.7.above_ref, bf16[4,64,128]{2,1,0:T(8,128)(2,1)S(1)} %collective-permute-done.8.both_ref), custom_call_target="tpu_custom_call" | custom-call | flops 1 | bytes 1024 | tf_op jit(solution)/shard_map/pallas_call | solution.py:305
  (19 shorter events, 0.6 us)
Async XLA Ops:
  0.0 27.3 %copy-start = (f32[16,128]{1,0:T(8,128)S(1)}, f32[16,128]{1,0:T(8,128)}, u32[]{:S(2)}) copy-start(f32[16,128]{1,0:T(8,128)} %refs_3_.5) | copy-start | bytes 24580
  1.4 26.0 %collective-permute-start.1 = (bf16[8,3,64,128]{3,2,1,0:T(8,128)(2,1)S(1)}, bf16[8,3,64,128]{3,2,1,0:T(8,128)(2,1)S(1)}, u32[]{:S(2)}, u32[]{:S(2)}) collective-permute-start(bf16[8,3,64,128]{3,2,1,0:T(8,128)(2,1)S(1)} %slice.61.refs_0_), channel_id=1, source_target_pairs={{0,1},{1,0},{2,3},{3,2},{4,5},{5,4},{6,7},{7,6},{8,9},{9,8},{10,11... | collective-permute-start | bytes 1179656 | tf_op jit(solution)/shard_map/ppermute | solution.py:206
  11.0 27.6 %collective-permute-start = (bf16[8,3,64,128]{3,2,1,0:T(8,128)(2,1)S(1)}, bf16[8,3,64,128]{3,2,1,0:T(8,128)(2,1)S(1)}, u32[]{:S(2)}, u32[]{:S(2)}) collective-permute-start(bf16[8,3,64,128]{3,2,1,0:T(8,128)(2,1)S(1)} %pad_maximum_fusion.refs_0_), channel_id=1, source_target_pairs={{0,1},{1,0},{2,3},{3,2},{4,5},{5,4},{6,7},{7,6},{8,9},{9,8},{10,11... | collective-permute-start | bytes 1179656 | tf_op jit(solution)/shard_map/ppermute | solution.py:206
  44.3 3.0 %collective-permute-start.2 = (bf16[64,64,128]{2,1,0:T(8,128)(2,1)S(1)}, bf16[64,64,128]{2,1,0:T(8,128)(2,1)S(1)}, u32[]{:S(2)}, u32[]{:S(2)}) collective-permute-start(bf16[64,64,128]{2,1,0:T(8,128)(2,1)S(1)} %shard_map.31), channel_id=1, source_target_pairs={{0,2},{2,0},{4,6},{6,4},{1,3},{3,1},{5,7},{7,5},{8,10},{10,8},{12,... | collective-permute-start | bytes 3145736 | tf_op jit(solution)/shard_map/ppermute | solution.py:206
  47.5 10.2 %collective-permute-start.3 = (bf16[16,64,128]{2,1,0:T(8,128)(2,1)S(1)}, bf16[16,64,128]{2,1,0:T(8,128)(2,1)S(1)}, u32[]{:S(2)}, u32[]{:S(2)}) collective-permute-start(bf16[16,64,128]{2,1,0:T(8,128)(2,1)S(1)} %get-tuple-element.25), channel_id=1, source_target_pairs={{0,12},{2,14},{4,8},{6,10},{8,4},{10,6},{12,0},{14,2},{16,28},{18,... | collective-permute-start | bytes 786440 | tf_op jit(solution)/shard_map/ppermute | solution.py:206
  50.6 12.6 %collective-permute-start.4 = (bf16[16,64,128]{2,1,0:T(8,128)(2,1)S(1)}, bf16[16,64,128]{2,1,0:T(8,128)(2,1)S(1)}, u32[]{:S(2)}, u32[]{:S(2)}) collective-permute-start(bf16[16,64,128]{2,1,0:T(8,128)(2,1)S(1)} %get-tuple-element.26), channel_id=1, source_target_pairs={{0,4},{2,6},{4,0},{6,2},{1,5},{3,7},{5,1},{7,3},{8,12},{10,14},{12... | collective-permute-start | bytes 786440 | tf_op jit(solution)/shard_map/ppermute | solution.py:206
  54.1 9.2 %collective-permute-start.5 = (bf16[16,64,128]{2,1,0:T(8,128)(2,1)S(1)}, bf16[16,64,128]{2,1,0:T(8,128)(2,1)S(1)}, u32[]{:S(2)}, u32[]{:S(2)}) collective-permute-start(bf16[16,64,128]{2,1,0:T(8,128)(2,1)S(1)} %fusion), channel_id=1, source_target_pairs={{0,8},{8,0},{16,24},{24,16},{1,9},{9,1},{17,25},{25,17},{2,10},{10... | collective-permute-start | bytes 786440 | tf_op jit(solution)/shard_map/ppermute | solution.py:206
  63.6 4.5 %collective-permute-start.6 = (bf16[4,64,128]{2,1,0:T(8,128)(2,1)S(1)}, bf16[4,64,128]{2,1,0:T(8,128)(2,1)S(1)}, u32[]{:S(2)}, u32[]{:S(2)}) collective-permute-start(bf16[4,64,128]{2,1,0:T(8,128)(2,1)S(1)} %get-tuple-element.28), channel_id=1, source_target_pairs={{0,1},{1,0},{2,3},{3,2},{4,5},{5,4},{6,7},{7,6},{8,9},{9,8},{10,11... | collective-permute-start | bytes 196616 | tf_op jit(solution)/shard_map/ppermute | solution.py:206
  65.1 5.5 %collective-permute-start.7 = (bf16[4,64,128]{2,1,0:T(8,128)(2,1)S(1)}, bf16[4,64,128]{2,1,0:T(8,128)(2,1)S(1)}, u32[]{:S(2)}, u32[]{:S(2)}) collective-permute-start(bf16[4,64,128]{2,1,0:T(8,128)(2,1)S(1)} %get-tuple-element.29), channel_id=1, source_target_pairs={{0,16},{8,24},{16,0},{24,8},{1,17},{9,25},{17,1},{25,9},{2,18},{10... | collective-permute-start | bytes 196616 | tf_op jit(solution)/shard_map/ppermute | solution.py:206
  67.6 6.1 %collective-permute-start.8 = (bf16[4,64,128]{2,1,0:T(8,128)(2,1)S(1)}, bf16[4,64,128]{2,1,0:T(8,128)(2,1)S(1)}, u32[]{:S(2)}, u32[]{:S(2)}) collective-permute-start(bf16[4,64,128]{2,1,0:T(8,128)(2,1)S(1)} %get-tuple-element.30), channel_id=1, source_target_pairs={{0,17},{1,16},{8,25},{9,24},{16,1},{17,0},{24,9},{25,8},{2,19},{3,... | collective-permute-start | bytes 196616 | tf_op jit(solution)/shard_map/ppermute | solution.py:206

commit v8 on v7

--- a/solution.py
+++ b/solution.py
@@ -38,21 +38,20 @@
     last = own_ref.shape[0] - 1
     share, cells = own_ref.shape[2:]
 
-    def edge(ref, axis, step):
-        at = lax.axis_index(axis) + step
-        inside = jnp.logical_and(at >= 0, at < lax.axis_size(axis))
-        at = jnp.clip(at, 0, lax.axis_size(axis) - 1)
-        values = ref[at, 0 if step < 0 else 1].astype(F32)
-        return jnp.where(inside, values, jnp.zeros_like(values))
-
-    before, after = edge(columns_ref, "gy", -1).T, edge(columns_ref, "gy", 1).T
-    above = edge(refs[0], "gx", -1) if 0 in rows else None
-    below = edge(refs[0], "gx", 1) if last in rows else None
+    def edge(step):
+        count = columns_ref.shape[0]
+        at = lax.axis_index("gy") + step
+        inside = jnp.logical_and(at >= 0, at < count)
+        values = columns_ref[jnp.clip(at, 0, count - 1), 0 if step < 0 else 1].astype(F32)
+        return jnp.where(inside, values, jnp.zeros_like(values)).T
+
+    before, after = edge(-1), edge(1)
+    above_ref, below_ref = refs[:2] if len(refs) > 1 else (None, None)
     lane = lax.broadcasted_iota(jnp.int32, (share, cells), 1)
     for place, x in enumerate(rows):
         for a in range(3):
-            down = above[a] if x == 0 else own_ref[x - 1, a].astype(F32)
-            up = below[a] if x == last else own_ref[x + 1, a].astype(F32)
+            down = (above_ref[0, a] if x == 0 else own_ref[x - 1, a]).astype(F32)
+            up = (below_ref[0, a] if x == last else own_ref[x + 1, a]).astype(F32)
             out_ref[place, a] = ((up - down) * 0.5).astype(BF16)
             value = own_ref[x, a].astype(F32)
             column = 3 * x + a
@@ -327,8 +326,10 @@
     other_inner = flip(own_inner, [("ma", 0)], sizes)
     columns = jnp.stack([own[:, :, :, -1], own[:, :, :, 0]]).reshape(2, 3 * row_count, share)
     columns = lax.all_gather(columns, "gy")
-    edge_rows = lax.all_gather(jnp.stack([own[-1], own[0]]), "gx")
-    own_outer_held, columns = barrier((own_outer, columns))
+    own_outer_held, edges, columns = barrier((own_outer, (own[-1:], own[:1]), columns))
+    forward, backward = neighbours("gx")
+    above = lax.ppermute(edges[0], "gx", forward)
+    below = lax.ppermute(edges[1], "gx", backward)
     other_outer = flip(own_outer_held, [("ma", 0)], sizes)
 
     so_far = partial_tensor(
@@ -340,8 +341,8 @@
         sizes,
         range(BLOCKS),
     )
-    edge_rows, so_far = barrier((edge_rows, so_far))
-    slopes_outer = slopes_of(own, outer_rows, columns, edge_rows)
+    columns, so_far = barrier((columns, so_far))
+    slopes_outer = slopes_of(own, outer_rows, columns, above, below)
     outer = functools.partial(
         partial_tensor, own_outer, other_outer, slopes_outer, rows=outer_rows, sizes=sizes, before=so_far
     )

time: 74.7 us -> 64.6 us (0.86)
  blocking collectives: 20.7 us -> 5.34 us
  starting transfers between devices: 11.5 us -> 17.2 us
    all_gather x1 -> x0, blocking collectives: 15.4 us -> none  [shards(): edge_rows = lax.all_gather(jnp.stack([own[-1], own[0]]), 'gx')]
    ppermute x0 -> x2, starting transfers between devices: none -> 4.77 us  [the longest x1 3.48 us: shards(): above = lax.ppermute(edges[0], 'gx', forward)]
    ppermute x9, starting transfers between devices: 11.5 us -> 12.4 us  [flip(): return lax.ppermute(array, axes, [(i, i ^ change) for i in range(count)])]
  transfers between devices with their start and end apart: 9 -> 11, of which waited for: 4 -> 5; matrix products, arithmetic and copies ran while one was open for 2% -> 2% of each run, Pallas kernels for 24% -> 28%
where the time goes in v8:
time: 64.6 us; the launch traced here: 64.4 us
  Pallas kernels  24.6 us (38%)
  starting transfers between devices  17.2 us (27%)
  waiting for transfers between devices  14.2 us (22%)
  blocking collectives  5.34 us (8%)
  local copies, waits for them, and re-layouts  2.64 us (4%)
    pallas_call x4, Pallas kernels, partial_tensor(): pl.pallas_call(body, grid=(len(blocks),), out_shape=out_shape, in_specs=i...  22 us
    ppermute x9, waiting for transfers between devices, flip(): return lax.ppermute(array, axes, [(i, i ^ change) for i in range(count)])  14.1 us
    ppermute x9, starting transfers between devices, flip(): return lax.ppermute(array, axes, [(i, i ^ change) for i in range(count)])  12.4 us
    all_gather x1, blocking collectives, shards(): columns = lax.all_gather(columns, 'gy')  5.34 us
    ppermute x1, starting transfers between devices, shards(): above = lax.ppermute(edges[0], 'gx', forward)  3.48 us
    pallas_call x2, Pallas kernels, slopes_of(): pl.pallas_call(functools.partial(slopes_kernel, rows=rows), out_shape=jax...  1.42 us
    unnamed x3, local copies, waits for them, and re-layouts  1.35 us
    ppermute x1, starting transfers between devices, shards(): below = lax.ppermute(edges[1], 'gx', backward)  1.29 us
  transfers between devices with their start and end apart: 11, of which 5 were waited for; matrix products, arithmetic and copies ran while one was open for 2% of the time, Pallas kernels for 28%

profile of v8, /device:TPU:0, one launch (start us, length us, event | category | flops | bytes accessed | tf_op | source)
XLA Modules:
  0.0 64.4 jit_solution(1325260916552056957)
XLA Ops:
  0.0 1.3 %copy.7 = bf16[3,64,16,128]{3,1,0,2:T(8,128)(2,1)S(1)} copy(bf16[3,64,16,128]{3,2,1,0:T(8,128)(2,1)} %param.2) | data formatting | bytes 1572864 | tf_op args[0]
  1.4 3.0 %collective-permute-start.1 = (bf16[8,3,64,128]{3,2,1,0:T(8,128)(2,1)S(1)}, bf16[8,3,64,128]{3,2,1,0:T(8,128)(2,1)S(1)}, u32[]{:S(2)}, u32[]{:S(2)}) collective-permute-start(bf16[8,3,64,128]{3,2,1,0:T(8,128)(2,1)S(1)} %slice.61.refs_0_), channel_id=1, source_target_pairs={{0,1},{1,0},{2,3},{3,2},{4,5},{5,4},{6,7},{7,6},{8,9},{9,8},{10,11... | collective-permute-start | bytes 1179656 | tf_op jit(solution)/shard_map/ppermute | solution.py:205
  4.4 1.2 %slice_reduce_fusion.1 = (bf16[16,3,64]{2,1,0:T(4,128)(2,1)S(1)}, bf16[16,3,64]{2,1,0:T(4,128)(2,1)S(1)}) fusion(bf16[16,3,64,128]{3,2,1,0:T(8,128)(2,1)S(1)} %bitcast.5), kind=kLoop, calls=%fused_computation.1 | loop fusion | bytes 24576 | tf_op jit(solution)/shard_map/slice | solution.py:327
  5.7 5.3 %all_gather.3.columns_ref = bf16[4,2,48,64]{3,2,1,0:T(8,128)(2,1)S(1)} all-gather(bf16[1,2,48,64]{3,2,1,0:T(8,128)(2,1)S(1)} %pad_maximum_fusion.1), channel_id=1, replica_groups=mesh['gx'=4,'gy'=4,'ma'=2] {'gy'}, dimensions={0}, use_global_device_ids=true | all-gather | bytes 61440 | tf_op jit(solution)/shard_map/all_gather | solution.py:328
  11.1 3.5 %collective-permute-start.2 = (bf16[1,3,64,128]{3,2,1,0:T(8,128)(2,1)S(1)}, bf16[1,3,64,128]{3,2,1,0:T(8,128)(2,1)S(1)}, u32[]{:S(2)}, u32[]{:S(2)}) collective-permute-start(bf16[1,3,64,128]{3,2,1,0:T(8,128)(2,1)S(1)} %get-tuple-element.23), channel_id=1, source_target_pairs={{0,8},{8,16},{16,24},{1,9},{9,17},{17,25},{2,10},{10,18},{18,26},{... | collective-permute-start | bytes 147464 | tf_op jit(solution)/shard_map/ppermute | solution.py:331
  14.6 1.3 %collective-permute-start.3 = (bf16[1,3,64,128]{3,2,1,0:T(8,128)(2,1)S(1)}, bf16[1,3,64,128]{3,2,1,0:T(8,128)(2,1)S(1)}, u32[]{:S(2)}, u32[]{:S(2)}) collective-permute-start(bf16[1,3,64,128]{3,2,1,0:T(8,128)(2,1)S(1)} %get-tuple-element.24), channel_id=1, source_target_pairs={{8,0},{16,8},{24,16},{9,1},{17,9},{25,17},{10,2},{18,10},{26,18},{... | collective-permute-start | bytes 147464 | tf_op jit(solution)/shard_map/ppermute | solution.py:332
  15.9 0.6 collective-permute-start
  16.5 0.7 %shard_map.28.refs_2_ = bf16[8,6,64,128]{3,2,1,0:T(8,128)(2,1)S(1)} custom-call(bf16[16,3,64,128]{3,2,1,0:T(8,128)(2,1)S(1)} %bitcast.7, bf16[4,2,48,64]{3,2,1,0:T(8,128)(2,1)S(1)} %all_gather.3.columns_ref), custom_call_target="tpu_custom_call" | custom-call | flops 1 | bytes 1024 | tf_op jit(solution)/shard_map/pallas_call | solution.py:65
  17.2 10.6 %shard_map.29.refs_4_ = f32[128,64,128]{2,1,0:T(8,128)S(1)} custom-call(bf16[8,3,64,128]{3,2,1,0:T(8,128)(2,1)S(1)} %slice.61.refs_0_, bf16[8,3,64,128]{3,2,1,0:T(8,128)(2,1)S(1)} %collective-permute-done.1.refs_1_, bf16[8,6,64,128]{3,2,1,0:T(8,128)(2,1)S(1)} %shard_map.28.refs_2_, f32[16,128]{1,0:T(8,128)S(1)} %copy-done), custom_call_target="tpu_custom_call" | custom-call | flops 8589934592 | bytes 4194304 | tf_op jit(solution)/shard_map/pallas_call | solution.py:172
  27.8 0.7 %shard_map.30.refs_2_ = bf16[8,6,64,128]{3,2,1,0:T(8,128)(2,1)S(1)} custom-call(bf16[16,3,64,128]{3,2,1,0:T(8,128)(2,1)S(1)} %bitcast.8, bf16[4,2,48,64]{3,2,1,0:T(8,128)(2,1)S(1)} %all_gather.3.columns_ref, bf16[1,3,64,128]{3,2,1,0:T(8,128)(2,1)S(1)} %collective-permute-done.2.refs_0_, bf16[1,3,64,128]{3,2,1,0:T(8,128)(2,1)S(1)} %collective-permute-done.3.refs_1_), custom_call_target="tpu_custom_call" | custom-call | flops 1 | bytes 1024 | tf_op jit(solution)/shard_map/pallas_call | solution.py:65
  28.5 5.7 %shard_map.31 = bf16[64,64,128]{2,1,0:T(8,128)(2,1)S(1)} custom-call(bf16[8,3,64,128]{3,2,1,0:T(8,128)(2,1)S(1)} %pad_maximum_fusion.refs_0_, bf16[8,3,64,128]{3,2,1,0:T(8,128)(2,1)S(1)} %collective-permute-done.refs_1_, bf16[8,6,64,128]{3,2,1,0:T(8,128)(2,1)S(1)} %shard_map.30.refs_2_, f32[16,128]{1,0:T(8,128)S(1)} %copy-done, ...), custom_call_target="tpu_custom_call" | custom-call | flops 4294967296 | bytes 4194304 | tf_op jit(solution)/shard_map/pallas_call | solution.py:172
  34.3 2.9 %shard_map.32 = f32[32,64,128]{2,1,0:T(8,128)S(1)} custom-call(bf16[8,3,64,128]{3,2,1,0:T(8,128)(2,1)S(1)} %pad_maximum_fusion.refs_0_, bf16[8,3,64,128]{3,2,1,0:T(8,128)(2,1)S(1)} %collective-permute-done.refs_1_, bf16[8,6,64,128]{3,2,1,0:T(8,128)(2,1)S(1)} %shard_map.30.refs_2_, f32[16,128]{1,0:T(8,128)S(1)} %copy-done, f32[128,64,128]{2,1,0:T(8,128)S(1)} %shard_map.29.refs_4_), custom_call_target="tpu_custom_call" | custom-call | flops 2147483648 | bytes 4194304 | tf_op jit(solution)/shard_map/pallas_call | solution.py:172
  37.4 3.6 %collective-permute-start.5 = (bf16[16,64,128]{2,1,0:T(8,128)(2,1)S(1)}, bf16[16,64,128]{2,1,0:T(8,128)(2,1)S(1)}, u32[]{:S(2)}, u32[]{:S(2)}) collective-permute-start(bf16[16,64,128]{2,1,0:T(8,128)(2,1)S(1)} %get-tuple-element.29), channel_id=1, source_target_pairs={{0,12},{2,14},{4,8},{6,10},{8,4},{10,6},{12,0},{14,2},{16,28},{18,... | collective-permute-start | bytes 786440 | tf_op jit(solution)/shard_map/ppermute | solution.py:205
  41.0 0.5 collective-permute-start.6
  41.6 2.9 %shard_map.33.refs_0_ = f32[32,64,128]{2,1,0:T(8,128)S(1)} custom-call(bf16[8,3,64,128]{3,2,1,0:T(8,128)(2,1)S(1)} %pad_maximum_fusion.refs_0_, bf16[8,3,64,128]{3,2,1,0:T(8,128)(2,1)S(1)} %collective-permute-done.refs_1_, bf16[8,6,64,128]{3,2,1,0:T(8,128)(2,1)S(1)} %shard_map.30.refs_2_, f32[16,128]{1,0:T(8,128)S(1)} %copy-done, ...), custom_call_target="tpu_custom_call" | custom-call | flops 2147483648 | bytes 4194304 | tf_op jit(solution)/shard_map/pallas_call | solution.py:172
  44.7 3.5 %collective-permute-done.5.refs_2_ = bf16[16,64,128]{2,1,0:T(8,128)(2,1)S(1)} collective-permute-done((bf16[16,64,128]{2,1,0:T(8,128)(2,1)S(1)}, bf16[16,64,128]{2,1,0:T(8,128)(2,1)S(1)}, u32[]{:S(2)}, u32[]{:S(2)}) %collective-permute-start.5) | collective-permute-done | bytes 262176 | tf_op jit(solution)/shard_map/ppermute | solution.py:205
  48.1 5.5 %collective-permute-done.6.refs_3_ = bf16[16,64,128]{2,1,0:T(8,128)(2,1)S(1)} collective-permute-done((bf16[16,64,128]{2,1,0:T(8,128)(2,1)S(1)}, bf16[16,64,128]{2,1,0:T(8,128)(2,1)S(1)}, u32[]{:S(2)}, u32[]{:S(2)}) %collective-permute-start.6) | collective-permute-done | bytes 262176 | tf_op jit(solution)/shard_map/ppermute | solution.py:205
  53.9 3.7 %collective-permute-start.10 = (bf16[4,64,128]{2,1,0:T(8,128)(2,1)S(1)}, bf16[4,64,128]{2,1,0:T(8,128)(2,1)S(1)}, u32[]{:S(2)}, u32[]{:S(2)}) collective-permute-start(bf16[4,64,128]{2,1,0:T(8,128)(2,1)S(1)} %get-tuple-element.34), channel_id=1, source_target_pairs={{0,17},{1,16},{8,25},{9,24},{16,1},{17,0},{24,9},{25,8},{2,19},{3,... | collective-permute-start | bytes 196616 | tf_op jit(solution)/shard_map/ppermute | solution.py:205
  57.6 0.5 collective-permute-start.8
  58.2 0.2 collective-permute-start.9
  58.4 3.1 %collective-permute-done.10.both_ref = bf16[4,64,128]{2,1,0:T(8,128)(2,1)S(1)} collective-permute-done((bf16[4,64,128]{2,1,0:T(8,128)(2,1)S(1)}, bf16[4,64,128]{2,1,0:T(8,128)(2,1)S(1)}, u32[]{:S(2)}, u32[]{:S(2)}) %collective-permute-start.10) | collective-permute-done | bytes 65568 | tf_op jit(solution)/shard_map/ppermute | solution.py:205
  61.5 0.7 %collective-permute-done.8.swapped_ref = bf16[4,64,128]{2,1,0:T(8,128)(2,1)S(1)} collective-permute-done((bf16[4,64,128]{2,1,0:T(8,128)(2,1)S(1)}, bf16[4,64,128]{2,1,0:T(8,128)(2,1)S(1)}, u32[]{:S(2)}, u32[]{:S(2)}) %collective-permute-start.8) | collective-permute-done | bytes 65568 | tf_op jit(solution)/shard_map/ppermute | solution.py:205
  62.2 1.4 %collective-permute-done.9.above_ref = bf16[4,64,128]{2,1,0:T(8,128)(2,1)S(1)} collective-permute-done((bf16[4,64,128]{2,1,0:T(8,128)(2,1)S(1)}, bf16[4,64,128]{2,1,0:T(8,128)(2,1)S(1)}, u32[]{:S(2)}, u32[]{:S(2)}) %collective-permute-start.9) | collective-permute-done | bytes 65568 | tf_op jit(solution)/shard_map/ppermute | solution.py:205
  63.6 0.8 %shard_map.36 = f32[8,64,128]{2,1,0:T(8,128)} custom-call(f32[4,64,128]{2,1,0:T(8,128)S(1)} %get-tuple-element.31.own_ref, bf16[4,64,128]{2,1,0:T(8,128)(2,1)S(1)} %collective-permute-done.8.swapped_ref, bf16[4,64,128]{2,1,0:T(8,128)(2,1)S(1)} %collective-permute-done.9.above_ref, bf16[4,64,128]{2,1,0:T(8,128)(2,1)S(1)} %collective-permute-done.10.both_ref), custom_call_target="tpu_custom_call" | custom-call | flops 1 | bytes 1024 | tf_op jit(solution)/shard_map/pallas_call | solution.py:304
  (21 shorter events, 0.9 us)
Async XLA Ops:
  0.0 17.2 %copy-start = (f32[16,128]{1,0:T(8,128)S(1)}, f32[16,128]{1,0:T(8,128)}, u32[]{:S(2)}) copy-start(f32[16,128]{1,0:T(8,128)} %refs_3_.5) | copy-start | bytes 24580
  1.4 15.8 %collective-permute-start.1 = (bf16[8,3,64,128]{3,2,1,0:T(8,128)(2,1)S(1)}, bf16[8,3,64,128]{3,2,1,0:T(8,128)(2,1)S(1)}, u32[]{:S(2)}, u32[]{:S(2)}) collective-permute-start(bf16[8,3,64,128]{3,2,1,0:T(8,128)(2,1)S(1)} %slice.61.refs_0_), channel_id=1, source_target_pairs={{0,1},{1,0},{2,3},{3,2},{4,5},{5,4},{6,7},{7,6},{8,9},{9,8},{10,11... | collective-permute-start | bytes 1179656 | tf_op jit(solution)/shard_map/ppermute | solution.py:205
  11.1 16.7 %collective-permute-start.2 = (bf16[1,3,64,128]{3,2,1,0:T(8,128)(2,1)S(1)}, bf16[1,3,64,128]{3,2,1,0:T(8,128)(2,1)S(1)}, u32[]{:S(2)}, u32[]{:S(2)}) collective-permute-start(bf16[1,3,64,128]{3,2,1,0:T(8,128)(2,1)S(1)} %get-tuple-element.23), channel_id=1, source_target_pairs={{0,8},{8,16},{16,24},{1,9},{9,17},{17,25},{2,10},{10,18},{18,26},{... | collective-permute-start | bytes 147464 | tf_op jit(solution)/shard_map/ppermute | solution.py:331
  14.6 13.2 %collective-permute-start.3 = (bf16[1,3,64,128]{3,2,1,0:T(8,128)(2,1)S(1)}, bf16[1,3,64,128]{3,2,1,0:T(8,128)(2,1)S(1)}, u32[]{:S(2)}, u32[]{:S(2)}) collective-permute-start(bf16[1,3,64,128]{3,2,1,0:T(8,128)(2,1)S(1)} %get-tuple-element.24), channel_id=1, source_target_pairs={{8,0},{16,8},{24,16},{9,1},{17,9},{25,17},{10,2},{18,10},{26,18},{... | collective-permute-start | bytes 147464 | tf_op jit(solution)/shard_map/ppermute | solution.py:332
  15.9 12.7 %collective-permute-start = (bf16[8,3,64,128]{3,2,1,0:T(8,128)(2,1)S(1)}, bf16[8,3,64,128]{3,2,1,0:T(8,128)(2,1)S(1)}, u32[]{:S(2)}, u32[]{:S(2)}) collective-permute-start(bf16[8,3,64,128]{3,2,1,0:T(8,128)(2,1)S(1)} %pad_maximum_fusion.refs_0_), channel_id=1, source_target_pairs={{0,1},{1,0},{2,3},{3,2},{4,5},{5,4},{6,7},{7,6},{8,9},{9,8},{10,11... | collective-permute-start | bytes 1179656 | tf_op jit(solution)/shard_map/ppermute | solution.py:205
  34.2 3.0 %collective-permute-start.4 = (bf16[64,64,128]{2,1,0:T(8,128)(2,1)S(1)}, bf16[64,64,128]{2,1,0:T(8,128)(2,1)S(1)}, u32[]{:S(2)}, u32[]{:S(2)}) collective-permute-start(bf16[64,64,128]{2,1,0:T(8,128)(2,1)S(1)} %shard_map.31), channel_id=1, source_target_pairs={{0,2},{2,0},{4,6},{6,4},{1,3},{3,1},{5,7},{7,5},{8,10},{10,8},{12,... | collective-permute-start | bytes 3145736 | tf_op jit(solution)/shard_map/ppermute | solution.py:205
  37.4 10.7 %collective-permute-start.5 = (bf16[16,64,128]{2,1,0:T(8,128)(2,1)S(1)}, bf16[16,64,128]{2,1,0:T(8,128)(2,1)S(1)}, u32[]{:S(2)}, u32[]{:S(2)}) collective-permute-start(bf16[16,64,128]{2,1,0:T(8,128)(2,1)S(1)} %get-tuple-element.29), channel_id=1, source_target_pairs={{0,12},{2,14},{4,8},{6,10},{8,4},{10,6},{12,0},{14,2},{16,28},{18,... | collective-permute-start | bytes 786440 | tf_op jit(solution)/shard_map/ppermute | solution.py:205
  41.0 12.6 %collective-permute-start.6 = (bf16[16,64,128]{2,1,0:T(8,128)(2,1)S(1)}, bf16[16,64,128]{2,1,0:T(8,128)(2,1)S(1)}, u32[]{:S(2)}, u32[]{:S(2)}) collective-permute-start(bf16[16,64,128]{2,1,0:T(8,128)(2,1)S(1)} %get-tuple-element.30), channel_id=1, source_target_pairs={{0,4},{2,6},{4,0},{6,2},{1,5},{3,7},{5,1},{7,3},{8,12},{10,14},{12... | collective-permute-start | bytes 786440 | tf_op jit(solution)/shard_map/ppermute | solution.py:205
  44.5 9.2 %collective-permute-start.7 = (bf16[16,64,128]{2,1,0:T(8,128)(2,1)S(1)}, bf16[16,64,128]{2,1,0:T(8,128)(2,1)S(1)}, u32[]{:S(2)}, u32[]{:S(2)}) collective-permute-start(bf16[16,64,128]{2,1,0:T(8,128)(2,1)S(1)} %fusion), channel_id=1, source_target_pairs={{0,8},{8,0},{16,24},{24,16},{1,9},{9,1},{17,25},{25,17},{2,10},{10... | collective-permute-start | bytes 786440 | tf_op jit(solution)/shard_map/ppermute | solution.py:205
  53.9 7.6 %collective-permute-start.10 = (bf16[4,64,128]{2,1,0:T(8,128)(2,1)S(1)}, bf16[4,64,128]{2,1,0:T(8,128)(2,1)S(1)}, u32[]{:S(2)}, u32[]{:S(2)}) collective-permute-start(bf16[4,64,128]{2,1,0:T(8,128)(2,1)S(1)} %get-tuple-element.34), channel_id=1, source_target_pairs={{0,17},{1,16},{8,25},{9,24},{16,1},{17,0},{24,9},{25,8},{2,19},{3,... | collective-permute-start | bytes 196616 | tf_op jit(solution)/shard_map/ppermute | solution.py:205
  57.6 4.5 %collective-permute-start.8 = (bf16[4,64,128]{2,1,0:T(8,128)(2,1)S(1)}, bf16[4,64,128]{2,1,0:T(8,128)(2,1)S(1)}, u32[]{:S(2)}, u32[]{:S(2)}) collective-permute-start(bf16[4,64,128]{2,1,0:T(8,128)(2,1)S(1)} %get-tuple-element.32), channel_id=1, source_target_pairs={{0,1},{1,0},{2,3},{3,2},{4,5},{5,4},{6,7},{7,6},{8,9},{9,8},{10,11... | collective-permute-start | bytes 196616 | tf_op jit(solution)/shard_map/ppermute | solution.py:205
  58.2 5.4 %collective-permute-start.9 = (bf16[4,64,128]{2,1,0:T(8,128)(2,1)S(1)}, bf16[4,64,128]{2,1,0:T(8,128)(2,1)S(1)}, u32[]{:S(2)}, u32[]{:S(2)}) collective-permute-start(bf16[4,64,128]{2,1,0:T(8,128)(2,1)S(1)} %get-tuple-element.33), channel_id=1, source_target_pairs={{0,16},{8,24},{16,0},{24,8},{1,17},{9,25},{17,1},{25,9},{2,18},{10... | collective-permute-start | bytes 196616 | tf_op jit(solution)/shard_map/ppermute | solution.py:205

commit v9 on v8

--- a/solution.py
+++ b/solution.py
@@ -46,12 +46,17 @@
         return jnp.where(inside, values, jnp.zeros_like(values)).T
 
     before, after = edge(-1), edge(1)
-    above_ref, below_ref = refs[:2] if len(refs) > 1 else (None, None)
+    here = lax.axis_index("gx")
+
+    def outside(ref, edge_of_grid, a):
+        values = ref[0, a].astype(F32)
+        return jnp.where(here == edge_of_grid, jnp.zeros_like(values), values)
+
     lane = lax.broadcasted_iota(jnp.int32, (share, cells), 1)
     for place, x in enumerate(rows):
         for a in range(3):
-            down = (above_ref[0, a] if x == 0 else own_ref[x - 1, a]).astype(F32)
-            up = (below_ref[0, a] if x == last else own_ref[x + 1, a]).astype(F32)
+            down = outside(refs[0], 0, a) if x == 0 else own_ref[x - 1, a].astype(F32)
+            up = outside(refs[1], lax.axis_size("gx") - 1, a) if x == last else own_ref[x + 1, a].astype(F32)
             out_ref[place, a] = ((up - down) * 0.5).astype(BF16)
             value = own_ref[x, a].astype(F32)
             column = 3 * x + a
@@ -76,7 +81,7 @@
     return left[0] * right[0] + left[1] * right[1] + left[2] * right[2]
 
 
-def tensor_kernel(*refs, bits, block, rows_each, first_block, stride, rows, scale, parts, outputs):
+def tensor_kernel(*refs, bits, block, rows_each, blocks, rows, scale, parts, outputs):
     own_ref, other_ref, slope_ref, volume_ref = refs[:4]
     left, right = refs[-2:]
     out_refs = refs[-2 - outputs : -2]
@@ -99,7 +104,7 @@
 
     here = (lax.axis_index("gx") * lax.axis_size("gy") + lax.axis_index("gy")) * rows_each
     start = here ^ (lax.axis_index("ma") << top)
-    position = (first_block + stride * step) * block
+    position = block_at(blocks, step) * block
     for place, bit in enumerate(bits):
         start = start ^ (((position >> place) & 1) << bit)
     columns = []
@@ -134,11 +139,22 @@
                 out_ref[...] = product.astype(out_ref.dtype)
 
 
-def partial_tensor(own, other, slopes, volumes, rows, sizes, blocks, before=None, dtypes=(F32,), parts=(0, 1)):
+def block_at(blocks, step):
+    block = blocks[0] + step
+    for n in range(1, len(blocks)):
+        jump = blocks[n] - blocks[n - 1] - 1
+        if jump:
+            block = block + jnp.where(step >= n, jump, 0)
+    return block
+
+
+def partial_tensor(
+    own, other, slopes, volumes, rows, sizes, blocks, before=None, first=0, dtypes=(F32,), cost=8
+):
     row_count, _, share, cells = own.shape
     modes = 2 * share
     block = modes // BLOCKS
-    stride = blocks[1] - blocks[0] if len(blocks) > 1 else 1
+    parts = (0, 1)
     outputs = len(dtypes)
     devices = sizes["gx"] * sizes["gy"]
     rows_each = modes // devices
@@ -147,8 +163,7 @@
         bits=source_bits(sizes, rows_each),
         block=block,
         rows_each=rows_each,
-        first_block=blocks[0],
-        stride=stride,
+        blocks=blocks,
         outputs=outputs,
         rows=rows,
         parts=parts,
@@ -160,12 +175,12 @@
     in_specs = [whole(array) for array in operands]
     if before is not None:
         operands.append(before)
-        in_specs.append(pl.BlockSpec(shape, lambda g: (blocks[0] + stride * g, 0, 0)))
+        in_specs.append(pl.BlockSpec(shape, lambda g: (first + g, 0, 0)))
     if outputs > 1:
         out_shape = [jax.ShapeDtypeStruct(shape, dtype) for dtype in dtypes]
         out_specs = [pl.BlockSpec(shape, lambda g: (0, 0, 0))] * outputs
     else:
-        out_shape = (pltpu.VMEM if len(blocks) == BLOCKS else jax.ShapeDtypeStruct)(
+        out_shape = (pltpu.VMEM if before is None else jax.ShapeDtypeStruct)(
             (len(blocks) * block, share, modes), dtypes[0]
         )
         out_specs = pl.BlockSpec(shape, lambda g: (g, 0, 0))
@@ -181,15 +196,14 @@
         ],
         compiler_params=pltpu.CompilerParams(vmem_limit_bytes=20 << 20),
         cost_estimate=pl.CostEstimate(
-            flops=4 * len(parts) * len(blocks) * block * share * modes * row_count * cells, bytes_accessed=4 << 20, transcendentals=0
+            flops=cost * len(blocks) * block * share * modes * row_count * cells, bytes_accessed=4 << 20, transcendentals=0
         ),
     )(*operands)
 
 
-def neighbours(axis):
+def ring(axis):
     count = lax.axis_size(axis)
-    forward = [(i, i + 1) for i in range(count - 1)]
-    return forward, [(target, source) for source, target in forward]
+    return [(i, (i + 1) % count) for i in range(count)], [((i + 1) % count, i) for i in range(count)]
 
 
 def flip(array, flips, sizes):
@@ -327,40 +341,34 @@
     columns = jnp.stack([own[:, :, :, -1], own[:, :, :, 0]]).reshape(2, 3 * row_count, share)
     columns = lax.all_gather(columns, "gy")
     own_outer_held, edges, columns = barrier((own_outer, (own[-1:], own[:1]), columns))
-    forward, backward = neighbours("gx")
+    forward, backward = ring("gx")
     above = lax.ppermute(edges[0], "gx", forward)
     below = lax.ppermute(edges[1], "gx", backward)
     other_outer = flip(own_outer_held, [("ma", 0)], sizes)
 
-    so_far = partial_tensor(
-        own_inner,
-        other_inner,
-        slopes_of(own, inner_rows, columns),
-        cell_volumes,
-        inner_rows,
-        sizes,
-        range(BLOCKS),
+    inner = functools.partial(
+        partial_tensor, own_inner, other_inner, slopes_of(own, inner_rows, columns), rows=inner_rows, sizes=sizes
     )
+    so_far = inner(cell_volumes, blocks=(1, 2, 3, 5, 6, 7))
     columns, so_far = barrier((columns, so_far))
     slopes_outer = slopes_of(own, outer_rows, columns, above, below)
     outer = functools.partial(
-        partial_tensor, own_outer, other_outer, slopes_outer, rows=outer_rows, sizes=sizes, before=so_far
+        partial_tensor, own_outer, other_outer, slopes_outer, rows=outer_rows, sizes=sizes
     )
     stages = stages_of(sizes)
     count = modes // BLOCKS
     cell_count = mode_fields.shape[2] * mode_fields.shape[3]
-    sent = outer(cell_volumes, blocks=(4, 5, 6, 7), dtypes=(BF16,))
+    sent = outer(cell_volumes, blocks=(5, 6, 7), before=so_far, first=3, dtypes=(BF16,))
     cell_volumes, sent = barrier((cell_volumes, sent))
     arrived = flip(sent, stages[0], sizes)
-    upper = outer(cell_volumes, blocks=(2, 3))
-    upper_terms = [upper, arrived[2 * count :]]
-    sent = [term_sum(upper_terms, at * count, (at + 1) * count).astype(BF16) for at in range(2)]
+    kept = outer(cell_volumes, blocks=(1, 2, 3), before=so_far)
+    sent = [term_sum([kept, arrived], at * count, (at + 1) * count).astype(BF16) for at in range(3)]
     cell_volumes, sent = barrier((cell_volumes, sent))
-    lower = outer(cell_volumes, blocks=(0, 1))
-    sent = [term_sum([lower, arrived], count, 2 * count).astype(BF16)] + sent
     received = exchange(stages[1], sent[::-1], sizes)
-    cost = 16 * count * modes * share * cell_count
-    terms = [summed([lower, arrived] + received[:2], count, cost), received[2]]
+    so_far = inner(cell_volumes, blocks=(4, 0), cost=1)
+    sent, kept = outer(cell_volumes, blocks=(4, 0), before=so_far, dtypes=(BF16, F32), cost=1)
+    arrived = flip(sent, stages[0], sizes)
+    terms = [summed(received, count, 16 * count * modes * share * cell_count), kept, arrived]
     for stage in stages[2:-1]:
         terms = terms + exchange(stage, sends(terms, count, stage), sizes)
         count = count >> len(stage)

time: 64.6 us -> 61.6 us (0.954)
  starting transfers between devices: 17.2 us -> 15.4 us
  waiting for transfers between devices: 14.2 us -> 12.6 us
    ppermute x1, starting transfers between devices: 3.48 us -> 1.63 us  [shards(): above = lax.ppermute(edges[0], 'gx', forward)]
    ppermute x9 -> x10, waiting for transfers between devices: 14.1 us -> 12.6 us  [flip(): return lax.ppermute(array, axes, [(i, i ^ change) for i in range(count)])]
    ppermute x1, starting transfers between devices: 1.29 us -> 2.25 us  [shards(): below = lax.ppermute(edges[1], 'gx', backward)]
    ppermute x9 -> x10, starting transfers between devices: 12.4 us -> 11.5 us  [flip(): return lax.ppermute(array, axes, [(i, i ^ change) for i in range(count)])]
    pallas_call x4 -> x5, Pallas kernels: 22 us -> 22.5 us  [partial_tensor(): pl.pallas_call(body, grid=(len(blocks),), out_shape=out_shape, in_specs=i...]
  transfers between devices with their start and end apart: 11 -> 12, of which waited for: 5 -> 6; matrix products, arithmetic and copies ran while one was open for 2% -> 2% of each run, Pallas kernels for 28% -> 32%
where the time goes in v9:
time: 61.6 us; the launch traced here: 61.4 us
  Pallas kernels  25 us (41%)
  starting transfers between devices  15.4 us (25%)
  waiting for transfers between devices  12.6 us (20%)
  blocking collectives  5.34 us (9%)
  local copies, waits for them, and re-layouts  2.63 us (4%)
    pallas_call x5, Pallas kernels, partial_tensor(): pl.pallas_call(body, grid=(len(blocks),), out_shape=out_shape, in_specs=i...  22.5 us
    ppermute x10, waiting for transfers between devices, flip(): return lax.ppermute(array, axes, [(i, i ^ change) for i in range(count)])  12.6 us
    ppermute x10, starting transfers between devices, flip(): return lax.ppermute(array, axes, [(i, i ^ change) for i in range(count)])  11.5 us
    all_gather x1, blocking collectives, shards(): columns = lax.all_gather(columns, 'gy')  5.34 us
    ppermute x1, starting transfers between devices, shards(): below = lax.ppermute(edges[1], 'gx', backward)  2.25 us
    ppermute x1, starting transfers between devices, shards(): above = lax.ppermute(edges[0], 'gx', forward)  1.63 us
    pallas_call x2, Pallas kernels, slopes_of(): pl.pallas_call(functools.partial(slopes_kernel, rows=rows), out_shape=jax...  1.4 us
    unnamed x3, local copies, waits for them, and re-layouts  1.34 us
  transfers between devices with their start and end apart: 12, of which 6 were waited for; matrix products, arithmetic and copies ran while one was open for 2% of the time, Pallas kernels for 32%

profile of v9, /device:TPU:0, one launch (start us, length us, event | category | flops | bytes accessed | tf_op | source)
XLA Modules:
  0.0 61.4 jit_solution(13745751799834848347)
XLA Ops:
  0.0 1.3 %copy.7 = bf16[3,64,16,128]{3,1,0,2:T(8,128)(2,1)S(1)} copy(bf16[3,64,16,128]{3,2,1,0:T(8,128)(2,1)} %param.2) | data formatting | bytes 1572864 | tf_op args[0]
  1.4 3.0 %collective-permute-start.1 = (bf16[8,3,64,128]{3,2,1,0:T(8,128)(2,1)S(1)}, bf16[8,3,64,128]{3,2,1,0:T(8,128)(2,1)S(1)}, u32[]{:S(2)}, u32[]{:S(2)}) collective-permute-start(bf16[8,3,64,128]{3,2,1,0:T(8,128)(2,1)S(1)} %slice.58.refs_0_), channel_id=1, source_target_pairs={{0,1},{1,0},{2,3},{3,2},{4,5},{5,4},{6,7},{7,6},{8,9},{9,8},{10,11... | collective-permute-start | bytes 1179656 | tf_op jit(solution)/shard_map/ppermute | solution.py:219
  4.4 1.2 %slice_reduce_fusion.1 = (bf16[16,3,64]{2,1,0:T(4,128)(2,1)S(1)}, bf16[16,3,64]{2,1,0:T(4,128)(2,1)S(1)}) fusion(bf16[16,3,64,128]{3,2,1,0:T(8,128)(2,1)S(1)} %bitcast.4), kind=kLoop, calls=%fused_computation.1 | loop fusion | bytes 24576 | tf_op jit(solution)/shard_map/slice | solution.py:341
  5.7 5.3 %all_gather.3.columns_ref = bf16[4,2,48,64]{3,2,1,0:T(8,128)(2,1)S(1)} all-gather(bf16[1,2,48,64]{3,2,1,0:T(8,128)(2,1)S(1)} %pad_maximum_fusion.1), channel_id=1, replica_groups=mesh['gx'=4,'gy'=4,'ma'=2] {'gy'}, dimensions={0}, use_global_device_ids=true | all-gather | bytes 61440 | tf_op jit(solution)/shard_map/all_gather | solution.py:342
  11.1 1.6 %collective-permute-start.2 = (bf16[1,3,64,128]{3,2,1,0:T(8,128)(2,1)S(1)}, bf16[1,3,64,128]{3,2,1,0:T(8,128)(2,1)S(1)}, u32[]{:S(2)}, u32[]{:S(2)}) collective-permute-start(bf16[1,3,64,128]{3,2,1,0:T(8,128)(2,1)S(1)} %get-tuple-element.26), channel_id=1, source_target_pairs={{0,8},{8,16},{16,24},{24,0},{1,9},{9,17},{17,25},{25,1},{2,10},{10... | collective-permute-start | bytes 147464 | tf_op jit(solution)/shard_map/ppermute | solution.py:345
  12.7 2.2 %collective-permute-start.3 = (bf16[1,3,64,128]{3,2,1,0:T(8,128)(2,1)S(1)}, bf16[1,3,64,128]{3,2,1,0:T(8,128)(2,1)S(1)}, u32[]{:S(2)}, u32[]{:S(2)}) collective-permute-start(bf16[1,3,64,128]{3,2,1,0:T(8,128)(2,1)S(1)} %get-tuple-element.27), channel_id=1, source_target_pairs={{8,0},{16,8},{24,16},{0,24},{9,1},{17,9},{25,17},{1,25},{10,2},{18... | collective-permute-start | bytes 147464 | tf_op jit(solution)/shard_map/ppermute | solution.py:346
  15.3 0.7 %shard_map.28.refs_2_ = bf16[8,6,64,128]{3,2,1,0:T(8,128)(2,1)S(1)} custom-call(bf16[16,3,64,128]{3,2,1,0:T(8,128)(2,1)S(1)} %bitcast.7, bf16[4,2,48,64]{3,2,1,0:T(8,128)(2,1)S(1)} %all_gather.3.columns_ref), custom_call_target="tpu_custom_call" | custom-call | flops 1 | bytes 1024 | tf_op jit(solution)/shard_map/pallas_call | solution.py:70
  16.1 8.0 %shard_map.29.refs_4_ = f32[96,64,128]{2,1,0:T(8,128)S(1)} custom-call(bf16[8,3,64,128]{3,2,1,0:T(8,128)(2,1)S(1)} %slice.58.refs_0_, bf16[8,3,64,128]{3,2,1,0:T(8,128)(2,1)S(1)} %collective-permute-done.1.refs_1_, bf16[8,6,64,128]{3,2,1,0:T(8,128)(2,1)S(1)} %shard_map.28.refs_2_, f32[16,128]{1,0:T(8,128)S(1)} %copy-done), custom_call_target="tpu_custom_call" | custom-call | flops 6442450944 | bytes 4194304 | tf_op jit(solution)/shard_map/pallas_call | solution.py:187
  24.1 0.7 %shard_map.30.refs_2_ = bf16[8,6,64,128]{3,2,1,0:T(8,128)(2,1)S(1)} custom-call(bf16[16,3,64,128]{3,2,1,0:T(8,128)(2,1)S(1)} %bitcast.8, bf16[4,2,48,64]{3,2,1,0:T(8,128)(2,1)S(1)} %all_gather.3.columns_ref, bf16[1,3,64,128]{3,2,1,0:T(8,128)(2,1)S(1)} %collective-permute-done.2.refs_0_, bf16[1,3,64,128]{3,2,1,0:T(8,128)(2,1)S(1)} %collective-permute-done.3.refs_1_), custom_call_target="tpu_custom_call" | custom-call | flops 1 | bytes 1024 | tf_op jit(solution)/shard_map/pallas_call | solution.py:70
  24.8 1.0 %collective-permute-done.refs_1_ = bf16[8,3,64,128]{3,2,1,0:T(8,128)(2,1)S(1)} collective-permute-done((bf16[8,3,64,128]{3,2,1,0:T(8,128)(2,1)S(1)}, bf16[8,3,64,128]{3,2,1,0:T(8,128)(2,1)S(1)}, u32[]{:S(2)}, u32[]{:S(2)}) %collective-permute-start) | collective-permute-done | bytes 393248 | tf_op jit(solution)/shard_map/ppermute | solution.py:219
  25.9 4.3 %shard_map.31 = bf16[48,64,128]{2,1,0:T(8,128)(2,1)S(1)} custom-call(bf16[8,3,64,128]{3,2,1,0:T(8,128)(2,1)S(1)} %pad_maximum_fusion.refs_0_, bf16[8,3,64,128]{3,2,1,0:T(8,128)(2,1)S(1)} %collective-permute-done.refs_1_, bf16[8,6,64,128]{3,2,1,0:T(8,128)(2,1)S(1)} %shard_map.30.refs_2_, f32[16,128]{1,0:T(8,128)S(1)} %copy-done, ...), custom_call_target="tpu_custom_call" | custom-call | flops 3221225472 | bytes 4194304 | tf_op jit(solution)/shard_map/pallas_call | solution.py:187
  30.3 4.3 %shard_map.32 = f32[48,64,128]{2,1,0:T(8,128)S(1)} custom-call(bf16[8,3,64,128]{3,2,1,0:T(8,128)(2,1)S(1)} %pad_maximum_fusion.refs_0_, bf16[8,3,64,128]{3,2,1,0:T(8,128)(2,1)S(1)} %collective-permute-done.refs_1_, bf16[8,6,64,128]{3,2,1,0:T(8,128)(2,1)S(1)} %shard_map.30.refs_2_, f32[16,128]{1,0:T(8,128)S(1)} %copy-done, f32[96,64,128]{2,1,0:T(8,128)S(1)} %shard_map.29.refs_4_), custom_call_target="tpu_custom_call" | custom-call | flops 3221225472 | bytes 4194304 | tf_op jit(solution)/shard_map/pallas_call | solution.py:187
  35.5 1.0 %collective-permute-start.6 = (bf16[16,64,128]{2,1,0:T(8,128)(2,1)S(1)}, bf16[16,64,128]{2,1,0:T(8,128)(2,1)S(1)}, u32[]{:S(2)}, u32[]{:S(2)}) collective-permute-start(bf16[16,64,128]{2,1,0:T(8,128)(2,1)S(1)} %get-tuple-element.32), channel_id=1, source_target_pairs={{0,4},{2,6},{4,0},{6,2},{1,5},{3,7},{5,1},{7,3},{8,12},{10,14},{12... | collective-permute-start | bytes 786440 | tf_op jit(solution)/shard_map/ppermute | solution.py:219
  36.4 1.9 %collective-permute-start.7 = (bf16[16,64,128]{2,1,0:T(8,128)(2,1)S(1)}, bf16[16,64,128]{2,1,0:T(8,128)(2,1)S(1)}, u32[]{:S(2)}, u32[]{:S(2)}) collective-permute-start(bf16[16,64,128]{2,1,0:T(8,128)(2,1)S(1)} %get-tuple-element.33), channel_id=1, source_target_pairs={{0,8},{8,0},{16,24},{24,16},{1,9},{9,1},{17,25},{25,17},{2,10},{10... | collective-permute-start | bytes 786440 | tf_op jit(solution)/shard_map/ppermute | solution.py:219
  38.4 2.8 %shard_map.34.refs_4_ = f32[32,64,128]{2,1,0:T(8,128)S(1)} custom-call(bf16[8,3,64,128]{3,2,1,0:T(8,128)(2,1)S(1)} %slice.58.refs_0_, bf16[8,3,64,128]{3,2,1,0:T(8,128)(2,1)S(1)} %collective-permute-done.1.refs_1_, bf16[8,6,64,128]{3,2,1,0:T(8,128)(2,1)S(1)} %shard_map.28.refs_2_, f32[16,128]{1,0:T(8,128)S(1)} %copy-done), custom_call_target="tpu_custom_call" | custom-call | flops 268435456 | bytes 4194304 | tf_op jit(solution)/shard_map/pallas_call | solution.py:187
  41.2 3.0 %shard_map.35 = (bf16[16,64,128]{2,1,0:T(8,128)(2,1)S(1)}, f32[16,64,128]{2,1,0:T(8,128)S(1)}) custom-call(bf16[8,3,64,128]{3,2,1,0:T(8,128)(2,1)S(1)} %pad_maximum_fusion.refs_0_, bf16[8,3,64,128]{3,2,1,0:T(8,128)(2,1)S(1)} %collective-permute-done.refs_1_, bf16[8,6,64,128]{3,2,1,0:T(8,128)(2,1)S(1)} %shard_map.30.refs_2_, f32[16,128]{1,0:T(8,128)S(1)} %copy-done, ...), custom_call_target="tpu_custom_call" | custom-call | flops 268435456 | bytes 4194304 | tf_op jit(solution)/shard_map/pallas_call | solution.py:187
  44.9 4.6 %collective-permute-done.6.refs_1_ = bf16[16,64,128]{2,1,0:T(8,128)(2,1)S(1)} collective-permute-done((bf16[16,64,128]{2,1,0:T(8,128)(2,1)S(1)}, bf16[16,64,128]{2,1,0:T(8,128)(2,1)S(1)}, u32[]{:S(2)}, u32[]{:S(2)}) %collective-permute-start.6) | collective-permute-done | bytes 262176 | tf_op jit(solution)/shard_map/ppermute | solution.py:219
  49.5 0.7 %collective-permute-done.7.refs_2_ = bf16[16,64,128]{2,1,0:T(8,128)(2,1)S(1)} collective-permute-done((bf16[16,64,128]{2,1,0:T(8,128)(2,1)S(1)}, bf16[16,64,128]{2,1,0:T(8,128)(2,1)S(1)}, u32[]{:S(2)}, u32[]{:S(2)}) %collective-permute-start.7) | collective-permute-done | bytes 262176 | tf_op jit(solution)/shard_map/ppermute | solution.py:219
  50.5 0.7 %collective-permute-start.9 = (bf16[4,64,128]{2,1,0:T(8,128)(2,1)S(1)}, bf16[4,64,128]{2,1,0:T(8,128)(2,1)S(1)}, u32[]{:S(2)}, u32[]{:S(2)}) collective-permute-start(bf16[4,64,128]{2,1,0:T(8,128)(2,1)S(1)} %get-tuple-element.38), channel_id=1, source_target_pairs={{0,1},{1,0},{2,3},{3,2},{4,5},{5,4},{6,7},{7,6},{8,9},{9,8},{10,11... | collective-permute-start | bytes 196616 | tf_op jit(solution)/shard_map/ppermute | solution.py:219
  51.2 0.8 %collective-permute-start.10 = (bf16[4,64,128]{2,1,0:T(8,128)(2,1)S(1)}, bf16[4,64,128]{2,1,0:T(8,128)(2,1)S(1)}, u32[]{:S(2)}, u32[]{:S(2)}) collective-permute-start(bf16[4,64,128]{2,1,0:T(8,128)(2,1)S(1)} %get-tuple-element.39), channel_id=1, source_target_pairs={{0,16},{8,24},{16,0},{24,8},{1,17},{9,25},{17,1},{25,9},{2,18},{10... | collective-permute-start | bytes 196616 | tf_op jit(solution)/shard_map/ppermute | solution.py:219
  52.0 3.0 %collective-permute-start.11 = (bf16[4,64,128]{2,1,0:T(8,128)(2,1)S(1)}, bf16[4,64,128]{2,1,0:T(8,128)(2,1)S(1)}, u32[]{:S(2)}, u32[]{:S(2)}) collective-permute-start(bf16[4,64,128]{2,1,0:T(8,128)(2,1)S(1)} %get-tuple-element.40), channel_id=1, source_target_pairs={{0,17},{1,16},{8,25},{9,24},{16,1},{17,0},{24,9},{25,8},{2,19},{3,... | collective-permute-start | bytes 196616 | tf_op jit(solution)/shard_map/ppermute | solution.py:219
  55.0 3.2 %collective-permute-done.10.above_ref = bf16[4,64,128]{2,1,0:T(8,128)(2,1)S(1)} collective-permute-done((bf16[4,64,128]{2,1,0:T(8,128)(2,1)S(1)}, bf16[4,64,128]{2,1,0:T(8,128)(2,1)S(1)}, u32[]{:S(2)}, u32[]{:S(2)}) %collective-permute-start.10) | collective-permute-done | bytes 65568 | tf_op jit(solution)/shard_map/ppermute | solution.py:219
  58.2 2.4 %collective-permute-done.11.both_ref = bf16[4,64,128]{2,1,0:T(8,128)(2,1)S(1)} collective-permute-done((bf16[4,64,128]{2,1,0:T(8,128)(2,1)S(1)}, bf16[4,64,128]{2,1,0:T(8,128)(2,1)S(1)}, u32[]{:S(2)}, u32[]{:S(2)}) %collective-permute-start.11) | collective-permute-done | bytes 65568 | tf_op jit(solution)/shard_map/ppermute | solution.py:219
  60.6 0.8 %shard_map.37 = f32[8,64,128]{2,1,0:T(8,128)} custom-call(f32[4,64,128]{2,1,0:T(8,128)S(1)} %get-tuple-element.37.own_ref, bf16[4,64,128]{2,1,0:T(8,128)(2,1)S(1)} %collective-permute-done.9.swapped_ref, bf16[4,64,128]{2,1,0:T(8,128)(2,1)S(1)} %collective-permute-done.10.above_ref, bf16[4,64,128]{2,1,0:T(8,128)(2,1)S(1)} %collective-permute-done.11.both_ref), custom_call_target="tpu_custom_call" | custom-call | flops 1 | bytes 1024 | tf_op jit(solution)/shard_map/pallas_call | solution.py:318
  (23 shorter events, 2.5 us)
Async XLA Ops:
  1.4 14.7 %collective-permute-start.1 = (bf16[8,3,64,128]{3,2,1,0:T(8,128)(2,1)S(1)}, bf16[8,3,64,128]{3,2,1,0:T(8,128)(2,1)S(1)}, u32[]{:S(2)}, u32[]{:S(2)}) collective-permute-start(bf16[8,3,64,128]{3,2,1,0:T(8,128)(2,1)S(1)} %slice.58.refs_0_), channel_id=1, source_target_pairs={{0,1},{1,0},{2,3},{3,2},{4,5},{5,4},{6,7},{7,6},{8,9},{9,8},{10,11... | collective-permute-start | bytes 1179656 | tf_op jit(solution)/shard_map/ppermute | solution.py:219
  5.6 10.5 %copy-start = (f32[16,128]{1,0:T(8,128)S(1)}, f32[16,128]{1,0:T(8,128)}, u32[]{:S(2)}) copy-start(f32[16,128]{1,0:T(8,128)} %refs_3_.6) | copy-start | bytes 24580
  11.1 13.0 %collective-permute-start.2 = (bf16[1,3,64,128]{3,2,1,0:T(8,128)(2,1)S(1)}, bf16[1,3,64,128]{3,2,1,0:T(8,128)(2,1)S(1)}, u32[]{:S(2)}, u32[]{:S(2)}) collective-permute-start(bf16[1,3,64,128]{3,2,1,0:T(8,128)(2,1)S(1)} %get-tuple-element.26), channel_id=1, source_target_pairs={{0,8},{8,16},{16,24},{24,0},{1,9},{9,17},{17,25},{25,1},{2,10},{10... | collective-permute-start | bytes 147464 | tf_op jit(solution)/shard_map/ppermute | solution.py:345
  12.7 11.4 %collective-permute-start.3 = (bf16[1,3,64,128]{3,2,1,0:T(8,128)(2,1)S(1)}, bf16[1,3,64,128]{3,2,1,0:T(8,128)(2,1)S(1)}, u32[]{:S(2)}, u32[]{:S(2)}) collective-permute-start(bf16[1,3,64,128]{3,2,1,0:T(8,128)(2,1)S(1)} %get-tuple-element.27), channel_id=1, source_target_pairs={{8,0},{16,8},{24,16},{0,24},{9,1},{17,9},{25,17},{1,25},{10,2},{18... | collective-permute-start | bytes 147464 | tf_op jit(solution)/shard_map/ppermute | solution.py:346
  14.9 10.9 %collective-permute-start = (bf16[8,3,64,128]{3,2,1,0:T(8,128)(2,1)S(1)}, bf16[8,3,64,128]{3,2,1,0:T(8,128)(2,1)S(1)}, u32[]{:S(2)}, u32[]{:S(2)}) collective-permute-start(bf16[8,3,64,128]{3,2,1,0:T(8,128)(2,1)S(1)} %pad_maximum_fusion.refs_0_), channel_id=1, source_target_pairs={{0,1},{1,0},{2,3},{3,2},{4,5},{5,4},{6,7},{7,6},{8,9},{9,8},{10,11... | collective-permute-start | bytes 1179656 | tf_op jit(solution)/shard_map/ppermute | solution.py:219
  30.2 4.4 %collective-permute-start.4 = (bf16[48,64,128]{2,1,0:T(8,128)(2,1)S(1)}, bf16[48,64,128]{2,1,0:T(8,128)(2,1)S(1)}, u32[]{:S(2)}, u32[]{:S(2)}) collective-permute-start(bf16[48,64,128]{2,1,0:T(8,128)(2,1)S(1)} %shard_map.31), channel_id=1, source_target_pairs={{0,2},{2,0},{4,6},{6,4},{1,3},{3,1},{5,7},{7,5},{8,10},{10,8},{12,... | collective-permute-start | bytes 2359304 | tf_op jit(solution)/shard_map/ppermute | solution.py:219
  34.8 10.1 %collective-permute-start.5 = (bf16[16,64,128]{2,1,0:T(8,128)(2,1)S(1)}, bf16[16,64,128]{2,1,0:T(8,128)(2,1)S(1)}, u32[]{:S(2)}, u32[]{:S(2)}) collective-permute-start(bf16[16,64,128]{2,1,0:T(8,128)(2,1)S(1)} %get-tuple-element.31), channel_id=1, source_target_pairs={{0,12},{2,14},{4,8},{6,10},{8,4},{10,6},{12,0},{14,2},{16,28},{18,... | collective-permute-start | bytes 786440 | tf_op jit(solution)/shard_map/ppermute | solution.py:219
  35.5 14.1 %collective-permute-start.6 = (bf16[16,64,128]{2,1,0:T(8,128)(2,1)S(1)}, bf16[16,64,128]{2,1,0:T(8,128)(2,1)S(1)}, u32[]{:S(2)}, u32[]{:S(2)}) collective-permute-start(bf16[16,64,128]{2,1,0:T(8,128)(2,1)S(1)} %get-tuple-element.32), channel_id=1, source_target_pairs={{0,4},{2,6},{4,0},{6,2},{1,5},{3,7},{5,1},{7,3},{8,12},{10,14},{12... | collective-permute-start | bytes 786440 | tf_op jit(solution)/shard_map/ppermute | solution.py:219
  36.4 13.8 %collective-permute-start.7 = (bf16[16,64,128]{2,1,0:T(8,128)(2,1)S(1)}, bf16[16,64,128]{2,1,0:T(8,128)(2,1)S(1)}, u32[]{:S(2)}, u32[]{:S(2)}) collective-permute-start(bf16[16,64,128]{2,1,0:T(8,128)(2,1)S(1)} %get-tuple-element.33), channel_id=1, source_target_pairs={{0,8},{8,0},{16,24},{24,16},{1,9},{9,1},{17,25},{25,17},{2,10},{10... | collective-permute-start | bytes 786440 | tf_op jit(solution)/shard_map/ppermute | solution.py:219
  44.2 6.1 %collective-permute-start.8 = (bf16[16,64,128]{2,1,0:T(8,128)(2,1)S(1)}, bf16[16,64,128]{2,1,0:T(8,128)(2,1)S(1)}, u32[]{:S(2)}, u32[]{:S(2)}) collective-permute-start(bf16[16,64,128]{2,1,0:T(8,128)(2,1)S(1)} %get-tuple-element.36), channel_id=1, source_target_pairs={{0,2},{2,0},{4,6},{6,4},{1,3},{3,1},{5,7},{7,5},{8,10},{10,8},{12,... | collective-permute-start | bytes 786440 | tf_op jit(solution)/shard_map/ppermute | solution.py:219
  50.5 4.5 %collective-permute-start.9 = (bf16[4,64,128]{2,1,0:T(8,128)(2,1)S(1)}, bf16[4,64,128]{2,1,0:T(8,128)(2,1)S(1)}, u32[]{:S(2)}, u32[]{:S(2)}) collective-permute-start(bf16[4,64,128]{2,1,0:T(8,128)(2,1)S(1)} %get-tuple-element.38), channel_id=1, source_target_pairs={{0,1},{1,0},{2,3},{3,2},{4,5},{5,4},{6,7},{7,6},{8,9},{9,8},{10,11... | collective-permute-start | bytes 196616 | tf_op jit(solution)/shard_map/ppermute | solution.py:219
  51.2 7.0 %collective-permute-start.10 = (bf16[4,64,128]{2,1,0:T(8,128)(2,1)S(1)}, bf16[4,64,128]{2,1,0:T(8,128)(2,1)S(1)}, u32[]{:S(2)}, u32[]{:S(2)}) collective-permute-start(bf16[4,64,128]{2,1,0:T(8,128)(2,1)S(1)} %get-tuple-element.39), channel_id=1, source_target_pairs={{0,16},{8,24},{16,0},{24,8},{1,17},{9,25},{17,1},{25,9},{2,18},{10... | collective-permute-start | bytes 196616 | tf_op jit(solution)/shard_map/ppermute | solution.py:219
  52.0 8.6 %collective-permute-start.11 = (bf16[4,64,128]{2,1,0:T(8,128)(2,1)S(1)}, bf16[4,64,128]{2,1,0:T(8,128)(2,1)S(1)}, u32[]{:S(2)}, u32[]{:S(2)}) collective-permute-start(bf16[4,64,128]{2,1,0:T(8,128)(2,1)S(1)} %get-tuple-element.40), channel_id=1, source_target_pairs={{0,17},{1,16},{8,25},{9,24},{16,1},{17,0},{24,9},{25,8},{2,19},{3,... | collective-permute-start | bytes 196616 | tf_op jit(solution)/shard_map/ppermute | solution.py:219

commit v10 on v9

--- a/solution.py
+++ b/solution.py
@@ -264,7 +264,7 @@
                 out[place] = total[swapped * share : (swapped + 1) * share].astype(out.dtype)
 
 
-def assemble_kernel(own_ref, swapped_ref, above_ref, both_ref, out_ref, *, pair):
+def assemble_kernel(own_ref, above_ref, both_ref, swapped_ref, out_ref, *, pair):
     count, share, width = own_ref.shape
     first = lax.axis_index("ma") == 0
     for place in range(count):
@@ -322,7 +322,7 @@
         out_specs=pl.BlockSpec(memory_space=pltpu.VMEM),
         compiler_params=pltpu.CompilerParams(vmem_limit_bytes=16 << 20),
         cost_estimate=pl.CostEstimate(flops=1, bytes_accessed=1024, transcendentals=0),
-    )(parts[0], arrived[1], arrived[2], arrived[3])
+    )(parts[0], arrived[2], arrived[3], arrived[1])
 
 
 def shards(mode_fields, cell_volumes, sizes):
@@ -358,13 +358,24 @@
     stages = stages_of(sizes)
     count = modes // BLOCKS
     cell_count = mode_fields.shape[2] * mode_fields.shape[3]
-    sent = outer(cell_volumes, blocks=(5, 6, 7), before=so_far, first=3, dtypes=(BF16,))
+    flips = dict(subsets(stages[1]))
+    sent = outer(cell_volumes, blocks=(7,), before=so_far, first=5, dtypes=(BF16,))
     cell_volumes, sent = barrier((cell_volumes, sent))
     arrived = flip(sent, stages[0], sizes)
-    kept = outer(cell_volumes, blocks=(1, 2, 3), before=so_far)
-    sent = [term_sum([kept, arrived], at * count, (at + 1) * count).astype(BF16) for at in range(3)]
+    kept = outer(cell_volumes, blocks=(3,), before=so_far, first=2)
+    sent = term_sum([kept, arrived], 0, count).astype(BF16)
     cell_volumes, sent = barrier((cell_volumes, sent))
-    received = exchange(stages[1], sent[::-1], sizes)
+    both = flip(sent, flips[3], sizes)
+
+    sent = outer(cell_volumes, blocks=(5, 6), before=so_far, first=3, dtypes=(BF16,), cost=1)
+    cell_volumes, sent = barrier((cell_volumes, sent))
+    arrived = flip(sent, stages[0], sizes)
+    kept = outer(cell_volumes, blocks=(1, 2), before=so_far, cost=1)
+    sent = [term_sum([kept, arrived], at * count, (at + 1) * count).astype(BF16) for at in range(2)]
+    cell_volumes, sent = barrier((cell_volumes, sent))
+    cell_volumes, both = barrier((cell_volumes, both))
+    received = [flip(sent[1], flips[2], sizes), flip(sent[0], flips[1], sizes), both]
+
     so_far = inner(cell_volumes, blocks=(4, 0), cost=1)
     sent, kept = outer(cell_volumes, blocks=(4, 0), before=so_far, dtypes=(BF16, F32), cost=1)
     arrived = flip(sent, stages[0], sizes)

time: 61.6 us -> 60.1 us (0.976)
  waiting for transfers between devices: 12.6 us -> 10.1 us
    ppermute x10 -> x11, waiting for transfers between devices: 12.6 us -> 10.1 us  [flip(): return lax.ppermute(array, axes, [(i, i ^ change) for i in range(count)])]
    ppermute x10 -> x11, starting transfers between devices: 11.5 us -> 12.1 us  [flip(): return lax.ppermute(array, axes, [(i, i ^ change) for i in range(count)])]
    pallas_call x5 -> x7, Pallas kernels: 22.5 us -> 22.9 us  [partial_tensor(): pl.pallas_call(body, grid=(len(blocks),), out_shape=out_shape, in_specs=i...]
  transfers between devices with their start and end apart: 12 -> 13, of which waited for: 6 -> 5; matrix products, arithmetic and copies ran while one was open for 2% -> 2% of each run, Pallas kernels for 32% -> 33%
where the time goes in v10:
time: 60.1 us; the launch traced here: 60 us
  Pallas kernels  25.5 us (42%)
  starting transfers between devices  15.9 us (26%)
  waiting for transfers between devices  10.1 us (17%)
  blocking collectives  5.34 us (9%)
  local copies, waits for them, and re-layouts  2.63 us (4%)
    pallas_call x7, Pallas kernels, partial_tensor(): pl.pallas_call(body, grid=(len(blocks),), out_shape=out_shape, in_specs=i...  22.9 us
    ppermute x11, starting transfers between devices, flip(): return lax.ppermute(array, axes, [(i, i ^ change) for i in range(count)])  12.1 us
    ppermute x11, waiting for transfers between devices, flip(): return lax.ppermute(array, axes, [(i, i ^ change) for i in range(count)])  10.1 us
    all_gather x1, blocking collectives, shards(): columns = lax.all_gather(columns, 'gy')  5.34 us
    ppermute x1, starting transfers between devices, shards(): below = lax.ppermute(edges[1], 'gx', backward)  2.25 us
    ppermute x1, starting transfers between devices, shards(): above = lax.ppermute(edges[0], 'gx', forward)  1.63 us
    pallas_call x2, Pallas kernels, slopes_of(): pl.pallas_call(functools.partial(slopes_kernel, rows=rows), out_shape=jax...  1.4 us
    unnamed x3, local copies, waits for them, and re-layouts  1.34 us
  transfers between devices with their start and end apart: 13, of which 5 were waited for; matrix products, arithmetic and copies ran while one was open for 2% of the time, Pallas kernels for 33%

profile of v10, /device:TPU:0, one launch (start us, length us, event | category | flops | bytes accessed | tf_op | source)
XLA Modules:
  0.0 60.0 jit_solution(6030054033789231518)
XLA Ops:
  0.0 1.3 %copy.7 = bf16[3,64,16,128]{3,1,0,2:T(8,128)(2,1)S(1)} copy(bf16[3,64,16,128]{3,2,1,0:T(8,128)(2,1)} %param.2) | data formatting | bytes 1572864 | tf_op args[0]
  1.4 3.0 %collective-permute-start.1 = (bf16[8,3,64,128]{3,2,1,0:T(8,128)(2,1)S(1)}, bf16[8,3,64,128]{3,2,1,0:T(8,128)(2,1)S(1)}, u32[]{:S(2)}, u32[]{:S(2)}) collective-permute-start(bf16[8,3,64,128]{3,2,1,0:T(8,128)(2,1)S(1)} %slice.50.refs_0_), channel_id=1, source_target_pairs={{0,1},{1,0},{2,3},{3,2},{4,5},{5,4},{6,7},{7,6},{8,9},{9,8},{10,11... | collective-permute-start | bytes 1179656 | tf_op jit(solution)/shard_map/ppermute | solution.py:219
  4.4 1.2 %slice_reduce_fusion.1 = (bf16[16,3,64]{2,1,0:T(4,128)(2,1)S(1)}, bf16[16,3,64]{2,1,0:T(4,128)(2,1)S(1)}) fusion(bf16[16,3,64,128]{3,2,1,0:T(8,128)(2,1)S(1)} %bitcast.4), kind=kLoop, calls=%fused_computation.1 | loop fusion | bytes 24576 | tf_op jit(solution)/shard_map/slice | solution.py:341
  5.7 5.3 %all_gather.3.columns_ref = bf16[4,2,48,64]{3,2,1,0:T(8,128)(2,1)S(1)} all-gather(bf16[1,2,48,64]{3,2,1,0:T(8,128)(2,1)S(1)} %pad_maximum_fusion.1), channel_id=1, replica_groups=mesh['gx'=4,'gy'=4,'ma'=2] {'gy'}, dimensions={0}, use_global_device_ids=true | all-gather | bytes 61440 | tf_op jit(solution)/shard_map/all_gather | solution.py:342
  11.1 1.6 %collective-permute-start.2 = (bf16[1,3,64,128]{3,2,1,0:T(8,128)(2,1)S(1)}, bf16[1,3,64,128]{3,2,1,0:T(8,128)(2,1)S(1)}, u32[]{:S(2)}, u32[]{:S(2)}) collective-permute-start(bf16[1,3,64,128]{3,2,1,0:T(8,128)(2,1)S(1)} %get-tuple-element.31), channel_id=1, source_target_pairs={{0,8},{8,16},{16,24},{24,0},{1,9},{9,17},{17,25},{25,1},{2,10},{10... | collective-permute-start | bytes 147464 | tf_op jit(solution)/shard_map/ppermute | solution.py:345
  12.7 2.2 %collective-permute-start.3 = (bf16[1,3,64,128]{3,2,1,0:T(8,128)(2,1)S(1)}, bf16[1,3,64,128]{3,2,1,0:T(8,128)(2,1)S(1)}, u32[]{:S(2)}, u32[]{:S(2)}) collective-permute-start(bf16[1,3,64,128]{3,2,1,0:T(8,128)(2,1)S(1)} %get-tuple-element.32), channel_id=1, source_target_pairs={{8,0},{16,8},{24,16},{0,24},{9,1},{17,9},{25,17},{1,25},{10,2},{18... | collective-permute-start | bytes 147464 | tf_op jit(solution)/shard_map/ppermute | solution.py:346
  15.3 0.7 %shard_map.28.refs_2_ = bf16[8,6,64,128]{3,2,1,0:T(8,128)(2,1)S(1)} custom-call(bf16[16,3,64,128]{3,2,1,0:T(8,128)(2,1)S(1)} %bitcast.7, bf16[4,2,48,64]{3,2,1,0:T(8,128)(2,1)S(1)} %all_gather.3.columns_ref), custom_call_target="tpu_custom_call" | custom-call | flops 1 | bytes 1024 | tf_op jit(solution)/shard_map/pallas_call | solution.py:70
  16.1 8.2 %shard_map.29.refs_4_ = f32[96,64,128]{2,1,0:T(8,128)S(1)} custom-call(bf16[8,3,64,128]{3,2,1,0:T(8,128)(2,1)S(1)} %slice.50.refs_0_, bf16[8,3,64,128]{3,2,1,0:T(8,128)(2,1)S(1)} %collective-permute-done.1.refs_1_, bf16[8,6,64,128]{3,2,1,0:T(8,128)(2,1)S(1)} %shard_map.28.refs_2_, f32[16,128]{1,0:T(8,128)S(1)} %copy-done), custom_call_target="tpu_custom_call" | custom-call | flops 6442450944 | bytes 4194304 | tf_op jit(solution)/shard_map/pallas_call | solution.py:187
  25.0 0.9 %collective-permute-done.refs_1_ = bf16[8,3,64,128]{3,2,1,0:T(8,128)(2,1)S(1)} collective-permute-done((bf16[8,3,64,128]{3,2,1,0:T(8,128)(2,1)S(1)}, bf16[8,3,64,128]{3,2,1,0:T(8,128)(2,1)S(1)}, u32[]{:S(2)}, u32[]{:S(2)}) %collective-permute-start) | collective-permute-done | bytes 393248 | tf_op jit(solution)/shard_map/ppermute | solution.py:219
  25.9 1.5 %shard_map.31 = bf16[16,64,128]{2,1,0:T(8,128)(2,1)S(1)} custom-call(bf16[8,3,64,128]{3,2,1,0:T(8,128)(2,1)S(1)} %pad_maximum_fusion.refs_0_, bf16[8,3,64,128]{3,2,1,0:T(8,128)(2,1)S(1)} %collective-permute-done.refs_1_, bf16[8,6,64,128]{3,2,1,0:T(8,128)(2,1)S(1)} %shard_map.30.refs_2_, f32[16,128]{1,0:T(8,128)S(1)} %copy-done, ...), custom_call_target="tpu_custom_call" | custom-call | flops 1073741824 | bytes 4194304 | tf_op jit(solution)/shard_map/pallas_call | solution.py:187
  27.5 1.5 %shard_map.32 = f32[16,64,128]{2,1,0:T(8,128)S(1)} custom-call(bf16[8,3,64,128]{3,2,1,0:T(8,128)(2,1)S(1)} %pad_maximum_fusion.refs_0_, bf16[8,3,64,128]{3,2,1,0:T(8,128)(2,1)S(1)} %collective-permute-done.refs_1_, bf16[8,6,64,128]{3,2,1,0:T(8,128)(2,1)S(1)} %shard_map.30.refs_2_, f32[16,128]{1,0:T(8,128)S(1)} %copy-done, f32[96,64,128]{2,1,0:T(8,128)S(1)} %shard_map.29.refs_4_), custom_call_target="tpu_custom_call" | custom-call | flops 1073741824 | bytes 4194304 | tf_op jit(solution)/shard_map/pallas_call | solution.py:187
  29.1 2.9 %shard_map.33 = bf16[32,64,128]{2,1,0:T(8,128)(2,1)S(1)} custom-call(bf16[8,3,64,128]{3,2,1,0:T(8,128)(2,1)S(1)} %pad_maximum_fusion.refs_0_, bf16[8,3,64,128]{3,2,1,0:T(8,128)(2,1)S(1)} %collective-permute-done.refs_1_, bf16[8,6,64,128]{3,2,1,0:T(8,128)(2,1)S(1)} %shard_map.30.refs_2_, f32[16,128]{1,0:T(8,128)S(1)} %copy-done, ...), custom_call_target="tpu_custom_call" | custom-call | flops 268435456 | bytes 4194304 | tf_op jit(solution)/shard_map/pallas_call | solution.py:187
  33.3 2.9 %shard_map.34 = f32[32,64,128]{2,1,0:T(8,128)S(1)} custom-call(bf16[8,3,64,128]{3,2,1,0:T(8,128)(2,1)S(1)} %pad_maximum_fusion.refs_0_, bf16[8,3,64,128]{3,2,1,0:T(8,128)(2,1)S(1)} %collective-permute-done.refs_1_, bf16[8,6,64,128]{3,2,1,0:T(8,128)(2,1)S(1)} %shard_map.30.refs_2_, f32[16,128]{1,0:T(8,128)S(1)} %copy-done, f32[96,64,128]{2,1,0:T(8,128)S(1)} %shard_map.29.refs_4_), custom_call_target="tpu_custom_call" | custom-call | flops 268435456 | bytes 4194304 | tf_op jit(solution)/shard_map/pallas_call | solution.py:187
  36.4 1.0 %collective-permute-start.6 = (bf16[16,64,128]{2,1,0:T(8,128)(2,1)S(1)}, bf16[16,64,128]{2,1,0:T(8,128)(2,1)S(1)}, u32[]{:S(2)}, u32[]{:S(2)}) collective-permute-start(bf16[16,64,128]{2,1,0:T(8,128)(2,1)S(1)} %get-tuple-element.39), channel_id=1, source_target_pairs={{0,4},{2,6},{4,0},{6,2},{1,5},{3,7},{5,1},{7,3},{8,12},{10,14},{12... | collective-permute-start | bytes 786440 | tf_op jit(solution)/shard_map/ppermute | solution.py:219
  37.3 1.9 %collective-permute-start.7 = (bf16[16,64,128]{2,1,0:T(8,128)(2,1)S(1)}, bf16[16,64,128]{2,1,0:T(8,128)(2,1)S(1)}, u32[]{:S(2)}, u32[]{:S(2)}) collective-permute-start(bf16[16,64,128]{2,1,0:T(8,128)(2,1)S(1)} %get-tuple-element.40), channel_id=1, source_target_pairs={{0,8},{8,0},{16,24},{24,16},{1,9},{9,1},{17,25},{25,17},{2,10},{10... | collective-permute-start | bytes 786440 | tf_op jit(solution)/shard_map/ppermute | solution.py:219
  39.3 3.5 %collective-permute-done.8.refs_2_ = bf16[16,64,128]{2,1,0:T(8,128)(2,1)S(1)} collective-permute-done((bf16[16,64,128]{2,1,0:T(8,128)(2,1)S(1)}, bf16[16,64,128]{2,1,0:T(8,128)(2,1)S(1)}, u32[]{:S(2)}, u32[]{:S(2)}) %collective-permute-start.8) | collective-permute-done | bytes 262176 | tf_op jit(solution)/shard_map/ppermute | solution.py:219
  42.7 2.8 %shard_map.36.refs_4_ = f32[32,64,128]{2,1,0:T(8,128)S(1)} custom-call(bf16[8,3,64,128]{3,2,1,0:T(8,128)(2,1)S(1)} %slice.50.refs_0_, bf16[8,3,64,128]{3,2,1,0:T(8,128)(2,1)S(1)} %collective-permute-done.1.refs_1_, bf16[8,6,64,128]{3,2,1,0:T(8,128)(2,1)S(1)} %shard_map.28.refs_2_, f32[16,128]{1,0:T(8,128)S(1)} %copy-done), custom_call_target="tpu_custom_call" | custom-call | flops 268435456 | bytes 4194304 | tf_op jit(solution)/shard_map/pallas_call | solution.py:187
  45.5 3.0 %shard_map.37 = (bf16[16,64,128]{2,1,0:T(8,128)(2,1)S(1)}, f32[16,64,128]{2,1,0:T(8,128)S(1)}) custom-call(bf16[8,3,64,128]{3,2,1,0:T(8,128)(2,1)S(1)} %pad_maximum_fusion.refs_0_, bf16[8,3,64,128]{3,2,1,0:T(8,128)(2,1)S(1)} %collective-permute-done.refs_1_, bf16[8,6,64,128]{3,2,1,0:T(8,128)(2,1)S(1)} %shard_map.30.refs_2_, f32[16,128]{1,0:T(8,128)S(1)} %copy-done, ...), custom_call_target="tpu_custom_call" | custom-call | flops 268435456 | bytes 4194304 | tf_op jit(solution)/shard_map/pallas_call | solution.py:187
  48.7 1.4 %collective-permute-done.9.refs_2_ = bf16[16,64,128]{2,1,0:T(8,128)(2,1)S(1)} collective-permute-done((bf16[16,64,128]{2,1,0:T(8,128)(2,1)S(1)}, bf16[16,64,128]{2,1,0:T(8,128)(2,1)S(1)}, u32[]{:S(2)}, u32[]{:S(2)}) %collective-permute-start.9) | collective-permute-done | bytes 262176 | tf_op jit(solution)/shard_map/ppermute | solution.py:219
  50.4 3.1 %collective-permute-start.11 = (bf16[4,64,128]{2,1,0:T(8,128)(2,1)S(1)}, bf16[4,64,128]{2,1,0:T(8,128)(2,1)S(1)}, u32[]{:S(2)}, u32[]{:S(2)}) collective-permute-start(bf16[4,64,128]{2,1,0:T(8,128)(2,1)S(1)} %get-tuple-element.49), channel_id=1, source_target_pairs={{0,17},{1,16},{8,25},{9,24},{16,1},{17,0},{24,9},{25,8},{2,19},{3,... | collective-permute-start | bytes 196616 | tf_op jit(solution)/shard_map/ppermute | solution.py:219
  53.6 1.2 %collective-permute-start.12 = (bf16[4,64,128]{2,1,0:T(8,128)(2,1)S(1)}, bf16[4,64,128]{2,1,0:T(8,128)(2,1)S(1)}, u32[]{:S(2)}, u32[]{:S(2)}) collective-permute-start(bf16[4,64,128]{2,1,0:T(8,128)(2,1)S(1)} %get-tuple-element.50), channel_id=1, source_target_pairs={{0,1},{1,0},{2,3},{3,2},{4,5},{5,4},{6,7},{7,6},{8,9},{9,8},{10,11... | collective-permute-start | bytes 196616 | tf_op jit(solution)/shard_map/ppermute | solution.py:219
  54.8 2.9 %collective-permute-done.10.above_ref = bf16[4,64,128]{2,1,0:T(8,128)(2,1)S(1)} collective-permute-done((bf16[4,64,128]{2,1,0:T(8,128)(2,1)S(1)}, bf16[4,64,128]{2,1,0:T(8,128)(2,1)S(1)}, u32[]{:S(2)}, u32[]{:S(2)}) %collective-permute-start.10) | collective-permute-done | bytes 65568 | tf_op jit(solution)/shard_map/ppermute | solution.py:219
  57.7 1.4 %collective-permute-done.11.both_ref = bf16[4,64,128]{2,1,0:T(8,128)(2,1)S(1)} collective-permute-done((bf16[4,64,128]{2,1,0:T(8,128)(2,1)S(1)}, bf16[4,64,128]{2,1,0:T(8,128)(2,1)S(1)}, u32[]{:S(2)}, u32[]{:S(2)}) %collective-permute-start.11) | collective-permute-done | bytes 65568 | tf_op jit(solution)/shard_map/ppermute | solution.py:219
  59.1 0.8 %shard_map.39 = f32[8,64,128]{2,1,0:T(8,128)} custom-call(f32[4,64,128]{2,1,0:T(8,128)S(1)} %get-tuple-element.47.own_ref, bf16[4,64,128]{2,1,0:T(8,128)(2,1)S(1)} %collective-permute-done.10.above_ref, bf16[4,64,128]{2,1,0:T(8,128)(2,1)S(1)} %collective-permute-done.11.both_ref, bf16[4,64,128]{2,1,0:T(8,128)(2,1)S(1)} %collective-permute-done.12.swapped_ref), custom_call_target="tpu_custom_call" | custom-call | flops 1 | bytes 1024 | tf_op jit(solution)/shard_map/pallas_call | solution.py:318
  (28 shorter events, 3.2 us)
Async XLA Ops:
  1.3 14.7 %copy-start = (f32[16,128]{1,0:T(8,128)S(1)}, f32[16,128]{1,0:T(8,128)}, u32[]{:S(2)}) copy-start(f32[16,128]{1,0:T(8,128)} %refs_3_.8) | copy-start | bytes 24580
  1.4 14.7 %collective-permute-start.1 = (bf16[8,3,64,128]{3,2,1,0:T(8,128)(2,1)S(1)}, bf16[8,3,64,128]{3,2,1,0:T(8,128)(2,1)S(1)}, u32[]{:S(2)}, u32[]{:S(2)}) collective-permute-start(bf16[8,3,64,128]{3,2,1,0:T(8,128)(2,1)S(1)} %slice.50.refs_0_), channel_id=1, source_target_pairs={{0,1},{1,0},{2,3},{3,2},{4,5},{5,4},{6,7},{7,6},{8,9},{9,8},{10,11... | collective-permute-start | bytes 1179656 | tf_op jit(solution)/shard_map/ppermute | solution.py:219
  11.1 13.2 %collective-permute-start.2 = (bf16[1,3,64,128]{3,2,1,0:T(8,128)(2,1)S(1)}, bf16[1,3,64,128]{3,2,1,0:T(8,128)(2,1)S(1)}, u32[]{:S(2)}, u32[]{:S(2)}) collective-permute-start(bf16[1,3,64,128]{3,2,1,0:T(8,128)(2,1)S(1)} %get-tuple-element.31), channel_id=1, source_target_pairs={{0,8},{8,16},{16,24},{24,0},{1,9},{9,17},{17,25},{25,1},{2,10},{10... | collective-permute-start | bytes 147464 | tf_op jit(solution)/shard_map/ppermute | solution.py:345
  12.7 11.6 %collective-permute-start.3 = (bf16[1,3,64,128]{3,2,1,0:T(8,128)(2,1)S(1)}, bf16[1,3,64,128]{3,2,1,0:T(8,128)(2,1)S(1)}, u32[]{:S(2)}, u32[]{:S(2)}) collective-permute-start(bf16[1,3,64,128]{3,2,1,0:T(8,128)(2,1)S(1)} %get-tuple-element.32), channel_id=1, source_target_pairs={{8,0},{16,8},{24,16},{0,24},{9,1},{17,9},{25,17},{1,25},{10,2},{18... | collective-permute-start | bytes 147464 | tf_op jit(solution)/shard_map/ppermute | solution.py:346
  14.9 10.9 %collective-permute-start = (bf16[8,3,64,128]{3,2,1,0:T(8,128)(2,1)S(1)}, bf16[8,3,64,128]{3,2,1,0:T(8,128)(2,1)S(1)}, u32[]{:S(2)}, u32[]{:S(2)}) collective-permute-start(bf16[8,3,64,128]{3,2,1,0:T(8,128)(2,1)S(1)} %pad_maximum_fusion.refs_0_), channel_id=1, source_target_pairs={{0,1},{1,0},{2,3},{3,2},{4,5},{5,4},{6,7},{7,6},{8,9},{9,8},{10,11... | collective-permute-start | bytes 1179656 | tf_op jit(solution)/shard_map/ppermute | solution.py:219
  27.4 1.6 %collective-permute-start.4 = (bf16[16,64,128]{2,1,0:T(8,128)(2,1)S(1)}, bf16[16,64,128]{2,1,0:T(8,128)(2,1)S(1)}, u32[]{:S(2)}, u32[]{:S(2)}) collective-permute-start(bf16[16,64,128]{2,1,0:T(8,128)(2,1)S(1)} %shard_map.31), channel_id=1, source_target_pairs={{0,2},{2,0},{4,6},{6,4},{1,3},{3,1},{5,7},{7,5},{8,10},{10,8},{12,... | collective-permute-start | bytes 786440 | tf_op jit(solution)/shard_map/ppermute | solution.py:219
  32.1 4.1 %collective-permute-start.5 = (bf16[32,64,128]{2,1,0:T(8,128)(2,1)S(1)}, bf16[32,64,128]{2,1,0:T(8,128)(2,1)S(1)}, u32[]{:S(2)}, u32[]{:S(2)}) collective-permute-start(bf16[32,64,128]{2,1,0:T(8,128)(2,1)S(1)} %shard_map.33), channel_id=1, source_target_pairs={{0,2},{2,0},{4,6},{6,4},{1,3},{3,1},{5,7},{7,5},{8,10},{10,8},{12,... | collective-permute-start | bytes 1572872 | tf_op jit(solution)/shard_map/ppermute | solution.py:219
  32.6 10.1 %collective-permute-start.8 = (bf16[16,64,128]{2,1,0:T(8,128)(2,1)S(1)}, bf16[16,64,128]{2,1,0:T(8,128)(2,1)S(1)}, u32[]{:S(2)}, u32[]{:S(2)}) collective-permute-start(bf16[16,64,128]{2,1,0:T(8,128)(2,1)S(1)} %add_convert_fusion), channel_id=1, source_target_pairs={{0,12},{2,14},{4,8},{6,10},{8,4},{10,6},{12,0},{14,2},{16,28},{18,... | collective-permute-start | bytes 786440 | tf_op jit(solution)/shard_map/ppermute | solution.py:219
  36.4 12.3 %collective-permute-start.6 = (bf16[16,64,128]{2,1,0:T(8,128)(2,1)S(1)}, bf16[16,64,128]{2,1,0:T(8,128)(2,1)S(1)}, u32[]{:S(2)}, u32[]{:S(2)}) collective-permute-start(bf16[16,64,128]{2,1,0:T(8,128)(2,1)S(1)} %get-tuple-element.39), channel_id=1, source_target_pairs={{0,4},{2,6},{4,0},{6,2},{1,5},{3,7},{5,1},{7,3},{8,12},{10,14},{12... | collective-permute-start | bytes 786440 | tf_op jit(solution)/shard_map/ppermute | solution.py:219
  37.3 11.3 %collective-permute-start.7 = (bf16[16,64,128]{2,1,0:T(8,128)(2,1)S(1)}, bf16[16,64,128]{2,1,0:T(8,128)(2,1)S(1)}, u32[]{:S(2)}, u32[]{:S(2)}) collective-permute-start(bf16[16,64,128]{2,1,0:T(8,128)(2,1)S(1)} %get-tuple-element.40), channel_id=1, source_target_pairs={{0,8},{8,0},{16,24},{24,16},{1,9},{9,1},{17,25},{25,17},{2,10},{10... | collective-permute-start | bytes 786440 | tf_op jit(solution)/shard_map/ppermute | solution.py:219
  48.5 1.6 %collective-permute-start.9 = (bf16[16,64,128]{2,1,0:T(8,128)(2,1)S(1)}, bf16[16,64,128]{2,1,0:T(8,128)(2,1)S(1)}, u32[]{:S(2)}, u32[]{:S(2)}) collective-permute-start(bf16[16,64,128]{2,1,0:T(8,128)(2,1)S(1)} %get-tuple-element.46), channel_id=1, source_target_pairs={{0,2},{2,0},{4,6},{6,4},{1,3},{3,1},{5,7},{7,5},{8,10},{10,8},{12,... | collective-permute-start | bytes 786440 | tf_op jit(solution)/shard_map/ppermute | solution.py:219
  50.3 7.3 %collective-permute-start.10 = (bf16[4,64,128]{2,1,0:T(8,128)(2,1)S(1)}, bf16[4,64,128]{2,1,0:T(8,128)(2,1)S(1)}, u32[]{:S(2)}, u32[]{:S(2)}) collective-permute-start(bf16[4,64,128]{2,1,0:T(8,128)(2,1)S(1)} %get-tuple-element.48), channel_id=1, source_target_pairs={{0,16},{8,24},{16,0},{24,8},{1,17},{9,25},{17,1},{25,9},{2,18},{10... | collective-permute-start | bytes 196616 | tf_op jit(solution)/shard_map/ppermute | solution.py:219
  50.4 8.7 %collective-permute-start.11 = (bf16[4,64,128]{2,1,0:T(8,128)(2,1)S(1)}, bf16[4,64,128]{2,1,0:T(8,128)(2,1)S(1)}, u32[]{:S(2)}, u32[]{:S(2)}) collective-permute-start(bf16[4,64,128]{2,1,0:T(8,128)(2,1)S(1)} %get-tuple-element.49), channel_id=1, source_target_pairs={{0,17},{1,16},{8,25},{9,24},{16,1},{17,0},{24,9},{25,8},{2,19},{3,... | collective-permute-start | bytes 196616 | tf_op jit(solution)/shard_map/ppermute | solution.py:219
  53.6 5.6 %collective-permute-start.12 = (bf16[4,64,128]{2,1,0:T(8,128)(2,1)S(1)}, bf16[4,64,128]{2,1,0:T(8,128)(2,1)S(1)}, u32[]{:S(2)}, u32[]{:S(2)}) collective-permute-start(bf16[4,64,128]{2,1,0:T(8,128)(2,1)S(1)} %get-tuple-element.50), channel_id=1, source_target_pairs={{0,1},{1,0},{2,3},{3,2},{4,5},{5,4},{6,7},{7,6},{8,9},{9,8},{10,11... | collective-permute-start | bytes 196616 | tf_op jit(solution)/shard_map/ppermute | solution.py:219

commit v11 on v10

--- a/solution.py
+++ b/solution.py
@@ -373,12 +373,14 @@
     kept = outer(cell_volumes, blocks=(1, 2), before=so_far, cost=1)
     sent = [term_sum([kept, arrived], at * count, (at + 1) * count).astype(BF16) for at in range(2)]
     cell_volumes, sent = barrier((cell_volumes, sent))
-    cell_volumes, both = barrier((cell_volumes, both))
-    received = [flip(sent[1], flips[2], sizes), flip(sent[0], flips[1], sizes), both]
+    received = [flip(sent[1], flips[2], sizes), flip(sent[0], flips[1], sizes)]
 
     so_far = inner(cell_volumes, blocks=(4, 0), cost=1)
-    sent, kept = outer(cell_volumes, blocks=(4, 0), before=so_far, dtypes=(BF16, F32), cost=1)
+    sent = outer(cell_volumes, blocks=(4,), before=so_far, dtypes=(BF16,), cost=1)
+    cell_volumes, sent, both = barrier((cell_volumes, sent, both))
     arrived = flip(sent, stages[0], sizes)
+    kept = outer(cell_volumes, blocks=(0,), before=so_far, first=1, cost=1)
+    received.append(both)
     terms = [summed(received, count, 16 * count * modes * share * cell_count), kept, arrived]
     for stage in stages[2:-1]:
         terms = terms + exchange(stage, sends(terms, count, stage), sizes)

time: 60.1 us -> 57.8 us (0.962)
  waiting for transfers between devices: 10.1 us -> 7.62 us
    ppermute x11, waiting for transfers between devices: 10.1 us -> 7.61 us  [flip(): return lax.ppermute(array, axes, [(i, i ^ change) for i in range(count)])]
    pallas_call x7 -> x8, Pallas kernels: 22.9 us -> 23.1 us  [partial_tensor(): pl.pallas_call(body, grid=(len(blocks),), out_shape=out_shape, in_specs=i...]
  transfers between devices with their start and end apart: 13 -> 13, of which waited for: 5 -> 5; matrix products, arithmetic and copies ran while one was open for 2% -> 3% of each run, Pallas kernels for 33% -> 35%
where the time goes in v11:
time: 57.8 us; the launch traced here: 57.6 us
  Pallas kernels  25.6 us (44%)
  starting transfers between devices  15.9 us (28%)
  waiting for transfers between devices  7.62 us (13%)
  blocking collectives  5.34 us (9%)
  local copies, waits for them, and re-layouts  2.63 us (5%)
    pallas_call x8, Pallas kernels, partial_tensor(): pl.pallas_call(body, grid=(len(blocks),), out_shape=out_shape, in_specs=i...  23.1 us
    ppermute x11, starting transfers between devices, flip(): return lax.ppermute(array, axes, [(i, i ^ change) for i in range(count)])  12.1 us
    ppermute x11, waiting for transfers between devices, flip(): return lax.ppermute(array, axes, [(i, i ^ change) for i in range(count)])  7.61 us
    all_gather x1, blocking collectives, shards(): columns = lax.all_gather(columns, 'gy')  5.34 us
    ppermute x1, starting transfers between devices, shards(): below = lax.ppermute(edges[1], 'gx', backward)  2.25 us
    ppermute x1, starting transfers between devices, shards(): above = lax.ppermute(edges[0], 'gx', forward)  1.63 us
    pallas_call x2, Pallas kernels, slopes_of(): pl.pallas_call(functools.partial(slopes_kernel, rows=rows), out_shape=jax...  1.4 us
    unnamed x3, local copies, waits for them, and re-layouts  1.34 us
  transfers between devices with their start and end apart: 13, of which 5 were waited for; matrix products, arithmetic and copies ran while one was open for 3% of the time, Pallas kernels for 35%

profile of v11, /device:TPU:0, one launch (start us, length us, event | category | flops | bytes accessed | tf_op | source)
XLA Modules:
  0.0 57.6 jit_solution(6697117828825498656)
XLA Ops:
  0.0 1.3 %copy.7 = bf16[3,64,16,128]{3,1,0,2:T(8,128)(2,1)S(1)} copy(bf16[3,64,16,128]{3,2,1,0:T(8,128)(2,1)} %param.2) | data formatting | bytes 1572864 | tf_op args[0]
  1.4 3.0 %collective-permute-start.1 = (bf16[8,3,64,128]{3,2,1,0:T(8,128)(2,1)S(1)}, bf16[8,3,64,128]{3,2,1,0:T(8,128)(2,1)S(1)}, u32[]{:S(2)}, u32[]{:S(2)}) collective-permute-start(bf16[8,3,64,128]{3,2,1,0:T(8,128)(2,1)S(1)} %slice.50.refs_0_), channel_id=1, source_target_pairs={{0,1},{1,0},{2,3},{3,2},{4,5},{5,4},{6,7},{7,6},{8,9},{9,8},{10,11... | collective-permute-start | bytes 1179656 | tf_op jit(solution)/shard_map/ppermute | solution.py:219
  4.4 1.2 %slice_reduce_fusion.1 = (bf16[16,3,64]{2,1,0:T(4,128)(2,1)S(1)}, bf16[16,3,64]{2,1,0:T(4,128)(2,1)S(1)}) fusion(bf16[16,3,64,128]{3,2,1,0:T(8,128)(2,1)S(1)} %bitcast.4), kind=kLoop, calls=%fused_computation.1 | loop fusion | bytes 24576 | tf_op jit(solution)/shard_map/slice | solution.py:341
  5.7 5.3 %all_gather.3.columns_ref = bf16[4,2,48,64]{3,2,1,0:T(8,128)(2,1)S(1)} all-gather(bf16[1,2,48,64]{3,2,1,0:T(8,128)(2,1)S(1)} %pad_maximum_fusion.1), channel_id=1, replica_groups=mesh['gx'=4,'gy'=4,'ma'=2] {'gy'}, dimensions={0}, use_global_device_ids=true | all-gather | bytes 61440 | tf_op jit(solution)/shard_map/all_gather | solution.py:342
  11.1 1.6 %collective-permute-start.2 = (bf16[1,3,64,128]{3,2,1,0:T(8,128)(2,1)S(1)}, bf16[1,3,64,128]{3,2,1,0:T(8,128)(2,1)S(1)}, u32[]{:S(2)}, u32[]{:S(2)}) collective-permute-start(bf16[1,3,64,128]{3,2,1,0:T(8,128)(2,1)S(1)} %get-tuple-element.30), channel_id=1, source_target_pairs={{0,8},{8,16},{16,24},{24,0},{1,9},{9,17},{17,25},{25,1},{2,10},{10... | collective-permute-start | bytes 147464 | tf_op jit(solution)/shard_map/ppermute | solution.py:345
  12.7 2.2 %collective-permute-start.3 = (bf16[1,3,64,128]{3,2,1,0:T(8,128)(2,1)S(1)}, bf16[1,3,64,128]{3,2,1,0:T(8,128)(2,1)S(1)}, u32[]{:S(2)}, u32[]{:S(2)}) collective-permute-start(bf16[1,3,64,128]{3,2,1,0:T(8,128)(2,1)S(1)} %get-tuple-element.31), channel_id=1, source_target_pairs={{8,0},{16,8},{24,16},{0,24},{9,1},{17,9},{25,17},{1,25},{10,2},{18... | collective-permute-start | bytes 147464 | tf_op jit(solution)/shard_map/ppermute | solution.py:346
  15.3 0.7 %shard_map.28.refs_2_ = bf16[8,6,64,128]{3,2,1,0:T(8,128)(2,1)S(1)} custom-call(bf16[16,3,64,128]{3,2,1,0:T(8,128)(2,1)S(1)} %bitcast.7, bf16[4,2,48,64]{3,2,1,0:T(8,128)(2,1)S(1)} %all_gather.3.columns_ref), custom_call_target="tpu_custom_call" | custom-call | flops 1 | bytes 1024 | tf_op jit(solution)/shard_map/pallas_call | solution.py:70
  16.1 8.0 %shard_map.29.refs_4_ = f32[96,64,128]{2,1,0:T(8,128)S(1)} custom-call(bf16[8,3,64,128]{3,2,1,0:T(8,128)(2,1)S(1)} %slice.50.refs_0_, bf16[8,3,64,128]{3,2,1,0:T(8,128)(2,1)S(1)} %collective-permute-done.1.refs_1_, bf16[8,6,64,128]{3,2,1,0:T(8,128)(2,1)S(1)} %shard_map.28.refs_2_, f32[16,128]{1,0:T(8,128)S(1)} %copy-done), custom_call_target="tpu_custom_call" | custom-call | flops 6442450944 | bytes 4194304 | tf_op jit(solution)/shard_map/pallas_call | solution.py:187
  24.8 1.1 %collective-permute-done.refs_1_ = bf16[8,3,64,128]{3,2,1,0:T(8,128)(2,1)S(1)} collective-permute-done((bf16[8,3,64,128]{3,2,1,0:T(8,128)(2,1)S(1)}, bf16[8,3,64,128]{3,2,1,0:T(8,128)(2,1)S(1)}, u32[]{:S(2)}, u32[]{:S(2)}) %collective-permute-start) | collective-permute-done | bytes 393248 | tf_op jit(solution)/shard_map/ppermute | solution.py:219
  25.9 1.5 %shard_map.31 = bf16[16,64,128]{2,1,0:T(8,128)(2,1)S(1)} custom-call(bf16[8,3,64,128]{3,2,1,0:T(8,128)(2,1)S(1)} %pad_maximum_fusion.refs_0_, bf16[8,3,64,128]{3,2,1,0:T(8,128)(2,1)S(1)} %collective-permute-done.refs_1_, bf16[8,6,64,128]{3,2,1,0:T(8,128)(2,1)S(1)} %shard_map.30.refs_2_, f32[16,128]{1,0:T(8,128)S(1)} %copy-done, ...), custom_call_target="tpu_custom_call" | custom-call | flops 1073741824 | bytes 4194304 | tf_op jit(solution)/shard_map/pallas_call | solution.py:187
  27.5 1.5 %shard_map.32 = f32[16,64,128]{2,1,0:T(8,128)S(1)} custom-call(bf16[8,3,64,128]{3,2,1,0:T(8,128)(2,1)S(1)} %pad_maximum_fusion.refs_0_, bf16[8,3,64,128]{3,2,1,0:T(8,128)(2,1)S(1)} %collective-permute-done.refs_1_, bf16[8,6,64,128]{3,2,1,0:T(8,128)(2,1)S(1)} %shard_map.30.refs_2_, f32[16,128]{1,0:T(8,128)S(1)} %copy-done, f32[96,64,128]{2,1,0:T(8,128)S(1)} %shard_map.29.refs_4_), custom_call_target="tpu_custom_call" | custom-call | flops 1073741824 | bytes 4194304 | tf_op jit(solution)/shard_map/pallas_call | solution.py:187
  29.1 2.9 %shard_map.33 = bf16[32,64,128]{2,1,0:T(8,128)(2,1)S(1)} custom-call(bf16[8,3,64,128]{3,2,1,0:T(8,128)(2,1)S(1)} %pad_maximum_fusion.refs_0_, bf16[8,3,64,128]{3,2,1,0:T(8,128)(2,1)S(1)} %collective-permute-done.refs_1_, bf16[8,6,64,128]{3,2,1,0:T(8,128)(2,1)S(1)} %shard_map.30.refs_2_, f32[16,128]{1,0:T(8,128)S(1)} %copy-done, ...), custom_call_target="tpu_custom_call" | custom-call | flops 268435456 | bytes 4194304 | tf_op jit(solution)/shard_map/pallas_call | solution.py:187
  33.3 2.9 %shard_map.34 = f32[32,64,128]{2,1,0:T(8,128)S(1)} custom-call(bf16[8,3,64,128]{3,2,1,0:T(8,128)(2,1)S(1)} %pad_maximum_fusion.refs_0_, bf16[8,3,64,128]{3,2,1,0:T(8,128)(2,1)S(1)} %collective-permute-done.refs_1_, bf16[8,6,64,128]{3,2,1,0:T(8,128)(2,1)S(1)} %shard_map.30.refs_2_, f32[16,128]{1,0:T(8,128)S(1)} %copy-done, f32[96,64,128]{2,1,0:T(8,128)S(1)} %shard_map.29.refs_4_), custom_call_target="tpu_custom_call" | custom-call | flops 268435456 | bytes 4194304 | tf_op jit(solution)/shard_map/pallas_call | solution.py:187
  36.4 1.0 %collective-permute-start.6 = (bf16[16,64,128]{2,1,0:T(8,128)(2,1)S(1)}, bf16[16,64,128]{2,1,0:T(8,128)(2,1)S(1)}, u32[]{:S(2)}, u32[]{:S(2)}) collective-permute-start(bf16[16,64,128]{2,1,0:T(8,128)(2,1)S(1)} %get-tuple-element.38), channel_id=1, source_target_pairs={{0,4},{2,6},{4,0},{6,2},{1,5},{3,7},{5,1},{7,3},{8,12},{10,14},{12... | collective-permute-start | bytes 786440 | tf_op jit(solution)/shard_map/ppermute | solution.py:219
  37.3 1.9 %collective-permute-start.7 = (bf16[16,64,128]{2,1,0:T(8,128)(2,1)S(1)}, bf16[16,64,128]{2,1,0:T(8,128)(2,1)S(1)}, u32[]{:S(2)}, u32[]{:S(2)}) collective-permute-start(bf16[16,64,128]{2,1,0:T(8,128)(2,1)S(1)} %get-tuple-element.39), channel_id=1, source_target_pairs={{0,8},{8,0},{16,24},{24,16},{1,9},{9,1},{17,25},{25,17},{2,10},{10... | collective-permute-start | bytes 786440 | tf_op jit(solution)/shard_map/ppermute | solution.py:219
  39.2 3.0 %shard_map.35.refs_4_ = f32[32,64,128]{2,1,0:T(8,128)S(1)} custom-call(bf16[8,3,64,128]{3,2,1,0:T(8,128)(2,1)S(1)} %slice.50.refs_0_, bf16[8,3,64,128]{3,2,1,0:T(8,128)(2,1)S(1)} %collective-permute-done.1.refs_1_, bf16[8,6,64,128]{3,2,1,0:T(8,128)(2,1)S(1)} %shard_map.28.refs_2_, f32[16,128]{1,0:T(8,128)S(1)} %copy-done), custom_call_target="tpu_custom_call" | custom-call | flops 268435456 | bytes 4194304 | tf_op jit(solution)/shard_map/pallas_call | solution.py:187
  42.3 1.6 %shard_map.36 = bf16[16,64,128]{2,1,0:T(8,128)(2,1)S(1)} custom-call(bf16[8,3,64,128]{3,2,1,0:T(8,128)(2,1)S(1)} %pad_maximum_fusion.refs_0_, bf16[8,3,64,128]{3,2,1,0:T(8,128)(2,1)S(1)} %collective-permute-done.refs_1_, bf16[8,6,64,128]{3,2,1,0:T(8,128)(2,1)S(1)} %shard_map.30.refs_2_, f32[16,128]{1,0:T(8,128)S(1)} %copy-done, ...), custom_call_target="tpu_custom_call" | custom-call | flops 134217728 | bytes 4194304 | tf_op jit(solution)/shard_map/pallas_call | solution.py:187
  43.9 1.5 %shard_map.38.refs_1_ = f32[16,64,128]{2,1,0:T(8,128)S(1)} custom-call(bf16[8,3,64,128]{3,2,1,0:T(8,128)(2,1)S(1)} %pad_maximum_fusion.refs_0_, bf16[8,3,64,128]{3,2,1,0:T(8,128)(2,1)S(1)} %collective-permute-done.refs_1_, bf16[8,6,64,128]{3,2,1,0:T(8,128)(2,1)S(1)} %shard_map.30.refs_2_, f32[16,128]{1,0:T(8,128)S(1)} %copy-done, ...), custom_call_target="tpu_custom_call" | custom-call | flops 134217728 | bytes 4194304 | tf_op jit(solution)/shard_map/pallas_call | solution.py:187
  45.5 2.0 %collective-permute-done.6.refs_0_ = bf16[16,64,128]{2,1,0:T(8,128)(2,1)S(1)} collective-permute-done((bf16[16,64,128]{2,1,0:T(8,128)(2,1)S(1)}, bf16[16,64,128]{2,1,0:T(8,128)(2,1)S(1)}, u32[]{:S(2)}, u32[]{:S(2)}) %collective-permute-start.6) | collective-permute-done | bytes 262176 | tf_op jit(solution)/shard_map/ppermute | solution.py:219
  48.6 2.4 %collective-permute-start.11 = (bf16[4,64,128]{2,1,0:T(8,128)(2,1)S(1)}, bf16[4,64,128]{2,1,0:T(8,128)(2,1)S(1)}, u32[]{:S(2)}, u32[]{:S(2)}) collective-permute-start(bf16[4,64,128]{2,1,0:T(8,128)(2,1)S(1)} %get-tuple-element.47), channel_id=1, source_target_pairs={{0,17},{1,16},{8,25},{9,24},{16,1},{17,0},{24,9},{25,8},{2,19},{3,... | collective-permute-start | bytes 196616 | tf_op jit(solution)/shard_map/ppermute | solution.py:219
  50.9 1.4 %collective-permute-start.12 = (bf16[4,64,128]{2,1,0:T(8,128)(2,1)S(1)}, bf16[4,64,128]{2,1,0:T(8,128)(2,1)S(1)}, u32[]{:S(2)}, u32[]{:S(2)}) collective-permute-start(bf16[4,64,128]{2,1,0:T(8,128)(2,1)S(1)} %get-tuple-element.48), channel_id=1, source_target_pairs={{0,1},{1,0},{2,3},{3,2},{4,5},{5,4},{6,7},{7,6},{8,9},{9,8},{10,11... | collective-permute-start | bytes 196616 | tf_op jit(solution)/shard_map/ppermute | solution.py:219
  52.3 3.3 %collective-permute-done.10.above_ref = bf16[4,64,128]{2,1,0:T(8,128)(2,1)S(1)} collective-permute-done((bf16[4,64,128]{2,1,0:T(8,128)(2,1)S(1)}, bf16[4,64,128]{2,1,0:T(8,128)(2,1)S(1)}, u32[]{:S(2)}, u32[]{:S(2)}) %collective-permute-start.10) | collective-permute-done | bytes 65568 | tf_op jit(solution)/shard_map/ppermute | solution.py:219
  55.6 1.2 %collective-permute-done.11.both_ref = bf16[4,64,128]{2,1,0:T(8,128)(2,1)S(1)} collective-permute-done((bf16[4,64,128]{2,1,0:T(8,128)(2,1)S(1)}, bf16[4,64,128]{2,1,0:T(8,128)(2,1)S(1)}, u32[]{:S(2)}, u32[]{:S(2)}) %collective-permute-start.11) | collective-permute-done | bytes 65568 | tf_op jit(solution)/shard_map/ppermute | solution.py:219
  56.8 0.8 %shard_map.40 = f32[8,64,128]{2,1,0:T(8,128)} custom-call(f32[4,64,128]{2,1,0:T(8,128)S(1)} %get-tuple-element.45.own_ref, bf16[4,64,128]{2,1,0:T(8,128)(2,1)S(1)} %collective-permute-done.10.above_ref, bf16[4,64,128]{2,1,0:T(8,128)(2,1)S(1)} %collective-permute-done.11.both_ref, bf16[4,64,128]{2,1,0:T(8,128)(2,1)S(1)} %collective-permute-done.12.swapped_ref), custom_call_target="tpu_custom_call" | custom-call | flops 1 | bytes 1024 | tf_op jit(solution)/shard_map/pallas_call | solution.py:318
  (29 shorter events, 3.9 us)
Async XLA Ops:
  1.3 14.7 %copy-start = (f32[16,128]{1,0:T(8,128)S(1)}, f32[16,128]{1,0:T(8,128)}, u32[]{:S(2)}) copy-start(f32[16,128]{1,0:T(8,128)} %refs_3_.9) | copy-start | bytes 24580
  1.4 14.7 %collective-permute-start.1 = (bf16[8,3,64,128]{3,2,1,0:T(8,128)(2,1)S(1)}, bf16[8,3,64,128]{3,2,1,0:T(8,128)(2,1)S(1)}, u32[]{:S(2)}, u32[]{:S(2)}) collective-permute-start(bf16[8,3,64,128]{3,2,1,0:T(8,128)(2,1)S(1)} %slice.50.refs_0_), channel_id=1, source_target_pairs={{0,1},{1,0},{2,3},{3,2},{4,5},{5,4},{6,7},{7,6},{8,9},{9,8},{10,11... | collective-permute-start | bytes 1179656 | tf_op jit(solution)/shard_map/ppermute | solution.py:219
  11.1 13.0 %collective-permute-start.2 = (bf16[1,3,64,128]{3,2,1,0:T(8,128)(2,1)S(1)}, bf16[1,3,64,128]{3,2,1,0:T(8,128)(2,1)S(1)}, u32[]{:S(2)}, u32[]{:S(2)}) collective-permute-start(bf16[1,3,64,128]{3,2,1,0:T(8,128)(2,1)S(1)} %get-tuple-element.30), channel_id=1, source_target_pairs={{0,8},{8,16},{16,24},{24,0},{1,9},{9,17},{17,25},{25,1},{2,10},{10... | collective-permute-start | bytes 147464 | tf_op jit(solution)/shard_map/ppermute | solution.py:345
  12.7 11.4 %collective-permute-start.3 = (bf16[1,3,64,128]{3,2,1,0:T(8,128)(2,1)S(1)}, bf16[1,3,64,128]{3,2,1,0:T(8,128)(2,1)S(1)}, u32[]{:S(2)}, u32[]{:S(2)}) collective-permute-start(bf16[1,3,64,128]{3,2,1,0:T(8,128)(2,1)S(1)} %get-tuple-element.31), channel_id=1, source_target_pairs={{8,0},{16,8},{24,16},{0,24},{9,1},{17,9},{25,17},{1,25},{10,2},{18... | collective-permute-start | bytes 147464 | tf_op jit(solution)/shard_map/ppermute | solution.py:346
  14.9 10.9 %collective-permute-start = (bf16[8,3,64,128]{3,2,1,0:T(8,128)(2,1)S(1)}, bf16[8,3,64,128]{3,2,1,0:T(8,128)(2,1)S(1)}, u32[]{:S(2)}, u32[]{:S(2)}) collective-permute-start(bf16[8,3,64,128]{3,2,1,0:T(8,128)(2,1)S(1)} %pad_maximum_fusion.refs_0_), channel_id=1, source_target_pairs={{0,1},{1,0},{2,3},{3,2},{4,5},{5,4},{6,7},{7,6},{8,9},{9,8},{10,11... | collective-permute-start | bytes 1179656 | tf_op jit(solution)/shard_map/ppermute | solution.py:219
  27.4 1.6 %collective-permute-start.4 = (bf16[16,64,128]{2,1,0:T(8,128)(2,1)S(1)}, bf16[16,64,128]{2,1,0:T(8,128)(2,1)S(1)}, u32[]{:S(2)}, u32[]{:S(2)}) collective-permute-start(bf16[16,64,128]{2,1,0:T(8,128)(2,1)S(1)} %shard_map.31), channel_id=1, source_target_pairs={{0,2},{2,0},{4,6},{6,4},{1,3},{3,1},{5,7},{7,5},{8,10},{10,8},{12,... | collective-permute-start | bytes 786440 | tf_op jit(solution)/shard_map/ppermute | solution.py:219
  32.1 4.1 %collective-permute-start.5 = (bf16[32,64,128]{2,1,0:T(8,128)(2,1)S(1)}, bf16[32,64,128]{2,1,0:T(8,128)(2,1)S(1)}, u32[]{:S(2)}, u32[]{:S(2)}) collective-permute-start(bf16[32,64,128]{2,1,0:T(8,128)(2,1)S(1)} %shard_map.33), channel_id=1, source_target_pairs={{0,2},{2,0},{4,6},{6,4},{1,3},{3,1},{5,7},{7,5},{8,10},{10,8},{12,... | collective-permute-start | bytes 1572872 | tf_op jit(solution)/shard_map/ppermute | solution.py:219
  32.6 11.2 %collective-permute-start.8 = (bf16[16,64,128]{2,1,0:T(8,128)(2,1)S(1)}, bf16[16,64,128]{2,1,0:T(8,128)(2,1)S(1)}, u32[]{:S(2)}, u32[]{:S(2)}) collective-permute-start(bf16[16,64,128]{2,1,0:T(8,128)(2,1)S(1)} %add_convert_fusion), channel_id=1, source_target_pairs={{0,12},{2,14},{4,8},{6,10},{8,4},{10,6},{12,0},{14,2},{16,28},{18,... | collective-permute-start | bytes 786440 | tf_op jit(solution)/shard_map/ppermute | solution.py:219
  36.4 11.1 %collective-permute-start.6 = (bf16[16,64,128]{2,1,0:T(8,128)(2,1)S(1)}, bf16[16,64,128]{2,1,0:T(8,128)(2,1)S(1)}, u32[]{:S(2)}, u32[]{:S(2)}) collective-permute-start(bf16[16,64,128]{2,1,0:T(8,128)(2,1)S(1)} %get-tuple-element.38), channel_id=1, source_target_pairs={{0,4},{2,6},{4,0},{6,2},{1,5},{3,7},{5,1},{7,3},{8,12},{10,14},{12... | collective-permute-start | bytes 786440 | tf_op jit(solution)/shard_map/ppermute | solution.py:219
  37.3 10.3 %collective-permute-start.7 = (bf16[16,64,128]{2,1,0:T(8,128)(2,1)S(1)}, bf16[16,64,128]{2,1,0:T(8,128)(2,1)S(1)}, u32[]{:S(2)}, u32[]{:S(2)}) collective-permute-start(bf16[16,64,128]{2,1,0:T(8,128)(2,1)S(1)} %get-tuple-element.39), channel_id=1, source_target_pairs={{0,8},{8,0},{16,24},{24,16},{1,9},{9,1},{17,25},{25,17},{2,10},{10... | collective-permute-start | bytes 786440 | tf_op jit(solution)/shard_map/ppermute | solution.py:219
  43.9 3.8 %collective-permute-start.9 = (bf16[16,64,128]{2,1,0:T(8,128)(2,1)S(1)}, bf16[16,64,128]{2,1,0:T(8,128)(2,1)S(1)}, u32[]{:S(2)}, u32[]{:S(2)}) collective-permute-start(bf16[16,64,128]{2,1,0:T(8,128)(2,1)S(1)} %shard_map.36), channel_id=1, source_target_pairs={{0,2},{2,0},{4,6},{6,4},{1,3},{3,1},{5,7},{7,5},{8,10},{10,8},{12,... | collective-permute-start | bytes 786440 | tf_op jit(solution)/shard_map/ppermute | solution.py:219
  47.9 7.7 %collective-permute-start.10 = (bf16[4,64,128]{2,1,0:T(8,128)(2,1)S(1)}, bf16[4,64,128]{2,1,0:T(8,128)(2,1)S(1)}, u32[]{:S(2)}, u32[]{:S(2)}) collective-permute-start(bf16[4,64,128]{2,1,0:T(8,128)(2,1)S(1)} %get-tuple-element.46), channel_id=1, source_target_pairs={{0,16},{8,24},{16,0},{24,8},{1,17},{9,25},{17,1},{25,9},{2,18},{10... | collective-permute-start | bytes 196616 | tf_op jit(solution)/shard_map/ppermute | solution.py:219
  48.6 8.2 %collective-permute-start.11 = (bf16[4,64,128]{2,1,0:T(8,128)(2,1)S(1)}, bf16[4,64,128]{2,1,0:T(8,128)(2,1)S(1)}, u32[]{:S(2)}, u32[]{:S(2)}) collective-permute-start(bf16[4,64,128]{2,1,0:T(8,128)(2,1)S(1)} %get-tuple-element.47), channel_id=1, source_target_pairs={{0,17},{1,16},{8,25},{9,24},{16,1},{17,0},{24,9},{25,8},{2,19},{3,... | collective-permute-start | bytes 196616 | tf_op jit(solution)/shard_map/ppermute | solution.py:219
  50.9 5.8 %collective-permute-start.12 = (bf16[4,64,128]{2,1,0:T(8,128)(2,1)S(1)}, bf16[4,64,128]{2,1,0:T(8,128)(2,1)S(1)}, u32[]{:S(2)}, u32[]{:S(2)}) collective-permute-start(bf16[4,64,128]{2,1,0:T(8,128)(2,1)S(1)} %get-tuple-element.48), channel_id=1, source_target_pairs={{0,1},{1,0},{2,3},{3,2},{4,5},{5,4},{6,7},{7,6},{8,9},{9,8},{10,11... | collective-permute-start | bytes 196616 | tf_op jit(solution)/shard_map/ppermute | solution.py:219

commit v12 on v11

--- a/solution.py
+++ b/solution.py
@@ -81,62 +81,61 @@
     return left[0] * right[0] + left[1] * right[1] + left[2] * right[2]
 
 
-def tensor_kernel(*refs, bits, block, rows_each, blocks, rows, scale, parts, outputs):
-    own_ref, other_ref, slope_ref, volume_ref = refs[:4]
-    left, right = refs[-2:]
-    out_refs = refs[-2 - outputs : -2]
-    before_ref = refs[4] if len(refs) == 7 + outputs else None
-    row_count, _, share, cells = own_ref.shape
+def tensor_kernel(*refs, bits, block, group, rows_each, blocks, rows, scale, has_before):
+    left, right, out_ref = refs[-2], refs[-1], refs[-3]
+    before_ref = refs[-4] if has_before else None
+    volume_ref = refs[0]
+    sets = [refs[1 + 3 * n : 4 + 3 * n] for n in range(len(rows))]
+    _, _, share, cells = sets[0][0].shape
+    places = [(n, x) for n in range(len(rows)) for x in range(len(rows[n]))]
     step = pl.program_id(0)
     top = bits_of(2 * share) - 1
 
     @pl.when(step == 0)
     def _():
-        for x in range(row_count):
-            weight = volume_ref[pl.ds(rows[x], 1), :] * scale
-            for half, ref in enumerate((own_ref, other_ref)):
+        for place, (n, x) in enumerate(places):
+            weight = volume_ref[pl.ds(rows[n][x], 1), :] * scale
+            for half, ref in enumerate(sets[n][:2]):
                 for a in range(3):
                     value = (weight * ref[x, a].astype(F32)).astype(BF16)
-                    left[x, a, half * share : (half + 1) * share, :] = value.astype(F32)
-                for place, b in enumerate(parts):
-                    lanes = len(parts) * x + place
+                    left[place, a, half * share : (half + 1) * share, :] = value.astype(F32)
+                for b in range(2):
+                    lanes = 2 * place + b
                     right[half * share : (half + 1) * share, lanes * cells : (lanes + 1) * cells] = ref[x, b]
 
     here = (lax.axis_index("gx") * lax.axis_size("gy") + lax.axis_index("gy")) * rows_each
-    start = here ^ (lax.axis_index("ma") << top)
-    position = block_at(blocks, step) * block
-    for place, bit in enumerate(bits):
-        start = start ^ (((position >> place) & 1) << bit)
-    columns = []
-    for x in range(row_count):
-        slopes = [slope_ref[x, n] for n in range(3 * len(parts))]
-        sums = [[] for _ in parts]
+    here = here ^ (lax.axis_index("ma") << top)
+    tests = []
+    for part in range(group):
+        start = here
+        position = block_at(blocks, step * group + part) * block
+        for place, bit in enumerate(bits):
+            start = start ^ (((position >> place) & 1) << bit)
         for row in range(block):
             offset = 0
             for place, bit in enumerate(bits):
                 offset |= ((row >> place) & 1) << bit
+            tests.append((start, offset))
+    columns = []
+    for place, (n, x) in enumerate(places):
+        slopes = [sets[n][2][x, m] for m in range(6)]
+        sums = [[], []]
+        for start, offset in tests:
             test = [
                 jnp.concatenate(
-                    [left[x, a, pl.ds(start ^ offset, 16, stride=0), :].astype(BF16)] * (share // 16), 0
+                    [left[place, a, pl.ds(start ^ offset, 16, stride=0), :].astype(BF16)] * (share // 16), 0
                 )
                 for a in range(3)
             ]
-            for place, found in enumerate(sums):
-                found.append(sum_of(test, slopes[3 * place : 3 * place + 3]))
+            for b, found in enumerate(sums):
+                found.append(sum_of(test, slopes[3 * b : 3 * b + 3]))
         columns += [jnp.concatenate(found, 0) for found in sums]
     sums = jnp.concatenate(columns, 1)
     product = lax.dot_general(sums, right[...], (((1,), (1,)), ((), ())), preferred_element_type=F32)
-    product = product.reshape(block, share, 2 * share)
+    product = product.reshape(out_ref.shape)
     if before_ref is not None:
         product = product + before_ref[...]
-    if outputs == 1:
-        out_refs[0][...] = product.astype(out_refs[0].dtype)
-    else:
-        for place, out_ref in enumerate(out_refs):
-
-            @pl.when(step == place)
-            def _(out_ref=out_ref):
-                out_ref[...] = product.astype(out_ref.dtype)
+    out_ref[...] = product.astype(out_ref.dtype)
 
 
 def block_at(blocks, step):
@@ -148,55 +147,48 @@
     return block
 
 
-def partial_tensor(
-    own, other, slopes, volumes, rows, sizes, blocks, before=None, first=0, dtypes=(F32,), cost=8
-):
-    row_count, _, share, cells = own.shape
+def partial_tensor(volumes, sets, sizes, blocks, before=None, first=0, dtype=F32, cost=8):
+    _, _, share, cells = sets[0][0].shape
     modes = 2 * share
     block = modes // BLOCKS
-    parts = (0, 1)
-    outputs = len(dtypes)
+    group = 2 if len(blocks) % 2 == 0 else 1
     devices = sizes["gx"] * sizes["gy"]
     rows_each = modes // devices
+    row_count = sum(len(rows) for *_, rows in sets)
     body = functools.partial(
         tensor_kernel,
         bits=source_bits(sizes, rows_each),
         block=block,
+        group=group,
         rows_each=rows_each,
         blocks=blocks,
-        outputs=outputs,
-        rows=rows,
-        parts=parts,
+        rows=[rows for *_, rows in sets],
         scale=1.0 / math.sqrt(volumes.shape[0] * volumes.shape[1] * devices),
+        has_before=before is not None,
     )
     whole = lambda array: pl.BlockSpec(array.shape, lambda g: (0,) * array.ndim, pipeline_mode=pl.Buffered(1))
-    shape = (block, share, modes)
-    operands = [own, other, slopes, volumes]
+    shape = (group * block, share, modes)
+    operands = [volumes] + [array for own, other, slopes, _ in sets for array in (own, other, slopes)]
     in_specs = [whole(array) for array in operands]
     if before is not None:
         operands.append(before)
-        in_specs.append(pl.BlockSpec(shape, lambda g: (first + g, 0, 0)))
-    if outputs > 1:
-        out_shape = [jax.ShapeDtypeStruct(shape, dtype) for dtype in dtypes]
-        out_specs = [pl.BlockSpec(shape, lambda g: (0, 0, 0))] * outputs
-    else:
-        out_shape = (pltpu.VMEM if before is None else jax.ShapeDtypeStruct)(
-            (len(blocks) * block, share, modes), dtypes[0]
-        )
-        out_specs = pl.BlockSpec(shape, lambda g: (g, 0, 0))
+        in_specs.append(pl.BlockSpec(shape, lambda g: (first // group + g, 0, 0)))
+    result = pltpu.VMEM if len(blocks) > 2 else jax.ShapeDtypeStruct
     return pl.pallas_call(
         body,
-        grid=(len(blocks),),
-        out_shape=out_shape,
+        grid=(len(blocks) // group,),
+        out_shape=result((len(blocks) * block, share, modes), dtype),
         in_specs=in_specs,
-        out_specs=out_specs,
+        out_specs=pl.BlockSpec(shape, lambda g: (g, 0, 0)),
         scratch_shapes=[
             pltpu.VMEM((row_count, 3, modes, cells), F32),
-            pltpu.VMEM((modes, row_count * len(parts) * cells), BF16),
+            pltpu.VMEM((modes, row_count * 2 * cells), BF16),
         ],
-        compiler_params=pltpu.CompilerParams(vmem_limit_bytes=20 << 20),
+        compiler_params=pltpu.CompilerParams(vmem_limit_bytes=24 << 20),
         cost_estimate=pl.CostEstimate(
-            flops=cost * len(blocks) * block * share * modes * row_count * cells, bytes_accessed=4 << 20, transcendentals=0
+            flops=cost * len(blocks) * block * share * modes * row_count * cells,
+            bytes_accessed=4 << 20,
+            transcendentals=0,
         ),
     )(*operands)
 
@@ -346,40 +338,34 @@
     below = lax.ppermute(edges[1], "gx", backward)
     other_outer = flip(own_outer_held, [("ma", 0)], sizes)
 
-    inner = functools.partial(
-        partial_tensor, own_inner, other_inner, slopes_of(own, inner_rows, columns), rows=inner_rows, sizes=sizes
-    )
-    so_far = inner(cell_volumes, blocks=(1, 2, 3, 5, 6, 7))
+    inner = [(own_inner, other_inner, slopes_of(own, inner_rows, columns), inner_rows)]
+    so_far = partial_tensor(cell_volumes, inner, sizes, (1, 2, 5, 6, 3, 7))
     columns, so_far = barrier((columns, so_far))
-    slopes_outer = slopes_of(own, outer_rows, columns, above, below)
-    outer = functools.partial(
-        partial_tensor, own_outer, other_outer, slopes_outer, rows=outer_rows, sizes=sizes
-    )
+    outer = [(own_outer, other_outer, slopes_of(own, outer_rows, columns, above, below), outer_rows)]
     stages = stages_of(sizes)
     count = modes // BLOCKS
     cell_count = mode_fields.shape[2] * mode_fields.shape[3]
     flips = dict(subsets(stages[1]))
-    sent = outer(cell_volumes, blocks=(7,), before=so_far, first=5, dtypes=(BF16,))
+    sent = partial_tensor(cell_volumes, outer, sizes, (7,), so_far, 5, BF16)
     cell_volumes, sent = barrier((cell_volumes, sent))
     arrived = flip(sent, stages[0], sizes)
-    kept = outer(cell_volumes, blocks=(3,), before=so_far, first=2)
+    kept = partial_tensor(cell_volumes, outer, sizes, (3,), so_far, 4)
     sent = term_sum([kept, arrived], 0, count).astype(BF16)
     cell_volumes, sent = barrier((cell_volumes, sent))
     both = flip(sent, flips[3], sizes)
 
-    sent = outer(cell_volumes, blocks=(5, 6), before=so_far, first=3, dtypes=(BF16,), cost=1)
+    sent = partial_tensor(cell_volumes, outer, sizes, (5, 6), so_far, 2, BF16, cost=1)
     cell_volumes, sent = barrier((cell_volumes, sent))
     arrived = flip(sent, stages[0], sizes)
-    kept = outer(cell_volumes, blocks=(1, 2), before=so_far, cost=1)
+    kept = partial_tensor(cell_volumes, outer, sizes, (1, 2), so_far, 0, cost=1)
     sent = [term_sum([kept, arrived], at * count, (at + 1) * count).astype(BF16) for at in range(2)]
     cell_volumes, sent = barrier((cell_volumes, sent))
     received = [flip(sent[1], flips[2], sizes), flip(sent[0], flips[1], sizes)]
 
-    so_far = inner(cell_volumes, blocks=(4, 0), cost=1)
-    sent = outer(cell_volumes, blocks=(4,), before=so_far, dtypes=(BF16,), cost=1)
+    sent = partial_tensor(cell_volumes, inner + outer, sizes, (4,), dtype=BF16, cost=1)
     cell_volumes, sent, both = barrier((cell_volumes, sent, both))
     arrived = flip(sent, stages[0], sizes)
-    kept = outer(cell_volumes, blocks=(0,), before=so_far, first=1, cost=1)
+    kept = partial_tensor(cell_volumes, inner + outer, sizes, (0,), cost=1)
     received.append(both)
     terms = [summed(received, count, 16 * count * modes * share * cell_count), kept, arrived]
     for stage in stages[2:-1]:

time: 57.8 us -> 57.5 us (level)
  Pallas kernels: 25.6 us -> 24.7 us
  waiting for transfers between devices: 7.62 us -> 8.34 us
    pallas_call x8 -> x7, Pallas kernels: 23.1 us -> 22.2 us  [partial_tensor(): pl.pallas_call(body, grid=(len(blocks) // group,), out_shape=result((len(...]
    ppermute x11, waiting for transfers between devices: 7.61 us -> 8.33 us  [flip(): return lax.ppermute(array, axes, [(i, i ^ change) for i in range(count)])]
  transfers between devices with their start and end apart: 13 -> 13, of which waited for: 5 -> 6; matrix products, arithmetic and copies ran while one was open for 3% -> 3% of each run, Pallas kernels for 35% -> 34%
where the time goes in v12:
time: 57.5 us; the launch traced here: 57.3 us
  Pallas kernels  24.7 us (43%)
  starting transfers between devices  15.9 us (28%)
  waiting for transfers between devices  8.34 us (15%)
  blocking collectives  5.34 us (9%)
  local copies, waits for them, and re-layouts  2.63 us (5%)
    pallas_call x7, Pallas kernels, partial_tensor(): pl.pallas_call(body, grid=(len(blocks) // group,), out_shape=result((len(...  22.2 us
    ppermute x11, starting transfers between devices, flip(): return lax.ppermute(array, axes, [(i, i ^ change) for i in range(count)])  12 us
    ppermute x11, waiting for transfers between devices, flip(): return lax.ppermute(array, axes, [(i, i ^ change) for i in range(count)])  8.33 us
    all_gather x1, blocking collectives, shards(): columns = lax.all_gather(columns, 'gy')  5.34 us
    ppermute x1, starting transfers between devices, shards(): below = lax.ppermute(edges[1], 'gx', backward)  2.25 us
    ppermute x1, starting transfers between devices, shards(): above = lax.ppermute(edges[0], 'gx', forward)  1.63 us
    pallas_call x2, Pallas kernels, slopes_of(): pl.pallas_call(functools.partial(slopes_kernel, rows=rows), out_shape=jax...  1.4 us
    unnamed x3, local copies, waits for them, and re-layouts  1.34 us
  transfers between devices with their start and end apart: 13, of which 6 were waited for; matrix products, arithmetic and copies ran while one was open for 3% of the time, Pallas kernels for 34%

profile of v12, /device:TPU:0, one launch (start us, length us, event | category | flops | bytes accessed | tf_op | source)
XLA Modules:
  0.0 57.3 jit_solution(11521175775499193503)
XLA Ops:
  0.0 1.3 %copy.7 = bf16[3,64,16,128]{3,1,0,2:T(8,128)(2,1)S(1)} copy(bf16[3,64,16,128]{3,2,1,0:T(8,128)(2,1)} %param.2) | data formatting | bytes 1572864 | tf_op args[0]
  1.4 3.0 %collective-permute-start.1 = (bf16[8,3,64,128]{3,2,1,0:T(8,128)(2,1)S(1)}, bf16[8,3,64,128]{3,2,1,0:T(8,128)(2,1)S(1)}, u32[]{:S(2)}, u32[]{:S(2)}) collective-permute-start(bf16[8,3,64,128]{3,2,1,0:T(8,128)(2,1)S(1)} %slice.50.refs_1_), channel_id=1, source_target_pairs={{0,1},{1,0},{2,3},{3,2},{4,5},{5,4},{6,7},{7,6},{8,9},{9,8},{10,11... | collective-permute-start | bytes 1179656 | tf_op jit(solution)/shard_map/ppermute | solution.py:211
  4.4 1.2 %slice_reduce_fusion.1 = (bf16[16,3,64]{2,1,0:T(4,128)(2,1)S(1)}, bf16[16,3,64]{2,1,0:T(4,128)(2,1)S(1)}) fusion(bf16[16,3,64,128]{3,2,1,0:T(8,128)(2,1)S(1)} %bitcast.4), kind=kLoop, calls=%fused_computation.1 | loop fusion | bytes 24576 | tf_op jit(solution)/shard_map/slice | solution.py:333
  5.7 5.3 %all_gather.3.columns_ref = bf16[4,2,48,64]{3,2,1,0:T(8,128)(2,1)S(1)} all-gather(bf16[1,2,48,64]{3,2,1,0:T(8,128)(2,1)S(1)} %pad_maximum_fusion.1), channel_id=1, replica_groups=mesh['gx'=4,'gy'=4,'ma'=2] {'gy'}, dimensions={0}, use_global_device_ids=true | all-gather | bytes 61440 | tf_op jit(solution)/shard_map/all_gather | solution.py:334
  11.1 1.6 %collective-permute-start.2 = (bf16[1,3,64,128]{3,2,1,0:T(8,128)(2,1)S(1)}, bf16[1,3,64,128]{3,2,1,0:T(8,128)(2,1)S(1)}, u32[]{:S(2)}, u32[]{:S(2)}) collective-permute-start(bf16[1,3,64,128]{3,2,1,0:T(8,128)(2,1)S(1)} %get-tuple-element.30), channel_id=1, source_target_pairs={{0,8},{8,16},{16,24},{24,0},{1,9},{9,17},{17,25},{25,1},{2,10},{10... | collective-permute-start | bytes 147464 | tf_op jit(solution)/shard_map/ppermute | solution.py:337
  12.7 2.2 %collective-permute-start.3 = (bf16[1,3,64,128]{3,2,1,0:T(8,128)(2,1)S(1)}, bf16[1,3,64,128]{3,2,1,0:T(8,128)(2,1)S(1)}, u32[]{:S(2)}, u32[]{:S(2)}) collective-permute-start(bf16[1,3,64,128]{3,2,1,0:T(8,128)(2,1)S(1)} %get-tuple-element.31), channel_id=1, source_target_pairs={{8,0},{16,8},{24,16},{0,24},{9,1},{17,9},{25,17},{1,25},{10,2},{18... | collective-permute-start | bytes 147464 | tf_op jit(solution)/shard_map/ppermute | solution.py:338
  15.3 0.7 %shard_map.28.refs_3_ = bf16[8,6,64,128]{3,2,1,0:T(8,128)(2,1)S(1)} custom-call(bf16[16,3,64,128]{3,2,1,0:T(8,128)(2,1)S(1)} %bitcast.7, bf16[4,2,48,64]{3,2,1,0:T(8,128)(2,1)S(1)} %all_gather.3.columns_ref), custom_call_target="tpu_custom_call" | custom-call | flops 1 | bytes 1024 | tf_op jit(solution)/shard_map/pallas_call | solution.py:70
  16.1 7.7 %shard_map.29.refs_4_ = f32[96,64,128]{2,1,0:T(8,128)S(1)} custom-call(f32[16,128]{1,0:T(8,128)S(1)} %copy-done, bf16[8,3,64,128]{3,2,1,0:T(8,128)(2,1)S(1)} %slice.50.refs_1_, bf16[8,3,64,128]{3,2,1,0:T(8,128)(2,1)S(1)} %collective-permute-done.1.refs_2_, bf16[8,6,64,128]{3,2,1,0:T(8,128)(2,1)S(1)} %shard_map.28.refs_3_), custom_call_target="tpu_custom_call" | custom-call | flops 6442450944 | bytes 4194304 | tf_op jit(solution)/shard_map/pallas_call | solution.py:177
  23.8 0.7 %shard_map.30.refs_3_.refs_6_ = bf16[8,6,64,128]{3,2,1,0:T(8,128)(2,1)S(1)} custom-call(bf16[16,3,64,128]{3,2,1,0:T(8,128)(2,1)S(1)} %bitcast.8, bf16[4,2,48,64]{3,2,1,0:T(8,128)(2,1)S(1)} %all_gather.3.columns_ref, bf16[1,3,64,128]{3,2,1,0:T(8,128)(2,1)S(1)} %collective-permute-done.2.refs_0_, bf16[1,3,64,128]{3,2,1,0:T(8,128)(2,1)S(1)} %collective-permute-done.3.refs_1_), custom_call_target="tpu_custom_call" | custom-call | flops 1 | bytes 1024 | tf_op jit(solution)/shard_map/pallas_call | solution.py:70
  24.5 1.3 %collective-permute-done.refs_2_.refs_5_ = bf16[8,3,64,128]{3,2,1,0:T(8,128)(2,1)S(1)} collective-permute-done((bf16[8,3,64,128]{3,2,1,0:T(8,128)(2,1)S(1)}, bf16[8,3,64,128]{3,2,1,0:T(8,128)(2,1)S(1)}, u32[]{:S(2)}, u32[]{:S(2)}) %collective-permute-start) | collective-permute-done | bytes 393248 | tf_op jit(solution)/shard_map/ppermute | solution.py:211
  25.9 1.5 %shard_map.31 = bf16[16,64,128]{2,1,0:T(8,128)(2,1)S(1)} custom-call(f32[16,128]{1,0:T(8,128)S(1)} %copy-done, bf16[8,3,64,128]{3,2,1,0:T(8,128)(2,1)S(1)} %pad_maximum_fusion.refs_1_.refs_4_, bf16[8,3,64,128]{3,2,1,0:T(8,128)(2,1)S(1)} %collective-permute-done.refs_2_.refs_5_, bf16[8,6,64,128]{3,2,1,0:T(8,128)(2,1)S(1)} %shard_map.30.refs_3_.refs_6_, ...), custom_call_target="tpu_custom_call" | custom-call | flops 1073741824 | bytes 4194304 | tf_op jit(solution)/shard_map/pallas_call | solution.py:177
  27.5 1.5 %shard_map.32 = f32[16,64,128]{2,1,0:T(8,128)S(1)} custom-call(f32[16,128]{1,0:T(8,128)S(1)} %copy-done, bf16[8,3,64,128]{3,2,1,0:T(8,128)(2,1)S(1)} %pad_maximum_fusion.refs_1_.refs_4_, bf16[8,3,64,128]{3,2,1,0:T(8,128)(2,1)S(1)} %collective-permute-done.refs_2_.refs_5_, bf16[8,6,64,128]{3,2,1,0:T(8,128)(2,1)S(1)} %shard_map.30.refs_3_.refs_6_, ...), custom_call_target="tpu_custom_call" | custom-call | flops 1073741824 | bytes 4194304 | tf_op jit(solution)/shard_map/pallas_call | solution.py:177
  29.1 2.7 %shard_map.33 = bf16[32,64,128]{2,1,0:T(8,128)(2,1)S(1)} custom-call(f32[16,128]{1,0:T(8,128)S(1)} %copy-done, bf16[8,3,64,128]{3,2,1,0:T(8,128)(2,1)S(1)} %pad_maximum_fusion.refs_1_.refs_4_, bf16[8,3,64,128]{3,2,1,0:T(8,128)(2,1)S(1)} %collective-permute-done.refs_2_.refs_5_, bf16[8,6,64,128]{3,2,1,0:T(8,128)(2,1)S(1)} %shard_map.30.refs_3_.refs_6_, ...), custom_call_target="tpu_custom_call" | custom-call | flops 268435456 | bytes 4194304 | tf_op jit(solution)/shard_map/pallas_call | solution.py:177
  33.0 2.7 %shard_map.34 = f32[32,64,128]{2,1,0:T(8,128)S(1)} custom-call(f32[16,128]{1,0:T(8,128)S(1)} %copy-done, bf16[8,3,64,128]{3,2,1,0:T(8,128)(2,1)S(1)} %pad_maximum_fusion.refs_1_.refs_4_, bf16[8,3,64,128]{3,2,1,0:T(8,128)(2,1)S(1)} %collective-permute-done.refs_2_.refs_5_, bf16[8,6,64,128]{3,2,1,0:T(8,128)(2,1)S(1)} %shard_map.30.refs_3_.refs_6_, ...), custom_call_target="tpu_custom_call" | custom-call | flops 268435456 | bytes 4194304 | tf_op jit(solution)/shard_map/pallas_call | solution.py:177
  35.9 1.0 %collective-permute-start.6 = (bf16[16,64,128]{2,1,0:T(8,128)(2,1)S(1)}, bf16[16,64,128]{2,1,0:T(8,128)(2,1)S(1)}, u32[]{:S(2)}, u32[]{:S(2)}) collective-permute-start(bf16[16,64,128]{2,1,0:T(8,128)(2,1)S(1)} %get-tuple-element.38), channel_id=1, source_target_pairs={{0,4},{2,6},{4,0},{6,2},{1,5},{3,7},{5,1},{7,3},{8,12},{10,14},{12... | collective-permute-start | bytes 786440 | tf_op jit(solution)/shard_map/ppermute | solution.py:211
  36.9 1.9 %collective-permute-start.7 = (bf16[16,64,128]{2,1,0:T(8,128)(2,1)S(1)}, bf16[16,64,128]{2,1,0:T(8,128)(2,1)S(1)}, u32[]{:S(2)}, u32[]{:S(2)}) collective-permute-start(bf16[16,64,128]{2,1,0:T(8,128)(2,1)S(1)} %get-tuple-element.39), channel_id=1, source_target_pairs={{0,8},{8,0},{16,24},{24,16},{1,9},{9,1},{17,25},{25,17},{2,10},{10... | collective-permute-start | bytes 786440 | tf_op jit(solution)/shard_map/ppermute | solution.py:211
  38.8 3.1 %shard_map.35 = bf16[16,64,128]{2,1,0:T(8,128)(2,1)S(1)} custom-call(f32[16,128]{1,0:T(8,128)S(1)} %copy-done, bf16[8,3,64,128]{3,2,1,0:T(8,128)(2,1)S(1)} %slice.50.refs_1_, bf16[8,3,64,128]{3,2,1,0:T(8,128)(2,1)S(1)} %collective-permute-done.1.refs_2_, bf16[8,6,64,128]{3,2,1,0:T(8,128)(2,1)S(1)} %shard_map.28.refs_3_, ...), custom_call_target="tpu_custom_call" | custom-call | flops 268435456 | bytes 4194304 | tf_op jit(solution)/shard_map/pallas_call | solution.py:177
  42.5 2.9 %shard_map.37.refs_1_ = f32[16,64,128]{2,1,0:T(8,128)S(1)} custom-call(f32[16,128]{1,0:T(8,128)S(1)} %copy-done, bf16[8,3,64,128]{3,2,1,0:T(8,128)(2,1)S(1)} %slice.50.refs_1_, bf16[8,3,64,128]{3,2,1,0:T(8,128)(2,1)S(1)} %collective-permute-done.1.refs_2_, bf16[8,6,64,128]{3,2,1,0:T(8,128)(2,1)S(1)} %shard_map.28.refs_3_, ...), custom_call_target="tpu_custom_call" | custom-call | flops 268435456 | bytes 4194304 | tf_op jit(solution)/shard_map/pallas_call | solution.py:177
  45.3 1.8 %collective-permute-done.6.refs_0_ = bf16[16,64,128]{2,1,0:T(8,128)(2,1)S(1)} collective-permute-done((bf16[16,64,128]{2,1,0:T(8,128)(2,1)S(1)}, bf16[16,64,128]{2,1,0:T(8,128)(2,1)S(1)}, u32[]{:S(2)}, u32[]{:S(2)}) %collective-permute-start.6) | collective-permute-done | bytes 262176 | tf_op jit(solution)/shard_map/ppermute | solution.py:211
  48.3 2.3 %collective-permute-start.11 = (bf16[4,64,128]{2,1,0:T(8,128)(2,1)S(1)}, bf16[4,64,128]{2,1,0:T(8,128)(2,1)S(1)}, u32[]{:S(2)}, u32[]{:S(2)}) collective-permute-start(bf16[4,64,128]{2,1,0:T(8,128)(2,1)S(1)} %get-tuple-element.47), channel_id=1, source_target_pairs={{0,17},{1,16},{8,25},{9,24},{16,1},{17,0},{24,9},{25,8},{2,19},{3,... | collective-permute-start | bytes 196616 | tf_op jit(solution)/shard_map/ppermute | solution.py:211
  50.6 1.5 %collective-permute-start.12 = (bf16[4,64,128]{2,1,0:T(8,128)(2,1)S(1)}, bf16[4,64,128]{2,1,0:T(8,128)(2,1)S(1)}, u32[]{:S(2)}, u32[]{:S(2)}) collective-permute-start(bf16[4,64,128]{2,1,0:T(8,128)(2,1)S(1)} %get-tuple-element.48), channel_id=1, source_target_pairs={{0,1},{1,0},{2,3},{3,2},{4,5},{5,4},{6,7},{7,6},{8,9},{9,8},{10,11... | collective-permute-start | bytes 196616 | tf_op jit(solution)/shard_map/ppermute | solution.py:211
  52.1 3.3 %collective-permute-done.10.above_ref = bf16[4,64,128]{2,1,0:T(8,128)(2,1)S(1)} collective-permute-done((bf16[4,64,128]{2,1,0:T(8,128)(2,1)S(1)}, bf16[4,64,128]{2,1,0:T(8,128)(2,1)S(1)}, u32[]{:S(2)}, u32[]{:S(2)}) %collective-permute-start.10) | collective-permute-done | bytes 65568 | tf_op jit(solution)/shard_map/ppermute | solution.py:211
  55.3 1.1 %collective-permute-done.11.both_ref = bf16[4,64,128]{2,1,0:T(8,128)(2,1)S(1)} collective-permute-done((bf16[4,64,128]{2,1,0:T(8,128)(2,1)S(1)}, bf16[4,64,128]{2,1,0:T(8,128)(2,1)S(1)}, u32[]{:S(2)}, u32[]{:S(2)}) %collective-permute-start.11) | collective-permute-done | bytes 65568 | tf_op jit(solution)/shard_map/ppermute | solution.py:211
  56.5 0.8 %shard_map.39 = f32[8,64,128]{2,1,0:T(8,128)} custom-call(f32[4,64,128]{2,1,0:T(8,128)S(1)} %get-tuple-element.45.own_ref, bf16[4,64,128]{2,1,0:T(8,128)(2,1)S(1)} %collective-permute-done.10.above_ref, bf16[4,64,128]{2,1,0:T(8,128)(2,1)S(1)} %collective-permute-done.11.both_ref, bf16[4,64,128]{2,1,0:T(8,128)(2,1)S(1)} %collective-permute-done.12.swapped_ref), custom_call_target="tpu_custom_call" | custom-call | flops 1 | bytes 1024 | tf_op jit(solution)/shard_map/pallas_call | solution.py:310
  (28 shorter events, 3.7 us)
Async XLA Ops:
  1.3 14.7 %copy-start = (f32[16,128]{1,0:T(8,128)S(1)}, f32[16,128]{1,0:T(8,128)}, u32[]{:S(2)}) copy-start(f32[16,128]{1,0:T(8,128)} %refs_0_.8) | copy-start | bytes 24580
  1.4 14.7 %collective-permute-start.1 = (bf16[8,3,64,128]{3,2,1,0:T(8,128)(2,1)S(1)}, bf16[8,3,64,128]{3,2,1,0:T(8,128)(2,1)S(1)}, u32[]{:S(2)}, u32[]{:S(2)}) collective-permute-start(bf16[8,3,64,128]{3,2,1,0:T(8,128)(2,1)S(1)} %slice.50.refs_1_), channel_id=1, source_target_pairs={{0,1},{1,0},{2,3},{3,2},{4,5},{5,4},{6,7},{7,6},{8,9},{9,8},{10,11... | collective-permute-start | bytes 1179656 | tf_op jit(solution)/shard_map/ppermute | solution.py:211
  11.1 12.7 %collective-permute-start.2 = (bf16[1,3,64,128]{3,2,1,0:T(8,128)(2,1)S(1)}, bf16[1,3,64,128]{3,2,1,0:T(8,128)(2,1)S(1)}, u32[]{:S(2)}, u32[]{:S(2)}) collective-permute-start(bf16[1,3,64,128]{3,2,1,0:T(8,128)(2,1)S(1)} %get-tuple-element.30), channel_id=1, source_target_pairs={{0,8},{8,16},{16,24},{24,0},{1,9},{9,17},{17,25},{25,1},{2,10},{10... | collective-permute-start | bytes 147464 | tf_op jit(solution)/shard_map/ppermute | solution.py:337
  12.7 11.1 %collective-permute-start.3 = (bf16[1,3,64,128]{3,2,1,0:T(8,128)(2,1)S(1)}, bf16[1,3,64,128]{3,2,1,0:T(8,128)(2,1)S(1)}, u32[]{:S(2)}, u32[]{:S(2)}) collective-permute-start(bf16[1,3,64,128]{3,2,1,0:T(8,128)(2,1)S(1)} %get-tuple-element.31), channel_id=1, source_target_pairs={{8,0},{16,8},{24,16},{0,24},{9,1},{17,9},{25,17},{1,25},{10,2},{18... | collective-permute-start | bytes 147464 | tf_op jit(solution)/shard_map/ppermute | solution.py:338
  14.9 10.9 %collective-permute-start = (bf16[8,3,64,128]{3,2,1,0:T(8,128)(2,1)S(1)}, bf16[8,3,64,128]{3,2,1,0:T(8,128)(2,1)S(1)}, u32[]{:S(2)}, u32[]{:S(2)}) collective-permute-start(bf16[8,3,64,128]{3,2,1,0:T(8,128)(2,1)S(1)} %pad_maximum_fusion.refs_1_.refs_4_), channel_id=1, source_target_pairs={{0,1},{1,0},{2,3},{3,2},{4,5},{5,4},{6,7},{7,6},{8,9},{9,8},{10,11... | collective-permute-start | bytes 1179656 | tf_op jit(solution)/shard_map/ppermute | solution.py:211
  27.4 1.6 %collective-permute-start.4 = (bf16[16,64,128]{2,1,0:T(8,128)(2,1)S(1)}, bf16[16,64,128]{2,1,0:T(8,128)(2,1)S(1)}, u32[]{:S(2)}, u32[]{:S(2)}) collective-permute-start(bf16[16,64,128]{2,1,0:T(8,128)(2,1)S(1)} %shard_map.31), channel_id=1, source_target_pairs={{0,2},{2,0},{4,6},{6,4},{1,3},{3,1},{5,7},{7,5},{8,10},{10,8},{12,... | collective-permute-start | bytes 786440 | tf_op jit(solution)/shard_map/ppermute | solution.py:211
  31.9 3.9 %collective-permute-start.5 = (bf16[32,64,128]{2,1,0:T(8,128)(2,1)S(1)}, bf16[32,64,128]{2,1,0:T(8,128)(2,1)S(1)}, u32[]{:S(2)}, u32[]{:S(2)}) collective-permute-start(bf16[32,64,128]{2,1,0:T(8,128)(2,1)S(1)} %shard_map.33), channel_id=1, source_target_pairs={{0,2},{2,0},{4,6},{6,4},{1,3},{3,1},{5,7},{7,5},{8,10},{10,8},{12,... | collective-permute-start | bytes 1572872 | tf_op jit(solution)/shard_map/ppermute | solution.py:211
  32.4 10.1 %collective-permute-start.8 = (bf16[16,64,128]{2,1,0:T(8,128)(2,1)S(1)}, bf16[16,64,128]{2,1,0:T(8,128)(2,1)S(1)}, u32[]{:S(2)}, u32[]{:S(2)}) collective-permute-start(bf16[16,64,128]{2,1,0:T(8,128)(2,1)S(1)} %add_convert_fusion), channel_id=1, source_target_pairs={{0,12},{2,14},{4,8},{6,10},{8,4},{10,6},{12,0},{14,2},{16,28},{18,... | collective-permute-start | bytes 786440 | tf_op jit(solution)/shard_map/ppermute | solution.py:211
  35.9 11.3 %collective-permute-start.6 = (bf16[16,64,128]{2,1,0:T(8,128)(2,1)S(1)}, bf16[16,64,128]{2,1,0:T(8,128)(2,1)S(1)}, u32[]{:S(2)}, u32[]{:S(2)}) collective-permute-start(bf16[16,64,128]{2,1,0:T(8,128)(2,1)S(1)} %get-tuple-element.38), channel_id=1, source_target_pairs={{0,4},{2,6},{4,0},{6,2},{1,5},{3,7},{5,1},{7,3},{8,12},{10,14},{12... | collective-permute-start | bytes 786440 | tf_op jit(solution)/shard_map/ppermute | solution.py:211
  36.9 10.5 %collective-permute-start.7 = (bf16[16,64,128]{2,1,0:T(8,128)(2,1)S(1)}, bf16[16,64,128]{2,1,0:T(8,128)(2,1)S(1)}, u32[]{:S(2)}, u32[]{:S(2)}) collective-permute-start(bf16[16,64,128]{2,1,0:T(8,128)(2,1)S(1)} %get-tuple-element.39), channel_id=1, source_target_pairs={{0,8},{8,0},{16,24},{24,16},{1,9},{9,1},{17,25},{25,17},{2,10},{10... | collective-permute-start | bytes 786440 | tf_op jit(solution)/shard_map/ppermute | solution.py:211
  42.5 4.9 %collective-permute-start.9 = (bf16[16,64,128]{2,1,0:T(8,128)(2,1)S(1)}, bf16[16,64,128]{2,1,0:T(8,128)(2,1)S(1)}, u32[]{:S(2)}, u32[]{:S(2)}) collective-permute-start(bf16[16,64,128]{2,1,0:T(8,128)(2,1)S(1)} %shard_map.35), channel_id=1, source_target_pairs={{0,2},{2,0},{4,6},{6,4},{1,3},{3,1},{5,7},{7,5},{8,10},{10,8},{12,... | collective-permute-start | bytes 786440 | tf_op jit(solution)/shard_map/ppermute | solution.py:211
  47.6 7.7 %collective-permute-start.10 = (bf16[4,64,128]{2,1,0:T(8,128)(2,1)S(1)}, bf16[4,64,128]{2,1,0:T(8,128)(2,1)S(1)}, u32[]{:S(2)}, u32[]{:S(2)}) collective-permute-start(bf16[4,64,128]{2,1,0:T(8,128)(2,1)S(1)} %get-tuple-element.46), channel_id=1, source_target_pairs={{0,16},{8,24},{16,0},{24,8},{1,17},{9,25},{17,1},{25,9},{2,18},{10... | collective-permute-start | bytes 196616 | tf_op jit(solution)/shard_map/ppermute | solution.py:211
  48.3 8.2 %collective-permute-start.11 = (bf16[4,64,128]{2,1,0:T(8,128)(2,1)S(1)}, bf16[4,64,128]{2,1,0:T(8,128)(2,1)S(1)}, u32[]{:S(2)}, u32[]{:S(2)}) collective-permute-start(bf16[4,64,128]{2,1,0:T(8,128)(2,1)S(1)} %get-tuple-element.47), channel_id=1, source_target_pairs={{0,17},{1,16},{8,25},{9,24},{16,1},{17,0},{24,9},{25,8},{2,19},{3,... | collective-permute-start | bytes 196616 | tf_op jit(solution)/shard_map/ppermute | solution.py:211
  50.6 5.9 %collective-permute-start.12 = (bf16[4,64,128]{2,1,0:T(8,128)(2,1)S(1)}, bf16[4,64,128]{2,1,0:T(8,128)(2,1)S(1)}, u32[]{:S(2)}, u32[]{:S(2)}) collective-permute-start(bf16[4,64,128]{2,1,0:T(8,128)(2,1)S(1)} %get-tuple-element.48), channel_id=1, source_target_pairs={{0,1},{1,0},{2,3},{3,2},{4,5},{5,4},{6,7},{7,6},{8,9},{9,8},{10,11... | collective-permute-start | bytes 196616 | tf_op jit(solution)/shard_map/ppermute | solution.py:211

commit v13 on v12

--- a/solution.py
+++ b/solution.py
@@ -332,13 +332,15 @@
     other_inner = flip(own_inner, [("ma", 0)], sizes)
     columns = jnp.stack([own[:, :, :, -1], own[:, :, :, 0]]).reshape(2, 3 * row_count, share)
     columns = lax.all_gather(columns, "gy")
-    own_outer_held, edges, columns = barrier((own_outer, (own[-1:], own[:1]), columns))
+    own_outer_held, columns = barrier((own_outer, columns))
+    slopes_inner = slopes_of(own, inner_rows, columns)
+    edges, slopes_inner = barrier(((own[-1:], own[:1]), slopes_inner))
     forward, backward = ring("gx")
     above = lax.ppermute(edges[0], "gx", forward)
     below = lax.ppermute(edges[1], "gx", backward)
     other_outer = flip(own_outer_held, [("ma", 0)], sizes)
 
-    inner = [(own_inner, other_inner, slopes_of(own, inner_rows, columns), inner_rows)]
+    inner = [(own_inner, other_inner, slopes_inner, inner_rows)]
     so_far = partial_tensor(cell_volumes, inner, sizes, (1, 2, 5, 6, 3, 7))
     columns, so_far = barrier((columns, so_far))
     outer = [(own_outer, other_outer, slopes_of(own, outer_rows, columns, above, below), outer_rows)]

time: 57.5 us -> 57.2 us (level)
  transfers between devices with their start and end apart: 13 -> 13, of which waited for: 6 -> 5; matrix products, arithmetic and copies ran while one was open for 3% -> 3% of each run, Pallas kernels for 34% -> 34%
where the time goes in v13:
time: 57.2 us; the launch traced here: 57.1 us
  Pallas kernels  24.7 us (43%)
  starting transfers between devices  15.9 us (28%)
  waiting for transfers between devices  8.04 us (14%)
  blocking collectives  5.34 us (9%)
  local copies, waits for them, and re-layouts  2.63 us (5%)
    pallas_call x7, Pallas kernels, partial_tensor(): pl.pallas_call(body, grid=(len(blocks) // group,), out_shape=result((len(...  22.2 us
    ppermute x11, starting transfers between devices, flip(): return lax.ppermute(array, axes, [(i, i ^ change) for i in range(count)])  11.8 us
    ppermute x11, waiting for transfers between devices, flip(): return lax.ppermute(array, axes, [(i, i ^ change) for i in range(count)])  8.04 us
    all_gather x1, blocking collectives, shards(): columns = lax.all_gather(columns, 'gy')  5.34 us
    ppermute x1, starting transfers between devices, shards(): below = lax.ppermute(edges[1], 'gx', backward)  2.09 us
    ppermute x1, starting transfers between devices, shards(): above = lax.ppermute(edges[0], 'gx', forward)  2.08 us
    pallas_call x2, Pallas kernels, slopes_of(): pl.pallas_call(functools.partial(slopes_kernel, rows=rows), out_shape=jax...  1.4 us
    unnamed x3, local copies, waits for them, and re-layouts  1.34 us
  transfers between devices with their start and end apart: 13, of which 5 were waited for; matrix products, arithmetic and copies ran while one was open for 3% of the time, Pallas kernels for 34%

profile of v13, /device:TPU:0, one launch (start us, length us, event | category | flops | bytes accessed | tf_op | source)
XLA Modules:
  0.0 57.1 jit_solution(12662429338405411124)
XLA Ops:
  0.0 1.3 %copy.7 = bf16[3,64,16,128]{3,1,0,2:T(8,128)(2,1)S(1)} copy(bf16[3,64,16,128]{3,2,1,0:T(8,128)(2,1)} %param.2) | data formatting | bytes 1572864 | tf_op args[0]
  1.4 3.0 %collective-permute-start.1 = (bf16[8,3,64,128]{3,2,1,0:T(8,128)(2,1)S(1)}, bf16[8,3,64,128]{3,2,1,0:T(8,128)(2,1)S(1)}, u32[]{:S(2)}, u32[]{:S(2)}) collective-permute-start(bf16[8,3,64,128]{3,2,1,0:T(8,128)(2,1)S(1)} %slice.48.refs_1_), channel_id=1, source_target_pairs={{0,1},{1,0},{2,3},{3,2},{4,5},{5,4},{6,7},{7,6},{8,9},{9,8},{10,11... | collective-permute-start | bytes 1179656 | tf_op jit(solution)/shard_map/ppermute | solution.py:211
  4.4 1.2 %slice_reduce_fusion.1 = (bf16[16,3,64]{2,1,0:T(4,128)(2,1)S(1)}, bf16[16,3,64]{2,1,0:T(4,128)(2,1)S(1)}) fusion(bf16[16,3,64,128]{3,2,1,0:T(8,128)(2,1)S(1)} %bitcast.4), kind=kLoop, calls=%fused_computation.1 | loop fusion | bytes 24576 | tf_op jit(solution)/shard_map/slice | solution.py:333
  5.7 5.3 %all_gather.3.columns_ref = bf16[4,2,48,64]{3,2,1,0:T(8,128)(2,1)S(1)} all-gather(bf16[1,2,48,64]{3,2,1,0:T(8,128)(2,1)S(1)} %pad_maximum_fusion.1), channel_id=1, replica_groups=mesh['gx'=4,'gy'=4,'ma'=2] {'gy'}, dimensions={0}, use_global_device_ids=true | all-gather | bytes 61440 | tf_op jit(solution)/shard_map/all_gather | solution.py:334
  11.2 0.7 %shard_map.28.refs_3_ = bf16[8,6,64,128]{3,2,1,0:T(8,128)(2,1)S(1)} custom-call(bf16[16,3,64,128]{3,2,1,0:T(8,128)(2,1)S(1)} %bitcast.6, bf16[4,2,48,64]{3,2,1,0:T(8,128)(2,1)S(1)} %all_gather.3.columns_ref), custom_call_target="tpu_custom_call" | custom-call | flops 1 | bytes 1024 | tf_op jit(solution)/shard_map/pallas_call | solution.py:70
  11.9 2.1 %collective-permute-start.2 = (bf16[1,3,64,128]{3,2,1,0:T(8,128)(2,1)S(1)}, bf16[1,3,64,128]{3,2,1,0:T(8,128)(2,1)S(1)}, u32[]{:S(2)}, u32[]{:S(2)}) collective-permute-start(bf16[1,3,64,128]{3,2,1,0:T(8,128)(2,1)S(1)} %get-tuple-element.32), channel_id=1, source_target_pairs={{0,8},{8,16},{16,24},{24,0},{1,9},{9,17},{17,25},{25,1},{2,10},{10... | collective-permute-start | bytes 147464 | tf_op jit(solution)/shard_map/ppermute | solution.py:339
  14.0 2.1 %collective-permute-start.3 = (bf16[1,3,64,128]{3,2,1,0:T(8,128)(2,1)S(1)}, bf16[1,3,64,128]{3,2,1,0:T(8,128)(2,1)S(1)}, u32[]{:S(2)}, u32[]{:S(2)}) collective-permute-start(bf16[1,3,64,128]{3,2,1,0:T(8,128)(2,1)S(1)} %get-tuple-element.33), channel_id=1, source_target_pairs={{8,0},{16,8},{24,16},{0,24},{9,1},{17,9},{25,17},{1,25},{10,2},{18... | collective-permute-start | bytes 147464 | tf_op jit(solution)/shard_map/ppermute | solution.py:340
  16.1 7.7 %shard_map.29.refs_4_ = f32[96,64,128]{2,1,0:T(8,128)S(1)} custom-call(f32[16,128]{1,0:T(8,128)S(1)} %copy-done, bf16[8,3,64,128]{3,2,1,0:T(8,128)(2,1)S(1)} %slice.48.refs_1_, bf16[8,3,64,128]{3,2,1,0:T(8,128)(2,1)S(1)} %collective-permute-done.1.refs_2_, bf16[8,6,64,128]{3,2,1,0:T(8,128)(2,1)S(1)} %shard_map.28.refs_3_), custom_call_target="tpu_custom_call" | custom-call | flops 6442450944 | bytes 4194304 | tf_op jit(solution)/shard_map/pallas_call | solution.py:177
  23.8 0.7 %shard_map.30.refs_3_.refs_6_ = bf16[8,6,64,128]{3,2,1,0:T(8,128)(2,1)S(1)} custom-call(bf16[16,3,64,128]{3,2,1,0:T(8,128)(2,1)S(1)} %bitcast.8, bf16[4,2,48,64]{3,2,1,0:T(8,128)(2,1)S(1)} %all_gather.3.columns_ref, bf16[1,3,64,128]{3,2,1,0:T(8,128)(2,1)S(1)} %collective-permute-done.2.refs_0_, bf16[1,3,64,128]{3,2,1,0:T(8,128)(2,1)S(1)} %collective-permute-done.3.refs_1_), custom_call_target="tpu_custom_call" | custom-call | flops 1 | bytes 1024 | tf_op jit(solution)/shard_map/pallas_call | solution.py:70
  24.6 1.5 %shard_map.31 = bf16[16,64,128]{2,1,0:T(8,128)(2,1)S(1)} custom-call(f32[16,128]{1,0:T(8,128)S(1)} %copy-done, bf16[8,3,64,128]{3,2,1,0:T(8,128)(2,1)S(1)} %pad_maximum_fusion.refs_1_.refs_4_, bf16[8,3,64,128]{3,2,1,0:T(8,128)(2,1)S(1)} %collective-permute-done.refs_2_.refs_5_, bf16[8,6,64,128]{3,2,1,0:T(8,128)(2,1)S(1)} %shard_map.30.refs_3_.refs_6_, ...), custom_call_target="tpu_custom_call" | custom-call | flops 1073741824 | bytes 4194304 | tf_op jit(solution)/shard_map/pallas_call | solution.py:177
  26.2 1.5 %shard_map.32 = f32[16,64,128]{2,1,0:T(8,128)S(1)} custom-call(f32[16,128]{1,0:T(8,128)S(1)} %copy-done, bf16[8,3,64,128]{3,2,1,0:T(8,128)(2,1)S(1)} %pad_maximum_fusion.refs_1_.refs_4_, bf16[8,3,64,128]{3,2,1,0:T(8,128)(2,1)S(1)} %collective-permute-done.refs_2_.refs_5_, bf16[8,6,64,128]{3,2,1,0:T(8,128)(2,1)S(1)} %shard_map.30.refs_3_.refs_6_, ...), custom_call_target="tpu_custom_call" | custom-call | flops 1073741824 | bytes 4194304 | tf_op jit(solution)/shard_map/pallas_call | solution.py:177
  27.8 2.7 %shard_map.33 = bf16[32,64,128]{2,1,0:T(8,128)(2,1)S(1)} custom-call(f32[16,128]{1,0:T(8,128)S(1)} %copy-done, bf16[8,3,64,128]{3,2,1,0:T(8,128)(2,1)S(1)} %pad_maximum_fusion.refs_1_.refs_4_, bf16[8,3,64,128]{3,2,1,0:T(8,128)(2,1)S(1)} %collective-permute-done.refs_2_.refs_5_, bf16[8,6,64,128]{3,2,1,0:T(8,128)(2,1)S(1)} %shard_map.30.refs_3_.refs_6_, ...), custom_call_target="tpu_custom_call" | custom-call | flops 268435456 | bytes 4194304 | tf_op jit(solution)/shard_map/pallas_call | solution.py:177
  31.1 0.9 %collective-permute-start.8 = (bf16[16,64,128]{2,1,0:T(8,128)(2,1)S(1)}, bf16[16,64,128]{2,1,0:T(8,128)(2,1)S(1)}, u32[]{:S(2)}, u32[]{:S(2)}) collective-permute-start(bf16[16,64,128]{2,1,0:T(8,128)(2,1)S(1)} %add_convert_fusion), channel_id=1, source_target_pairs={{0,12},{2,14},{4,8},{6,10},{8,4},{10,6},{12,0},{14,2},{16,28},{18,... | collective-permute-start | bytes 786440 | tf_op jit(solution)/shard_map/ppermute | solution.py:211
  32.0 2.7 %shard_map.34 = f32[32,64,128]{2,1,0:T(8,128)S(1)} custom-call(f32[16,128]{1,0:T(8,128)S(1)} %copy-done, bf16[8,3,64,128]{3,2,1,0:T(8,128)(2,1)S(1)} %pad_maximum_fusion.refs_1_.refs_4_, bf16[8,3,64,128]{3,2,1,0:T(8,128)(2,1)S(1)} %collective-permute-done.refs_2_.refs_5_, bf16[8,6,64,128]{3,2,1,0:T(8,128)(2,1)S(1)} %shard_map.30.refs_3_.refs_6_, ...), custom_call_target="tpu_custom_call" | custom-call | flops 268435456 | bytes 4194304 | tf_op jit(solution)/shard_map/pallas_call | solution.py:177
  34.8 0.9 %collective-permute-start.6 = (bf16[16,64,128]{2,1,0:T(8,128)(2,1)S(1)}, bf16[16,64,128]{2,1,0:T(8,128)(2,1)S(1)}, u32[]{:S(2)}, u32[]{:S(2)}) collective-permute-start(bf16[16,64,128]{2,1,0:T(8,128)(2,1)S(1)} %get-tuple-element.40), channel_id=1, source_target_pairs={{0,4},{2,6},{4,0},{6,2},{1,5},{3,7},{5,1},{7,3},{8,12},{10,14},{12... | collective-permute-start | bytes 786440 | tf_op jit(solution)/shard_map/ppermute | solution.py:211
  35.7 1.8 %collective-permute-start.7 = (bf16[16,64,128]{2,1,0:T(8,128)(2,1)S(1)}, bf16[16,64,128]{2,1,0:T(8,128)(2,1)S(1)}, u32[]{:S(2)}, u32[]{:S(2)}) collective-permute-start(bf16[16,64,128]{2,1,0:T(8,128)(2,1)S(1)} %get-tuple-element.41), channel_id=1, source_target_pairs={{0,8},{8,0},{16,24},{24,16},{1,9},{9,1},{17,25},{25,17},{2,10},{10... | collective-permute-start | bytes 786440 | tf_op jit(solution)/shard_map/ppermute | solution.py:211
  37.5 3.1 %shard_map.35 = bf16[16,64,128]{2,1,0:T(8,128)(2,1)S(1)} custom-call(f32[16,128]{1,0:T(8,128)S(1)} %copy-done, bf16[8,3,64,128]{3,2,1,0:T(8,128)(2,1)S(1)} %slice.48.refs_1_, bf16[8,3,64,128]{3,2,1,0:T(8,128)(2,1)S(1)} %collective-permute-done.1.refs_2_, bf16[8,6,64,128]{3,2,1,0:T(8,128)(2,1)S(1)} %shard_map.28.refs_3_, ...), custom_call_target="tpu_custom_call" | custom-call | flops 268435456 | bytes 4194304 | tf_op jit(solution)/shard_map/pallas_call | solution.py:177
  41.2 2.9 %shard_map.37.refs_1_ = f32[16,64,128]{2,1,0:T(8,128)S(1)} custom-call(f32[16,128]{1,0:T(8,128)S(1)} %copy-done, bf16[8,3,64,128]{3,2,1,0:T(8,128)(2,1)S(1)} %slice.48.refs_1_, bf16[8,3,64,128]{3,2,1,0:T(8,128)(2,1)S(1)} %collective-permute-done.1.refs_2_, bf16[8,6,64,128]{3,2,1,0:T(8,128)(2,1)S(1)} %shard_map.28.refs_3_, ...), custom_call_target="tpu_custom_call" | custom-call | flops 268435456 | bytes 4194304 | tf_op jit(solution)/shard_map/pallas_call | solution.py:177
  44.0 1.8 %collective-permute-done.6.refs_0_ = bf16[16,64,128]{2,1,0:T(8,128)(2,1)S(1)} collective-permute-done((bf16[16,64,128]{2,1,0:T(8,128)(2,1)S(1)}, bf16[16,64,128]{2,1,0:T(8,128)(2,1)S(1)}, u32[]{:S(2)}, u32[]{:S(2)}) %collective-permute-start.6) | collective-permute-done | bytes 262176 | tf_op jit(solution)/shard_map/ppermute | solution.py:211
  46.4 0.8 %collective-permute-start.10 = (bf16[4,64,128]{2,1,0:T(8,128)(2,1)S(1)}, bf16[4,64,128]{2,1,0:T(8,128)(2,1)S(1)}, u32[]{:S(2)}, u32[]{:S(2)}) collective-permute-start(bf16[4,64,128]{2,1,0:T(8,128)(2,1)S(1)} %get-tuple-element.48), channel_id=1, source_target_pairs={{0,16},{8,24},{16,0},{24,8},{1,17},{9,25},{17,1},{25,9},{2,18},{10... | collective-permute-start | bytes 196616 | tf_op jit(solution)/shard_map/ppermute | solution.py:211
  47.2 3.1 %collective-permute-start.11 = (bf16[4,64,128]{2,1,0:T(8,128)(2,1)S(1)}, bf16[4,64,128]{2,1,0:T(8,128)(2,1)S(1)}, u32[]{:S(2)}, u32[]{:S(2)}) collective-permute-start(bf16[4,64,128]{2,1,0:T(8,128)(2,1)S(1)} %get-tuple-element.49), channel_id=1, source_target_pairs={{0,17},{1,16},{8,25},{9,24},{16,1},{17,0},{24,9},{25,8},{2,19},{3,... | collective-permute-start | bytes 196616 | tf_op jit(solution)/shard_map/ppermute | solution.py:211
  50.9 2.6 %collective-permute-done.10.above_ref = bf16[4,64,128]{2,1,0:T(8,128)(2,1)S(1)} collective-permute-done((bf16[4,64,128]{2,1,0:T(8,128)(2,1)S(1)}, bf16[4,64,128]{2,1,0:T(8,128)(2,1)S(1)}, u32[]{:S(2)}, u32[]{:S(2)}) %collective-permute-start.10) | collective-permute-done | bytes 65568 | tf_op jit(solution)/shard_map/ppermute | solution.py:211
  53.4 2.8 %collective-permute-done.11.both_ref = bf16[4,64,128]{2,1,0:T(8,128)(2,1)S(1)} collective-permute-done((bf16[4,64,128]{2,1,0:T(8,128)(2,1)S(1)}, bf16[4,64,128]{2,1,0:T(8,128)(2,1)S(1)}, u32[]{:S(2)}, u32[]{:S(2)}) %collective-permute-start.11) | collective-permute-done | bytes 65568 | tf_op jit(solution)/shard_map/ppermute | solution.py:211
  56.2 0.8 %shard_map.39 = f32[8,64,128]{2,1,0:T(8,128)} custom-call(f32[4,64,128]{2,1,0:T(8,128)S(1)} %get-tuple-element.47.own_ref, bf16[4,64,128]{2,1,0:T(8,128)(2,1)S(1)} %collective-permute-done.10.above_ref, bf16[4,64,128]{2,1,0:T(8,128)(2,1)S(1)} %collective-permute-done.11.both_ref, bf16[4,64,128]{2,1,0:T(8,128)(2,1)S(1)} %collective-permute-done.12.swapped_ref), custom_call_target="tpu_custom_call" | custom-call | flops 1 | bytes 1024 | tf_op jit(solution)/shard_map/pallas_call | solution.py:310
  (28 shorter events, 2.8 us)
Async XLA Ops:
  1.3 14.8 %copy-start = (f32[16,128]{1,0:T(8,128)S(1)}, f32[16,128]{1,0:T(8,128)}, u32[]{:S(2)}) copy-start(f32[16,128]{1,0:T(8,128)} %refs_0_.8) | copy-start | bytes 24580
  1.4 14.7 %collective-permute-start.1 = (bf16[8,3,64,128]{3,2,1,0:T(8,128)(2,1)S(1)}, bf16[8,3,64,128]{3,2,1,0:T(8,128)(2,1)S(1)}, u32[]{:S(2)}, u32[]{:S(2)}) collective-permute-start(bf16[8,3,64,128]{3,2,1,0:T(8,128)(2,1)S(1)} %slice.48.refs_1_), channel_id=1, source_target_pairs={{0,1},{1,0},{2,3},{3,2},{4,5},{5,4},{6,7},{7,6},{8,9},{9,8},{10,11... | collective-permute-start | bytes 1179656 | tf_op jit(solution)/shard_map/ppermute | solution.py:211
  11.0 13.5 %collective-permute-start = (bf16[8,3,64,128]{3,2,1,0:T(8,128)(2,1)S(1)}, bf16[8,3,64,128]{3,2,1,0:T(8,128)(2,1)S(1)}, u32[]{:S(2)}, u32[]{:S(2)}) collective-permute-start(bf16[8,3,64,128]{3,2,1,0:T(8,128)(2,1)S(1)} %pad_maximum_fusion.refs_1_.refs_4_), channel_id=1, source_target_pairs={{0,1},{1,0},{2,3},{3,2},{4,5},{5,4},{6,7},{7,6},{8,9},{9,8},{10,11... | collective-permute-start | bytes 1179656 | tf_op jit(solution)/shard_map/ppermute | solution.py:211
  11.9 11.9 %collective-permute-start.2 = (bf16[1,3,64,128]{3,2,1,0:T(8,128)(2,1)S(1)}, bf16[1,3,64,128]{3,2,1,0:T(8,128)(2,1)S(1)}, u32[]{:S(2)}, u32[]{:S(2)}) collective-permute-start(bf16[1,3,64,128]{3,2,1,0:T(8,128)(2,1)S(1)} %get-tuple-element.32), channel_id=1, source_target_pairs={{0,8},{8,16},{16,24},{24,0},{1,9},{9,17},{17,25},{25,1},{2,10},{10... | collective-permute-start | bytes 147464 | tf_op jit(solution)/shard_map/ppermute | solution.py:339
  14.0 9.8 %collective-permute-start.3 = (bf16[1,3,64,128]{3,2,1,0:T(8,128)(2,1)S(1)}, bf16[1,3,64,128]{3,2,1,0:T(8,128)(2,1)S(1)}, u32[]{:S(2)}, u32[]{:S(2)}) collective-permute-start(bf16[1,3,64,128]{3,2,1,0:T(8,128)(2,1)S(1)} %get-tuple-element.33), channel_id=1, source_target_pairs={{8,0},{16,8},{24,16},{0,24},{9,1},{17,9},{25,17},{1,25},{10,2},{18... | collective-permute-start | bytes 147464 | tf_op jit(solution)/shard_map/ppermute | solution.py:340
  26.1 1.6 %collective-permute-start.4 = (bf16[16,64,128]{2,1,0:T(8,128)(2,1)S(1)}, bf16[16,64,128]{2,1,0:T(8,128)(2,1)S(1)}, u32[]{:S(2)}, u32[]{:S(2)}) collective-permute-start(bf16[16,64,128]{2,1,0:T(8,128)(2,1)S(1)} %shard_map.31), channel_id=1, source_target_pairs={{0,2},{2,0},{4,6},{6,4},{1,3},{3,1},{5,7},{7,5},{8,10},{10,8},{12,... | collective-permute-start | bytes 786440 | tf_op jit(solution)/shard_map/ppermute | solution.py:211
  30.6 4.1 %collective-permute-start.5 = (bf16[32,64,128]{2,1,0:T(8,128)(2,1)S(1)}, bf16[32,64,128]{2,1,0:T(8,128)(2,1)S(1)}, u32[]{:S(2)}, u32[]{:S(2)}) collective-permute-start(bf16[32,64,128]{2,1,0:T(8,128)(2,1)S(1)} %shard_map.33), channel_id=1, source_target_pairs={{0,2},{2,0},{4,6},{6,4},{1,3},{3,1},{5,7},{7,5},{8,10},{10,8},{12,... | collective-permute-start | bytes 1572872 | tf_op jit(solution)/shard_map/ppermute | solution.py:211
  31.1 10.1 %collective-permute-start.8 = (bf16[16,64,128]{2,1,0:T(8,128)(2,1)S(1)}, bf16[16,64,128]{2,1,0:T(8,128)(2,1)S(1)}, u32[]{:S(2)}, u32[]{:S(2)}) collective-permute-start(bf16[16,64,128]{2,1,0:T(8,128)(2,1)S(1)} %add_convert_fusion), channel_id=1, source_target_pairs={{0,12},{2,14},{4,8},{6,10},{8,4},{10,6},{12,0},{14,2},{16,28},{18,... | collective-permute-start | bytes 786440 | tf_op jit(solution)/shard_map/ppermute | solution.py:211
  34.8 11.1 %collective-permute-start.6 = (bf16[16,64,128]{2,1,0:T(8,128)(2,1)S(1)}, bf16[16,64,128]{2,1,0:T(8,128)(2,1)S(1)}, u32[]{:S(2)}, u32[]{:S(2)}) collective-permute-start(bf16[16,64,128]{2,1,0:T(8,128)(2,1)S(1)} %get-tuple-element.40), channel_id=1, source_target_pairs={{0,4},{2,6},{4,0},{6,2},{1,5},{3,7},{5,1},{7,3},{8,12},{10,14},{12... | collective-permute-start | bytes 786440 | tf_op jit(solution)/shard_map/ppermute | solution.py:211
  35.7 10.5 %collective-permute-start.7 = (bf16[16,64,128]{2,1,0:T(8,128)(2,1)S(1)}, bf16[16,64,128]{2,1,0:T(8,128)(2,1)S(1)}, u32[]{:S(2)}, u32[]{:S(2)}) collective-permute-start(bf16[16,64,128]{2,1,0:T(8,128)(2,1)S(1)} %get-tuple-element.41), channel_id=1, source_target_pairs={{0,8},{8,0},{16,24},{24,16},{1,9},{9,1},{17,25},{25,17},{2,10},{10... | collective-permute-start | bytes 786440 | tf_op jit(solution)/shard_map/ppermute | solution.py:211
  41.2 5.1 %collective-permute-start.9 = (bf16[16,64,128]{2,1,0:T(8,128)(2,1)S(1)}, bf16[16,64,128]{2,1,0:T(8,128)(2,1)S(1)}, u32[]{:S(2)}, u32[]{:S(2)}) collective-permute-start(bf16[16,64,128]{2,1,0:T(8,128)(2,1)S(1)} %shard_map.35), channel_id=1, source_target_pairs={{0,2},{2,0},{4,6},{6,4},{1,3},{3,1},{5,7},{7,5},{8,10},{10,8},{12,... | collective-permute-start | bytes 786440 | tf_op jit(solution)/shard_map/ppermute | solution.py:211
  46.4 7.0 %collective-permute-start.10 = (bf16[4,64,128]{2,1,0:T(8,128)(2,1)S(1)}, bf16[4,64,128]{2,1,0:T(8,128)(2,1)S(1)}, u32[]{:S(2)}, u32[]{:S(2)}) collective-permute-start(bf16[4,64,128]{2,1,0:T(8,128)(2,1)S(1)} %get-tuple-element.48), channel_id=1, source_target_pairs={{0,16},{8,24},{16,0},{24,8},{1,17},{9,25},{17,1},{25,9},{2,18},{10... | collective-permute-start | bytes 196616 | tf_op jit(solution)/shard_map/ppermute | solution.py:211
  47.2 9.0 %collective-permute-start.11 = (bf16[4,64,128]{2,1,0:T(8,128)(2,1)S(1)}, bf16[4,64,128]{2,1,0:T(8,128)(2,1)S(1)}, u32[]{:S(2)}, u32[]{:S(2)}) collective-permute-start(bf16[4,64,128]{2,1,0:T(8,128)(2,1)S(1)} %get-tuple-element.49), channel_id=1, source_target_pairs={{0,17},{1,16},{8,25},{9,24},{16,1},{17,0},{24,9},{25,8},{2,19},{3,... | collective-permute-start | bytes 196616 | tf_op jit(solution)/shard_map/ppermute | solution.py:211
  50.3 5.9 %collective-permute-start.12 = (bf16[4,64,128]{2,1,0:T(8,128)(2,1)S(1)}, bf16[4,64,128]{2,1,0:T(8,128)(2,1)S(1)}, u32[]{:S(2)}, u32[]{:S(2)}) collective-permute-start(bf16[4,64,128]{2,1,0:T(8,128)(2,1)S(1)} %get-tuple-element.50), channel_id=1, source_target_pairs={{0,1},{1,0},{2,3},{3,2},{4,5},{5,4},{6,7},{7,6},{8,9},{9,8},{10,11... | collective-permute-start | bytes 196616 | tf_op jit(solution)/shard_map/ppermute | solution.py:211

commit v14 on v13

--- a/solution.py
+++ b/solution.py
@@ -181,7 +181,7 @@
         in_specs=in_specs,
         out_specs=pl.BlockSpec(shape, lambda g: (g, 0, 0)),
         scratch_shapes=[
-            pltpu.VMEM((row_count, 3, modes, cells), F32),
+            pltpu.VMEM((row_count, 3, modes + 16, cells), F32),
             pltpu.VMEM((modes, row_count * 2 * cells), BF16),
         ],
         compiler_params=pltpu.CompilerParams(vmem_limit_bytes=24 << 20),

time: 57.2 us -> 57.2 us (level)
  no operation moved by 1% of the time
where the time goes in v14:
time: 57.2 us; the launch traced here: 57 us
  Pallas kernels  24.7 us (43%)
  starting transfers between devices  15.9 us (28%)
  waiting for transfers between devices  8.03 us (14%)
  blocking collectives  5.34 us (9%)
  local copies, waits for them, and re-layouts  2.63 us (5%)
    pallas_call x7, Pallas kernels, partial_tensor(): pl.pallas_call(body, grid=(len(blocks) // group,), out_shape=result((len(...  22.1 us
    ppermute x11, starting transfers between devices, flip(): return lax.ppermute(array, axes, [(i, i ^ change) for i in range(count)])  11.8 us
    ppermute x11, waiting for transfers between devices, flip(): return lax.ppermute(array, axes, [(i, i ^ change) for i in range(count)])  8.03 us
    all_gather x1, blocking collectives, shards(): columns = lax.all_gather(columns, 'gy')  5.34 us
    ppermute x1, starting transfers between devices, shards(): below = lax.ppermute(edges[1], 'gx', backward)  2.09 us
    ppermute x1, starting transfers between devices, shards(): above = lax.ppermute(edges[0], 'gx', forward)  2.08 us
    pallas_call x2, Pallas kernels, slopes_of(): pl.pallas_call(functools.partial(slopes_kernel, rows=rows), out_shape=jax...  1.4 us
    unnamed x3, local copies, waits for them, and re-layouts  1.34 us
  transfers between devices with their start and end apart: 13, of which 5 were waited for; matrix products, arithmetic and copies ran while one was open for 3% of the time, Pallas kernels for 34%

profile of v14, /device:TPU:0, one launch (start us, length us, event | category | flops | bytes accessed | tf_op | source)
XLA Modules:
  0.0 57.0 jit_solution(10772079590686222812)
XLA Ops:
  0.0 1.3 %copy.7 = bf16[3,64,16,128]{3,1,0,2:T(8,128)(2,1)S(1)} copy(bf16[3,64,16,128]{3,2,1,0:T(8,128)(2,1)} %param.2) | data formatting | bytes 1572864 | tf_op args[0]
  1.4 3.0 %collective-permute-start.1 = (bf16[8,3,64,128]{3,2,1,0:T(8,128)(2,1)S(1)}, bf16[8,3,64,128]{3,2,1,0:T(8,128)(2,1)S(1)}, u32[]{:S(2)}, u32[]{:S(2)}) collective-permute-start(bf16[8,3,64,128]{3,2,1,0:T(8,128)(2,1)S(1)} %slice.48.refs_1_), channel_id=1, source_target_pairs={{0,1},{1,0},{2,3},{3,2},{4,5},{5,4},{6,7},{7,6},{8,9},{9,8},{10,11... | collective-permute-start | bytes 1179656 | tf_op jit(solution)/shard_map/ppermute | solution.py:211
  4.4 1.2 %slice_reduce_fusion.1 = (bf16[16,3,64]{2,1,0:T(4,128)(2,1)S(1)}, bf16[16,3,64]{2,1,0:T(4,128)(2,1)S(1)}) fusion(bf16[16,3,64,128]{3,2,1,0:T(8,128)(2,1)S(1)} %bitcast.4), kind=kLoop, calls=%fused_computation.1 | loop fusion | bytes 24576 | tf_op jit(solution)/shard_map/slice | solution.py:333
  5.7 5.3 %all_gather.3.columns_ref = bf16[4,2,48,64]{3,2,1,0:T(8,128)(2,1)S(1)} all-gather(bf16[1,2,48,64]{3,2,1,0:T(8,128)(2,1)S(1)} %pad_maximum_fusion.1), channel_id=1, replica_groups=mesh['gx'=4,'gy'=4,'ma'=2] {'gy'}, dimensions={0}, use_global_device_ids=true | all-gather | bytes 61440 | tf_op jit(solution)/shard_map/all_gather | solution.py:334
  11.2 0.7 %shard_map.28.refs_3_ = bf16[8,6,64,128]{3,2,1,0:T(8,128)(2,1)S(1)} custom-call(bf16[16,3,64,128]{3,2,1,0:T(8,128)(2,1)S(1)} %bitcast.6, bf16[4,2,48,64]{3,2,1,0:T(8,128)(2,1)S(1)} %all_gather.3.columns_ref), custom_call_target="tpu_custom_call" | custom-call | flops 1 | bytes 1024 | tf_op jit(solution)/shard_map/pallas_call | solution.py:70
  11.9 2.1 %collective-permute-start.2 = (bf16[1,3,64,128]{3,2,1,0:T(8,128)(2,1)S(1)}, bf16[1,3,64,128]{3,2,1,0:T(8,128)(2,1)S(1)}, u32[]{:S(2)}, u32[]{:S(2)}) collective-permute-start(bf16[1,3,64,128]{3,2,1,0:T(8,128)(2,1)S(1)} %get-tuple-element.32), channel_id=1, source_target_pairs={{0,8},{8,16},{16,24},{24,0},{1,9},{9,17},{17,25},{25,1},{2,10},{10... | collective-permute-start | bytes 147464 | tf_op jit(solution)/shard_map/ppermute | solution.py:339
  14.0 2.1 %collective-permute-start.3 = (bf16[1,3,64,128]{3,2,1,0:T(8,128)(2,1)S(1)}, bf16[1,3,64,128]{3,2,1,0:T(8,128)(2,1)S(1)}, u32[]{:S(2)}, u32[]{:S(2)}) collective-permute-start(bf16[1,3,64,128]{3,2,1,0:T(8,128)(2,1)S(1)} %get-tuple-element.33), channel_id=1, source_target_pairs={{8,0},{16,8},{24,16},{0,24},{9,1},{17,9},{25,17},{1,25},{10,2},{18... | collective-permute-start | bytes 147464 | tf_op jit(solution)/shard_map/ppermute | solution.py:340
  16.1 7.7 %shard_map.29.refs_4_ = f32[96,64,128]{2,1,0:T(8,128)S(1)} custom-call(f32[16,128]{1,0:T(8,128)S(1)} %copy-done, bf16[8,3,64,128]{3,2,1,0:T(8,128)(2,1)S(1)} %slice.48.refs_1_, bf16[8,3,64,128]{3,2,1,0:T(8,128)(2,1)S(1)} %collective-permute-done.1.refs_2_, bf16[8,6,64,128]{3,2,1,0:T(8,128)(2,1)S(1)} %shard_map.28.refs_3_), custom_call_target="tpu_custom_call" | custom-call | flops 6442450944 | bytes 4194304 | tf_op jit(solution)/shard_map/pallas_call | solution.py:177
  23.8 0.7 %shard_map.30.refs_3_.refs_6_ = bf16[8,6,64,128]{3,2,1,0:T(8,128)(2,1)S(1)} custom-call(bf16[16,3,64,128]{3,2,1,0:T(8,128)(2,1)S(1)} %bitcast.8, bf16[4,2,48,64]{3,2,1,0:T(8,128)(2,1)S(1)} %all_gather.3.columns_ref, bf16[1,3,64,128]{3,2,1,0:T(8,128)(2,1)S(1)} %collective-permute-done.2.refs_0_, bf16[1,3,64,128]{3,2,1,0:T(8,128)(2,1)S(1)} %collective-permute-done.3.refs_1_), custom_call_target="tpu_custom_call" | custom-call | flops 1 | bytes 1024 | tf_op jit(solution)/shard_map/pallas_call | solution.py:70
  24.5 1.6 %shard_map.31 = bf16[16,64,128]{2,1,0:T(8,128)(2,1)S(1)} custom-call(f32[16,128]{1,0:T(8,128)S(1)} %copy-done, bf16[8,3,64,128]{3,2,1,0:T(8,128)(2,1)S(1)} %pad_maximum_fusion.refs_1_.refs_4_, bf16[8,3,64,128]{3,2,1,0:T(8,128)(2,1)S(1)} %collective-permute-done.refs_2_.refs_5_, bf16[8,6,64,128]{3,2,1,0:T(8,128)(2,1)S(1)} %shard_map.30.refs_3_.refs_6_, ...), custom_call_target="tpu_custom_call" | custom-call | flops 1073741824 | bytes 4194304 | tf_op jit(solution)/shard_map/pallas_call | solution.py:177
  26.2 1.5 %shard_map.32 = f32[16,64,128]{2,1,0:T(8,128)S(1)} custom-call(f32[16,128]{1,0:T(8,128)S(1)} %copy-done, bf16[8,3,64,128]{3,2,1,0:T(8,128)(2,1)S(1)} %pad_maximum_fusion.refs_1_.refs_4_, bf16[8,3,64,128]{3,2,1,0:T(8,128)(2,1)S(1)} %collective-permute-done.refs_2_.refs_5_, bf16[8,6,64,128]{3,2,1,0:T(8,128)(2,1)S(1)} %shard_map.30.refs_3_.refs_6_, ...), custom_call_target="tpu_custom_call" | custom-call | flops 1073741824 | bytes 4194304 | tf_op jit(solution)/shard_map/pallas_call | solution.py:177
  27.8 2.7 %shard_map.33 = bf16[32,64,128]{2,1,0:T(8,128)(2,1)S(1)} custom-call(f32[16,128]{1,0:T(8,128)S(1)} %copy-done, bf16[8,3,64,128]{3,2,1,0:T(8,128)(2,1)S(1)} %pad_maximum_fusion.refs_1_.refs_4_, bf16[8,3,64,128]{3,2,1,0:T(8,128)(2,1)S(1)} %collective-permute-done.refs_2_.refs_5_, bf16[8,6,64,128]{3,2,1,0:T(8,128)(2,1)S(1)} %shard_map.30.refs_3_.refs_6_, ...), custom_call_target="tpu_custom_call" | custom-call | flops 268435456 | bytes 4194304 | tf_op jit(solution)/shard_map/pallas_call | solution.py:177
  31.1 0.9 %collective-permute-start.8 = (bf16[16,64,128]{2,1,0:T(8,128)(2,1)S(1)}, bf16[16,64,128]{2,1,0:T(8,128)(2,1)S(1)}, u32[]{:S(2)}, u32[]{:S(2)}) collective-permute-start(bf16[16,64,128]{2,1,0:T(8,128)(2,1)S(1)} %add_convert_fusion), channel_id=1, source_target_pairs={{0,12},{2,14},{4,8},{6,10},{8,4},{10,6},{12,0},{14,2},{16,28},{18,... | collective-permute-start | bytes 786440 | tf_op jit(solution)/shard_map/ppermute | solution.py:211
  31.9 2.7 %shard_map.34 = f32[32,64,128]{2,1,0:T(8,128)S(1)} custom-call(f32[16,128]{1,0:T(8,128)S(1)} %copy-done, bf16[8,3,64,128]{3,2,1,0:T(8,128)(2,1)S(1)} %pad_maximum_fusion.refs_1_.refs_4_, bf16[8,3,64,128]{3,2,1,0:T(8,128)(2,1)S(1)} %collective-permute-done.refs_2_.refs_5_, bf16[8,6,64,128]{3,2,1,0:T(8,128)(2,1)S(1)} %shard_map.30.refs_3_.refs_6_, ...), custom_call_target="tpu_custom_call" | custom-call | flops 268435456 | bytes 4194304 | tf_op jit(solution)/shard_map/pallas_call | solution.py:177
  34.8 0.9 %collective-permute-start.6 = (bf16[16,64,128]{2,1,0:T(8,128)(2,1)S(1)}, bf16[16,64,128]{2,1,0:T(8,128)(2,1)S(1)}, u32[]{:S(2)}, u32[]{:S(2)}) collective-permute-start(bf16[16,64,128]{2,1,0:T(8,128)(2,1)S(1)} %get-tuple-element.40), channel_id=1, source_target_pairs={{0,4},{2,6},{4,0},{6,2},{1,5},{3,7},{5,1},{7,3},{8,12},{10,14},{12... | collective-permute-start | bytes 786440 | tf_op jit(solution)/shard_map/ppermute | solution.py:211
  35.6 1.8 %collective-permute-start.7 = (bf16[16,64,128]{2,1,0:T(8,128)(2,1)S(1)}, bf16[16,64,128]{2,1,0:T(8,128)(2,1)S(1)}, u32[]{:S(2)}, u32[]{:S(2)}) collective-permute-start(bf16[16,64,128]{2,1,0:T(8,128)(2,1)S(1)} %get-tuple-element.41), channel_id=1, source_target_pairs={{0,8},{8,0},{16,24},{24,16},{1,9},{9,1},{17,25},{25,17},{2,10},{10... | collective-permute-start | bytes 786440 | tf_op jit(solution)/shard_map/ppermute | solution.py:211
  37.5 3.1 %shard_map.35 = bf16[16,64,128]{2,1,0:T(8,128)(2,1)S(1)} custom-call(f32[16,128]{1,0:T(8,128)S(1)} %copy-done, bf16[8,3,64,128]{3,2,1,0:T(8,128)(2,1)S(1)} %slice.48.refs_1_, bf16[8,3,64,128]{3,2,1,0:T(8,128)(2,1)S(1)} %collective-permute-done.1.refs_2_, bf16[8,6,64,128]{3,2,1,0:T(8,128)(2,1)S(1)} %shard_map.28.refs_3_, ...), custom_call_target="tpu_custom_call" | custom-call | flops 268435456 | bytes 4194304 | tf_op jit(solution)/shard_map/pallas_call | solution.py:177
  41.2 2.9 %shard_map.37.refs_1_ = f32[16,64,128]{2,1,0:T(8,128)S(1)} custom-call(f32[16,128]{1,0:T(8,128)S(1)} %copy-done, bf16[8,3,64,128]{3,2,1,0:T(8,128)(2,1)S(1)} %slice.48.refs_1_, bf16[8,3,64,128]{3,2,1,0:T(8,128)(2,1)S(1)} %collective-permute-done.1.refs_2_, bf16[8,6,64,128]{3,2,1,0:T(8,128)(2,1)S(1)} %shard_map.28.refs_3_, ...), custom_call_target="tpu_custom_call" | custom-call | flops 268435456 | bytes 4194304 | tf_op jit(solution)/shard_map/pallas_call | solution.py:177
  44.0 1.8 %collective-permute-done.6.refs_0_ = bf16[16,64,128]{2,1,0:T(8,128)(2,1)S(1)} collective-permute-done((bf16[16,64,128]{2,1,0:T(8,128)(2,1)S(1)}, bf16[16,64,128]{2,1,0:T(8,128)(2,1)S(1)}, u32[]{:S(2)}, u32[]{:S(2)}) %collective-permute-start.6) | collective-permute-done | bytes 262176 | tf_op jit(solution)/shard_map/ppermute | solution.py:211
  46.4 0.8 %collective-permute-start.10 = (bf16[4,64,128]{2,1,0:T(8,128)(2,1)S(1)}, bf16[4,64,128]{2,1,0:T(8,128)(2,1)S(1)}, u32[]{:S(2)}, u32[]{:S(2)}) collective-permute-start(bf16[4,64,128]{2,1,0:T(8,128)(2,1)S(1)} %get-tuple-element.48), channel_id=1, source_target_pairs={{0,16},{8,24},{16,0},{24,8},{1,17},{9,25},{17,1},{25,9},{2,18},{10... | collective-permute-start | bytes 196616 | tf_op jit(solution)/shard_map/ppermute | solution.py:211
  47.2 3.1 %collective-permute-start.11 = (bf16[4,64,128]{2,1,0:T(8,128)(2,1)S(1)}, bf16[4,64,128]{2,1,0:T(8,128)(2,1)S(1)}, u32[]{:S(2)}, u32[]{:S(2)}) collective-permute-start(bf16[4,64,128]{2,1,0:T(8,128)(2,1)S(1)} %get-tuple-element.49), channel_id=1, source_target_pairs={{0,17},{1,16},{8,25},{9,24},{16,1},{17,0},{24,9},{25,8},{2,19},{3,... | collective-permute-start | bytes 196616 | tf_op jit(solution)/shard_map/ppermute | solution.py:211
  50.8 2.6 %collective-permute-done.10.above_ref = bf16[4,64,128]{2,1,0:T(8,128)(2,1)S(1)} collective-permute-done((bf16[4,64,128]{2,1,0:T(8,128)(2,1)S(1)}, bf16[4,64,128]{2,1,0:T(8,128)(2,1)S(1)}, u32[]{:S(2)}, u32[]{:S(2)}) %collective-permute-start.10) | collective-permute-done | bytes 65568 | tf_op jit(solution)/shard_map/ppermute | solution.py:211
  53.4 2.8 %collective-permute-done.11.both_ref = bf16[4,64,128]{2,1,0:T(8,128)(2,1)S(1)} collective-permute-done((bf16[4,64,128]{2,1,0:T(8,128)(2,1)S(1)}, bf16[4,64,128]{2,1,0:T(8,128)(2,1)S(1)}, u32[]{:S(2)}, u32[]{:S(2)}) %collective-permute-start.11) | collective-permute-done | bytes 65568 | tf_op jit(solution)/shard_map/ppermute | solution.py:211
  56.2 0.8 %shard_map.39 = f32[8,64,128]{2,1,0:T(8,128)} custom-call(f32[4,64,128]{2,1,0:T(8,128)S(1)} %get-tuple-element.47.own_ref, bf16[4,64,128]{2,1,0:T(8,128)(2,1)S(1)} %collective-permute-done.10.above_ref, bf16[4,64,128]{2,1,0:T(8,128)(2,1)S(1)} %collective-permute-done.11.both_ref, bf16[4,64,128]{2,1,0:T(8,128)(2,1)S(1)} %collective-permute-done.12.swapped_ref), custom_call_target="tpu_custom_call" | custom-call | flops 1 | bytes 1024 | tf_op jit(solution)/shard_map/pallas_call | solution.py:310
  (28 shorter events, 2.8 us)
Async XLA Ops:
  1.3 14.8 %copy-start = (f32[16,128]{1,0:T(8,128)S(1)}, f32[16,128]{1,0:T(8,128)}, u32[]{:S(2)}) copy-start(f32[16,128]{1,0:T(8,128)} %refs_0_.8) | copy-start | bytes 24580
  1.4 14.7 %collective-permute-start.1 = (bf16[8,3,64,128]{3,2,1,0:T(8,128)(2,1)S(1)}, bf16[8,3,64,128]{3,2,1,0:T(8,128)(2,1)S(1)}, u32[]{:S(2)}, u32[]{:S(2)}) collective-permute-start(bf16[8,3,64,128]{3,2,1,0:T(8,128)(2,1)S(1)} %slice.48.refs_1_), channel_id=1, source_target_pairs={{0,1},{1,0},{2,3},{3,2},{4,5},{5,4},{6,7},{7,6},{8,9},{9,8},{10,11... | collective-permute-start | bytes 1179656 | tf_op jit(solution)/shard_map/ppermute | solution.py:211
  11.0 13.5 %collective-permute-start = (bf16[8,3,64,128]{3,2,1,0:T(8,128)(2,1)S(1)}, bf16[8,3,64,128]{3,2,1,0:T(8,128)(2,1)S(1)}, u32[]{:S(2)}, u32[]{:S(2)}) collective-permute-start(bf16[8,3,64,128]{3,2,1,0:T(8,128)(2,1)S(1)} %pad_maximum_fusion.refs_1_.refs_4_), channel_id=1, source_target_pairs={{0,1},{1,0},{2,3},{3,2},{4,5},{5,4},{6,7},{7,6},{8,9},{9,8},{10,11... | collective-permute-start | bytes 1179656 | tf_op jit(solution)/shard_map/ppermute | solution.py:211
  11.9 11.9 %collective-permute-start.2 = (bf16[1,3,64,128]{3,2,1,0:T(8,128)(2,1)S(1)}, bf16[1,3,64,128]{3,2,1,0:T(8,128)(2,1)S(1)}, u32[]{:S(2)}, u32[]{:S(2)}) collective-permute-start(bf16[1,3,64,128]{3,2,1,0:T(8,128)(2,1)S(1)} %get-tuple-element.32), channel_id=1, source_target_pairs={{0,8},{8,16},{16,24},{24,0},{1,9},{9,17},{17,25},{25,1},{2,10},{10... | collective-permute-start | bytes 147464 | tf_op jit(solution)/shard_map/ppermute | solution.py:339
  14.0 9.8 %collective-permute-start.3 = (bf16[1,3,64,128]{3,2,1,0:T(8,128)(2,1)S(1)}, bf16[1,3,64,128]{3,2,1,0:T(8,128)(2,1)S(1)}, u32[]{:S(2)}, u32[]{:S(2)}) collective-permute-start(bf16[1,3,64,128]{3,2,1,0:T(8,128)(2,1)S(1)} %get-tuple-element.33), channel_id=1, source_target_pairs={{8,0},{16,8},{24,16},{0,24},{9,1},{17,9},{25,17},{1,25},{10,2},{18... | collective-permute-start | bytes 147464 | tf_op jit(solution)/shard_map/ppermute | solution.py:340
  26.1 1.6 %collective-permute-start.4 = (bf16[16,64,128]{2,1,0:T(8,128)(2,1)S(1)}, bf16[16,64,128]{2,1,0:T(8,128)(2,1)S(1)}, u32[]{:S(2)}, u32[]{:S(2)}) collective-permute-start(bf16[16,64,128]{2,1,0:T(8,128)(2,1)S(1)} %shard_map.31), channel_id=1, source_target_pairs={{0,2},{2,0},{4,6},{6,4},{1,3},{3,1},{5,7},{7,5},{8,10},{10,8},{12,... | collective-permute-start | bytes 786440 | tf_op jit(solution)/shard_map/ppermute | solution.py:211
  30.5 4.1 %collective-permute-start.5 = (bf16[32,64,128]{2,1,0:T(8,128)(2,1)S(1)}, bf16[32,64,128]{2,1,0:T(8,128)(2,1)S(1)}, u32[]{:S(2)}, u32[]{:S(2)}) collective-permute-start(bf16[32,64,128]{2,1,0:T(8,128)(2,1)S(1)} %shard_map.33), channel_id=1, source_target_pairs={{0,2},{2,0},{4,6},{6,4},{1,3},{3,1},{5,7},{7,5},{8,10},{10,8},{12,... | collective-permute-start | bytes 1572872 | tf_op jit(solution)/shard_map/ppermute | solution.py:211
  31.1 10.1 %collective-permute-start.8 = (bf16[16,64,128]{2,1,0:T(8,128)(2,1)S(1)}, bf16[16,64,128]{2,1,0:T(8,128)(2,1)S(1)}, u32[]{:S(2)}, u32[]{:S(2)}) collective-permute-start(bf16[16,64,128]{2,1,0:T(8,128)(2,1)S(1)} %add_convert_fusion), channel_id=1, source_target_pairs={{0,12},{2,14},{4,8},{6,10},{8,4},{10,6},{12,0},{14,2},{16,28},{18,... | collective-permute-start | bytes 786440 | tf_op jit(solution)/shard_map/ppermute | solution.py:211
  34.8 11.1 %collective-permute-start.6 = (bf16[16,64,128]{2,1,0:T(8,128)(2,1)S(1)}, bf16[16,64,128]{2,1,0:T(8,128)(2,1)S(1)}, u32[]{:S(2)}, u32[]{:S(2)}) collective-permute-start(bf16[16,64,128]{2,1,0:T(8,128)(2,1)S(1)} %get-tuple-element.40), channel_id=1, source_target_pairs={{0,4},{2,6},{4,0},{6,2},{1,5},{3,7},{5,1},{7,3},{8,12},{10,14},{12... | collective-permute-start | bytes 786440 | tf_op jit(solution)/shard_map/ppermute | solution.py:211
  35.6 10.5 %collective-permute-start.7 = (bf16[16,64,128]{2,1,0:T(8,128)(2,1)S(1)}, bf16[16,64,128]{2,1,0:T(8,128)(2,1)S(1)}, u32[]{:S(2)}, u32[]{:S(2)}) collective-permute-start(bf16[16,64,128]{2,1,0:T(8,128)(2,1)S(1)} %get-tuple-element.41), channel_id=1, source_target_pairs={{0,8},{8,0},{16,24},{24,16},{1,9},{9,1},{17,25},{25,17},{2,10},{10... | collective-permute-start | bytes 786440 | tf_op jit(solution)/shard_map/ppermute | solution.py:211
  41.2 5.0 %collective-permute-start.9 = (bf16[16,64,128]{2,1,0:T(8,128)(2,1)S(1)}, bf16[16,64,128]{2,1,0:T(8,128)(2,1)S(1)}, u32[]{:S(2)}, u32[]{:S(2)}) collective-permute-start(bf16[16,64,128]{2,1,0:T(8,128)(2,1)S(1)} %shard_map.35), channel_id=1, source_target_pairs={{0,2},{2,0},{4,6},{6,4},{1,3},{3,1},{5,7},{7,5},{8,10},{10,8},{12,... | collective-permute-start | bytes 786440 | tf_op jit(solution)/shard_map/ppermute | solution.py:211
  46.4 7.0 %collective-permute-start.10 = (bf16[4,64,128]{2,1,0:T(8,128)(2,1)S(1)}, bf16[4,64,128]{2,1,0:T(8,128)(2,1)S(1)}, u32[]{:S(2)}, u32[]{:S(2)}) collective-permute-start(bf16[4,64,128]{2,1,0:T(8,128)(2,1)S(1)} %get-tuple-element.48), channel_id=1, source_target_pairs={{0,16},{8,24},{16,0},{24,8},{1,17},{9,25},{17,1},{25,9},{2,18},{10... | collective-permute-start | bytes 196616 | tf_op jit(solution)/shard_map/ppermute | solution.py:211
  47.2 9.0 %collective-permute-start.11 = (bf16[4,64,128]{2,1,0:T(8,128)(2,1)S(1)}, bf16[4,64,128]{2,1,0:T(8,128)(2,1)S(1)}, u32[]{:S(2)}, u32[]{:S(2)}) collective-permute-start(bf16[4,64,128]{2,1,0:T(8,128)(2,1)S(1)} %get-tuple-element.49), channel_id=1, source_target_pairs={{0,17},{1,16},{8,25},{9,24},{16,1},{17,0},{24,9},{25,8},{2,19},{3,... | collective-permute-start | bytes 196616 | tf_op jit(solution)/shard_map/ppermute | solution.py:211
  50.3 5.9 %collective-permute-start.12 = (bf16[4,64,128]{2,1,0:T(8,128)(2,1)S(1)}, bf16[4,64,128]{2,1,0:T(8,128)(2,1)S(1)}, u32[]{:S(2)}, u32[]{:S(2)}) collective-permute-start(bf16[4,64,128]{2,1,0:T(8,128)(2,1)S(1)} %get-tuple-element.50), channel_id=1, source_target_pairs={{0,1},{1,0},{2,3},{3,2},{4,5},{5,4},{6,7},{7,6},{8,9},{9,8},{10,11... | collective-permute-start | bytes 196616 | tf_op jit(solution)/shard_map/ppermute | solution.py:211

commit v15 on v14

--- a/solution.py
+++ b/solution.py
@@ -256,7 +256,7 @@
                 out[place] = total[swapped * share : (swapped + 1) * share].astype(out.dtype)
 
 
-def assemble_kernel(own_ref, above_ref, both_ref, swapped_ref, out_ref, *, pair):
+def assemble_kernel(own_ref, both_ref, above_ref, swapped_ref, out_ref, *, pair):
     count, share, width = own_ref.shape
     first = lax.axis_index("ma") == 0
     for place in range(count):
@@ -314,7 +314,7 @@
         out_specs=pl.BlockSpec(memory_space=pltpu.VMEM),
         compiler_params=pltpu.CompilerParams(vmem_limit_bytes=16 << 20),
         cost_estimate=pl.CostEstimate(flops=1, bytes_accessed=1024, transcendentals=0),
-    )(parts[0], arrived[2], arrived[3], arrived[1])
+    )(parts[0], arrived[3], arrived[2], arrived[1])
 
 
 def shards(mode_fields, cell_volumes, sizes):

time: 57.2 us -> 57.2 us (level)
  no operation moved by 1% of the time
where the time goes in v15:
time: 57.2 us; the launch traced here: 57 us
  Pallas kernels  24.7 us (43%)
  starting transfers between devices  15.9 us (28%)
  waiting for transfers between devices  8.03 us (14%)
  blocking collectives  5.34 us (9%)
  local copies, waits for them, and re-layouts  2.63 us (5%)
    pallas_call x7, Pallas kernels, partial_tensor(): pl.pallas_call(body, grid=(len(blocks) // group,), out_shape=result((len(...  22.1 us
    ppermute x11, starting transfers between devices, flip(): return lax.ppermute(array, axes, [(i, i ^ change) for i in range(count)])  11.8 us
    ppermute x11, waiting for transfers between devices, flip(): return lax.ppermute(array, axes, [(i, i ^ change) for i in range(count)])  8.03 us
    all_gather x1, blocking collectives, shards(): columns = lax.all_gather(columns, 'gy')  5.34 us
    ppermute x1, starting transfers between devices, shards(): below = lax.ppermute(edges[1], 'gx', backward)  2.09 us
    ppermute x1, starting transfers between devices, shards(): above = lax.ppermute(edges[0], 'gx', forward)  2.08 us
    pallas_call x2, Pallas kernels, slopes_of(): pl.pallas_call(functools.partial(slopes_kernel, rows=rows), out_shape=jax...  1.4 us
    unnamed x3, local copies, waits for them, and re-layouts  1.34 us
  transfers between devices with their start and end apart: 13, of which 5 were waited for; matrix products, arithmetic and copies ran while one was open for 3% of the time, Pallas kernels for 34%

profile of v15, /device:TPU:0, one launch (start us, length us, event | category | flops | bytes accessed | tf_op | source)
XLA Modules:
  0.0 57.0 jit_solution(16790530110137459743)
XLA Ops:
  0.0 1.3 %copy.7 = bf16[3,64,16,128]{3,1,0,2:T(8,128)(2,1)S(1)} copy(bf16[3,64,16,128]{3,2,1,0:T(8,128)(2,1)} %param.2) | data formatting | bytes 1572864 | tf_op args[0]
  1.4 3.0 %collective-permute-start.1 = (bf16[8,3,64,128]{3,2,1,0:T(8,128)(2,1)S(1)}, bf16[8,3,64,128]{3,2,1,0:T(8,128)(2,1)S(1)}, u32[]{:S(2)}, u32[]{:S(2)}) collective-permute-start(bf16[8,3,64,128]{3,2,1,0:T(8,128)(2,1)S(1)} %slice.48.refs_1_), channel_id=1, source_target_pairs={{0,1},{1,0},{2,3},{3,2},{4,5},{5,4},{6,7},{7,6},{8,9},{9,8},{10,11... | collective-permute-start | bytes 1179656 | tf_op jit(solution)/shard_map/ppermute | solution.py:211
  4.4 1.2 %slice_reduce_fusion.1 = (bf16[16,3,64]{2,1,0:T(4,128)(2,1)S(1)}, bf16[16,3,64]{2,1,0:T(4,128)(2,1)S(1)}) fusion(bf16[16,3,64,128]{3,2,1,0:T(8,128)(2,1)S(1)} %bitcast.4), kind=kLoop, calls=%fused_computation.1 | loop fusion | bytes 24576 | tf_op jit(solution)/shard_map/slice | solution.py:333
  5.7 5.3 %all_gather.3.columns_ref = bf16[4,2,48,64]{3,2,1,0:T(8,128)(2,1)S(1)} all-gather(bf16[1,2,48,64]{3,2,1,0:T(8,128)(2,1)S(1)} %pad_maximum_fusion.1), channel_id=1, replica_groups=mesh['gx'=4,'gy'=4,'ma'=2] {'gy'}, dimensions={0}, use_global_device_ids=true | all-gather | bytes 61440 | tf_op jit(solution)/shard_map/all_gather | solution.py:334
  11.2 0.7 %shard_map.28.refs_3_ = bf16[8,6,64,128]{3,2,1,0:T(8,128)(2,1)S(1)} custom-call(bf16[16,3,64,128]{3,2,1,0:T(8,128)(2,1)S(1)} %bitcast.6, bf16[4,2,48,64]{3,2,1,0:T(8,128)(2,1)S(1)} %all_gather.3.columns_ref), custom_call_target="tpu_custom_call" | custom-call | flops 1 | bytes 1024 | tf_op jit(solution)/shard_map/pallas_call | solution.py:70
  11.9 2.1 %collective-permute-start.2 = (bf16[1,3,64,128]{3,2,1,0:T(8,128)(2,1)S(1)}, bf16[1,3,64,128]{3,2,1,0:T(8,128)(2,1)S(1)}, u32[]{:S(2)}, u32[]{:S(2)}) collective-permute-start(bf16[1,3,64,128]{3,2,1,0:T(8,128)(2,1)S(1)} %get-tuple-element.32), channel_id=1, source_target_pairs={{0,8},{8,16},{16,24},{24,0},{1,9},{9,17},{17,25},{25,1},{2,10},{10... | collective-permute-start | bytes 147464 | tf_op jit(solution)/shard_map/ppermute | solution.py:339
  14.0 2.1 %collective-permute-start.3 = (bf16[1,3,64,128]{3,2,1,0:T(8,128)(2,1)S(1)}, bf16[1,3,64,128]{3,2,1,0:T(8,128)(2,1)S(1)}, u32[]{:S(2)}, u32[]{:S(2)}) collective-permute-start(bf16[1,3,64,128]{3,2,1,0:T(8,128)(2,1)S(1)} %get-tuple-element.33), channel_id=1, source_target_pairs={{8,0},{16,8},{24,16},{0,24},{9,1},{17,9},{25,17},{1,25},{10,2},{18... | collective-permute-start | bytes 147464 | tf_op jit(solution)/shard_map/ppermute | solution.py:340
  16.1 7.7 %shard_map.29.refs_4_ = f32[96,64,128]{2,1,0:T(8,128)S(1)} custom-call(f32[16,128]{1,0:T(8,128)S(1)} %copy-done, bf16[8,3,64,128]{3,2,1,0:T(8,128)(2,1)S(1)} %slice.48.refs_1_, bf16[8,3,64,128]{3,2,1,0:T(8,128)(2,1)S(1)} %collective-permute-done.1.refs_2_, bf16[8,6,64,128]{3,2,1,0:T(8,128)(2,1)S(1)} %shard_map.28.refs_3_), custom_call_target="tpu_custom_call" | custom-call | flops 6442450944 | bytes 4194304 | tf_op jit(solution)/shard_map/pallas_call | solution.py:177
  23.8 0.7 %shard_map.30.refs_3_.refs_6_ = bf16[8,6,64,128]{3,2,1,0:T(8,128)(2,1)S(1)} custom-call(bf16[16,3,64,128]{3,2,1,0:T(8,128)(2,1)S(1)} %bitcast.8, bf16[4,2,48,64]{3,2,1,0:T(8,128)(2,1)S(1)} %all_gather.3.columns_ref, bf16[1,3,64,128]{3,2,1,0:T(8,128)(2,1)S(1)} %collective-permute-done.2.refs_0_, bf16[1,3,64,128]{3,2,1,0:T(8,128)(2,1)S(1)} %collective-permute-done.3.refs_1_), custom_call_target="tpu_custom_call" | custom-call | flops 1 | bytes 1024 | tf_op jit(solution)/shard_map/pallas_call | solution.py:70
  24.5 1.6 %shard_map.31 = bf16[16,64,128]{2,1,0:T(8,128)(2,1)S(1)} custom-call(f32[16,128]{1,0:T(8,128)S(1)} %copy-done, bf16[8,3,64,128]{3,2,1,0:T(8,128)(2,1)S(1)} %pad_maximum_fusion.refs_1_.refs_4_, bf16[8,3,64,128]{3,2,1,0:T(8,128)(2,1)S(1)} %collective-permute-done.refs_2_.refs_5_, bf16[8,6,64,128]{3,2,1,0:T(8,128)(2,1)S(1)} %shard_map.30.refs_3_.refs_6_, ...), custom_call_target="tpu_custom_call" | custom-call | flops 1073741824 | bytes 4194304 | tf_op jit(solution)/shard_map/pallas_call | solution.py:177
  26.2 1.5 %shard_map.32 = f32[16,64,128]{2,1,0:T(8,128)S(1)} custom-call(f32[16,128]{1,0:T(8,128)S(1)} %copy-done, bf16[8,3,64,128]{3,2,1,0:T(8,128)(2,1)S(1)} %pad_maximum_fusion.refs_1_.refs_4_, bf16[8,3,64,128]{3,2,1,0:T(8,128)(2,1)S(1)} %collective-permute-done.refs_2_.refs_5_, bf16[8,6,64,128]{3,2,1,0:T(8,128)(2,1)S(1)} %shard_map.30.refs_3_.refs_6_, ...), custom_call_target="tpu_custom_call" | custom-call | flops 1073741824 | bytes 4194304 | tf_op jit(solution)/shard_map/pallas_call | solution.py:177
  27.8 2.7 %shard_map.33 = bf16[32,64,128]{2,1,0:T(8,128)(2,1)S(1)} custom-call(f32[16,128]{1,0:T(8,128)S(1)} %copy-done, bf16[8,3,64,128]{3,2,1,0:T(8,128)(2,1)S(1)} %pad_maximum_fusion.refs_1_.refs_4_, bf16[8,3,64,128]{3,2,1,0:T(8,128)(2,1)S(1)} %collective-permute-done.refs_2_.refs_5_, bf16[8,6,64,128]{3,2,1,0:T(8,128)(2,1)S(1)} %shard_map.30.refs_3_.refs_6_, ...), custom_call_target="tpu_custom_call" | custom-call | flops 268435456 | bytes 4194304 | tf_op jit(solution)/shard_map/pallas_call | solution.py:177
  31.1 0.9 %collective-permute-start.8 = (bf16[16,64,128]{2,1,0:T(8,128)(2,1)S(1)}, bf16[16,64,128]{2,1,0:T(8,128)(2,1)S(1)}, u32[]{:S(2)}, u32[]{:S(2)}) collective-permute-start(bf16[16,64,128]{2,1,0:T(8,128)(2,1)S(1)} %add_convert_fusion), channel_id=1, source_target_pairs={{0,12},{2,14},{4,8},{6,10},{8,4},{10,6},{12,0},{14,2},{16,28},{18,... | collective-permute-start | bytes 786440 | tf_op jit(solution)/shard_map/ppermute | solution.py:211
  31.9 2.7 %shard_map.34 = f32[32,64,128]{2,1,0:T(8,128)S(1)} custom-call(f32[16,128]{1,0:T(8,128)S(1)} %copy-done, bf16[8,3,64,128]{3,2,1,0:T(8,128)(2,1)S(1)} %pad_maximum_fusion.refs_1_.refs_4_, bf16[8,3,64,128]{3,2,1,0:T(8,128)(2,1)S(1)} %collective-permute-done.refs_2_.refs_5_, bf16[8,6,64,128]{3,2,1,0:T(8,128)(2,1)S(1)} %shard_map.30.refs_3_.refs_6_, ...), custom_call_target="tpu_custom_call" | custom-call | flops 268435456 | bytes 4194304 | tf_op jit(solution)/shard_map/pallas_call | solution.py:177
  34.8 0.9 %collective-permute-start.6 = (bf16[16,64,128]{2,1,0:T(8,128)(2,1)S(1)}, bf16[16,64,128]{2,1,0:T(8,128)(2,1)S(1)}, u32[]{:S(2)}, u32[]{:S(2)}) collective-permute-start(bf16[16,64,128]{2,1,0:T(8,128)(2,1)S(1)} %get-tuple-element.40), channel_id=1, source_target_pairs={{0,4},{2,6},{4,0},{6,2},{1,5},{3,7},{5,1},{7,3},{8,12},{10,14},{12... | collective-permute-start | bytes 786440 | tf_op jit(solution)/shard_map/ppermute | solution.py:211
  35.6 1.8 %collective-permute-start.7 = (bf16[16,64,128]{2,1,0:T(8,128)(2,1)S(1)}, bf16[16,64,128]{2,1,0:T(8,128)(2,1)S(1)}, u32[]{:S(2)}, u32[]{:S(2)}) collective-permute-start(bf16[16,64,128]{2,1,0:T(8,128)(2,1)S(1)} %get-tuple-element.41), channel_id=1, source_target_pairs={{0,8},{8,0},{16,24},{24,16},{1,9},{9,1},{17,25},{25,17},{2,10},{10... | collective-permute-start | bytes 786440 | tf_op jit(solution)/shard_map/ppermute | solution.py:211
  37.5 3.1 %shard_map.35 = bf16[16,64,128]{2,1,0:T(8,128)(2,1)S(1)} custom-call(f32[16,128]{1,0:T(8,128)S(1)} %copy-done, bf16[8,3,64,128]{3,2,1,0:T(8,128)(2,1)S(1)} %slice.48.refs_1_, bf16[8,3,64,128]{3,2,1,0:T(8,128)(2,1)S(1)} %collective-permute-done.1.refs_2_, bf16[8,6,64,128]{3,2,1,0:T(8,128)(2,1)S(1)} %shard_map.28.refs_3_, ...), custom_call_target="tpu_custom_call" | custom-call | flops 268435456 | bytes 4194304 | tf_op jit(solution)/shard_map/pallas_call | solution.py:177
  41.2 2.9 %shard_map.37.refs_1_ = f32[16,64,128]{2,1,0:T(8,128)S(1)} custom-call(f32[16,128]{1,0:T(8,128)S(1)} %copy-done, bf16[8,3,64,128]{3,2,1,0:T(8,128)(2,1)S(1)} %slice.48.refs_1_, bf16[8,3,64,128]{3,2,1,0:T(8,128)(2,1)S(1)} %collective-permute-done.1.refs_2_, bf16[8,6,64,128]{3,2,1,0:T(8,128)(2,1)S(1)} %shard_map.28.refs_3_, ...), custom_call_target="tpu_custom_call" | custom-call | flops 268435456 | bytes 4194304 | tf_op jit(solution)/shard_map/pallas_call | solution.py:177
  44.0 1.8 %collective-permute-done.6.refs_0_ = bf16[16,64,128]{2,1,0:T(8,128)(2,1)S(1)} collective-permute-done((bf16[16,64,128]{2,1,0:T(8,128)(2,1)S(1)}, bf16[16,64,128]{2,1,0:T(8,128)(2,1)S(1)}, u32[]{:S(2)}, u32[]{:S(2)}) %collective-permute-start.6) | collective-permute-done | bytes 262176 | tf_op jit(solution)/shard_map/ppermute | solution.py:211
  46.4 1.7 %collective-permute-start.10 = (bf16[4,64,128]{2,1,0:T(8,128)(2,1)S(1)}, bf16[4,64,128]{2,1,0:T(8,128)(2,1)S(1)}, u32[]{:S(2)}, u32[]{:S(2)}) collective-permute-start(bf16[4,64,128]{2,1,0:T(8,128)(2,1)S(1)} %get-tuple-element.48), channel_id=1, source_target_pairs={{0,17},{1,16},{8,25},{9,24},{16,1},{17,0},{24,9},{25,8},{2,19},{3,... | collective-permute-start | bytes 196616 | tf_op jit(solution)/shard_map/ppermute | solution.py:211
  48.1 2.2 %collective-permute-start.11 = (bf16[4,64,128]{2,1,0:T(8,128)(2,1)S(1)}, bf16[4,64,128]{2,1,0:T(8,128)(2,1)S(1)}, u32[]{:S(2)}, u32[]{:S(2)}) collective-permute-start(bf16[4,64,128]{2,1,0:T(8,128)(2,1)S(1)} %get-tuple-element.49), channel_id=1, source_target_pairs={{0,16},{8,24},{16,0},{24,8},{1,17},{9,25},{17,1},{25,9},{2,18},{10... | collective-permute-start | bytes 196616 | tf_op jit(solution)/shard_map/ppermute | solution.py:211
  50.8 4.2 %collective-permute-done.10.both_ref = bf16[4,64,128]{2,1,0:T(8,128)(2,1)S(1)} collective-permute-done((bf16[4,64,128]{2,1,0:T(8,128)(2,1)S(1)}, bf16[4,64,128]{2,1,0:T(8,128)(2,1)S(1)}, u32[]{:S(2)}, u32[]{:S(2)}) %collective-permute-start.10) | collective-permute-done | bytes 65568 | tf_op jit(solution)/shard_map/ppermute | solution.py:211
  55.0 1.2 %collective-permute-done.11.above_ref = bf16[4,64,128]{2,1,0:T(8,128)(2,1)S(1)} collective-permute-done((bf16[4,64,128]{2,1,0:T(8,128)(2,1)S(1)}, bf16[4,64,128]{2,1,0:T(8,128)(2,1)S(1)}, u32[]{:S(2)}, u32[]{:S(2)}) %collective-permute-start.11) | collective-permute-done | bytes 65568 | tf_op jit(solution)/shard_map/ppermute | solution.py:211
  56.2 0.8 %shard_map.39 = f32[8,64,128]{2,1,0:T(8,128)} custom-call(f32[4,64,128]{2,1,0:T(8,128)S(1)} %get-tuple-element.47.own_ref, bf16[4,64,128]{2,1,0:T(8,128)(2,1)S(1)} %collective-permute-done.10.both_ref, bf16[4,64,128]{2,1,0:T(8,128)(2,1)S(1)} %collective-permute-done.11.above_ref, bf16[4,64,128]{2,1,0:T(8,128)(2,1)S(1)} %collective-permute-done.12.swapped_ref), custom_call_target="tpu_custom_call" | custom-call | flops 1 | bytes 1024 | tf_op jit(solution)/shard_map/pallas_call | solution.py:310
  (28 shorter events, 2.8 us)
Async XLA Ops:
  1.3 14.8 %copy-start = (f32[16,128]{1,0:T(8,128)S(1)}, f32[16,128]{1,0:T(8,128)}, u32[]{:S(2)}) copy-start(f32[16,128]{1,0:T(8,128)} %refs_0_.8) | copy-start | bytes 24580
  1.4 14.7 %collective-permute-start.1 = (bf16[8,3,64,128]{3,2,1,0:T(8,128)(2,1)S(1)}, bf16[8,3,64,128]{3,2,1,0:T(8,128)(2,1)S(1)}, u32[]{:S(2)}, u32[]{:S(2)}) collective-permute-start(bf16[8,3,64,128]{3,2,1,0:T(8,128)(2,1)S(1)} %slice.48.refs_1_), channel_id=1, source_target_pairs={{0,1},{1,0},{2,3},{3,2},{4,5},{5,4},{6,7},{7,6},{8,9},{9,8},{10,11... | collective-permute-start | bytes 1179656 | tf_op jit(solution)/shard_map/ppermute | solution.py:211
  11.0 13.5 %collective-permute-start = (bf16[8,3,64,128]{3,2,1,0:T(8,128)(2,1)S(1)}, bf16[8,3,64,128]{3,2,1,0:T(8,128)(2,1)S(1)}, u32[]{:S(2)}, u32[]{:S(2)}) collective-permute-start(bf16[8,3,64,128]{3,2,1,0:T(8,128)(2,1)S(1)} %pad_maximum_fusion.refs_1_.refs_4_), channel_id=1, source_target_pairs={{0,1},{1,0},{2,3},{3,2},{4,5},{5,4},{6,7},{7,6},{8,9},{9,8},{10,11... | collective-permute-start | bytes 1179656 | tf_op jit(solution)/shard_map/ppermute | solution.py:211
  11.9 11.9 %collective-permute-start.2 = (bf16[1,3,64,128]{3,2,1,0:T(8,128)(2,1)S(1)}, bf16[1,3,64,128]{3,2,1,0:T(8,128)(2,1)S(1)}, u32[]{:S(2)}, u32[]{:S(2)}) collective-permute-start(bf16[1,3,64,128]{3,2,1,0:T(8,128)(2,1)S(1)} %get-tuple-element.32), channel_id=1, source_target_pairs={{0,8},{8,16},{16,24},{24,0},{1,9},{9,17},{17,25},{25,1},{2,10},{10... | collective-permute-start | bytes 147464 | tf_op jit(solution)/shard_map/ppermute | solution.py:339
  14.0 9.8 %collective-permute-start.3 = (bf16[1,3,64,128]{3,2,1,0:T(8,128)(2,1)S(1)}, bf16[1,3,64,128]{3,2,1,0:T(8,128)(2,1)S(1)}, u32[]{:S(2)}, u32[]{:S(2)}) collective-permute-start(bf16[1,3,64,128]{3,2,1,0:T(8,128)(2,1)S(1)} %get-tuple-element.33), channel_id=1, source_target_pairs={{8,0},{16,8},{24,16},{0,24},{9,1},{17,9},{25,17},{1,25},{10,2},{18... | collective-permute-start | bytes 147464 | tf_op jit(solution)/shard_map/ppermute | solution.py:340
  26.1 1.6 %collective-permute-start.4 = (bf16[16,64,128]{2,1,0:T(8,128)(2,1)S(1)}, bf16[16,64,128]{2,1,0:T(8,128)(2,1)S(1)}, u32[]{:S(2)}, u32[]{:S(2)}) collective-permute-start(bf16[16,64,128]{2,1,0:T(8,128)(2,1)S(1)} %shard_map.31), channel_id=1, source_target_pairs={{0,2},{2,0},{4,6},{6,4},{1,3},{3,1},{5,7},{7,5},{8,10},{10,8},{12,... | collective-permute-start | bytes 786440 | tf_op jit(solution)/shard_map/ppermute | solution.py:211
  30.5 4.1 %collective-permute-start.5 = (bf16[32,64,128]{2,1,0:T(8,128)(2,1)S(1)}, bf16[32,64,128]{2,1,0:T(8,128)(2,1)S(1)}, u32[]{:S(2)}, u32[]{:S(2)}) collective-permute-start(bf16[32,64,128]{2,1,0:T(8,128)(2,1)S(1)} %shard_map.33), channel_id=1, source_target_pairs={{0,2},{2,0},{4,6},{6,4},{1,3},{3,1},{5,7},{7,5},{8,10},{10,8},{12,... | collective-permute-start | bytes 1572872 | tf_op jit(solution)/shard_map/ppermute | solution.py:211
  31.1 10.1 %collective-permute-start.8 = (bf16[16,64,128]{2,1,0:T(8,128)(2,1)S(1)}, bf16[16,64,128]{2,1,0:T(8,128)(2,1)S(1)}, u32[]{:S(2)}, u32[]{:S(2)}) collective-permute-start(bf16[16,64,128]{2,1,0:T(8,128)(2,1)S(1)} %add_convert_fusion), channel_id=1, source_target_pairs={{0,12},{2,14},{4,8},{6,10},{8,4},{10,6},{12,0},{14,2},{16,28},{18,... | collective-permute-start | bytes 786440 | tf_op jit(solution)/shard_map/ppermute | solution.py:211
  34.8 11.1 %collective-permute-start.6 = (bf16[16,64,128]{2,1,0:T(8,128)(2,1)S(1)}, bf16[16,64,128]{2,1,0:T(8,128)(2,1)S(1)}, u32[]{:S(2)}, u32[]{:S(2)}) collective-permute-start(bf16[16,64,128]{2,1,0:T(8,128)(2,1)S(1)} %get-tuple-element.40), channel_id=1, source_target_pairs={{0,4},{2,6},{4,0},{6,2},{1,5},{3,7},{5,1},{7,3},{8,12},{10,14},{12... | collective-permute-start | bytes 786440 | tf_op jit(solution)/shard_map/ppermute | solution.py:211
  35.6 10.5 %collective-permute-start.7 = (bf16[16,64,128]{2,1,0:T(8,128)(2,1)S(1)}, bf16[16,64,128]{2,1,0:T(8,128)(2,1)S(1)}, u32[]{:S(2)}, u32[]{:S(2)}) collective-permute-start(bf16[16,64,128]{2,1,0:T(8,128)(2,1)S(1)} %get-tuple-element.41), channel_id=1, source_target_pairs={{0,8},{8,0},{16,24},{24,16},{1,9},{9,1},{17,25},{25,17},{2,10},{10... | collective-permute-start | bytes 786440 | tf_op jit(solution)/shard_map/ppermute | solution.py:211
  41.2 5.0 %collective-permute-start.9 = (bf16[16,64,128]{2,1,0:T(8,128)(2,1)S(1)}, bf16[16,64,128]{2,1,0:T(8,128)(2,1)S(1)}, u32[]{:S(2)}, u32[]{:S(2)}) collective-permute-start(bf16[16,64,128]{2,1,0:T(8,128)(2,1)S(1)} %shard_map.35), channel_id=1, source_target_pairs={{0,2},{2,0},{4,6},{6,4},{1,3},{3,1},{5,7},{7,5},{8,10},{10,8},{12,... | collective-permute-start | bytes 786440 | tf_op jit(solution)/shard_map/ppermute | solution.py:211
  46.4 8.6 %collective-permute-start.10 = (bf16[4,64,128]{2,1,0:T(8,128)(2,1)S(1)}, bf16[4,64,128]{2,1,0:T(8,128)(2,1)S(1)}, u32[]{:S(2)}, u32[]{:S(2)}) collective-permute-start(bf16[4,64,128]{2,1,0:T(8,128)(2,1)S(1)} %get-tuple-element.48), channel_id=1, source_target_pairs={{0,17},{1,16},{8,25},{9,24},{16,1},{17,0},{24,9},{25,8},{2,19},{3,... | collective-permute-start | bytes 196616 | tf_op jit(solution)/shard_map/ppermute | solution.py:211
  48.1 8.1 %collective-permute-start.11 = (bf16[4,64,128]{2,1,0:T(8,128)(2,1)S(1)}, bf16[4,64,128]{2,1,0:T(8,128)(2,1)S(1)}, u32[]{:S(2)}, u32[]{:S(2)}) collective-permute-start(bf16[4,64,128]{2,1,0:T(8,128)(2,1)S(1)} %get-tuple-element.49), channel_id=1, source_target_pairs={{0,16},{8,24},{16,0},{24,8},{1,17},{9,25},{17,1},{25,9},{2,18},{10... | collective-permute-start | bytes 196616 | tf_op jit(solution)/shard_map/ppermute | solution.py:211
  50.3 5.9 %collective-permute-start.12 = (bf16[4,64,128]{2,1,0:T(8,128)(2,1)S(1)}, bf16[4,64,128]{2,1,0:T(8,128)(2,1)S(1)}, u32[]{:S(2)}, u32[]{:S(2)}) collective-permute-start(bf16[4,64,128]{2,1,0:T(8,128)(2,1)S(1)} %get-tuple-element.50), channel_id=1, source_target_pairs={{0,1},{1,0},{2,3},{3,2},{4,5},{5,4},{6,7},{7,6},{8,9},{9,8},{10,11... | collective-permute-start | bytes 196616 | tf_op jit(solution)/shard_map/ppermute | solution.py:211
